TPU v7x, 128 devices: a whole 4x4x4 slice. The times are simulated.
128 devices in a mesh: row: 8 (over y_lo, z), col: 16 (over y_hi, x, core).
Axes of the slice: x: 4, y: 4 (y_hi: 2, y_lo: 2; y = y_hi * 2 + y_lo), z: 4, core: 2. Of those that a mesh axis runs over, the one named last changes fastest.
Arguments:
- embedding: float32 [16384, 256], P(('row', 'col')), may hold values from -6 to 6
- seed_cluster: int32 [16384], P(('row', 'col')), may hold values from 0 to 127
Outputs:
- log_member: float32 [16384, 128], P(('row', 'col'))
All inputs are finite; a program needn't handle non-finite values.
Results may differ from a plain program's by a relative error of at most 0.0003.
Values sent between devices are 32-bit elements; how exact they have to be, the bound alone decides.
No kernel may reach another device: no remote copies, remote signals or barrier semaphores. Data moves between devices by JAX's collectives and lax.ppermute only.
A program may use at most 64 MiB of HBM per device.

v0:
```python
import jax
import jax.numpy as jnp
from jax import lax
from jax.sharding import Mesh
from jax.sharding import PartitionSpec as P

CLUSTER_COUNT = 128
SWEEPS = 2
COL = ("col_0", "col_1", "col_2")
ROW = ("row_0", "row_1")
ROW_COL = ("row_0", "row_1", "col_0", "col_1", "col_2")


ANNEAL_TEMP_VALUE = 0.02


def from_everyone(x, axis):
    copies = jnp.broadcast_to(x, (lax.axis_size(axis), *x.shape))
    return lax.all_to_all(copies, axis, split_axis=0, concat_axis=0, tiled=True)


def in_order(blocks, dim):
    shape = list(blocks.shape[1:])
    shape[dim] *= blocks.shape[0]
    return jnp.moveaxis(blocks, 0, dim).reshape(shape)


def gathered_by_axis(x, axes, dim):
    far, near = axes
    blocks = from_everyone(from_everyone(x, far), near)
    return in_order(blocks.swapaxes(0, 1).reshape(-1, *x.shape), dim)


def gather_directly(x, axis, dim):
    blocks = from_everyone(x, axis)
    return in_order(blocks, dim)


def padded_to(lines, peers):
    spare = -len(lines) % peers
    return jnp.pad(lines, [(0, spare)] + [(0, 0)] * (lines.ndim - 1))


def in_blocks(x, dim, peers):
    before, after = (x.shape[:dim], x.shape[dim + 1 :])
    return jnp.moveaxis(x.reshape(*before, peers, -1, *after), dim, 0)


def sent_and_summed(x, axis, dim):
    peers = lax.axis_size(axis)
    blocks = lax.all_to_all(in_blocks(x, dim, peers), axis, 0, 0, tiled=True)
    return jnp.sum(blocks, axis=0)


def sum_in_two_steps(x, axes, dim):
    far, near = axes
    own = sent_and_summed(in_blocks(x, dim, lax.axis_size(far)), near, dim + 1)
    return jnp.sum(lax.all_to_all(own, far, 0, 0, tiled=True), axis=0)


def total_of(x, axes):
    lines = x.reshape(-1, x.shape[-1])
    padded = padded_to(lines, lax.axis_size(axes[0]) * lax.axis_size(axes[1]))
    whole = gathered_by_axis(sum_in_two_steps(padded, axes, 0), axes, 0)
    return lax.slice_in_dim(whole, 0, len(lines)).reshape(x.shape)


def by_axis(x, axes):
    for axis in axes:
        x = lax.psum(x, axis)
    return x


def shards(embedding, seed_cluster):
    per_device = embedding.shape[0]
    row_coords = gathered_by_axis(embedding, (("col_0", "col_1"), "col_2"), 0)
    col_coords, col_seeds = (
        gather_directly(embedding, ROW, 0),
        gather_directly(seed_cluster, ROW, 0),
    )
    row_sq = jnp.sum(row_coords * row_coords, axis=1)
    col_sq = jnp.sum(col_coords * col_coords, axis=1)
    inner = jnp.dot(row_coords, col_coords.T, precision=lax.Precision.HIGHEST)
    distance = jnp.sqrt(row_sq[:, None] + col_sq[None, :] - 2.0 * inner + 1.0)
    cluster_labels = jnp.arange(CLUSTER_COUNT, dtype=jnp.int32)
    member_cols = (
        0.5 * (col_seeds[:, None] == cluster_labels[None, :]).astype(jnp.float32)
        + 0.5 / CLUSTER_COUNT
    )
    member_own = (
        0.5 * (seed_cluster[:, None] == cluster_labels[None, :]).astype(jnp.float32)
        + 0.5 / CLUSTER_COUNT
    )
    log_member = jnp.zeros((per_device, CLUSTER_COUNT), jnp.float32)
    for sweep in range(SWEEPS):
        columns = member_cols
        summed_weights = total_of(
            jnp.dot(distance, columns, precision=lax.Precision.HIGHEST),
            (("col_0", "col_1"), "col_2"),
        )
        attraction = lax.dynamic_slice_in_dim(
            summed_weights, lax.axis_index(COL) * per_device, per_device, 0
        )
        counts, cohesion = (
            by_axis(jnp.sum(member_own, axis=0), ROW_COL),
            by_axis(jnp.sum(member_own * attraction, axis=0), ROW_COL),
        )
        pair_energy = attraction / counts[None, :] - cohesion[None, :] / (
            2.0 * counts[None, :] ** 2
        )
        member_logits = -pair_energy / ANNEAL_TEMP_VALUE
        highest = jnp.max(member_logits, axis=1, keepdims=True)
        log_member = (
            member_logits
            - highest
            - jnp.log(jnp.sum(jnp.exp(member_logits - highest), axis=1, keepdims=True))
        )
        member_own = jnp.exp(log_member)
        if sweep + 1 < SWEEPS:
            member_cols = gather_directly(member_own, ROW, 0)
    return log_member


def solution(mesh):
    finer = Mesh(mesh.devices.reshape(2, 4, 2, 4, 2), ("row_0", "row_1", "col_0", "col_1", "col_2"))
    placed = (P(ROW_COL, None), P(ROW_COL))
    return jax.shard_map(
        shards, mesh=finer, in_specs=placed, out_specs=P(ROW_COL, None), check_vma=False
    )
```

profile of v0, /device:TPU:1, one launch (start us, length us, event | category | flops | bytes accessed | tf_op | source)
XLA Modules:
  0.0 247.6 jit_solution(4716282031314174073)
XLA Ops:
  2.0 23.8 %all_to_all.66 = f32[8,128,256]{2,1,0:T(8,128)S(1)} all-to-all(f32[8,128,256]{2,1,0:T(8,128)} %broadcast_in_dim.16), channel_id=1, replica_groups=mesh['row_0'=2,'row_1'=4,'col_0'=2,'col_1'=4,'col_2'=2] {'col_0','col_1'}, dimensions={0} | all-to-all | bytes 2097152 | tf_op jit(solution)/shard_map/all_to_all | solution.py:19
  26.0 6.9 %all_to_all.67 = f32[2,8,128,256]{3,2,1,0:T(8,128)S(1)} all-to-all(f32[2,8,128,256]{3,2,1,0:T(8,128)S(1)} %broadcast_in_dim.17), channel_id=1, replica_groups=mesh['row_0'=2,'row_1'=4,'col_0'=2,'col_1'=4,'col_2'=2] {'col_2'}, dimensions={0} | all-to-all | bytes 4194304 | tf_op jit(solution)/shard_map/all_to_all | solution.py:19
  32.9 5.1 %all-to-all-start.2 = ((f32[8,128,256]{2,1,0:T(8,128)}), f32[8,128,256]{2,1,0:T(8,128)S(1)}, u32[]{:S(2)}, u32[]{:S(2)}) async-start(f32[8,128,256]{2,1,0:T(8,128)} %broadcast_in_dim.16), calls=%async_computation.2 | async-start | bytes 2097152 | tf_op jit(solution)/shard_map/all_to_all | solution.py:19
  40.0 13.0 %all-to-all-done.2 = f32[8,128,256]{2,1,0:T(8,128)S(1)} async-done(((f32[8,128,256]{2,1,0:T(8,128)}), f32[8,128,256]{2,1,0:T(8,128)S(1)}, u32[]{:S(2)}, u32[]{:S(2)}) %all-to-all-start.2) | async-done | bytes 1048608 | tf_op jit(solution)/shard_map/all_to_all | solution.py:19
  57.5 13.6 %add_sqrt_fusion = f32[2048,1024]{1,0:T(8,128)} fusion(f32[2048,256]{1,0:T(8,128)} %bitcast.38, f32[1024,256]{1,0:T(8,128)S(1)} %bitcast.35, f32[1024]{0:T(1024)S(1)} %bitcast.50, f32[2048]{0:T(1024)S(1)} %bitcast.49), kind=kOutput, calls=%fused_computation | convolution fusion | flops 6450839552 | bytes 11546624 | tf_op jit(solution)/shard_map/dot_general | solution.py:83
  71.1 9.2 %fusion.1 = f32[2048,128]{1,0:T(8,128)S(1)} fusion(f32[2048,1024]{1,0:T(8,128)} %add_sqrt_fusion, s32[1024]{0:T(1024)S(1)} %bitcast.48), kind=kOutput, calls=%fused_computation.6 | convolution fusion | flops 3221618688 | bytes 9441280 | tf_op jit(solution)/shard_map/dot_general | solution.py:98
  80.4 5.0 %all_to_all.68 = f32[2,8,128,128]{3,2,1,0:T(8,128)S(1)} all-to-all(f32[2,8,128,128]{3,2,1,0:T(8,128)S(1)} %bitcast.36), channel_id=1, replica_groups=mesh['row_0'=2,'row_1'=4,'col_0'=2,'col_1'=4,'col_2'=2] {'col_2'}, dimensions={0} | all-to-all | bytes 2097152 | tf_op jit(solution)/shard_map/all_to_all | solution.py:51
  85.4 13.9 %all_to_all.69 = f32[8,128,128]{2,1,0:T(8,128)S(1)} all-to-all(f32[8,128,128]{2,1,0:T(8,128)S(1)} %reduce_sum.110), channel_id=1, replica_groups=mesh['row_0'=2,'row_1'=4,'col_0'=2,'col_1'=4,'col_2'=2] {'col_0','col_1'}, dimensions={0} | all-to-all | bytes 1048576 | tf_op jit(solution)/shard_map/all_to_all | solution.py:58
  103.8 11.4 %all-to-all-done.6 = f32[8,128,128]{2,1,0:T(8,128)S(1)} async-done(((f32[8,128,128]{2,1,0:T(8,128)}), f32[8,128,128]{2,1,0:T(8,128)S(1)}, u32[]{:S(2)}, u32[]{:S(2)}) %all-to-all-start.6) | async-done | bytes 524320 | tf_op jit(solution)/shard_map/all_to_all | solution.py:19
  115.3 5.3 %all_to_all.70 = f32[2,8,128,128]{3,2,1,0:T(8,128)S(1)} all-to-all(f32[2,8,128,128]{3,2,1,0:T(8,128)S(1)} %broadcast_in_dim.20), channel_id=1, replica_groups=mesh['row_0'=2,'row_1'=4,'col_0'=2,'col_1'=4,'col_2'=2] {'col_2'}, dimensions={0} | all-to-all | bytes 2097152 | tf_op jit(solution)/shard_map/all_to_all | solution.py:19
  125.0 8.4 %all-reduce.3 = (f32[128]{0:T(128)S(1)}, f32[128]{0:T(128)S(1)}) all-reduce(f32[128]{0:T(128)S(1)} %get-tuple-element.27, f32[128]{0:T(128)S(1)} %get-tuple-element.28), channel_id=1, replica_groups=mesh['row_0'=2,'row_1'=4,'col_0'=2,'col_1'=4,'col_2'=2] {'row_1'}, use_global_device_ids=true, to_apply=%region_12.13 | all-reduce | flops 256 | bytes 2048 | tf_op jit(solution)/shard_map/psum | solution.py:70
  133.5 5.3 %all-reduce.7 = (f32[128]{0:T(128)S(1)}, f32[128]{0:T(128)S(1)}) all-reduce(f32[128]{0:T(128)S(1)} %get-tuple-element.15, f32[128]{0:T(128)S(1)} %get-tuple-element.16), channel_id=1, replica_groups=mesh['row_0'=2,'row_1'=4,'col_0'=2,'col_1'=4,'col_2'=2] {'col_0'}, use_global_device_ids=true, to_apply=%region_13.14 | all-reduce | flops 256 | bytes 2048 | tf_op jit(solution)/shard_map/psum | solution.py:70
  138.7 6.6 %all-reduce.1 = (f32[128]{0:T(128)S(1)}, f32[128]{0:T(128)S(1)}) all-reduce(f32[128]{0:T(128)S(1)} %get-tuple-element.23, f32[128]{0:T(128)S(1)} %get-tuple-element.24), channel_id=1, replica_groups=mesh['row_0'=2,'row_1'=4,'col_0'=2,'col_1'=4,'col_2'=2] {'col_1'}, use_global_device_ids=true, to_apply=%region_14.15 | all-reduce | flops 256 | bytes 2048 | tf_op jit(solution)/shard_map/psum | solution.py:70
  145.3 9.0 %all-reduce.5 = (f32[128]{0:T(128)S(1)}, f32[128]{0:T(128)S(1)}) all-reduce(f32[128]{0:T(128)S(1)} %get-tuple-element.11, f32[128]{0:T(128)S(1)} %get-tuple-element.12), channel_id=1, replica_groups=mesh['row_0'=2,'row_1'=4,'col_0'=2,'col_1'=4,'col_2'=2] {'col_2'}, use_global_device_ids=true, to_apply=%region_15.16 | all-reduce | flops 256 | bytes 2048 | tf_op jit(solution)/shard_map/psum | solution.py:70
  154.8 11.6 %all_to_all.71 = f32[8,128,128]{2,1,0:T(8,128)S(1)} all-to-all(f32[8,128,128]{2,1,0:T(8,128)S(1)} %broadcast_in_dim.21), channel_id=1, replica_groups=mesh['row_0'=2,'row_1'=4,'col_0'=2,'col_1'=4,'col_2'=2] {'row_0','row_1'}, dimensions={0} | all-to-all | bytes 1048576 | tf_op jit(solution)/shard_map/all_to_all | solution.py:19
  166.4 9.1 %convolution_bitcast_fusion = f32[2,8,128,128]{3,2,0,1:T(8,128)S(1)} fusion(f32[8,2,128,1024]{3,2,1,0:T(8,128)} %bitcast.33, f32[1024,128,1,1]{1,0,3,2:T(8,128)S(1)} %bitcast.37), kind=kOutput, calls=%fused_computation.3 | convolution fusion | flops 3221225472 | bytes 9961472 | tf_op jit(solution)/shard_map/dot_general | solution.py:98
  175.6 6.4 %all_to_all.72 = f32[2,8,128,128]{3,2,1,0:T(8,128)S(1)} all-to-all(f32[2,8,128,128]{3,2,1,0:T(8,128)S(1)} %copy.14), channel_id=1, replica_groups=mesh['row_0'=2,'row_1'=4,'col_0'=2,'col_1'=4,'col_2'=2] {'col_2'}, dimensions={0} | all-to-all | bytes 2097152 | tf_op jit(solution)/shard_map/all_to_all | solution.py:51
  182.0 13.8 %all_to_all.73 = f32[8,128,128]{2,1,0:T(8,128)S(1)} all-to-all(f32[8,128,128]{2,1,0:T(8,128)S(1)} %reduce_sum.115), channel_id=1, replica_groups=mesh['row_0'=2,'row_1'=4,'col_0'=2,'col_1'=4,'col_2'=2] {'col_0','col_1'}, dimensions={0} | all-to-all | bytes 1048576 | tf_op jit(solution)/shard_map/all_to_all | solution.py:58
  195.9 12.7 %all_to_all.74 = f32[8,128,128]{2,1,0:T(8,128)S(1)} all-to-all(f32[8,128,128]{2,1,0:T(8,128)S(1)} %broadcast_in_dim.22), channel_id=1, replica_groups=mesh['row_0'=2,'row_1'=4,'col_0'=2,'col_1'=4,'col_2'=2] {'col_0','col_1'}, dimensions={0} | all-to-all | bytes 1048576 | tf_op jit(solution)/shard_map/all_to_all | solution.py:19
  208.8 6.4 %all_to_all.75 = f32[2,8,128,128]{3,2,1,0:T(8,128)S(1)} all-to-all(f32[2,8,128,128]{3,2,1,0:T(8,128)S(1)} %broadcast_in_dim.23), channel_id=1, replica_groups=mesh['row_0'=2,'row_1'=4,'col_0'=2,'col_1'=4,'col_2'=2] {'col_2'}, dimensions={0} | all-to-all | bytes 2097152 | tf_op jit(solution)/shard_map/all_to_all | solution.py:19
  219.2 6.5 %all-reduce.2 = (f32[128]{0:T(128)S(1)}, f32[128]{0:T(128)S(1)}) all-reduce(f32[128]{0:T(128)S(1)} %get-tuple-element.25, f32[128]{0:T(128)S(1)} %get-tuple-element.26), channel_id=1, replica_groups=mesh['row_0'=2,'row_1'=4,'col_0'=2,'col_1'=4,'col_2'=2] {'row_1'}, use_global_device_ids=true, to_apply=%region_28.29 | all-reduce | flops 256 | bytes 2048 | tf_op jit(solution)/shard_map/psum | solution.py:70
  225.7 5.3 %all-reduce.6 = (f32[128]{0:T(128)S(1)}, f32[128]{0:T(128)S(1)}) all-reduce(f32[128]{0:T(128)S(1)} %get-tuple-element.13, f32[128]{0:T(128)S(1)} %get-tuple-element.14), channel_id=1, replica_groups=mesh['row_0'=2,'row_1'=4,'col_0'=2,'col_1'=4,'col_2'=2] {'col_0'}, use_global_device_ids=true, to_apply=%region_29.30 | all-reduce | flops 256 | bytes 2048 | tf_op jit(solution)/shard_map/psum | solution.py:70
  230.9 6.8 %all-reduce = (f32[128]{0:T(128)S(1)}, f32[128]{0:T(128)S(1)}) all-reduce(f32[128]{0:T(128)S(1)} %get-tuple-element.21, f32[128]{0:T(128)S(1)} %get-tuple-element.22), channel_id=1, replica_groups=mesh['row_0'=2,'row_1'=4,'col_0'=2,'col_1'=4,'col_2'=2] {'col_1'}, use_global_device_ids=true, to_apply=%region_30.31 | all-reduce | flops 256 | bytes 2048 | tf_op jit(solution)/shard_map/psum | solution.py:70
  237.7 8.8 %all-reduce.4 = (f32[128]{0:T(128)S(1)}, f32[128]{0:T(128)S(1)}) all-reduce(f32[128]{0:T(128)S(1)} %get-tuple-element.9, f32[128]{0:T(128)S(1)} %get-tuple-element.10), channel_id=1, replica_groups=mesh['row_0'=2,'row_1'=4,'col_0'=2,'col_1'=4,'col_2'=2] {'col_2'}, use_global_device_ids=true, to_apply=%region_31.32 | all-reduce | flops 256 | bytes 2048 | tf_op jit(solution)/shard_map/psum | solution.py:70
  (38 shorter events, 23.6 us)
Async XLA Ops:
  25.8 27.2 %copy-start = (s32[128]{0:T(128)S(1)}, s32[128]{0:T(128)}, u32[]{:S(2)}) copy-start(s32[128]{0:T(128)} %param.3) | copy-start | bytes 1540
  32.9 20.1 %all-to-all-start.2 = ((f32[8,128,256]{2,1,0:T(8,128)}), f32[8,128,256]{2,1,0:T(8,128)S(1)}, u32[]{:S(2)}, u32[]{:S(2)}) async-start(f32[8,128,256]{2,1,0:T(8,128)} %broadcast_in_dim.16), calls=%async_computation.2 | async-start | bytes 2097152 | tf_op jit(solution)/shard_map/all_to_all | solution.py:19
  53.6 17.5 %all-to-all-start.3 = ((s32[8,1,128]{2,1,0:T(1,128)}), s32[8,1,128]{2,1,0:T(1,128)S(1)}, u32[]{:S(2)}, u32[]{:S(2)}) async-start(s32[8,1,128]{2,1,0:T(1,128)} %broadcast_in_dim.18), calls=%async_computation.3 | async-start | bytes 8192 | tf_op jit(solution)/shard_map/all_to_all | solution.py:19
  100.3 14.9 %all-to-all-start.6 = ((f32[8,128,128]{2,1,0:T(8,128)}), f32[8,128,128]{2,1,0:T(8,128)S(1)}, u32[]{:S(2)}, u32[]{:S(2)}) async-start(f32[8,128,128]{2,1,0:T(8,128)} %broadcast_in_dim.19), calls=%async_computation.6 | async-start | bytes 1048576 | tf_op jit(solution)/shard_map/all_to_all | solution.py:19
where the time goes:
time: 249 us; the launch traced here: 248 us
  blocking collectives  170 us (68%)
  matrix products  31.9 us (13%)
  waiting for transfers between devices  24.4 us (10%)
  starting transfers between devices  12.3 us (5%)
  local copies, waits for them, and re-layouts  5.86 us (2%)
  other arithmetic  2.54 us (1%)
    all_to_all x6, blocking collectives, from_everyone(): return lax.all_to_all(copies, axis, split_axis=0, concat_axis=0, tiled=True)  66.7 us
    psum x10, blocking collectives, by_axis(): x = lax.psum(x, axis)  64.7 us
    all_to_all x2, blocking collectives, sum_in_two_steps(): return jnp.sum(lax.all_to_all(own, far, 0, 0, tiled=True), axis=0)  27.7 us
    all_to_all x3, waiting for transfers between devices, from_everyone(): return lax.all_to_all(copies, axis, split_axis=0, concat_axis=0, tiled=True)  24.4 us
    dot_general x2, matrix products, shards(): jnp.dot(distance, columns, precision=lax.Precision.HIGHEST)  18.3 us
    dot_general x1, matrix products, shards(): inner = jnp.dot(row_coords, col_coords.T, precision=lax.Precision.HIGHEST)  13.6 us
    all_to_all x3, starting transfers between devices, from_everyone(): return lax.all_to_all(copies, axis, split_axis=0, concat_axis=0, tiled=True)  12.3 us
    all_to_all x2, blocking collectives, sent_and_summed(): blocks = lax.all_to_all(in_blocks(x, dim, peers), axis, 0, 0, tiled=True)  11.3 us
  transfers between devices with their start and end apart: 3, of which 2 were waited for; matrix products, arithmetic and copies ran while one was open for 6% of the time, Pallas kernels for 0%

commit v1 on v0

v1 whole, which is shorter than its diff:
```python
import itertools

import jax
import jax.numpy as jnp
from jax import lax
from jax.sharding import Mesh
from jax.sharding import PartitionSpec as P

CLUSTER_COUNT = 128
ANNEAL_TEMP_VALUE = 0.02
SIDE = 8

EVERY = ("y_lo", "z", "y_hi", "x", "core")
SIZES = (2, 4, 2, 4, 2)


def place(y_lo, z, y_hi, x, core):
    return (((y_lo * 4 + z) * 2 + y_hi) * 4 + x) * 2 + core


def column_groups():
    groups = []
    for pair, x, core in itertools.product(range(2), range(4), range(2)):
        groups.append([place(lo, z, lo ^ pair, x, core) for lo in range(2) for z in range(4)])
    return groups


COLUMN_GROUPS = column_groups()


def exchange_rows(blocks):
    return lax.all_to_all(blocks, ("y_lo", "x"), 0, 0, tiled=True)


def exchange_columns(blocks):
    return lax.all_to_all(blocks, EVERY, 0, 0, axis_index_groups=COLUMN_GROUPS, tiled=True)


def copies(x, count):
    return jnp.broadcast_to(x, (count, *x.shape))


def other_core(x):
    return lax.ppermute(x, "core", [(0, 1), (1, 0)])


def first_member(seeds):
    labels = jnp.arange(CLUSTER_COUNT, dtype=jnp.float32)
    return 0.5 * (seeds[:, None] == labels[None, :]).astype(jnp.float32) + 0.5 / CLUSTER_COUNT


def log_softmax_energy(attraction, counts, cohesion):
    energy = attraction / counts - cohesion / (2.0 * counts**2)
    logits = -energy / ANNEAL_TEMP_VALUE
    highest = jnp.max(logits, axis=1, keepdims=True)
    return logits - highest - jnp.log(jnp.sum(jnp.exp(logits - highest), axis=1, keepdims=True))


def points_of(blocks, points):
    return blocks[:, :points].reshape(-1, blocks.shape[-1])


def shards(embedding, seed_cluster):
    points, width = embedding.shape
    side = jnp.concatenate([seed_cluster.astype(jnp.float32), jnp.sum(embedding * embedding, axis=1)])
    block = jnp.concatenate([embedding, jnp.broadcast_to(side, (SIDE, width))], axis=0)
    spread = copies(block, 8)
    rows = exchange_rows(spread)
    columns = [exchange_columns(spread)]
    columns.append(other_core(columns[0]))

    row_points, row_side = points_of(rows, points), rows[:, points]
    row_seeds, row_sq = row_side[:, :points].reshape(-1), row_side[:, points:].reshape(-1)
    distances, weighted = [], 0.0
    for part in columns:
        part_side = part[:, points]
        seeds, sq = part_side[:, :points].reshape(-1), part_side[:, points:].reshape(-1)
        inner = jnp.dot(row_points, points_of(part, points).T, precision=lax.Precision.HIGH)
        distance = jnp.sqrt(row_sq[:, None] + sq[None, :] - 2.0 * inner + 1.0)
        distances.append(distance)
        weighted = weighted + jnp.dot(distance, first_member(seeds), precision=lax.Precision.HIGH)

    own = first_member(seed_cluster.astype(jnp.float32))
    small = jnp.stack([jnp.sum(first_member(row_seeds) * weighted, axis=0), jnp.sum(own, axis=0)])

    def summed(weighted, small):
        tail = copies(jnp.pad(small, ((0, SIDE - len(small)), (0, 0))), 8)
        blocks = jnp.concatenate([weighted.reshape(8, points, -1), tail], axis=1)
        return jnp.sum(exchange_rows(blocks), axis=0)

    first = summed(weighted, small)
    firsts = [exchange_columns(copies(first, 8))]
    firsts.append(other_core(firsts[0]))
    totals = sum(jnp.sum(part[:, points : points + 2], axis=0) for part in firsts)
    cohesion, counts = totals[:1], totals[1:]

    weighted, sizes = 0.0, 0.0
    for part, distance in zip(firsts, distances):
        member = jnp.exp(log_softmax_energy(points_of(part, points), counts, cohesion))
        sizes = sizes + jnp.sum(member, axis=0, keepdims=True)
        weighted = weighted + jnp.dot(distance, member, precision=lax.Precision.HIGH)
    own = jnp.exp(log_softmax_energy(first[:points], counts, cohesion))

    second = summed(weighted, sizes)
    attraction, counts = second[:points], second[points : points + 1]
    parts = lax.all_to_all(copies(jnp.sum(own * attraction, axis=0, keepdims=True), 128), EVERY, 0, 0, tiled=True)
    return log_softmax_energy(attraction, counts, jnp.sum(parts, axis=0))


def solution(mesh):
    finer = Mesh(mesh.devices.reshape(SIZES), EVERY)
    return jax.shard_map(
        shards, mesh=finer, in_specs=(P(EVERY, None), P(EVERY)), out_specs=P(EVERY, None), check_vma=False
    )
```

time: 249 us -> 131 us (0.53)
  blocking collectives: 170 us -> 62.2 us
  matrix products: 31.9 us -> 19 us
  other arithmetic: 2.54 us -> 7.9 us
  local copies, waits for them, and re-layouts: 5.86 us -> 1.48 us
    psum x10 -> x0, blocking collectives: 64.7 us -> none  [by_axis(): x = lax.psum(x, axis)]
    all_to_all x10 -> x4, blocking collectives: 106 us -> 62.2 us  [the longest x2 37.2 us: exchange_columns(): lax.all_to_all(blocks, EVERY, 0, 0, axis_index_groups=COLUMN_GROUPS, tile...]
    dot_general x3 -> x6, matrix products: 31.9 us -> 19 us  [the longest x2 7.54 us: shards(): jnp.dot(distance, first_member(seeds), precision=lax.Precision.HIGH)]
    ppermute x0 -> x2, starting transfers between devices: none -> 6.37 us  [other_core(): return lax.ppermute(x, 'core', [(0, 1), (1, 0)])]
    all_to_all x3 -> x2, starting transfers between devices: 12.3 us -> 7.56 us  [exchange_rows(): return lax.all_to_all(blocks, ('y_lo', 'x'), 0, 0, tiled=True)]
    broadcast_in_dim x8 -> x6, local copies, waits for them, and re-layouts: 3.95 us -> 1.15 us  [the longest x5 1.15 us: copies(): return jnp.broadcast_to(x, (count, *x.shape))]
    all_to_all x3 -> x2, waiting for transfers between devices: 24.4 us -> 23.9 us  [exchange_rows(): return lax.all_to_all(blocks, ('y_lo', 'x'), 0, 0, tiled=True)]
  transfers between devices with their start and end apart: 3 -> 4, of which waited for: 2 -> 3; matrix products, arithmetic and copies ran while one was open for 6% -> 5% of each run, Pallas kernels for 0% -> 0%
where the time goes in v1:
time: 131 us; the launch traced here: 130 us
  blocking collectives  62.2 us (47%)
  waiting for transfers between devices  25.5 us (19%)
  matrix products  19 us (15%)
  starting transfers between devices  13.9 us (11%)
  other arithmetic  7.9 us (6%)
  local copies, waits for them, and re-layouts  1.48 us (1%)
    all_to_all x2, blocking collectives, exchange_columns(): lax.all_to_all(blocks, EVERY, 0, 0, axis_index_groups=COLUMN_GROUPS, tile...  37.2 us
    all_to_all x2, waiting for transfers between devices, exchange_rows(): return lax.all_to_all(blocks, ('y_lo', 'x'), 0, 0, tiled=True)  23.9 us
    all_to_all x1, blocking collectives, shards(): lax.all_to_all(copies(jnp.sum(own * attraction, axis=0, keepdims=True), 1...  13.2 us
    all_to_all x1, blocking collectives, exchange_rows(): return lax.all_to_all(blocks, ('y_lo', 'x'), 0, 0, tiled=True)  11.7 us
    all_to_all x2, starting transfers between devices, exchange_rows(): return lax.all_to_all(blocks, ('y_lo', 'x'), 0, 0, tiled=True)  7.56 us
    dot_general x2, matrix products, shards(): jnp.dot(distance, first_member(seeds), precision=lax.Precision.HIGH)  7.54 us
    dot_general x2, matrix products, shards(): jnp.dot(distance, member, precision=lax.Precision.HIGH)  7.52 us
    ppermute x2, starting transfers between devices, other_core(): return lax.ppermute(x, 'core', [(0, 1), (1, 0)])  6.37 us
  transfers between devices with their start and end apart: 4, of which 3 were waited for; matrix products, arithmetic and copies ran while one was open for 5% of the time, Pallas kernels for 0%

profile of v1, /device:TPU:1, one launch (start us, length us, event | category | flops | bytes accessed | tf_op | source)
XLA Modules:
  0.0 130.3 jit_solution(14426314238257837002)
XLA Ops:
  0.0 0.7 convert_element_type.4
  0.7 1.0 multiply_reduce_fusion.1
  1.7 0.9 pad_maximum_fusion.2
  2.6 1.1 broadcast_in_dim.13
  3.7 24.7 %all_to_all.30 = f32[8,136,256]{2,1,0:T(8,128)S(1)} all-to-all(f32[8,136,256]{2,1,0:T(8,128)} %broadcast_in_dim.13), channel_id=1, replica_groups={{0,16,32,48,72,88,104,120},{1,17,33,49,73,89,105,121},{2,18,34,50,74,90..., dimensions={0} | all-to-all | bytes 2228224 | tf_op jit(solution)/shard_map/all_to_all | solution.py:36
  28.3 4.0 %all-to-all-start = ((f32[8,136,256]{2,1,0:T(8,128)}), f32[8,136,256]{2,1,0:T(8,128)S(1)}, u32[]{:S(2)}, u32[]{:S(2)}) async-start(f32[8,136,256]{2,1,0:T(8,128)} %broadcast_in_dim.13), calls=%async_computation | async-start | bytes 2228224 | tf_op jit(solution)/shard_map/all_to_all | solution.py:32
  32.5 2.7 %collective-permute-start = (f32[8,136,256]{2,1,0:T(8,128)S(1)}, f32[8,136,256]{2,1,0:T(8,128)S(1)}, u32[]{:S(2)}, u32[]{:S(2)}) collective-permute-start(f32[8,136,256]{2,1,0:T(8,128)S(1)} %all_to_all.30), channel_id=1, source_target_pairs={{0,1},{1,0},{2,3},{3,2},{4,5},{5,4},{6,7},{7,6},{8,9},{9,8},{10,11... | collective-permute-start | bytes 3342344 | tf_op jit(solution)/shard_map/ppermute | solution.py:44
  35.2 13.7 %all-to-all-done = f32[8,136,256]{2,1,0:T(8,128)S(1)} async-done(((f32[8,136,256]{2,1,0:T(8,128)}), f32[8,136,256]{2,1,0:T(8,128)S(1)}, u32[]{:S(2)}, u32[]{:S(2)}) %all-to-all-start) | async-done | bytes 1114144 | tf_op jit(solution)/shard_map/all_to_all | solution.py:32
  49.1 2.0 %fusion.69 = f32[1024,1024]{1,0:T(8,128)S(1)} fusion(f32[1024,256]{1,0:T(8,128)S(1)} %bitcast.83, f32[1024,256]{1,0:T(8,128)S(1)} %bitcast.85), kind=kOutput, calls=%fused_computation.116 | convolution fusion | flops 1610612736 | bytes 6291456 | tf_op jit(solution)/shard_map/dot_general | solution.py:78
  51.0 3.8 %fusion.1 = f32[1024,128]{1,0:T(8,128)S(1)} fusion(f32[1024,1024]{1,0:T(8,128)S(1)} %fusion.69, f32[1024]{0:T(1024)S(1)} %get-tuple-element.18, f32[1024]{0:T(1024)S(1)} %get-tuple-element.14, f32[1024]{0:T(1024)S(1)} %get-tuple-element.17), kind=kOutput, calls=%fused_computation.3 | convolution fusion | flops 809893888 | bytes 4730880 | tf_op jit(solution)/shard_map/dot_general | solution.py:81
  55.0 2.0 %fusion.70 = f32[1024,1024]{1,0:T(8,128)S(1)} fusion(f32[1024,256]{1,0:T(8,128)S(1)} %bitcast.84, f32[1024,256]{1,0:T(8,128)S(1)} %bitcast.86), kind=kOutput, calls=%fused_computation.117 | convolution fusion | flops 1610612736 | bytes 6291456 | tf_op jit(solution)/shard_map/dot_general | solution.py:78
  56.9 3.8 %multiply_reduce_fusion = (f32[128]{0:T(128)S(1)}, f32[1024,128]{1,0:T(8,128)S(1)}) fusion(f32[1024]{0:T(1024)S(1)} %get-tuple-element.13, f32[1024,128]{1,0:T(8,128)S(1)} %fusion.1, f32[1024]{0:T(1024)S(1)} %get-tuple-element.15, f32[1024,1024]{1,0:T(8,128)S(1)} %fusion.70, f32[1024]{0:T(1024)S(1)} %get-tuple-element.16, f32[1024]{0:T(1024)S(1)} %get-tuple-element.14), kind=kOutput, calls=%fused_computation.46 | convolution fusion | flops 810680192 | bytes 5259776 | tf_op jit(solution)/shard_map/dot_general | solution.py:81
  60.8 11.7 %all_to_all.31 = f32[8,136,128]{2,1,0:T(8,128)S(1)} all-to-all(f32[8,136,128]{2,1,0:T(8,128)S(1)} %pad_maximum_fusion), channel_id=1, replica_groups=mesh['y_lo'=2,'z'=4,'y_hi'=2,'x'=4,'core'=2] {'y_lo','x'}, dimensions={0} | all-to-all | bytes 1114112 | tf_op jit(solution)/shard_map/all_to_all | solution.py:32
  72.6 12.5 %all_to_all.32 = f32[8,136,128]{2,1,0:T(8,128)S(1)} all-to-all(f32[8,136,128]{2,1,0:T(8,128)S(1)} %broadcast_in_dim.15), channel_id=1, replica_groups={{0,16,32,48,72,88,104,120},{1,17,33,49,73,89,105,121},{2,18,34,50,74,90..., dimensions={0} | all-to-all | bytes 1114112 | tf_op jit(solution)/shard_map/all_to_all | solution.py:36
  85.1 3.7 %collective-permute-start.1 = (f32[8,136,128]{2,1,0:T(8,128)S(1)}, f32[8,136,128]{2,1,0:T(8,128)S(1)}, u32[]{:S(2)}, u32[]{:S(2)}) collective-permute-start(f32[8,136,128]{2,1,0:T(8,128)S(1)} %all_to_all.32), channel_id=1, source_target_pairs={{0,1},{1,0},{2,3},{3,2},{4,5},{5,4},{6,7},{7,6},{8,9},{9,8},{10,11... | collective-permute-start | bytes 1671176 | tf_op jit(solution)/shard_map/ppermute | solution.py:44
  88.8 1.6 %collective-permute-done.1 = f32[8,136,128]{2,1,0:T(8,128)S(1)} collective-permute-done((f32[8,136,128]{2,1,0:T(8,128)S(1)}, f32[8,136,128]{2,1,0:T(8,128)S(1)}, u32[]{:S(2)}, u32[]{:S(2)}) %collective-permute-start.1) | collective-permute-done | bytes 557088 | tf_op jit(solution)/shard_map/ppermute | solution.py:44
  91.9 1.0 fusion.27
  92.9 3.7 %fusion = f32[1024,128]{1,0:T(8,128)S(1)} fusion(f32[1024,128]{1,0:T(8,128)S(1)} %get-tuple-element.24, f32[1024,1024]{1,0:T(8,128)S(1)} %copy-done.1, f32[1024]{0:T(1024)S(1)} %get-tuple-element.18, f32[1024]{0:T(1024)S(1)} %get-tuple-element.14), kind=kOutput, calls=%fused_computation.2 | convolution fusion | flops 809500672 | bytes 5251072 | tf_op jit(solution)/shard_map/dot_general | solution.py:101
  97.0 3.8 %fusion.21 = f32[1024,128]{1,0:T(8,128)S(1)} fusion(f32[1024,128]{1,0:T(8,128)S(1)} %fusion, f32[1024,128]{1,0:T(8,128)S(1)} %get-tuple-element.23, f32[1024,1024]{1,0:T(8,128)S(1)} %copy-done.3, f32[1024]{0:T(1024)S(1)} %get-tuple-element.16, f32[1024]{0:T(1024)S(1)} %get-tuple-element.14), kind=kOutput, calls=%fused_computation.23 | convolution fusion | flops 809631744 | bytes 5775360 | tf_op jit(solution)/shard_map/dot_general | solution.py:101
  100.8 0.8 pad_maximum_fusion.1
  101.6 3.5 %all-to-all-start.4 = ((f32[8,136,128]{2,1,0:T(8,128)}), f32[8,136,128]{2,1,0:T(8,128)S(1)}, u32[]{:S(2)}, u32[]{:S(2)}) async-start(f32[8,136,128]{2,1,0:T(8,128)} %pad_maximum_fusion.1), calls=%async_computation.4 | async-start | bytes 1114112 | tf_op jit(solution)/shard_map/all_to_all | solution.py:32
  105.5 10.2 %all-to-all-done.4 = f32[8,136,128]{2,1,0:T(8,128)S(1)} async-done(((f32[8,136,128]{2,1,0:T(8,128)}), f32[8,136,128]{2,1,0:T(8,128)S(1)}, u32[]{:S(2)}, u32[]{:S(2)}) %all-to-all-start.4) | async-done | bytes 557088 | tf_op jit(solution)/shard_map/all_to_all | solution.py:32
  115.9 13.2 %all_to_all.33 = f32[128,1,128]{2,1,0:T(1,128)S(1)} all-to-all(f32[128,1,128]{2,1,0:T(1,128)S(1)} %broadcast_in_dim.17), channel_id=1, replica_groups=mesh['y_lo'=2,'z'=4,'y_hi'=2,'x'=4,'core'=2] {'y_lo','z','y_hi','x','core'}, dimensions={0} | all-to-all | bytes 131072 | tf_op jit(solution)/shard_map/all_to_all | solution.py:106
  129.5 0.7 subtract_subtract_fusion
  (53 shorter events, 3.2 us)
Async XLA Ops:
  28.3 20.5 %all-to-all-start = ((f32[8,136,256]{2,1,0:T(8,128)}), f32[8,136,256]{2,1,0:T(8,128)S(1)}, u32[]{:S(2)}, u32[]{:S(2)}) async-start(f32[8,136,256]{2,1,0:T(8,128)} %broadcast_in_dim.13), calls=%async_computation | async-start | bytes 2228224 | tf_op jit(solution)/shard_map/all_to_all | solution.py:32
  32.5 22.3 %collective-permute-start = (f32[8,136,256]{2,1,0:T(8,128)S(1)}, f32[8,136,256]{2,1,0:T(8,128)S(1)}, u32[]{:S(2)}, u32[]{:S(2)}) collective-permute-start(f32[8,136,256]{2,1,0:T(8,128)S(1)} %all_to_all.30), channel_id=1, source_target_pairs={{0,1},{1,0},{2,3},{3,2},{4,5},{5,4},{6,7},{7,6},{8,9},{9,8},{10,11... | collective-permute-start | bytes 3342344 | tf_op jit(solution)/shard_map/ppermute | solution.py:44
  51.0 3.9 %copy-start = (f32[1024,1024]{1,0:T(8,128)}, f32[1024,1024]{1,0:T(8,128)S(1)}, u32[]{:S(2)}) copy-start(f32[1024,1024]{1,0:T(8,128)S(1)} %fusion.69) | copy-start | bytes 12582916
  56.9 3.8 %copy-start.2 = (f32[1024,1024]{1,0:T(8,128)}, f32[1024,1024]{1,0:T(8,128)S(1)}, u32[]{:S(2)}) copy-start(f32[1024,1024]{1,0:T(8,128)S(1)} %fusion.70) | copy-start | bytes 12582916
  72.5 20.3 %copy-start.1 = (f32[1024,1024]{1,0:T(8,128)S(1)}, f32[1024,1024]{1,0:T(8,128)}, u32[]{:S(2)}) copy-start(f32[1024,1024]{1,0:T(8,128)} %copy-done) | copy-start | bytes 12582916
  85.1 5.3 %collective-permute-start.1 = (f32[8,136,128]{2,1,0:T(8,128)S(1)}, f32[8,136,128]{2,1,0:T(8,128)S(1)}, u32[]{:S(2)}, u32[]{:S(2)}) collective-permute-start(f32[8,136,128]{2,1,0:T(8,128)S(1)} %all_to_all.32), channel_id=1, source_target_pairs={{0,1},{1,0},{2,3},{3,2},{4,5},{5,4},{6,7},{7,6},{8,9},{9,8},{10,11... | collective-permute-start | bytes 1671176 | tf_op jit(solution)/shard_map/ppermute | solution.py:44
  92.8 4.1 %copy-start.3 = (f32[1024,1024]{1,0:T(8,128)S(1)}, f32[1024,1024]{1,0:T(8,128)}, u32[]{:S(2)}) copy-start(f32[1024,1024]{1,0:T(8,128)} %copy-done.2) | copy-start | bytes 12582916
  101.6 14.1 %all-to-all-start.4 = ((f32[8,136,128]{2,1,0:T(8,128)}), f32[8,136,128]{2,1,0:T(8,128)S(1)}, u32[]{:S(2)}, u32[]{:S(2)}) async-start(f32[8,136,128]{2,1,0:T(8,128)} %pad_maximum_fusion.1), calls=%async_computation.4 | async-start | bytes 1114112 | tf_op jit(solution)/shard_map/all_to_all | solution.py:32

commit v2 on v1

--- a/solution.py
+++ b/solution.py
@@ -36,6 +36,33 @@
     return lax.all_to_all(blocks, EVERY, 0, 0, axis_index_groups=COLUMN_GROUPS, tiled=True)
 
 
+def row_peers(x):
+    found = []
+    for flip, step in itertools.product(range(2), range(4)):
+        pairs = []
+        for lo, z, hi, at, core in itertools.product(*map(range, SIZES)):
+            pairs.append((place(lo ^ flip, z, hi, (at + step) % 4, core), place(lo, z, hi, at, core)))
+        found.append(lax.ppermute(x, EVERY, pairs) if flip or step else x)
+    return jnp.stack(found)
+
+
+def by_member(blocks):
+    _, *rest = blocks.shape
+    blocks = blocks.reshape(2, 4, *rest)
+    blocks = lax.dynamic_slice_in_dim(jnp.concatenate([blocks] * 2, 1), (4 - lax.axis_index("x")) % 4, 4, 1)
+    blocks = lax.dynamic_slice_in_dim(jnp.concatenate([blocks] * 2, 0), lax.axis_index("y_lo"), 2, 0)
+    return blocks.reshape(8, *rest)
+
+
+def halves(x):
+    high = lax.reduce_precision(x, 8, 7)
+    return high.astype(jnp.bfloat16), (x - high).astype(jnp.bfloat16)
+
+
+def product(a, b):
+    return jnp.dot(a, b, preferred_element_type=jnp.float32)
+
+
 def copies(x, count):
     return jnp.broadcast_to(x, (count, *x.shape))
 
@@ -65,7 +92,7 @@
     side = jnp.concatenate([seed_cluster.astype(jnp.float32), jnp.sum(embedding * embedding, axis=1)])
     block = jnp.concatenate([embedding, jnp.broadcast_to(side, (SIDE, width))], axis=0)
     spread = copies(block, 8)
-    rows = exchange_rows(spread)
+    rows = row_peers(block)
     columns = [exchange_columns(spread)]
     columns.append(other_core(columns[0]))
 
@@ -77,15 +104,17 @@
         seeds, sq = part_side[:, :points].reshape(-1), part_side[:, points:].reshape(-1)
         inner = jnp.dot(row_points, points_of(part, points).T, precision=lax.Precision.HIGH)
         distance = jnp.sqrt(row_sq[:, None] + sq[None, :] - 2.0 * inner + 1.0)
-        distances.append(distance)
-        weighted = weighted + jnp.dot(distance, first_member(seeds), precision=lax.Precision.HIGH)
+        high, low = halves(distance)
+        distances.append((high, low))
+        member = first_member(seeds).astype(jnp.bfloat16)
+        weighted = weighted + product(high, member) + product(low, member)
 
     own = first_member(seed_cluster.astype(jnp.float32))
     small = jnp.stack([jnp.sum(first_member(row_seeds) * weighted, axis=0), jnp.sum(own, axis=0)])
 
     def summed(weighted, small):
         tail = copies(jnp.pad(small, ((0, SIDE - len(small)), (0, 0))), 8)
-        blocks = jnp.concatenate([weighted.reshape(8, points, -1), tail], axis=1)
+        blocks = jnp.concatenate([by_member(weighted.reshape(8, points, -1)), tail], axis=1)
         return jnp.sum(exchange_rows(blocks), axis=0)
 
     first = summed(weighted, small)
@@ -98,7 +127,8 @@
     for part, distance in zip(firsts, distances):
         member = jnp.exp(log_softmax_energy(points_of(part, points), counts, cohesion))
         sizes = sizes + jnp.sum(member, axis=0, keepdims=True)
-        weighted = weighted + jnp.dot(distance, member, precision=lax.Precision.HIGH)
+        (high, low), (member_high, member_low) = distance, halves(member)
+        weighted = weighted + product(high, member_high) + product(high, member_low) + product(low, member_high)
     own = jnp.exp(log_softmax_energy(first[:points], counts, cohesion))
 
     second = summed(weighted, sizes)

time: 131 us -> 119 us (0.908)
  blocking collectives: 62.2 us -> 39.9 us
  starting transfers between devices: 13.9 us -> 27 us
  matrix products: 19 us -> 15.5 us
  waiting for transfers between devices: 25.5 us -> 23.2 us
  local copies, waits for them, and re-layouts: 1.48 us -> 3.56 us
    all_to_all x2 -> x1, blocking collectives: 37.2 us -> 13.8 us  [exchange_columns(): lax.all_to_all(blocks, EVERY, 0, 0, axis_index_groups=COLUMN_GROUPS, tile...]
    all_to_all x2 -> x1, waiting for transfers between devices: 23.9 us -> 10.2 us  [exchange_rows(): return lax.all_to_all(blocks, ('y_lo', 'x'), 0, 0, tiled=True)]
    all_to_all x0 -> x1, waiting for transfers between devices: none -> 11.2 us  [exchange_columns(): lax.all_to_all(blocks, EVERY, 0, 0, axis_index_groups=COLUMN_GROUPS, tile...]
    ppermute x0 -> x7, starting transfers between devices: none -> 9.44 us  [row_peers(): found.append(lax.ppermute(x, EVERY, pairs) if flip or step else x)]
    all_to_all x0 -> x1, starting transfers between devices: none -> 7.48 us  [exchange_columns(): lax.all_to_all(blocks, EVERY, 0, 0, axis_index_groups=COLUMN_GROUPS, tile...]
    dot_general x4 -> x10, matrix products: 15.1 us -> 7.61 us  [product(): return jnp.dot(a, b, preferred_element_type=jnp.float32)]
    all_to_all x2 -> x1, starting transfers between devices: 7.56 us -> 3.54 us  [exchange_rows(): return lax.all_to_all(blocks, ('y_lo', 'x'), 0, 0, tiled=True)]
    dot_general x2, matrix products: 3.92 us -> 7.91 us  [shards(): jnp.dot(row_points, points_of(part, points).T, precision=lax.Precision.HIGH)]
  transfers between devices with their start and end apart: 4 -> 11, of which waited for: 3 -> 4; matrix products, arithmetic and copies ran while one was open for 5% -> 3% of each run, Pallas kernels for 0% -> 0%
where the time goes in v2:
time: 119 us; the launch traced here: 118 us
  blocking collectives  39.9 us (34%)
  starting transfers between devices  27 us (23%)
  waiting for transfers between devices  23.2 us (19%)
  matrix products  15.5 us (13%)
  other arithmetic  8.38 us (7%)
  local copies, waits for them, and re-layouts  3.56 us (3%)
    all_to_all x1, blocking collectives, exchange_columns(): lax.all_to_all(blocks, EVERY, 0, 0, axis_index_groups=COLUMN_GROUPS, tile...  13.8 us
    all_to_all x1, blocking collectives, shards(): lax.all_to_all(copies(jnp.sum(own * attraction, axis=0, keepdims=True), 1...  13.2 us
    all_to_all x1, blocking collectives, exchange_rows(): return lax.all_to_all(blocks, ('y_lo', 'x'), 0, 0, tiled=True)  12.9 us
    all_to_all x1, waiting for transfers between devices, exchange_columns(): lax.all_to_all(blocks, EVERY, 0, 0, axis_index_groups=COLUMN_GROUPS, tile...  11.2 us
    all_to_all x1, waiting for transfers between devices, exchange_rows(): return lax.all_to_all(blocks, ('y_lo', 'x'), 0, 0, tiled=True)  10.2 us
    ppermute x7, starting transfers between devices, row_peers(): found.append(lax.ppermute(x, EVERY, pairs) if flip or step else x)  9.44 us
    dot_general x2, matrix products, shards(): jnp.dot(row_points, points_of(part, points).T, precision=lax.Precision.HIGH)  7.91 us
    dot_general x10, matrix products, product(): return jnp.dot(a, b, preferred_element_type=jnp.float32)  7.61 us
  transfers between devices with their start and end apart: 11, of which 4 were waited for; matrix products, arithmetic and copies ran while one was open for 3% of the time, Pallas kernels for 0%

profile of v2, /device:TPU:1, one launch (start us, length us, event | category | flops | bytes accessed | tf_op | source)
XLA Modules:
  0.0 118.1 jit_solution(2921710726939852949)
XLA Ops:
  0.7 1.0 multiply_reduce_fusion.1
  1.7 0.9 pad_maximum_fusion.2
  2.7 3.4 %collective-permute-start = (f32[136,256]{1,0:T(8,128)S(1)}, f32[136,256]{1,0:T(8,128)S(1)}, u32[]{:S(2)}, u32[]{:S(2)}) collective-permute-start(f32[136,256]{1,0:T(8,128)S(1)} %pad_maximum_fusion.2), channel_id=1, source_target_pairs={{2,0},{3,1},{4,2},{5,3},{6,4},{7,5},{0,6},{1,7},{10,8},{11,9},{12,... | collective-permute-start | bytes 417800 | tf_op jit(solution)/shard_map/ppermute | solution.py:45
  7.2 1.3 %collective-permute-start.3 = (f32[136,256]{1,0:T(8,128)S(1)}, f32[136,256]{1,0:T(8,128)S(1)}, u32[]{:S(2)}, u32[]{:S(2)}) collective-permute-start(f32[136,256]{1,0:T(8,128)S(1)} %pad_maximum_fusion.2), channel_id=1, source_target_pairs={{64,0},{65,1},{66,2},{67,3},{68,4},{69,5},{70,6},{71,7},{72,8},{73... | collective-permute-start | bytes 417800 | tf_op jit(solution)/shard_map/ppermute | solution.py:45
  8.5 2.0 %collective-permute-start.4 = (f32[136,256]{1,0:T(8,128)S(1)}, f32[136,256]{1,0:T(8,128)S(1)}, u32[]{:S(2)}, u32[]{:S(2)}) collective-permute-start(f32[136,256]{1,0:T(8,128)S(1)} %pad_maximum_fusion.2), channel_id=1, source_target_pairs={{66,0},{67,1},{68,2},{69,3},{70,4},{71,5},{64,6},{65,7},{74,8},{75... | collective-permute-start | bytes 417800 | tf_op jit(solution)/shard_map/ppermute | solution.py:45
  10.4 1.1 broadcast_in_dim.13
  11.5 7.5 %all-to-all-start = ((f32[8,136,256]{2,1,0:T(8,128)}), f32[8,136,256]{2,1,0:T(8,128)S(1)}, u32[]{:S(2)}, u32[]{:S(2)}) async-start(f32[8,136,256]{2,1,0:T(8,128)} %broadcast_in_dim.13), calls=%async_computation | async-start | bytes 2228224 | tf_op jit(solution)/shard_map/all_to_all | solution.py:36
  19.1 1.2 collective-permute-start.5
  20.9 11.2 %all-to-all-done = f32[8,136,256]{2,1,0:T(8,128)S(1)} async-done(((f32[8,136,256]{2,1,0:T(8,128)}), f32[8,136,256]{2,1,0:T(8,128)S(1)}, u32[]{:S(2)}, u32[]{:S(2)}) %all-to-all-start) | async-done | bytes 1114144 | tf_op jit(solution)/shard_map/all_to_all | solution.py:36
  32.1 3.9 %collective-permute-start.7 = (f32[8,136,256]{2,1,0:T(8,128)S(1)}, f32[8,136,256]{2,1,0:T(8,128)S(1)}, u32[]{:S(2)}, u32[]{:S(2)}) collective-permute-start(f32[8,136,256]{2,1,0:T(8,128)S(1)} %all-to-all-done), channel_id=1, source_target_pairs={{0,1},{1,0},{2,3},{3,2},{4,5},{5,4},{6,7},{7,6},{8,9},{9,8},{10,11... | collective-permute-start | bytes 3342344 | tf_op jit(solution)/shard_map/ppermute | solution.py:71
  36.4 2.0 %fusion.61 = f32[1024,1024]{1,0:T(8,128)S(1)} fusion(f32[1024,256]{1,0:T(8,128)S(1)} %bitcast.109, f32[1024,256]{1,0:T(8,128)S(1)} %bitcast.111), kind=kOutput, calls=%fused_computation.140 | convolution fusion | flops 1610612736 | bytes 6291456 | tf_op jit(solution)/shard_map/dot_general | solution.py:105
  38.6 5.9 %fusion.1 = (bf16[1024,1024]{1,0:T(8,128)(2,1)S(1)}, bf16[1024,1024]{1,0:T(8,128)(2,1)S(1)}, bf16[1024,1024]{1,0:T(8,128)(2,1)S(1)}, bf16[1024,1024]{1,0:T(8,128)(2,1)S(1)}) fusion(f32[1024]{0:T(1024)S(1)} %get-tuple-element.35, f32[1024]{0:T(1024)S(1)} %get-tuple-element.18, f32[1024,1024]{1,0:T(8,128)S(1)} %fusion.61, f32[1024]{0:T(1024)S(1)} %get-tuple-element.22, ...), kind=kOutput, calls=%fused_computation.5 | convolution fusion | flops 1627389952 | bytes 14692352 | tf_op jit(solution)/shard_map/dot_general | solution.py:105
  46.5 0.8 convolution_add_fusion.6
  47.3 0.8 multiply_reduce_fusion
  48.5 12.9 %all_to_all.25 = f32[8,136,128]{2,1,0:T(8,128)S(1)} all-to-all(f32[8,136,128]{2,1,0:T(8,128)S(1)} %pad_maximum_fusion), channel_id=1, replica_groups=mesh['y_lo'=2,'z'=4,'y_hi'=2,'x'=4,'core'=2] {'y_lo','x'}, dimensions={0} | all-to-all | bytes 1114112 | tf_op jit(solution)/shard_map/all_to_all | solution.py:32
  61.5 13.8 %all_to_all.26 = f32[8,136,128]{2,1,0:T(8,128)S(1)} all-to-all(f32[8,136,128]{2,1,0:T(8,128)S(1)} %broadcast_in_dim.15), channel_id=1, replica_groups={{0,16,32,48,72,88,104,120},{1,17,33,49,73,89,105,121},{2,18,34,50,74,90..., dimensions={0} | all-to-all | bytes 1114112 | tf_op jit(solution)/shard_map/all_to_all | solution.py:36
  75.2 2.6 %collective-permute-start.8 = (f32[8,136,128]{2,1,0:T(8,128)S(1)}, f32[8,136,128]{2,1,0:T(8,128)S(1)}, u32[]{:S(2)}, u32[]{:S(2)}) collective-permute-start(f32[8,136,128]{2,1,0:T(8,128)S(1)} %all_to_all.26), channel_id=1, source_target_pairs={{0,1},{1,0},{2,3},{3,2},{4,5},{5,4},{6,7},{7,6},{8,9},{9,8},{10,11... | collective-permute-start | bytes 1671176 | tf_op jit(solution)/shard_map/ppermute | solution.py:71
  77.9 1.6 %collective-permute-done.8 = f32[8,136,128]{2,1,0:T(8,128)S(1)} collective-permute-done((f32[8,136,128]{2,1,0:T(8,128)S(1)}, f32[8,136,128]{2,1,0:T(8,128)S(1)}, u32[]{:S(2)}, u32[]{:S(2)}) %collective-permute-start.8) | collective-permute-done | bytes 557088 | tf_op jit(solution)/shard_map/ppermute | solution.py:71
  80.9 1.0 fusion.13
  83.3 0.9 copy-done.1
  86.4 0.9 copy-done.5
  89.4 3.5 %all-to-all-start.3 = ((f32[8,136,128]{2,1,0:T(8,128)}), f32[8,136,128]{2,1,0:T(8,128)S(1)}, u32[]{:S(2)}, u32[]{:S(2)}) async-start(f32[8,136,128]{2,1,0:T(8,128)} %pad_maximum_fusion.1), calls=%async_computation.3 | async-start | bytes 1114112 | tf_op jit(solution)/shard_map/all_to_all | solution.py:32
  93.3 10.2 %all-to-all-done.3 = f32[8,136,128]{2,1,0:T(8,128)S(1)} async-done(((f32[8,136,128]{2,1,0:T(8,128)}), f32[8,136,128]{2,1,0:T(8,128)S(1)}, u32[]{:S(2)}, u32[]{:S(2)}) %all-to-all-start.3) | async-done | bytes 557088 | tf_op jit(solution)/shard_map/all_to_all | solution.py:32
  103.7 13.2 %all_to_all.27 = f32[128,1,128]{2,1,0:T(1,128)S(1)} all-to-all(f32[128,1,128]{2,1,0:T(1,128)S(1)} %broadcast_in_dim.17), channel_id=1, replica_groups=mesh['y_lo'=2,'z'=4,'y_hi'=2,'x'=4,'core'=2] {'y_lo','z','y_hi','x','core'}, dimensions={0} | all-to-all | bytes 131072 | tf_op jit(solution)/shard_map/all_to_all | solution.py:136
  (89 shorter events, 13.9 us)
Async XLA Ops:
  0.0 19.0 %copy-start.6 = (f32[128,256]{1,0:T(8,128)S(1)}, f32[128,256]{1,0:T(8,128)}, u32[]{:S(2)}) copy-start(f32[128,256]{1,0:T(8,128)} %param.2) | copy-start | bytes 393220
  2.7 16.4 %collective-permute-start = (f32[136,256]{1,0:T(8,128)S(1)}, f32[136,256]{1,0:T(8,128)S(1)}, u32[]{:S(2)}, u32[]{:S(2)}) collective-permute-start(f32[136,256]{1,0:T(8,128)S(1)} %pad_maximum_fusion.2), channel_id=1, source_target_pairs={{2,0},{3,1},{4,2},{5,3},{6,4},{7,5},{0,6},{1,7},{10,8},{11,9},{12,... | collective-permute-start | bytes 417800 | tf_op jit(solution)/shard_map/ppermute | solution.py:45
  6.0 14.3 %collective-permute-start.1 = (f32[136,256]{1,0:T(8,128)S(1)}, f32[136,256]{1,0:T(8,128)S(1)}, u32[]{:S(2)}, u32[]{:S(2)}) collective-permute-start(f32[136,256]{1,0:T(8,128)S(1)} %pad_maximum_fusion.2), channel_id=1, source_target_pairs={{4,0},{5,1},{6,2},{7,3},{0,4},{1,5},{2,6},{3,7},{12,8},{13,9},{14,... | collective-permute-start | bytes 417800 | tf_op jit(solution)/shard_map/ppermute | solution.py:45
  6.5 14.3 %collective-permute-start.2 = (f32[136,256]{1,0:T(8,128)S(1)}, f32[136,256]{1,0:T(8,128)S(1)}, u32[]{:S(2)}, u32[]{:S(2)}) collective-permute-start(f32[136,256]{1,0:T(8,128)S(1)} %pad_maximum_fusion.2), channel_id=1, source_target_pairs={{6,0},{7,1},{0,2},{1,3},{2,4},{3,5},{4,6},{5,7},{14,8},{15,9},{8,1... | collective-permute-start | bytes 417800 | tf_op jit(solution)/shard_map/ppermute | solution.py:45
  7.2 13.7 %collective-permute-start.3 = (f32[136,256]{1,0:T(8,128)S(1)}, f32[136,256]{1,0:T(8,128)S(1)}, u32[]{:S(2)}, u32[]{:S(2)}) collective-permute-start(f32[136,256]{1,0:T(8,128)S(1)} %pad_maximum_fusion.2), channel_id=1, source_target_pairs={{64,0},{65,1},{66,2},{67,3},{68,4},{69,5},{70,6},{71,7},{72,8},{73... | collective-permute-start | bytes 417800 | tf_op jit(solution)/shard_map/ppermute | solution.py:45
  8.5 27.6 %collective-permute-start.4 = (f32[136,256]{1,0:T(8,128)S(1)}, f32[136,256]{1,0:T(8,128)S(1)}, u32[]{:S(2)}, u32[]{:S(2)}) collective-permute-start(f32[136,256]{1,0:T(8,128)S(1)} %pad_maximum_fusion.2), channel_id=1, source_target_pairs={{66,0},{67,1},{68,2},{69,3},{70,4},{71,5},{64,6},{65,7},{74,8},{75... | collective-permute-start | bytes 417800 | tf_op jit(solution)/shard_map/ppermute | solution.py:45
  11.5 20.7 %all-to-all-start = ((f32[8,136,256]{2,1,0:T(8,128)}), f32[8,136,256]{2,1,0:T(8,128)S(1)}, u32[]{:S(2)}, u32[]{:S(2)}) async-start(f32[8,136,256]{2,1,0:T(8,128)} %broadcast_in_dim.13), calls=%async_computation | async-start | bytes 2228224 | tf_op jit(solution)/shard_map/all_to_all | solution.py:36
  19.1 17.0 %collective-permute-start.5 = (f32[136,256]{1,0:T(8,128)S(1)}, f32[136,256]{1,0:T(8,128)S(1)}, u32[]{:S(2)}, u32[]{:S(2)}) collective-permute-start(f32[136,256]{1,0:T(8,128)S(1)} %pad_maximum_fusion.2), channel_id=1, source_target_pairs={{68,0},{69,1},{70,2},{71,3},{64,4},{65,5},{66,6},{67,7},{76,8},{77... | collective-permute-start | bytes 417800 | tf_op jit(solution)/shard_map/ppermute | solution.py:45
  20.3 15.8 %collective-permute-start.6 = (f32[136,256]{1,0:T(8,128)S(1)}, f32[136,256]{1,0:T(8,128)S(1)}, u32[]{:S(2)}, u32[]{:S(2)}) collective-permute-start(f32[136,256]{1,0:T(8,128)S(1)} %pad_maximum_fusion.2), channel_id=1, source_target_pairs={{70,0},{71,1},{64,2},{65,3},{66,4},{67,5},{68,6},{69,7},{78,8},{79... | collective-permute-start | bytes 417800 | tf_op jit(solution)/shard_map/ppermute | solution.py:45
  32.1 6.3 %collective-permute-start.7 = (f32[8,136,256]{2,1,0:T(8,128)S(1)}, f32[8,136,256]{2,1,0:T(8,128)S(1)}, u32[]{:S(2)}, u32[]{:S(2)}) collective-permute-start(f32[8,136,256]{2,1,0:T(8,128)S(1)} %all-to-all-done), channel_id=1, source_target_pairs={{0,1},{1,0},{2,3},{3,2},{4,5},{5,4},{6,7},{7,6},{8,9},{9,8},{10,11... | collective-permute-start | bytes 3342344 | tf_op jit(solution)/shard_map/ppermute | solution.py:71
  44.5 1.7 %copy-start = (bf16[1024,1024]{1,0:T(8,128)(2,1)}, bf16[1024,1024]{1,0:T(8,128)(2,1)S(1)}, u32[]{:S(2)}) copy-start(bf16[1024,1024]{1,0:T(8,128)(2,1)S(1)} %get-tuple-element.28) | copy-start | bytes 6291460
  44.5 1.9 %copy-start.2 = (bf16[1024,1024]{1,0:T(8,128)(2,1)}, bf16[1024,1024]{1,0:T(8,128)(2,1)S(1)}, u32[]{:S(2)}) copy-start(bf16[1024,1024]{1,0:T(8,128)(2,1)S(1)} %get-tuple-element.27) | copy-start | bytes 6291460
  44.5 2.8 %copy-start.4 = (bf16[1024,1024]{1,0:T(8,128)(2,1)}, bf16[1024,1024]{1,0:T(8,128)(2,1)S(1)}, u32[]{:S(2)}) copy-start(bf16[1024,1024]{1,0:T(8,128)(2,1)S(1)} %get-tuple-element.9) | copy-start | bytes 6291460
  75.2 4.2 %collective-permute-start.8 = (f32[8,136,128]{2,1,0:T(8,128)S(1)}, f32[8,136,128]{2,1,0:T(8,128)S(1)}, u32[]{:S(2)}, u32[]{:S(2)}) collective-permute-start(f32[8,136,128]{2,1,0:T(8,128)S(1)} %all_to_all.26), channel_id=1, source_target_pairs={{0,1},{1,0},{2,3},{3,2},{4,5},{5,4},{6,7},{7,6},{8,9},{9,8},{10,11... | collective-permute-start | bytes 1671176 | tf_op jit(solution)/shard_map/ppermute | solution.py:71
  80.2 1.7 %copy-start.3 = (bf16[1024,1024]{1,0:T(8,128)(2,1)S(1)}, bf16[1024,1024]{1,0:T(8,128)(2,1)}, u32[]{:S(2)}) copy-start(bf16[1024,1024]{1,0:T(8,128)(2,1)} %copy-done.2) | copy-start | bytes 6291460
  82.6 1.6 %copy-start.1 = (bf16[1024,1024]{1,0:T(8,128)(2,1)S(1)}, bf16[1024,1024]{1,0:T(8,128)(2,1)}, u32[]{:S(2)}) copy-start(bf16[1024,1024]{1,0:T(8,128)(2,1)} %copy-done) | copy-start | bytes 6291460
  85.6 1.6 %copy-start.5 = (bf16[1024,1024]{1,0:T(8,128)(2,1)S(1)}, bf16[1024,1024]{1,0:T(8,128)(2,1)}, u32[]{:S(2)}) copy-start(bf16[1024,1024]{1,0:T(8,128)(2,1)} %copy-done.4) | copy-start | bytes 6291460
  89.4 14.1 %all-to-all-start.3 = ((f32[8,136,128]{2,1,0:T(8,128)}), f32[8,136,128]{2,1,0:T(8,128)S(1)}, u32[]{:S(2)}, u32[]{:S(2)}) async-start(f32[8,136,128]{2,1,0:T(8,128)} %pad_maximum_fusion.1), calls=%async_computation.3 | async-start | bytes 1114112 | tf_op jit(solution)/shard_map/all_to_all | solution.py:32

commit v3 on v2

--- a/solution.py
+++ b/solution.py
@@ -36,14 +36,17 @@
     return lax.all_to_all(blocks, EVERY, 0, 0, axis_index_groups=COLUMN_GROUPS, tiled=True)
 
 
+def moved(x, flip, step):
+    pairs = []
+    for lo, z, hi, at, core in itertools.product(*map(range, SIZES)):
+        pairs.append((place(lo ^ flip, z, hi, (at + step) % 4, core), place(lo, z, hi, at, core)))
+    return lax.ppermute(x, EVERY, pairs)
+
+
 def row_peers(x):
-    found = []
-    for flip, step in itertools.product(range(2), range(4)):
-        pairs = []
-        for lo, z, hi, at, core in itertools.product(*map(range, SIZES)):
-            pairs.append((place(lo ^ flip, z, hi, (at + step) % 4, core), place(lo, z, hi, at, core)))
-        found.append(lax.ppermute(x, EVERY, pairs) if flip or step else x)
-    return jnp.stack(found)
+    pair = jnp.stack([x, moved(x, 1, 0)])
+    ring = [pair] + [moved(pair, 0, step) for step in range(1, 4)]
+    return jnp.stack(ring, axis=1).reshape(8, *x.shape)
 
 
 def by_member(blocks):
@@ -93,7 +96,7 @@
     block = jnp.concatenate([embedding, jnp.broadcast_to(side, (SIDE, width))], axis=0)
     spread = copies(block, 8)
     rows = row_peers(block)
-    columns = [exchange_columns(spread)]
+    rows, *columns = lax.optimization_barrier((rows, exchange_columns(spread)))
     columns.append(other_core(columns[0]))
 
     row_points, row_side = points_of(rows, points), rows[:, points]

time: 119 us -> 120 us (level)
  starting transfers between devices: 27 us -> 18.9 us
  waiting for transfers between devices: 23.2 us -> 30.9 us
  blocking collectives: 39.9 us -> 41.6 us
    ppermute x7 -> x4, waiting for transfers between devices: 0.02 us -> 19 us  [moved(): return lax.ppermute(x, EVERY, pairs)]
    all_to_all x1, waiting for transfers between devices: 11.2 us -> 0.01 us  [exchange_columns(): lax.all_to_all(blocks, EVERY, 0, 0, axis_index_groups=COLUMN_GROUPS, tile...]
    ppermute x7 -> x4, starting transfers between devices: 9.44 us -> 3.81 us  [moved(): return lax.ppermute(x, EVERY, pairs)]
    ppermute x2, starting transfers between devices: 6.57 us -> 3.19 us  [other_core(): return lax.ppermute(x, 'core', [(0, 1), (1, 0)])]
    all_to_all x1, blocking collectives: 13.8 us -> 15.4 us  [exchange_columns(): lax.all_to_all(blocks, EVERY, 0, 0, axis_index_groups=COLUMN_GROUPS, tile...]
  transfers between devices with their start and end apart: 11 -> 8, of which waited for: 4 -> 7; matrix products, arithmetic and copies ran while one was open for 3% -> 2% of each run, Pallas kernels for 0% -> 0%
where the time goes in v3:
time: 120 us; the launch traced here: 119 us
  blocking collectives  41.6 us (35%)
  waiting for transfers between devices  30.9 us (26%)
  starting transfers between devices  18.9 us (16%)
  matrix products  15.5 us (13%)
  other arithmetic  8.47 us (7%)
  local copies, waits for them, and re-layouts  3.45 us (3%)
    ppermute x4, waiting for transfers between devices, moved(): return lax.ppermute(x, EVERY, pairs)  19 us
    all_to_all x1, blocking collectives, exchange_columns(): lax.all_to_all(blocks, EVERY, 0, 0, axis_index_groups=COLUMN_GROUPS, tile...  15.4 us
    all_to_all x1, blocking collectives, shards(): lax.all_to_all(copies(jnp.sum(own * attraction, axis=0, keepdims=True), 1...  13.2 us
    all_to_all x1, blocking collectives, exchange_rows(): return lax.all_to_all(blocks, ('y_lo', 'x'), 0, 0, tiled=True)  12.9 us
    all_to_all x1, waiting for transfers between devices, exchange_rows(): return lax.all_to_all(blocks, ('y_lo', 'x'), 0, 0, tiled=True)  10.2 us
    all_to_all x1, starting transfers between devices, exchange_columns(): lax.all_to_all(blocks, EVERY, 0, 0, axis_index_groups=COLUMN_GROUPS, tile...  8.31 us
    dot_general x2, matrix products, shards(): jnp.dot(row_points, points_of(part, points).T, precision=lax.Precision.HIGH)  7.9 us
    dot_general x10, matrix products, product(): return jnp.dot(a, b, preferred_element_type=jnp.float32)  7.63 us
  transfers between devices with their start and end apart: 8, of which 7 were waited for; matrix products, arithmetic and copies ran while one was open for 2% of the time, Pallas kernels for 0%

profile of v3, /device:TPU:1, one launch (start us, length us, event | category | flops | bytes accessed | tf_op | source)
XLA Modules:
  0.0 119.2 jit_solution(10929006419807854907)
XLA Ops:
  0.7 1.0 multiply_reduce_fusion.1
  1.7 0.9 fusion.57
  2.6 1.1 broadcast_in_dim.13
  3.7 8.3 %all-to-all-start = ((f32[8,136,256]{2,1,0:T(8,128)}), f32[8,136,256]{2,1,0:T(8,128)S(1)}, u32[]{:S(2)}, u32[]{:S(2)}) async-start(f32[8,136,256]{2,1,0:T(8,128)} %broadcast_in_dim.13), calls=%async_computation | async-start | bytes 2228224 | tf_op jit(solution)/shard_map/all_to_all | solution.py:36
  12.1 4.1 %collective-permute-done = f32[136,256]{1,0:T(8,128)S(1)} collective-permute-done((f32[136,256]{1,0:T(8,128)S(1)}, f32[136,256]{1,0:T(8,128)S(1)}, u32[]{:S(2)}, u32[]{:S(2)}) %collective-permute-start) | collective-permute-done | bytes 139296 | tf_op jit(solution)/shard_map/ppermute | solution.py:43
  16.3 2.5 %collective-permute-start.1 = (f32[2,136,256]{2,1,0:T(8,128)S(1)}, f32[2,136,256]{2,1,0:T(8,128)S(1)}, u32[]{:S(2)}, u32[]{:S(2)}) collective-permute-start(f32[2,136,256]{2,1,0:T(8,128)S(1)} %get-tuple-element.20), channel_id=1, source_target_pairs={{2,0},{3,1},{4,2},{5,3},{6,4},{7,5},{0,6},{1,7},{10,8},{11,9},{12,... | collective-permute-start | bytes 835592 | tf_op jit(solution)/shard_map/ppermute | solution.py:43
  19.9 3.8 %collective-permute-done.1 = f32[2,136,256]{2,1,0:T(8,128)S(1)} collective-permute-done((f32[2,136,256]{2,1,0:T(8,128)S(1)}, f32[2,136,256]{2,1,0:T(8,128)S(1)}, u32[]{:S(2)}, u32[]{:S(2)}) %collective-permute-start.1) | collective-permute-done | bytes 278560 | tf_op jit(solution)/shard_map/ppermute | solution.py:43
  23.7 2.7 %collective-permute-done.2 = f32[2,136,256]{2,1,0:T(8,128)S(1)} collective-permute-done((f32[2,136,256]{2,1,0:T(8,128)S(1)}, f32[2,136,256]{2,1,0:T(8,128)S(1)}, u32[]{:S(2)}, u32[]{:S(2)}) %collective-permute-start.2) | collective-permute-done | bytes 278560 | tf_op jit(solution)/shard_map/ppermute | solution.py:43
  26.4 8.5 %collective-permute-done.3 = f32[2,136,256]{2,1,0:T(8,128)S(1)} collective-permute-done((f32[2,136,256]{2,1,0:T(8,128)S(1)}, f32[2,136,256]{2,1,0:T(8,128)S(1)}, u32[]{:S(2)}, u32[]{:S(2)}) %collective-permute-start.3) | collective-permute-done | bytes 278560 | tf_op jit(solution)/shard_map/ppermute | solution.py:43
  35.9 2.0 %fusion.63 = f32[1024,1024]{1,0:T(8,128)S(1)} fusion(f32[1024,256]{1,0:T(8,128)S(1)} %bitcast.110, f32[1024,256]{1,0:T(8,128)S(1)} %bitcast.112), kind=kOutput, calls=%fused_computation.136 | convolution fusion | flops 1610612736 | bytes 6291456 | tf_op jit(solution)/shard_map/dot_general | solution.py:108
  38.0 5.9 %fusion.1 = (bf16[1024,1024]{1,0:T(8,128)(2,1)S(1)}, bf16[1024,1024]{1,0:T(8,128)(2,1)S(1)}, bf16[1024,1024]{1,0:T(8,128)(2,1)S(1)}, bf16[1024,1024]{1,0:T(8,128)(2,1)S(1)}) fusion(f32[1024]{0:T(1024)S(1)} %get-tuple-element.43, f32[1024]{0:T(1024)S(1)} %get-tuple-element.26, f32[1024,1024]{1,0:T(8,128)S(1)} %fusion.63, f32[1024]{0:T(1024)S(1)} %get-tuple-element.30, ...), kind=kOutput, calls=%fused_computation.5 | convolution fusion | flops 1627389952 | bytes 14692352 | tf_op jit(solution)/shard_map/dot_general | solution.py:108
  44.8 0.8 convolution_add_fusion.7
  45.9 0.8 convolution_add_fusion.6
  46.8 0.8 multiply_reduce_fusion
  47.9 12.9 %all_to_all.25 = f32[8,136,128]{2,1,0:T(8,128)S(1)} all-to-all(f32[8,136,128]{2,1,0:T(8,128)S(1)} %pad_maximum_fusion.1), channel_id=1, replica_groups=mesh['y_lo'=2,'z'=4,'y_hi'=2,'x'=4,'core'=2] {'y_lo','x'}, dimensions={0} | all-to-all | bytes 1114112 | tf_op jit(solution)/shard_map/all_to_all | solution.py:32
  60.9 15.4 %all_to_all.26 = f32[8,136,128]{2,1,0:T(8,128)S(1)} all-to-all(f32[8,136,128]{2,1,0:T(8,128)S(1)} %broadcast_in_dim.15), channel_id=1, replica_groups={{0,16,32,48,72,88,104,120},{1,17,33,49,73,89,105,121},{2,18,34,50,74,90..., dimensions={0} | all-to-all | bytes 1114112 | tf_op jit(solution)/shard_map/all_to_all | solution.py:36
  76.4 2.6 %collective-permute-start.5 = (f32[8,136,128]{2,1,0:T(8,128)S(1)}, f32[8,136,128]{2,1,0:T(8,128)S(1)}, u32[]{:S(2)}, u32[]{:S(2)}) collective-permute-start(f32[8,136,128]{2,1,0:T(8,128)S(1)} %all_to_all.26), channel_id=1, source_target_pairs={{0,1},{1,0},{2,3},{3,2},{4,5},{5,4},{6,7},{7,6},{8,9},{9,8},{10,11... | collective-permute-start | bytes 1671176 | tf_op jit(solution)/shard_map/ppermute | solution.py:74
  79.0 1.6 %collective-permute-done.5 = f32[8,136,128]{2,1,0:T(8,128)S(1)} collective-permute-done((f32[8,136,128]{2,1,0:T(8,128)S(1)}, f32[8,136,128]{2,1,0:T(8,128)S(1)}, u32[]{:S(2)}, u32[]{:S(2)}) %collective-permute-start.5) | collective-permute-done | bytes 557088 | tf_op jit(solution)/shard_map/ppermute | solution.py:74
  82.1 1.0 fusion.13
  84.5 0.9 copy-done.1
  87.5 0.9 copy-done.5
  90.6 3.5 %all-to-all-start.3 = ((f32[8,136,128]{2,1,0:T(8,128)}), f32[8,136,128]{2,1,0:T(8,128)S(1)}, u32[]{:S(2)}, u32[]{:S(2)}) async-start(f32[8,136,128]{2,1,0:T(8,128)} %pad_maximum_fusion.2), calls=%async_computation.3 | async-start | bytes 1114112 | tf_op jit(solution)/shard_map/all_to_all | solution.py:32
  94.4 10.2 %all-to-all-done.3 = f32[8,136,128]{2,1,0:T(8,128)S(1)} async-done(((f32[8,136,128]{2,1,0:T(8,128)}), f32[8,136,128]{2,1,0:T(8,128)S(1)}, u32[]{:S(2)}, u32[]{:S(2)}) %all-to-all-start.3) | async-done | bytes 557088 | tf_op jit(solution)/shard_map/all_to_all | solution.py:32
  104.9 13.2 %all_to_all.27 = f32[128,1,128]{2,1,0:T(1,128)S(1)} all-to-all(f32[128,1,128]{2,1,0:T(1,128)S(1)} %broadcast_in_dim.17), channel_id=1, replica_groups=mesh['y_lo'=2,'z'=4,'y_hi'=2,'x'=4,'core'=2] {'y_lo','z','y_hi','x','core'}, dimensions={0} | all-to-all | bytes 131072 | tf_op jit(solution)/shard_map/all_to_all | solution.py:139
  (75 shorter events, 13.3 us)
Async XLA Ops:
  3.7 31.3 %all-to-all-start = ((f32[8,136,256]{2,1,0:T(8,128)}), f32[8,136,256]{2,1,0:T(8,128)S(1)}, u32[]{:S(2)}, u32[]{:S(2)}) async-start(f32[8,136,256]{2,1,0:T(8,128)} %broadcast_in_dim.13), calls=%async_computation | async-start | bytes 2228224 | tf_op jit(solution)/shard_map/all_to_all | solution.py:36
  12.0 4.2 %collective-permute-start = (f32[136,256]{1,0:T(8,128)S(1)}, f32[136,256]{1,0:T(8,128)S(1)}, u32[]{:S(2)}, u32[]{:S(2)}) collective-permute-start(f32[136,256]{1,0:T(8,128)S(1)} %get-tuple-element.22), channel_id=1, source_target_pairs={{64,0},{65,1},{66,2},{67,3},{68,4},{69,5},{70,6},{71,7},{72,8},{73... | collective-permute-start | bytes 417800 | tf_op jit(solution)/shard_map/ppermute | solution.py:43
  16.3 7.5 %collective-permute-start.1 = (f32[2,136,256]{2,1,0:T(8,128)S(1)}, f32[2,136,256]{2,1,0:T(8,128)S(1)}, u32[]{:S(2)}, u32[]{:S(2)}) collective-permute-start(f32[2,136,256]{2,1,0:T(8,128)S(1)} %get-tuple-element.20), channel_id=1, source_target_pairs={{2,0},{3,1},{4,2},{5,3},{6,4},{7,5},{0,6},{1,7},{10,8},{11,9},{12,... | collective-permute-start | bytes 835592 | tf_op jit(solution)/shard_map/ppermute | solution.py:43
  18.8 7.6 %collective-permute-start.2 = (f32[2,136,256]{2,1,0:T(8,128)S(1)}, f32[2,136,256]{2,1,0:T(8,128)S(1)}, u32[]{:S(2)}, u32[]{:S(2)}) collective-permute-start(f32[2,136,256]{2,1,0:T(8,128)S(1)} %get-tuple-element.20), channel_id=1, source_target_pairs={{4,0},{5,1},{6,2},{7,3},{0,4},{1,5},{2,6},{3,7},{12,8},{13,9},{14,... | collective-permute-start | bytes 835592 | tf_op jit(solution)/shard_map/ppermute | solution.py:43
  19.3 15.5 %collective-permute-start.3 = (f32[2,136,256]{2,1,0:T(8,128)S(1)}, f32[2,136,256]{2,1,0:T(8,128)S(1)}, u32[]{:S(2)}, u32[]{:S(2)}) collective-permute-start(f32[2,136,256]{2,1,0:T(8,128)S(1)} %get-tuple-element.20), channel_id=1, source_target_pairs={{6,0},{7,1},{0,2},{1,3},{2,4},{3,5},{4,6},{5,7},{14,8},{15,9},{8,1... | collective-permute-start | bytes 835592 | tf_op jit(solution)/shard_map/ppermute | solution.py:43
  35.0 3.0 %collective-permute-start.4 = (f32[8,136,256]{2,1,0:T(8,128)S(1)}, f32[8,136,256]{2,1,0:T(8,128)S(1)}, u32[]{:S(2)}, u32[]{:S(2)}) collective-permute-start(f32[8,136,256]{2,1,0:T(8,128)S(1)} %all-to-all-done), channel_id=1, source_target_pairs={{0,1},{1,0},{2,3},{3,2},{4,5},{5,4},{6,7},{7,6},{8,9},{9,8},{10,11... | collective-permute-start | bytes 3342344 | tf_op jit(solution)/shard_map/ppermute | solution.py:74
  44.0 1.7 %copy-start = (bf16[1024,1024]{1,0:T(8,128)(2,1)}, bf16[1024,1024]{1,0:T(8,128)(2,1)S(1)}, u32[]{:S(2)}) copy-start(bf16[1024,1024]{1,0:T(8,128)(2,1)S(1)} %get-tuple-element.36) | copy-start | bytes 6291460
  44.0 1.9 %copy-start.2 = (bf16[1024,1024]{1,0:T(8,128)(2,1)}, bf16[1024,1024]{1,0:T(8,128)(2,1)S(1)}, u32[]{:S(2)}) copy-start(bf16[1024,1024]{1,0:T(8,128)(2,1)S(1)} %get-tuple-element.35) | copy-start | bytes 6291460
  44.0 2.8 %copy-start.4 = (bf16[1024,1024]{1,0:T(8,128)(2,1)}, bf16[1024,1024]{1,0:T(8,128)(2,1)S(1)}, u32[]{:S(2)}) copy-start(bf16[1024,1024]{1,0:T(8,128)(2,1)S(1)} %get-tuple-element.13) | copy-start | bytes 6291460
  76.4 4.2 %collective-permute-start.5 = (f32[8,136,128]{2,1,0:T(8,128)S(1)}, f32[8,136,128]{2,1,0:T(8,128)S(1)}, u32[]{:S(2)}, u32[]{:S(2)}) collective-permute-start(f32[8,136,128]{2,1,0:T(8,128)S(1)} %all_to_all.26), channel_id=1, source_target_pairs={{0,1},{1,0},{2,3},{3,2},{4,5},{5,4},{6,7},{7,6},{8,9},{9,8},{10,11... | collective-permute-start | bytes 1671176 | tf_op jit(solution)/shard_map/ppermute | solution.py:74
  81.4 1.7 %copy-start.3 = (bf16[1024,1024]{1,0:T(8,128)(2,1)S(1)}, bf16[1024,1024]{1,0:T(8,128)(2,1)}, u32[]{:S(2)}) copy-start(bf16[1024,1024]{1,0:T(8,128)(2,1)} %copy-done.2) | copy-start | bytes 6291460
  83.8 1.6 %copy-start.1 = (bf16[1024,1024]{1,0:T(8,128)(2,1)S(1)}, bf16[1024,1024]{1,0:T(8,128)(2,1)}, u32[]{:S(2)}) copy-start(bf16[1024,1024]{1,0:T(8,128)(2,1)} %copy-done) | copy-start | bytes 6291460
  86.8 1.6 %copy-start.5 = (bf16[1024,1024]{1,0:T(8,128)(2,1)S(1)}, bf16[1024,1024]{1,0:T(8,128)(2,1)}, u32[]{:S(2)}) copy-start(bf16[1024,1024]{1,0:T(8,128)(2,1)} %copy-done.4) | copy-start | bytes 6291460
  90.6 14.1 %all-to-all-start.3 = ((f32[8,136,128]{2,1,0:T(8,128)}), f32[8,136,128]{2,1,0:T(8,128)S(1)}, u32[]{:S(2)}, u32[]{:S(2)}) async-start(f32[8,136,128]{2,1,0:T(8,128)} %pad_maximum_fusion.2), calls=%async_computation.3 | async-start | bytes 1114112 | tf_op jit(solution)/shard_map/all_to_all | solution.py:32

commit v4 on v3

v4 whole, which is shorter than its diff:
```python
import itertools

import jax
import jax.numpy as jnp
from jax import lax
from jax.experimental import pallas as pl
from jax.experimental.pallas import tpu as pltpu
from jax.sharding import Mesh
from jax.sharding import PartitionSpec as P

CLUSTER_COUNT = 128
ANNEAL_TEMP_VALUE = 0.02
SIDE = 8

EVERY = ("y_lo", "z", "y_hi", "x", "core")
SIZES = (2, 4, 2, 4, 2)


def place(y_lo, z, y_hi, x, core):
    return (((y_lo * 4 + z) * 2 + y_hi) * 4 + x) * 2 + core


def column_groups():
    groups = []
    for pair, x, core in itertools.product(range(2), range(4), range(2)):
        groups.append([place(lo, z, lo ^ pair, x, core) for lo in range(2) for z in range(4)])
    return groups


COLUMN_GROUPS = column_groups()


def exchange_rows(blocks):
    return lax.all_to_all(blocks, ("y_lo", "x"), 0, 0, tiled=True)


def exchange_columns(blocks):
    return lax.all_to_all(blocks, EVERY, 0, 0, axis_index_groups=COLUMN_GROUPS, tiled=True)


def moved(x, flip, step):
    pairs = []
    for lo, z, hi, at, core in itertools.product(*map(range, SIZES)):
        pairs.append((place(lo ^ flip, z, hi, (at + step) % 4, core), place(lo, z, hi, at, core)))
    return lax.ppermute(x, EVERY, pairs)


def row_peers(x):
    pair = jnp.stack([x, moved(x, 1, 0)])
    ring = [pair] + [moved(pair, 0, step) for step in range(1, 4)]
    return jnp.stack(ring, axis=1).reshape(8, *x.shape)


def member_order():
    y_lo, x = lax.axis_index("y_lo"), lax.axis_index("x")
    offset = jnp.arange(8, dtype=jnp.int32)
    return (y_lo ^ (offset // 4)) * 4 + (x + offset % 4) % 4


def halves(x):
    high = x.astype(jnp.bfloat16)
    return high, (x - high.astype(jnp.float32)).astype(jnp.bfloat16)


def product(a, b):
    return jnp.dot(a, b, preferred_element_type=jnp.float32)


def seed_member(seeds):
    labels = lax.broadcasted_iota(jnp.int32, (CLUSTER_COUNT, seeds.shape[1]), 0).astype(jnp.float32)
    return 0.5 * (labels == seeds).astype(jnp.float32).T + 0.5 / CLUSTER_COUNT


def store_by_member(order, total, tail, out):
    points = out.shape[1] - SIDE
    for offset in range(8):
        member = order[offset]
        out[member, pl.ds(0, points)] = total[pl.ds(offset * points, points)]
        out[member, pl.ds(points, SIDE)] = tail


def tail_rows(*lines):
    at = lax.broadcasted_iota(jnp.int32, (SIDE, CLUSTER_COUNT), 0)
    tail = jnp.zeros((SIDE, CLUSTER_COUNT), jnp.float32)
    for index, line in enumerate(lines):
        tail = jnp.where(at == index, line, tail)
    return tail


STEPS = 8
TILE = 256
CHUNK = 256


def pair_kernel(order, rows, own, other, high_out, low_out, out, left, squares, total):
    step = pl.program_id(0)
    points, width = rows.shape[1] - SIDE, rows.shape[2]

    @pl.when(step == 0)
    def _():
        for offset in range(8):
            x = rows[offset, pl.ds(0, points)]
            at = pl.ds(offset * points, points)
            squares[at] = jnp.broadcast_to(jnp.sum(x * x, axis=1, keepdims=True) + 1.0, (points, 128))
            high, low = halves(-2.0 * x)
            left[at, pl.ds(0, width)] = high
            left[at, pl.ds(width, width)] = high
            left[at, pl.ds(2 * width, width)] = low
        total[...] = jnp.zeros_like(total)

    columns = jnp.where(step < STEPS // 2, own[...], other[...])
    high, low = halves(columns[:, :points].reshape(TILE, width))
    right = jnp.concatenate([high, low, high], axis=1)
    side = [columns[block, points : points + 1] for block in range(2)]
    sq = jnp.concatenate([line[:, points:] for line in side], axis=1)
    member = jnp.concatenate([seed_member(line[:, :points]) for line in side], axis=0).astype(jnp.bfloat16)
    for chunk in range(total.shape[0] // CHUNK):
        at = pl.ds(chunk * CHUNK, CHUNK)
        inner = lax.dot_general(left[at], right, (((1,), (1,)), ((), ())), preferred_element_type=jnp.float32)
        squared = inner + jnp.concatenate([squares[at]] * 2, axis=1) + sq
        high, low = halves(squared * lax.rsqrt(squared))
        high_out[0, at] = high
        low_out[0, at] = low
        total[at] += product(high, member) + product(low, member)

    @pl.when(step == STEPS - 1)
    def _():
        cohesion = jnp.zeros((1, CLUSTER_COUNT), jnp.float32)
        for offset in range(8):
            member = seed_member(rows[offset, pl.ds(points, 1)][:, :points])
            if offset == 0:
                counts = jnp.sum(member, axis=0, keepdims=True)
            cohesion += jnp.sum(member * total[pl.ds(offset * points, points)], axis=0, keepdims=True)
        store_by_member(order, total, tail_rows(cohesion, counts), out)


def member_kernel(order, own, other, high_in, low_in, out, sums, total):
    step = pl.program_id(0)
    points = own.shape[1] - SIDE

    @pl.when(step == 0)
    def _():
        sums[...] = jnp.zeros_like(sums)
        for block in range(8):
            sums[...] += own[block, pl.ds(points, SIDE)] + other[block, pl.ds(points, SIDE)]
        sums[pl.ds(2, 1)] = jnp.zeros((1, CLUSTER_COUNT), jnp.float32)
        total[...] = jnp.zeros_like(total)

    first = (step % (STEPS // 2)) * 2
    attraction = jnp.where(step < STEPS // 2, own[pl.ds(first, 2)], other[pl.ds(first, 2)])
    attraction = attraction[:, :points].reshape(TILE, CLUSTER_COUNT)
    member = jnp.exp(log_softmax_energy(attraction, sums[pl.ds(1, 1)], sums[pl.ds(0, 1)]))
    sums[pl.ds(2, 1)] += jnp.sum(member, axis=0, keepdims=True)
    high, low = halves(member)
    both = jnp.concatenate([high, low], axis=1)
    for chunk in range(total.shape[0] // CHUNK):
        at = pl.ds(chunk * CHUNK, CHUNK)
        wide = product(high_in[0, at], both)
        total[at] += wide[:, :CLUSTER_COUNT] + wide[:, CLUSTER_COUNT:] + product(low_in[0, at], high)

    @pl.when(step == STEPS - 1)
    def _():
        store_by_member(order, total, tail_rows(sums[pl.ds(2, 1)]), out)


PARAMS = pltpu.CompilerParams(dimension_semantics=("arbitrary",), vmem_limit_bytes=40 << 20)


def pairs(order, rows, own, other):
    blocks, lines, width = rows.shape
    tall = blocks * (lines - SIDE)
    half = STEPS // 2
    tile = lambda where: pl.BlockSpec((2, lines, width), where)
    piece = pl.BlockSpec((1, tall, TILE), lambda step, order: (step, 0, 0))
    kept = jax.ShapeDtypeStruct((STEPS, tall, TILE), jnp.bfloat16)
    return pl.pallas_call(
        pair_kernel,
        out_shape=(kept, kept, jax.ShapeDtypeStruct((blocks, lines, CLUSTER_COUNT), jnp.float32)),
        grid_spec=pltpu.PrefetchScalarGridSpec(
            num_scalar_prefetch=1,
            grid=(STEPS,),
            in_specs=[
                pl.BlockSpec((blocks, lines, width), lambda step, order: (0, 0, 0)),
                tile(lambda step, order: (jnp.minimum(step, half - 1), 0, 0)),
                tile(lambda step, order: (jnp.maximum(step - half, 0), 0, 0)),
            ],
            out_specs=[piece, piece, pl.BlockSpec((blocks, lines, CLUSTER_COUNT), lambda step, order: (0, 0, 0))],
            scratch_shapes=[
                pltpu.VMEM((tall, 3 * width), jnp.bfloat16),
                pltpu.VMEM((tall, 128), jnp.float32),
                pltpu.VMEM((tall, CLUSTER_COUNT), jnp.float32),
            ],
        ),
        compiler_params=PARAMS,
        name="pairs",
    )(order, rows, own, other)


def members(order, own, other, high, low):
    blocks, lines, clusters = own.shape
    tall = blocks * (lines - SIDE)
    whole = pl.BlockSpec((blocks, lines, clusters), lambda step, order: (0, 0, 0))
    piece = pl.BlockSpec((1, tall, TILE), lambda step, order: (step, 0, 0))
    return pl.pallas_call(
        member_kernel,
        out_shape=jax.ShapeDtypeStruct(own.shape, jnp.float32),
        grid_spec=pltpu.PrefetchScalarGridSpec(
            num_scalar_prefetch=1,
            grid=(STEPS,),
            in_specs=[whole, whole, piece, piece],
            out_specs=whole,
            scratch_shapes=[pltpu.VMEM((SIDE, clusters), jnp.float32), pltpu.VMEM((tall, clusters), jnp.float32)],
        ),
        compiler_params=PARAMS,
        name="members",
    )(order, own, other, high, low)


def copies(x, count):
    return jnp.broadcast_to(x, (count, *x.shape))


def other_core(x):
    return lax.ppermute(x, "core", [(0, 1), (1, 0)])


def log_softmax_energy(attraction, counts, cohesion):
    energy = attraction / counts - cohesion / (2.0 * counts**2)
    logits = -energy / ANNEAL_TEMP_VALUE
    highest = jnp.max(logits, axis=1, keepdims=True)
    return logits - highest - jnp.log(jnp.sum(jnp.exp(logits - highest), axis=1, keepdims=True))


def shards(embedding, seed_cluster):
    points, width = embedding.shape
    side = jnp.concatenate([seed_cluster.astype(jnp.float32), jnp.sum(embedding * embedding, axis=1)])
    block = jnp.concatenate([embedding, jnp.broadcast_to(side, (SIDE, width))], axis=0)
    rows = row_peers(block)
    rows, columns = lax.optimization_barrier((rows, exchange_columns(copies(block, 8))))
    order = member_order()
    high, low, weighted = pairs(order, rows, columns, other_core(columns))

    first = jnp.sum(exchange_rows(weighted), axis=0)
    firsts = exchange_columns(copies(first, 8))
    others = other_core(firsts)
    weighted = members(order, firsts, others, high, low)
    cohesion, counts = jnp.sum(firsts[:, points : points + 2] + others[:, points : points + 2], axis=0)
    own = jnp.exp(log_softmax_energy(first[:points], counts, cohesion))

    second = jnp.sum(exchange_rows(weighted), axis=0)
    attraction, counts = second[:points], second[points : points + 1]
    parts = lax.all_to_all(copies(jnp.sum(own * attraction, axis=0, keepdims=True), 128), EVERY, 0, 0, tiled=True)
    return log_softmax_energy(attraction, counts, jnp.sum(parts, axis=0))


def solution(mesh):
    finer = Mesh(mesh.devices.reshape(SIZES), EVERY)
    return jax.shard_map(
        shards, mesh=finer, in_specs=(P(EVERY, None), P(EVERY)), out_specs=P(EVERY, None), check_vma=False
    )
```

time: 120 us -> 128 us (1.067)
  Pallas kernels: 0 us -> 20.6 us
  matrix products: 15.5 us -> 0 us
  local copies, waits for them, and re-layouts: 3.45 us -> 9.5 us
  other arithmetic: 8.47 us -> 4.34 us
  blocking collectives: 41.6 us -> 43.7 us
  waiting for transfers between devices: 30.9 us -> 29.2 us
  starting transfers between devices: 18.9 us -> 20.5 us
    pallas_call x0 -> x2, Pallas kernels: none -> 20.6 us  [the longest x1 13.9 us: pairs(): pl.pallas_call(pair_kernel, out_shape=(kept, kept, jax.ShapeDtypeStruct((...]
    dot_general x12 -> x0, matrix products: 15.5 us -> none  [the longest x2 7.9 us: shards(): jnp.dot(row_points, points_of(part, points).T, precision=lax.Precision.HIGH)]
    unnamed x15 -> x8, local copies, waits for them, and re-layouts: 2 us -> 8.26 us
    ppermute x4, waiting for transfers between devices: 19 us -> 15 us  [moved(): return lax.ppermute(x, EVERY, pairs)]
    ppermute x2, waiting for transfers between devices: 1.63 us -> 3.95 us  [other_core(): return lax.ppermute(x, 'core', [(0, 1), (1, 0)])]
    concatenate x6 -> x0, other arithmetic: 1.31 us -> none  [the longest x2 0.87 us: summed(): jnp.concatenate([by_member(weighted.reshape(8, points, -1)), tail], axis=1)]
  transfers between devices with their start and end apart: 8 -> 8, of which waited for: 7 -> 6; matrix products, arithmetic and copies ran while one was open for 2% -> 0% of each run, Pallas kernels for 0% -> 0%
where the time goes in v4:
time: 128 us
  blocking collectives  43.7 us (34%)
  waiting for transfers between devices  29.2 us (23%)
  Pallas kernels  20.6 us (16%)
  starting transfers between devices  20.5 us (16%)
  local copies, waits for them, and re-layouts  9.5 us (7%)
  other arithmetic  4.34 us (3%)
    all_to_all x1, blocking collectives, exchange_columns(): lax.all_to_all(blocks, EVERY, 0, 0, axis_index_groups=COLUMN_GROUPS, tile...  16.3 us
    ppermute x4, waiting for transfers between devices, moved(): return lax.ppermute(x, EVERY, pairs)  15 us
    all_to_all x1, blocking collectives, exchange_rows(): return lax.all_to_all(blocks, ('y_lo', 'x'), 0, 0, tiled=True)  14.1 us
    pallas_call x1, Pallas kernels, pairs(): pl.pallas_call(pair_kernel, out_shape=(kept, kept, jax.ShapeDtypeStruct((...  13.9 us
    all_to_all x1, blocking collectives, shards(): lax.all_to_all(copies(jnp.sum(own * attraction, axis=0, keepdims=True), 1...  13.2 us
    all_to_all x1, waiting for transfers between devices, exchange_rows(): return lax.all_to_all(blocks, ('y_lo', 'x'), 0, 0, tiled=True)  10.2 us
    all_to_all x1, starting transfers between devices, exchange_columns(): lax.all_to_all(blocks, EVERY, 0, 0, axis_index_groups=COLUMN_GROUPS, tile...  8.31 us
    unnamed x8, local copies, waits for them, and re-layouts  8.26 us
  transfers between devices with their start and end apart: 8, of which 6 were waited for; matrix products, arithmetic and copies ran while one was open for 0% of the time, Pallas kernels for 0%

profile of v4, /device:TPU:1, one launch (start us, length us, event | category | flops | bytes accessed | tf_op | source)
XLA Modules:
  0.0 128.0 jit_solution(16936017449244590431)
XLA Ops:
  0.7 1.0 multiply_reduce_fusion
  1.7 0.9 fusion.11
  2.6 1.1 broadcast_in_dim.9
  3.7 8.3 %all-to-all-start = ((f32[8,136,256]{2,1,0:T(8,128)}), f32[8,136,256]{2,1,0:T(8,128)S(1)}, u32[]{:S(2)}, u32[]{:S(2)}) async-start(f32[8,136,256]{2,1,0:T(8,128)} %broadcast_in_dim.9), calls=%async_computation | async-start | bytes 2228224 | tf_op jit(solution)/shard_map/all_to_all | solution.py:38
  12.1 4.1 %collective-permute-done = f32[136,256]{1,0:T(8,128)S(1)} collective-permute-done((f32[136,256]{1,0:T(8,128)S(1)}, f32[136,256]{1,0:T(8,128)S(1)}, u32[]{:S(2)}, u32[]{:S(2)}) %collective-permute-start) | collective-permute-done | bytes 139296 | tf_op jit(solution)/shard_map/ppermute | solution.py:45
  16.3 2.8 %collective-permute-start.2 = (f32[2,136,256]{2,1,0:T(8,128)S(1)}, f32[2,136,256]{2,1,0:T(8,128)S(1)}, u32[]{:S(2)}, u32[]{:S(2)}) collective-permute-start(f32[2,136,256]{2,1,0:T(8,128)S(1)} %get-tuple-element.16), channel_id=1, source_target_pairs={{4,0},{5,1},{6,2},{7,3},{0,4},{1,5},{2,6},{3,7},{12,8},{13,9},{14,... | collective-permute-start | bytes 835592 | tf_op jit(solution)/shard_map/ppermute | solution.py:45
  19.1 0.9 collective-permute-start.1
  20.6 3.6 %collective-permute-done.2 = f32[2,136,256]{2,1,0:T(8,128)S(1)} collective-permute-done((f32[2,136,256]{2,1,0:T(8,128)S(1)}, f32[2,136,256]{2,1,0:T(8,128)S(1)}, u32[]{:S(2)}, u32[]{:S(2)}) %collective-permute-start.2) | collective-permute-done | bytes 278560 | tf_op jit(solution)/shard_map/ppermute | solution.py:45
  24.1 7.3 %collective-permute-done.1 = f32[2,136,256]{2,1,0:T(8,128)S(1)} collective-permute-done((f32[2,136,256]{2,1,0:T(8,128)S(1)}, f32[2,136,256]{2,1,0:T(8,128)S(1)}, u32[]{:S(2)}, u32[]{:S(2)}) %collective-permute-start.1) | collective-permute-done | bytes 278560 | tf_op jit(solution)/shard_map/ppermute | solution.py:45
  31.7 1.6 %collective-permute-start.4 = (f32[8,136,256]{2,1,0:T(8,128)S(1)}, f32[8,136,256]{2,1,0:T(8,128)S(1)}, u32[]{:S(2)}, u32[]{:S(2)}) collective-permute-start(f32[8,136,256]{2,1,0:T(8,128)S(1)} %all-to-all-done.own), channel_id=1, source_target_pairs={{0,1},{1,0},{2,3},{3,2},{4,5},{5,4},{6,7},{7,6},{8,9},{9,8},{10,11... | collective-permute-start | bytes 3342344 | tf_op jit(solution)/shard_map/ppermute | solution.py:224
  33.3 2.4 %collective-permute-done.4.other = f32[8,136,256]{2,1,0:T(8,128)S(1)} collective-permute-done((f32[8,136,256]{2,1,0:T(8,128)S(1)}, f32[8,136,256]{2,1,0:T(8,128)S(1)}, u32[]{:S(2)}, u32[]{:S(2)}) %collective-permute-start.4) | collective-permute-done | bytes 1114144 | tf_op jit(solution)/shard_map/ppermute | solution.py:224
  35.7 13.9 %pairs.1 = (bf16[8,1024,256]{2,1,0:T(8,128)(2,1)S(1)}, bf16[8,1024,256]{2,1,0:T(8,128)(2,1)S(1)}, f32[8,136,128]{2,1,0:T(8,128)S(1)}) custom-call(s32[8]{0:T(128)S(1)} %fusion.5.order, f32[8,136,256]{2,1,0:T(8,128)S(1)} %bitcast.22, f32[8,136,256]{2,1,0:T(8,128)S(1)} %all-to-all-done.own, f32[8,136,256]{2,1,0:T(8,128)S(1)} %collective-permute-done.4.other), custom_call_target="tpu_custom_call" | custom-call | tf_op jit(solution)/shard_map/pairs/pallas_call | solution.py:176
  49.7 1.9 %copy-done = bf16[8,1024,256]{2,1,0:T(8,128)(2,1)} copy-done((bf16[8,1024,256]{2,1,0:T(8,128)(2,1)}, bf16[8,1024,256]{2,1,0:T(8,128)(2,1)S(1)}, u32[]{:S(2)}) %copy-start) | copy-done | bytes 4194328
  51.6 2.0 %copy-done.2 = bf16[8,1024,256]{2,1,0:T(8,128)(2,1)} copy-done((bf16[8,1024,256]{2,1,0:T(8,128)(2,1)}, bf16[8,1024,256]{2,1,0:T(8,128)(2,1)S(1)}, u32[]{:S(2)}) %copy-start.2) | copy-done | bytes 4194328
  53.5 14.1 %all_to_all.25 = f32[8,136,128]{2,1,0:T(8,128)S(1)} all-to-all(f32[8,136,128]{2,1,0:T(8,128)S(1)} %get-tuple-element.12), channel_id=1, replica_groups=mesh['y_lo'=2,'z'=4,'y_hi'=2,'x'=4,'core'=2] {'y_lo','x'}, dimensions={0} | all-to-all | bytes 1114112 | tf_op jit(solution)/shard_map/all_to_all | solution.py:34
  67.8 16.3 %all_to_all.26.own = f32[8,136,128]{2,1,0:T(8,128)S(1)} all-to-all(f32[8,136,128]{2,1,0:T(8,128)S(1)} %broadcast_in_dim.20), channel_id=1, replica_groups={{0,16,32,48,72,88,104,120},{1,17,33,49,73,89,105,121},{2,18,34,50,74,90..., dimensions={0} | all-to-all | bytes 1114112 | tf_op jit(solution)/shard_map/all_to_all | solution.py:38
  84.1 2.6 %collective-permute-start.5 = (f32[8,136,128]{2,1,0:T(8,128)S(1)}, f32[8,136,128]{2,1,0:T(8,128)S(1)}, u32[]{:S(2)}, u32[]{:S(2)}) collective-permute-start(f32[8,136,128]{2,1,0:T(8,128)S(1)} %all_to_all.26.own), channel_id=1, source_target_pairs={{0,1},{1,0},{2,3},{3,2},{4,5},{5,4},{6,7},{7,6},{8,9},{9,8},{10,11... | collective-permute-start | bytes 1671176 | tf_op jit(solution)/shard_map/ppermute | solution.py:224
  86.7 1.6 %collective-permute-done.5.other = f32[8,136,128]{2,1,0:T(8,128)S(1)} collective-permute-done((f32[8,136,128]{2,1,0:T(8,128)S(1)}, f32[8,136,128]{2,1,0:T(8,128)S(1)}, u32[]{:S(2)}, u32[]{:S(2)}) %collective-permute-start.5) | collective-permute-done | bytes 557088 | tf_op jit(solution)/shard_map/ppermute | solution.py:224
  88.3 2.2 %copy-done.1 = bf16[8,1024,256]{2,1,0:T(8,128)(2,1)S(1)} copy-done((bf16[8,1024,256]{2,1,0:T(8,128)(2,1)S(1)}, bf16[8,1024,256]{2,1,0:T(8,128)(2,1)}, u32[]{:S(2)}) %copy-start.1) | copy-done | bytes 4194328
  90.5 2.2 %copy-done.3 = bf16[8,1024,256]{2,1,0:T(8,128)(2,1)S(1)} copy-done((bf16[8,1024,256]{2,1,0:T(8,128)(2,1)S(1)}, bf16[8,1024,256]{2,1,0:T(8,128)(2,1)}, u32[]{:S(2)}) %copy-start.3) | copy-done | bytes 4194328
  92.7 6.6 %members.1 = f32[8,136,128]{2,1,0:T(8,128)} custom-call(s32[8]{0:T(128)S(1)} %fusion.5.order, f32[8,136,128]{2,1,0:T(8,128)S(1)} %all_to_all.26.own, f32[8,136,128]{2,1,0:T(8,128)S(1)} %collective-permute-done.5.other, bf16[8,1024,256]{2,1,0:T(8,128)(2,1)S(1)} %copy-done.1, bf16[8,1024,256]{2,1,0:T(8,128)(2,1)S(1)} %copy-done.3), custom_call_target="tpu_custom_call" | custom-call | tf_op jit(solution)/shard_map/members/pallas_call | solution.py:204
  99.3 3.5 %all-to-all-start.3 = ((f32[8,136,128]{2,1,0:T(8,128)}), f32[8,136,128]{2,1,0:T(8,128)S(1)}, u32[]{:S(2)}, u32[]{:S(2)}) async-start(f32[8,136,128]{2,1,0:T(8,128)} %members.1), calls=%async_computation.3 | async-start | bytes 1114112 | tf_op jit(solution)/shard_map/all_to_all | solution.py:34
  103.2 10.2 %all-to-all-done.3 = f32[8,136,128]{2,1,0:T(8,128)S(1)} async-done(((f32[8,136,128]{2,1,0:T(8,128)}), f32[8,136,128]{2,1,0:T(8,128)S(1)}, u32[]{:S(2)}, u32[]{:S(2)}) %all-to-all-start.3) | async-done | bytes 557088 | tf_op jit(solution)/shard_map/all_to_all | solution.py:34
  113.6 13.2 %all_to_all.27 = f32[128,1,128]{2,1,0:T(1,128)S(1)} all-to-all(f32[128,1,128]{2,1,0:T(1,128)S(1)} %broadcast_in_dim.21), channel_id=1, replica_groups=mesh['y_lo'=2,'z'=4,'y_hi'=2,'x'=4,'core'=2] {'y_lo','z','y_hi','x','core'}, dimensions={0} | all-to-all | bytes 131072 | tf_op jit(solution)/shard_map/all_to_all | solution.py:252
  (31 shorter events, 3.3 us)
Async XLA Ops:
  3.7 28.0 %all-to-all-start = ((f32[8,136,256]{2,1,0:T(8,128)}), f32[8,136,256]{2,1,0:T(8,128)S(1)}, u32[]{:S(2)}, u32[]{:S(2)}) async-start(f32[8,136,256]{2,1,0:T(8,128)} %broadcast_in_dim.9), calls=%async_computation | async-start | bytes 2228224 | tf_op jit(solution)/shard_map/all_to_all | solution.py:38
  12.0 4.2 %collective-permute-start = (f32[136,256]{1,0:T(8,128)S(1)}, f32[136,256]{1,0:T(8,128)S(1)}, u32[]{:S(2)}, u32[]{:S(2)}) collective-permute-start(f32[136,256]{1,0:T(8,128)S(1)} %get-tuple-element.18), channel_id=1, source_target_pairs={{64,0},{65,1},{66,2},{67,3},{68,4},{69,5},{70,6},{71,7},{72,8},{73... | collective-permute-start | bytes 417800 | tf_op jit(solution)/shard_map/ppermute | solution.py:45
  16.3 7.9 %collective-permute-start.2 = (f32[2,136,256]{2,1,0:T(8,128)S(1)}, f32[2,136,256]{2,1,0:T(8,128)S(1)}, u32[]{:S(2)}, u32[]{:S(2)}) collective-permute-start(f32[2,136,256]{2,1,0:T(8,128)S(1)} %get-tuple-element.16), channel_id=1, source_target_pairs={{4,0},{5,1},{6,2},{7,3},{0,4},{1,5},{2,6},{3,7},{12,8},{13,9},{14,... | collective-permute-start | bytes 835592 | tf_op jit(solution)/shard_map/ppermute | solution.py:45
  19.1 12.4 %collective-permute-start.1 = (f32[2,136,256]{2,1,0:T(8,128)S(1)}, f32[2,136,256]{2,1,0:T(8,128)S(1)}, u32[]{:S(2)}, u32[]{:S(2)}) collective-permute-start(f32[2,136,256]{2,1,0:T(8,128)S(1)} %get-tuple-element.16), channel_id=1, source_target_pairs={{2,0},{3,1},{4,2},{5,3},{6,4},{7,5},{0,6},{1,7},{10,8},{11,9},{12,... | collective-permute-start | bytes 835592 | tf_op jit(solution)/shard_map/ppermute | solution.py:45
  19.9 11.5 %collective-permute-start.3 = (f32[2,136,256]{2,1,0:T(8,128)S(1)}, f32[2,136,256]{2,1,0:T(8,128)S(1)}, u32[]{:S(2)}, u32[]{:S(2)}) collective-permute-start(f32[2,136,256]{2,1,0:T(8,128)S(1)} %get-tuple-element.16), channel_id=1, source_target_pairs={{6,0},{7,1},{0,2},{1,3},{2,4},{3,5},{4,6},{5,7},{14,8},{15,9},{8,1... | collective-permute-start | bytes 835592 | tf_op jit(solution)/shard_map/ppermute | solution.py:45
  31.7 4.0 %collective-permute-start.4 = (f32[8,136,256]{2,1,0:T(8,128)S(1)}, f32[8,136,256]{2,1,0:T(8,128)S(1)}, u32[]{:S(2)}, u32[]{:S(2)}) collective-permute-start(f32[8,136,256]{2,1,0:T(8,128)S(1)} %all-to-all-done.own), channel_id=1, source_target_pairs={{0,1},{1,0},{2,3},{3,2},{4,5},{5,4},{6,7},{7,6},{8,9},{9,8},{10,11... | collective-permute-start | bytes 3342344 | tf_op jit(solution)/shard_map/ppermute | solution.py:224
  49.6 1.9 %copy-start = (bf16[8,1024,256]{2,1,0:T(8,128)(2,1)}, bf16[8,1024,256]{2,1,0:T(8,128)(2,1)S(1)}, u32[]{:S(2)}) copy-start(bf16[8,1024,256]{2,1,0:T(8,128)(2,1)S(1)} %get-tuple-element.13.high_in) | copy-start | bytes 12582916
  51.6 2.0 %copy-start.2 = (bf16[8,1024,256]{2,1,0:T(8,128)(2,1)}, bf16[8,1024,256]{2,1,0:T(8,128)(2,1)S(1)}, u32[]{:S(2)}) copy-start(bf16[8,1024,256]{2,1,0:T(8,128)(2,1)S(1)} %get-tuple-element.14.low_in) | copy-start | bytes 12582916
  84.1 4.2 %collective-permute-start.5 = (f32[8,136,128]{2,1,0:T(8,128)S(1)}, f32[8,136,128]{2,1,0:T(8,128)S(1)}, u32[]{:S(2)}, u32[]{:S(2)}) collective-permute-start(f32[8,136,128]{2,1,0:T(8,128)S(1)} %all_to_all.26.own), channel_id=1, source_target_pairs={{0,1},{1,0},{2,3},{3,2},{4,5},{5,4},{6,7},{7,6},{8,9},{9,8},{10,11... | collective-permute-start | bytes 1671176 | tf_op jit(solution)/shard_map/ppermute | solution.py:224
  88.3 2.2 %copy-start.1 = (bf16[8,1024,256]{2,1,0:T(8,128)(2,1)S(1)}, bf16[8,1024,256]{2,1,0:T(8,128)(2,1)}, u32[]{:S(2)}) copy-start(bf16[8,1024,256]{2,1,0:T(8,128)(2,1)} %copy-done) | copy-start | bytes 12582916
  90.5 2.2 %copy-start.3 = (bf16[8,1024,256]{2,1,0:T(8,128)(2,1)S(1)}, bf16[8,1024,256]{2,1,0:T(8,128)(2,1)}, u32[]{:S(2)}) copy-start(bf16[8,1024,256]{2,1,0:T(8,128)(2,1)} %copy-done.2) | copy-start | bytes 12582916
  99.3 14.1 %all-to-all-start.3 = ((f32[8,136,128]{2,1,0:T(8,128)}), f32[8,136,128]{2,1,0:T(8,128)S(1)}, u32[]{:S(2)}, u32[]{:S(2)}) async-start(f32[8,136,128]{2,1,0:T(8,128)} %members.1), calls=%async_computation.3 | async-start | bytes 1114112 | tf_op jit(solution)/shard_map/all_to_all | solution.py:34

commit v5 on v1

v5 whole, which is shorter than its diff:
```python
import itertools

import jax
import jax.numpy as jnp
from jax import lax
from jax.experimental import pallas as pl
from jax.experimental.pallas import tpu as pltpu
from jax.sharding import Mesh
from jax.sharding import PartitionSpec as P

CLUSTER_COUNT = 128
ANNEAL_TEMP_VALUE = 0.02
SIDE = 8

EVERY = ("y_lo", "z", "y_hi", "x", "core")
SIZES = (2, 4, 2, 4, 2)


def place(y_lo, z, y_hi, x, core):
    return (((y_lo * 4 + z) * 2 + y_hi) * 4 + x) * 2 + core


def column_groups():
    groups = []
    for pair, x, core in itertools.product(range(2), range(4), range(2)):
        groups.append([place(lo, z, lo ^ pair, x, core) for lo in range(2) for z in range(4)])
    return groups


COLUMN_GROUPS = column_groups()


def exchange_rows(blocks):
    return lax.all_to_all(blocks, ("y_lo", "x"), 0, 0, tiled=True)


def exchange_columns(blocks):
    return lax.all_to_all(blocks, EVERY, 0, 0, axis_index_groups=COLUMN_GROUPS, tiled=True)


def moved(x, flip, step):
    pairs = []
    for lo, z, hi, at, core in itertools.product(*map(range, SIZES)):
        pairs.append((place(lo ^ flip, z, hi, (at + step) % 4, core), place(lo, z, hi, at, core)))
    return lax.ppermute(x, EVERY, pairs)


def row_peers(x):
    pair = jnp.stack([x, moved(x, 1, 0)])
    return [pair] + [moved(pair, 0, step) for step in range(1, 4)]


def member_order():
    y_lo, x = lax.axis_index("y_lo"), lax.axis_index("x")
    offset = jnp.arange(8, dtype=jnp.int32)
    return (y_lo ^ (offset % 2)) * 4 + (x + offset // 2) % 4


def halves(x):
    high = x.astype(jnp.bfloat16)
    return high, (x - high.astype(jnp.float32)).astype(jnp.bfloat16)


def product(a, b):
    return jnp.dot(a, b, preferred_element_type=jnp.float32)


def seed_member(seeds):
    labels = lax.broadcasted_iota(jnp.int32, (CLUSTER_COUNT, seeds.shape[1]), 0).astype(jnp.float32)
    return 0.5 * (labels == seeds).astype(jnp.float32).T + 0.5 / CLUSTER_COUNT


def tail_rows(*lines):
    at = lax.broadcasted_iota(jnp.int32, (SIDE, CLUSTER_COUNT), 0)
    tail = jnp.zeros((SIDE, CLUSTER_COUNT), jnp.float32)
    for index, line in enumerate(lines):
        tail = jnp.where(at == index, line, tail)
    return tail


def column_kernel(own, other, right, squares, member):
    points, width = own.shape[1] - SIDE, own.shape[2]
    for source, start in ((own, 0), (other, 8)):
        for block in range(8):
            at = pl.ds((start + block) * points, points)
            high, low = halves(source[block, pl.ds(0, points)])
            right[at, pl.ds(0, width)] = high
            right[at, pl.ds(width, width)] = low
            right[at, pl.ds(2 * width, width)] = high
            line = source[block, pl.ds(points, 1)]
            squares[:, at] = jnp.broadcast_to(line[:, points:], (SIDE, points))
            member[at] = seed_member(line[:, :points]).astype(jnp.bfloat16)


def pair_kernel(rows, right, squares, member, high_out, low_out, out):
    blocks, lines, width = rows.shape
    points = lines - SIDE
    x = rows[:, pl.ds(0, points)].reshape(blocks * points, width)
    square = jnp.sum(x * x, axis=1, keepdims=True) + 1.0
    high, low = halves(-2.0 * x)
    left = jnp.concatenate([high, high, low], axis=1)
    inner = lax.dot_general(left, right[...], (((1,), (1,)), ((), ())), preferred_element_type=jnp.float32)
    squared = inner + square + squares[pl.ds(0, 1)]
    high, low = halves(squared * lax.rsqrt(squared))
    high_out[...] = high
    low_out[...] = low
    total = product(high, member[...]) + product(low, member[...])
    cohesion = jnp.zeros((1, CLUSTER_COUNT), jnp.float32)
    counts = []
    for block in range(blocks):
        own = seed_member(rows[block, pl.ds(points, 1)][:, :points])
        part = total[block * points : (block + 1) * points]
        out[block, pl.ds(0, points)] = part
        cohesion += jnp.sum(own * part, axis=0, keepdims=True)
        counts.append(jnp.sum(own, axis=0, keepdims=True))
    out[0, pl.ds(points, SIDE)] = tail_rows(cohesion, counts[0])


def place_kernel(order, first, second, third, fourth, out):
    parts = (first, second, third, fourth)
    points = first.shape[1] - SIDE
    cohesion = sum(part[0, pl.ds(points, 1)] for part in parts)
    tail = tail_rows(cohesion, first[0, pl.ds(points + 1, 1)])
    for offset in range(8):
        member = order[offset]
        out[member, pl.ds(0, points)] = parts[offset // 2][offset % 2, pl.ds(0, points)]
        out[member, pl.ds(points, SIDE)] = tail


def member_kernel(order, own, other, *rest):
    *kept, out, both = rest
    points = own.shape[1] - SIDE
    sums = jnp.zeros((SIDE, CLUSTER_COUNT), jnp.float32)
    for block in range(8):
        sums += own[block, pl.ds(points, SIDE)] + other[block, pl.ds(points, SIDE)]
    cohesion, counts = sums[0:1], sums[1:2]
    sizes = jnp.zeros((1, CLUSTER_COUNT), jnp.float32)
    for source, start in ((own, 0), (other, 8)):
        for block in range(8):
            member = jnp.exp(log_softmax_energy(source[block, pl.ds(0, points)], counts, cohesion))
            sizes += jnp.sum(member, axis=0, keepdims=True)
            at = pl.ds((start + block) * points, points)
            both[at, pl.ds(0, CLUSTER_COUNT)], both[at, pl.ds(CLUSTER_COUNT, CLUSTER_COUNT)] = halves(member)
    tail = tail_rows(sizes)
    for step in range(4):
        wide = product(kept[2 * step][...], both[...])
        total = product(kept[2 * step + 1][...], both[:, pl.ds(0, CLUSTER_COUNT)])
        total += wide[:, :CLUSTER_COUNT] + wide[:, CLUSTER_COUNT:]
        for block in range(2):
            place_at = order[2 * step + block]
            out[place_at, pl.ds(0, points)] = total[block * points : (block + 1) * points]
            out[place_at, pl.ds(points, SIDE)] = tail


def sum_kernel(blocks, out, *spread):
    total = blocks[0]
    for block in range(1, 8):
        total += blocks[block]
    out[...] = total
    for copy in spread:
        copy[...] = jnp.broadcast_to(total, copy.shape)


def on_chip(kernel, name, shapes, inputs, with_order=False, scratch=()):
    vmem = pl.BlockSpec(memory_space=pltpu.VMEM)
    specs = [vmem] * len(inputs)
    if with_order:
        specs[0] = pl.BlockSpec(memory_space=pltpu.SMEM)
    shapes = [jax.ShapeDtypeStruct(*shape) for shape in shapes]
    return pl.pallas_call(
        kernel,
        out_shape=shapes,
        in_specs=specs,
        out_specs=[vmem] * len(shapes),
        scratch_shapes=scratch,
        compiler_params=pltpu.CompilerParams(vmem_limit_bytes=12 << 20),
        name=name,
    )(*inputs)


def copies(x, count):
    return jnp.broadcast_to(x, (count, *x.shape))


def other_core(x):
    return lax.ppermute(x, "core", [(0, 1), (1, 0)])


def log_softmax_energy(attraction, counts, cohesion):
    energy = attraction / counts - cohesion / (2.0 * counts**2)
    logits = -energy / ANNEAL_TEMP_VALUE
    highest = jnp.max(logits, axis=1, keepdims=True)
    return logits - highest - jnp.log(jnp.sum(jnp.exp(logits - highest), axis=1, keepdims=True))


def shards(embedding, seed_cluster):
    points, width = embedding.shape
    side = jnp.concatenate([seed_cluster.astype(jnp.float32), jnp.sum(embedding * embedding, axis=1)])
    block = jnp.concatenate([embedding, jnp.broadcast_to(side, (SIDE, width))], axis=0)
    columns = exchange_columns(copies(block, 8))
    rows = row_peers(block)
    columns, _ = lax.optimization_barrier((columns, rows[1]))
    order = member_order()
    tall = 16 * points
    prepared = on_chip(
        column_kernel,
        "columns",
        [((tall, 3 * width), jnp.bfloat16), ((SIDE, tall), jnp.float32), ((tall, CLUSTER_COUNT), jnp.bfloat16)],
        [columns, other_core(columns)],
    )
    kept, weighted = [], []
    for two in rows:
        piece = ((2 * points, tall), jnp.bfloat16)
        out = ((2, points + SIDE, CLUSTER_COUNT), jnp.float32)
        high, low, part = on_chip(pair_kernel, "pairs", [piece, piece, out], [two, *prepared])
        kept += [high, low]
        weighted.append(part)
    exchange = [((8, points + SIDE, CLUSTER_COUNT), jnp.float32)]
    (weighted,) = on_chip(place_kernel, "place", exchange, [order, *weighted], with_order=True)

    line = ((points + SIDE, CLUSTER_COUNT), jnp.float32)
    first, spread = on_chip(sum_kernel, "sum_spread", [line, *exchange], [exchange_rows(weighted)])
    firsts = exchange_columns(spread)
    others = other_core(firsts)
    (weighted,) = on_chip(
        member_kernel,
        "members",
        exchange,
        [order, firsts, others, *kept],
        with_order=True,
        scratch=[pltpu.VMEM((tall, 2 * CLUSTER_COUNT), jnp.bfloat16)],
    )
    cohesion, counts = jnp.sum(firsts[:, points : points + 2] + others[:, points : points + 2], axis=0)
    own = jnp.exp(log_softmax_energy(first[:points], counts, cohesion))

    (second,) = on_chip(sum_kernel, "sum", [line], [exchange_rows(weighted)])
    attraction, counts = second[:points], second[points : points + 1]
    parts = lax.all_to_all(copies(jnp.sum(own * attraction, axis=0, keepdims=True), 128), EVERY, 0, 0, tiled=True)
    return log_softmax_energy(attraction, counts, jnp.sum(parts, axis=0))


def solution(mesh):
    finer = Mesh(mesh.devices.reshape(SIZES), EVERY)
    return jax.shard_map(
        shards, mesh=finer, in_specs=(P(EVERY, None), P(EVERY)), out_specs=P(EVERY, None), check_vma=False
    )
```

time: 131 us -> 111 us (0.85)
  blocking collectives: 62.2 us -> 37.7 us
  matrix products: 19 us -> 0 us
  Pallas kernels: 0 us -> 13 us
  starting transfers between devices: 13.9 us -> 24.2 us
  waiting for transfers between devices: 25.5 us -> 30.5 us
  other arithmetic: 7.9 us -> 4.18 us
    all_to_all x2 -> x1, blocking collectives: 37.2 us -> 12.4 us  [exchange_columns(): lax.all_to_all(blocks, EVERY, 0, 0, axis_index_groups=COLUMN_GROUPS, tile...]
    dot_general x6 -> x0, matrix products: 19 us -> none  [the longest x2 7.54 us: shards(): jnp.dot(distance, first_member(seeds), precision=lax.Precision.HIGH)]
    ppermute x0 -> x4, waiting for transfers between devices: none -> 15 us  [moved(): return lax.ppermute(x, EVERY, pairs)]
    all_to_all x2 -> x1, waiting for transfers between devices: 23.9 us -> 10.2 us  [exchange_rows(): return lax.all_to_all(blocks, ('y_lo', 'x'), 0, 0, tiled=True)]
    pallas_call x0 -> x9, Pallas kernels: none -> 13 us  [on_chip(): pl.pallas_call(kernel, out_shape=shapes, in_specs=specs, out_specs=[vmem]...]
    all_to_all x0 -> x1, starting transfers between devices: none -> 8.31 us  [exchange_columns(): lax.all_to_all(blocks, EVERY, 0, 0, axis_index_groups=COLUMN_GROUPS, tile...]
    ppermute x0 -> x4, starting transfers between devices: none -> 6.34 us  [moved(): return lax.ppermute(x, EVERY, pairs)]
    all_to_all x2 -> x1, starting transfers between devices: 7.56 us -> 3.54 us  [exchange_rows(): return lax.all_to_all(blocks, ('y_lo', 'x'), 0, 0, tiled=True)]
  transfers between devices with their start and end apart: 4 -> 8, of which waited for: 3 -> 7; matrix products, arithmetic and copies ran while one was open for 5% -> 0% of each run, Pallas kernels for 0% -> 5%
where the time goes in v5:
time: 111 us
  blocking collectives  37.7 us (34%)
  waiting for transfers between devices  30.5 us (27%)
  starting transfers between devices  24.2 us (22%)
  Pallas kernels  13 us (12%)
  other arithmetic  4.18 us (4%)
  local copies, waits for them, and re-layouts  1.11 us (1%)
    ppermute x4, waiting for transfers between devices, moved(): return lax.ppermute(x, EVERY, pairs)  15 us
    all_to_all x1, blocking collectives, shards(): lax.all_to_all(copies(jnp.sum(own * attraction, axis=0, keepdims=True), 1...  13.2 us
    pallas_call x9, Pallas kernels, on_chip(): pl.pallas_call(kernel, out_shape=shapes, in_specs=specs, out_specs=[vmem]...  13 us
    all_to_all x1, blocking collectives, exchange_columns(): lax.all_to_all(blocks, EVERY, 0, 0, axis_index_groups=COLUMN_GROUPS, tile...  12.4 us
    all_to_all x1, blocking collectives, exchange_rows(): return lax.all_to_all(blocks, ('y_lo', 'x'), 0, 0, tiled=True)  12 us
    all_to_all x1, waiting for transfers between devices, exchange_rows(): return lax.all_to_all(blocks, ('y_lo', 'x'), 0, 0, tiled=True)  10.2 us
    all_to_all x1, starting transfers between devices, exchange_columns(): lax.all_to_all(blocks, EVERY, 0, 0, axis_index_groups=COLUMN_GROUPS, tile...  8.31 us
    ppermute x4, starting transfers between devices, moved(): return lax.ppermute(x, EVERY, pairs)  6.34 us
  transfers between devices with their start and end apart: 8, of which 7 were waited for; matrix products, arithmetic and copies ran while one was open for 0% of the time, Pallas kernels for 5%

profile of v5, /device:TPU:1, one launch (start us, length us, event | category | flops | bytes accessed | tf_op | source)
XLA Modules:
  0.0 110.8 jit_solution(9785824693420073478)
XLA Ops:
  0.7 1.0 multiply_reduce_fusion
  2.6 1.1 broadcast_in_dim.7
  3.7 8.3 %all-to-all-start = ((f32[8,136,256]{2,1,0:T(8,128)}), f32[8,136,256]{2,1,0:T(8,128)S(1)}, u32[]{:S(2)}, u32[]{:S(2)}) async-start(f32[8,136,256]{2,1,0:T(8,128)} %broadcast_in_dim.7), calls=%async_computation | async-start | bytes 2228224 | tf_op jit(solution)/shard_map/all_to_all | solution.py:38
  12.1 4.1 %collective-permute-done = f32[136,256]{1,0:T(8,128)S(1)} collective-permute-done((f32[136,256]{1,0:T(8,128)S(1)}, f32[136,256]{1,0:T(8,128)S(1)}, u32[]{:S(2)}, u32[]{:S(2)}) %collective-permute-start) | collective-permute-done | bytes 139296 | tf_op jit(solution)/shard_map/ppermute | solution.py:45
  16.3 2.5 %collective-permute-start.1 = (f32[2,136,256]{2,1,0:T(8,128)S(1)}, f32[2,136,256]{2,1,0:T(8,128)S(1)}, u32[]{:S(2)}, u32[]{:S(2)}) collective-permute-start(f32[2,136,256]{2,1,0:T(8,128)S(1)} %pad_maximum_fusion.rows), channel_id=1, source_target_pairs={{2,0},{3,1},{4,2},{5,3},{6,4},{7,5},{0,6},{1,7},{10,8},{11,9},{12,... | collective-permute-start | bytes 835592 | tf_op jit(solution)/shard_map/ppermute | solution.py:45
  18.8 4.1 %collective-permute-done.1.rows = f32[2,136,256]{2,1,0:T(8,128)S(1)} collective-permute-done((f32[2,136,256]{2,1,0:T(8,128)S(1)}, f32[2,136,256]{2,1,0:T(8,128)S(1)}, u32[]{:S(2)}, u32[]{:S(2)}) %collective-permute-start.1) | collective-permute-done | bytes 278560 | tf_op jit(solution)/shard_map/ppermute | solution.py:45
  22.9 3.8 %all-to-all-done.own = f32[8,136,256]{2,1,0:T(8,128)S(1)} async-done(((f32[8,136,256]{2,1,0:T(8,128)}), f32[8,136,256]{2,1,0:T(8,128)S(1)}, u32[]{:S(2)}, u32[]{:S(2)}) %all-to-all-start) | async-done | bytes 1114144 | tf_op jit(solution)/shard_map/all_to_all | solution.py:38
  26.6 2.5 %collective-permute-start.2 = (f32[8,136,256]{2,1,0:T(8,128)S(1)}, f32[8,136,256]{2,1,0:T(8,128)S(1)}, u32[]{:S(2)}, u32[]{:S(2)}) collective-permute-start(f32[8,136,256]{2,1,0:T(8,128)S(1)} %all-to-all-done.own), channel_id=1, source_target_pairs={{0,1},{1,0},{2,3},{3,2},{4,5},{5,4},{6,7},{7,6},{8,9},{9,8},{10,11... | collective-permute-start | bytes 3342344 | tf_op jit(solution)/shard_map/ppermute | solution.py:186
  29.1 1.2 %collective-permute-start.4 = (f32[2,136,256]{2,1,0:T(8,128)S(1)}, f32[2,136,256]{2,1,0:T(8,128)S(1)}, u32[]{:S(2)}, u32[]{:S(2)}) collective-permute-start(f32[2,136,256]{2,1,0:T(8,128)S(1)} %pad_maximum_fusion.rows), channel_id=1, source_target_pairs={{6,0},{7,1},{0,2},{1,3},{2,4},{3,5},{4,6},{5,7},{14,8},{15,9},{8,1... | collective-permute-start | bytes 835592 | tf_op jit(solution)/shard_map/ppermute | solution.py:45
  30.3 2.5 %collective-permute-start.3 = (f32[2,136,256]{2,1,0:T(8,128)S(1)}, f32[2,136,256]{2,1,0:T(8,128)S(1)}, u32[]{:S(2)}, u32[]{:S(2)}) collective-permute-start(f32[2,136,256]{2,1,0:T(8,128)S(1)} %pad_maximum_fusion.rows), channel_id=1, source_target_pairs={{4,0},{5,1},{6,2},{7,3},{0,4},{1,5},{2,6},{3,7},{12,8},{13,9},{14,... | collective-permute-start | bytes 835592 | tf_op jit(solution)/shard_map/ppermute | solution.py:45
  33.3 1.8 %pairs.4 = (bf16[256,2048]{1,0:T(8,128)(2,1)S(1)}, bf16[256,2048]{1,0:T(8,128)(2,1)S(1)}, f32[2,136,128]{2,1,0:T(8,128)S(1)}) custom-call(f32[2,136,256]{2,1,0:T(8,128)S(1)} %pad_maximum_fusion.rows, bf16[2048,768]{1,0:T(8,128)(2,1)S(1)} %get-tuple-element.24.right, f32[8,2048]{1,0:T(8,128)S(1)} %get-tuple-element.25.squares, ...), custom_call_target="tpu_custom_call" | custom-call | tf_op jit(solution)/shard_map/pairs/pallas_call | solution.py:170
  35.1 1.8 %pairs.5 = (bf16[256,2048]{1,0:T(8,128)(2,1)S(1)}, bf16[256,2048]{1,0:T(8,128)(2,1)S(1)}, f32[2,136,128]{2,1,0:T(8,128)S(1)}) custom-call(f32[2,136,256]{2,1,0:T(8,128)S(1)} %collective-permute-done.1.rows, bf16[2048,768]{1,0:T(8,128)(2,1)S(1)} %get-tuple-element.24.right, f32[8,2048]{1,0:T(8,128)S(1)} %get-tuple-element.25.squares, ...), custom_call_target="tpu_custom_call" | custom-call | tf_op jit(solution)/shard_map/pairs/pallas_call | solution.py:170
  36.9 1.7 %collective-permute-done.4.rows = f32[2,136,256]{2,1,0:T(8,128)S(1)} collective-permute-done((f32[2,136,256]{2,1,0:T(8,128)S(1)}, f32[2,136,256]{2,1,0:T(8,128)S(1)}, u32[]{:S(2)}, u32[]{:S(2)}) %collective-permute-start.4) | collective-permute-done | bytes 278560 | tf_op jit(solution)/shard_map/ppermute | solution.py:45
  38.6 1.8 %pairs.7 = (bf16[256,2048]{1,0:T(8,128)(2,1)S(1)}, bf16[256,2048]{1,0:T(8,128)(2,1)S(1)}, f32[2,136,128]{2,1,0:T(8,128)S(1)}) custom-call(f32[2,136,256]{2,1,0:T(8,128)S(1)} %collective-permute-done.4.rows, bf16[2048,768]{1,0:T(8,128)(2,1)S(1)} %get-tuple-element.24.right, f32[8,2048]{1,0:T(8,128)S(1)} %get-tuple-element.25.squares, ...), custom_call_target="tpu_custom_call" | custom-call | tf_op jit(solution)/shard_map/pairs/pallas_call | solution.py:170
  40.4 5.2 %collective-permute-done.3.rows = f32[2,136,256]{2,1,0:T(8,128)S(1)} collective-permute-done((f32[2,136,256]{2,1,0:T(8,128)S(1)}, f32[2,136,256]{2,1,0:T(8,128)S(1)}, u32[]{:S(2)}, u32[]{:S(2)}) %collective-permute-start.3) | collective-permute-done | bytes 278560 | tf_op jit(solution)/shard_map/ppermute | solution.py:45
  45.5 1.8 %pairs.6 = (bf16[256,2048]{1,0:T(8,128)(2,1)S(1)}, bf16[256,2048]{1,0:T(8,128)(2,1)S(1)}, f32[2,136,128]{2,1,0:T(8,128)S(1)}) custom-call(f32[2,136,256]{2,1,0:T(8,128)S(1)} %collective-permute-done.3.rows, bf16[2048,768]{1,0:T(8,128)(2,1)S(1)} %get-tuple-element.24.right, f32[8,2048]{1,0:T(8,128)S(1)} %get-tuple-element.25.squares, ...), custom_call_target="tpu_custom_call" | custom-call | tf_op jit(solution)/shard_map/pairs/pallas_call | solution.py:170
  47.9 12.0 %all_to_all.25.blocks = f32[8,136,128]{2,1,0:T(8,128)S(1)} all-to-all(f32[8,136,128]{2,1,0:T(8,128)S(1)} %place.1), channel_id=1, replica_groups=mesh['y_lo'=2,'z'=4,'y_hi'=2,'x'=4,'core'=2] {'y_lo','x'}, dimensions={0} | all-to-all | bytes 1114112 | tf_op jit(solution)/shard_map/all_to_all | solution.py:34
  60.0 12.4 %all_to_all.26.own = f32[8,136,128]{2,1,0:T(8,128)S(1)} all-to-all(f32[8,136,128]{2,1,0:T(8,128)S(1)} %get-tuple-element.31), channel_id=1, replica_groups={{0,16,32,48,72,88,104,120},{1,17,33,49,73,89,105,121},{2,18,34,50,74,90..., dimensions={0} | all-to-all | bytes 1114112 | tf_op jit(solution)/shard_map/all_to_all | solution.py:38
  72.4 3.5 %collective-permute-start.5 = (f32[8,136,128]{2,1,0:T(8,128)S(1)}, f32[8,136,128]{2,1,0:T(8,128)S(1)}, u32[]{:S(2)}, u32[]{:S(2)}) collective-permute-start(f32[8,136,128]{2,1,0:T(8,128)S(1)} %all_to_all.26.own), channel_id=1, source_target_pairs={{0,1},{1,0},{2,3},{3,2},{4,5},{5,4},{6,7},{7,6},{8,9},{9,8},{10,11... | collective-permute-start | bytes 1671176 | tf_op jit(solution)/shard_map/ppermute | solution.py:186
  76.0 1.6 %collective-permute-done.5.other = f32[8,136,128]{2,1,0:T(8,128)S(1)} collective-permute-done((f32[8,136,128]{2,1,0:T(8,128)S(1)}, f32[8,136,128]{2,1,0:T(8,128)S(1)}, u32[]{:S(2)}, u32[]{:S(2)}) %collective-permute-start.5) | collective-permute-done | bytes 557088 | tf_op jit(solution)/shard_map/ppermute | solution.py:186
  77.6 4.6 %members.1 = f32[8,136,128]{2,1,0:T(8,128)} custom-call(s32[8]{0:T(128)S(1)} %fusion.1.order, f32[8,136,128]{2,1,0:T(8,128)S(1)} %all_to_all.26.own, f32[8,136,128]{2,1,0:T(8,128)S(1)} %collective-permute-done.5.other, bf16[256,2048]{1,0:T(8,128)(2,1)S(1)} %get-tuple-element.32.rest_0_, bf16[256,2048]{1,0:T(8,128)(2,1)S(1)} %get-tuple-element.33.rest_1_, ...), custom_call_target="tpu_custom_call" | custom-call | tf_op jit(solution)/shard_map/members/pallas_call | solution.py:170
  82.2 3.5 %all-to-all-start.3 = ((f32[8,136,128]{2,1,0:T(8,128)}), f32[8,136,128]{2,1,0:T(8,128)S(1)}, u32[]{:S(2)}, u32[]{:S(2)}) async-start(f32[8,136,128]{2,1,0:T(8,128)} %members.1), calls=%async_computation.3 | async-start | bytes 1114112 | tf_op jit(solution)/shard_map/all_to_all | solution.py:34
  86.1 10.2 %all-to-all-done.3.blocks = f32[8,136,128]{2,1,0:T(8,128)S(1)} async-done(((f32[8,136,128]{2,1,0:T(8,128)}), f32[8,136,128]{2,1,0:T(8,128)S(1)}, u32[]{:S(2)}, u32[]{:S(2)}) %all-to-all-start.3) | async-done | bytes 557088 | tf_op jit(solution)/shard_map/all_to_all | solution.py:34
  96.5 13.2 %all_to_all.27 = f32[128,1,128]{2,1,0:T(1,128)S(1)} all-to-all(f32[128,1,128]{2,1,0:T(1,128)S(1)} %broadcast_in_dim.8), channel_id=1, replica_groups=mesh['y_lo'=2,'z'=4,'y_hi'=2,'x'=4,'core'=2] {'y_lo','z','y_hi','x','core'}, dimensions={0} | all-to-all | bytes 131072 | tf_op jit(solution)/shard_map/all_to_all | solution.py:238
  (25 shorter events, 4.6 us)
Async XLA Ops:
  3.7 22.9 %all-to-all-start = ((f32[8,136,256]{2,1,0:T(8,128)}), f32[8,136,256]{2,1,0:T(8,128)S(1)}, u32[]{:S(2)}, u32[]{:S(2)}) async-start(f32[8,136,256]{2,1,0:T(8,128)} %broadcast_in_dim.7), calls=%async_computation | async-start | bytes 2228224 | tf_op jit(solution)/shard_map/all_to_all | solution.py:38
  12.0 4.2 %collective-permute-start = (f32[136,256]{1,0:T(8,128)S(1)}, f32[136,256]{1,0:T(8,128)S(1)}, u32[]{:S(2)}, u32[]{:S(2)}) collective-permute-start(f32[136,256]{1,0:T(8,128)S(1)} %get-tuple-element.42), channel_id=1, source_target_pairs={{64,0},{65,1},{66,2},{67,3},{68,4},{69,5},{70,6},{71,7},{72,8},{73... | collective-permute-start | bytes 417800 | tf_op jit(solution)/shard_map/ppermute | solution.py:45
  16.3 6.6 %collective-permute-start.1 = (f32[2,136,256]{2,1,0:T(8,128)S(1)}, f32[2,136,256]{2,1,0:T(8,128)S(1)}, u32[]{:S(2)}, u32[]{:S(2)}) collective-permute-start(f32[2,136,256]{2,1,0:T(8,128)S(1)} %pad_maximum_fusion.rows), channel_id=1, source_target_pairs={{2,0},{3,1},{4,2},{5,3},{6,4},{7,5},{0,6},{1,7},{10,8},{11,9},{12,... | collective-permute-start | bytes 835592 | tf_op jit(solution)/shard_map/ppermute | solution.py:45
  26.6 6.1 %collective-permute-start.2 = (f32[8,136,256]{2,1,0:T(8,128)S(1)}, f32[8,136,256]{2,1,0:T(8,128)S(1)}, u32[]{:S(2)}, u32[]{:S(2)}) collective-permute-start(f32[8,136,256]{2,1,0:T(8,128)S(1)} %all-to-all-done.own), channel_id=1, source_target_pairs={{0,1},{1,0},{2,3},{3,2},{4,5},{5,4},{6,7},{7,6},{8,9},{9,8},{10,11... | collective-permute-start | bytes 3342344 | tf_op jit(solution)/shard_map/ppermute | solution.py:186
  29.1 9.5 %collective-permute-start.4 = (f32[2,136,256]{2,1,0:T(8,128)S(1)}, f32[2,136,256]{2,1,0:T(8,128)S(1)}, u32[]{:S(2)}, u32[]{:S(2)}) collective-permute-start(f32[2,136,256]{2,1,0:T(8,128)S(1)} %pad_maximum_fusion.rows), channel_id=1, source_target_pairs={{6,0},{7,1},{0,2},{1,3},{2,4},{3,5},{4,6},{5,7},{14,8},{15,9},{8,1... | collective-permute-start | bytes 835592 | tf_op jit(solution)/shard_map/ppermute | solution.py:45
  30.3 15.2 %collective-permute-start.3 = (f32[2,136,256]{2,1,0:T(8,128)S(1)}, f32[2,136,256]{2,1,0:T(8,128)S(1)}, u32[]{:S(2)}, u32[]{:S(2)}) collective-permute-start(f32[2,136,256]{2,1,0:T(8,128)S(1)} %pad_maximum_fusion.rows), channel_id=1, source_target_pairs={{4,0},{5,1},{6,2},{7,3},{0,4},{1,5},{2,6},{3,7},{12,8},{13,9},{14,... | collective-permute-start | bytes 835592 | tf_op jit(solution)/shard_map/ppermute | solution.py:45
  72.4 5.1 %collective-permute-start.5 = (f32[8,136,128]{2,1,0:T(8,128)S(1)}, f32[8,136,128]{2,1,0:T(8,128)S(1)}, u32[]{:S(2)}, u32[]{:S(2)}) collective-permute-start(f32[8,136,128]{2,1,0:T(8,128)S(1)} %all_to_all.26.own), channel_id=1, source_target_pairs={{0,1},{1,0},{2,3},{3,2},{4,5},{5,4},{6,7},{7,6},{8,9},{9,8},{10,11... | collective-permute-start | bytes 1671176 | tf_op jit(solution)/shard_map/ppermute | solution.py:186
  82.2 14.1 %all-to-all-start.3 = ((f32[8,136,128]{2,1,0:T(8,128)}), f32[8,136,128]{2,1,0:T(8,128)S(1)}, u32[]{:S(2)}, u32[]{:S(2)}) async-start(f32[8,136,128]{2,1,0:T(8,128)} %members.1), calls=%async_computation.3 | async-start | bytes 1114112 | tf_op jit(solution)/shard_map/all_to_all | solution.py:34

commit v6 on v5

--- a/solution.py
+++ b/solution.py
@@ -46,14 +46,15 @@
 
 
 def row_peers(x):
-    pair = jnp.stack([x, moved(x, 1, 0)])
-    return [pair] + [moved(pair, 0, step) for step in range(1, 4)]
+    return [moved(x, flip, step) if flip or step else x for flip in range(2) for step in (0, 1, 3, 2)]
 
 
 def member_order():
     y_lo, x = lax.axis_index("y_lo"), lax.axis_index("x")
     offset = jnp.arange(8, dtype=jnp.int32)
-    return (y_lo ^ (offset % 2)) * 4 + (x + offset // 2) % 4
+    step = offset % 4
+    step = jnp.where(step < 2, step, 5 - step)
+    return (y_lo ^ (offset // 4)) * 4 + (x + step) % 4
 
 
 def halves(x):
@@ -92,10 +93,10 @@
             member[at] = seed_member(line[:, :points]).astype(jnp.bfloat16)
 
 
-def pair_kernel(rows, right, squares, member, high_out, low_out, out):
-    blocks, lines, width = rows.shape
-    points = lines - SIDE
-    x = rows[:, pl.ds(0, points)].reshape(blocks * points, width)
+def pair_kernel(first, second, right, squares, member, high_out, low_out, out):
+    rows = (first, second)
+    points, width = first.shape[0] - SIDE, first.shape[1]
+    x = jnp.concatenate([block[pl.ds(0, points)] for block in rows], axis=0)
     square = jnp.sum(x * x, axis=1, keepdims=True) + 1.0
     high, low = halves(-2.0 * x)
     left = jnp.concatenate([high, high, low], axis=1)
@@ -107,8 +108,8 @@
     total = product(high, member[...]) + product(low, member[...])
     cohesion = jnp.zeros((1, CLUSTER_COUNT), jnp.float32)
     counts = []
-    for block in range(blocks):
-        own = seed_member(rows[block, pl.ds(points, 1)][:, :points])
+    for block in range(2):
+        own = seed_member(rows[block][pl.ds(points, 1)][:, :points])
         part = total[block * points : (block + 1) * points]
         out[block, pl.ds(0, points)] = part
         cohesion += jnp.sum(own * part, axis=0, keepdims=True)
@@ -199,7 +200,7 @@
     block = jnp.concatenate([embedding, jnp.broadcast_to(side, (SIDE, width))], axis=0)
     columns = exchange_columns(copies(block, 8))
     rows = row_peers(block)
-    columns, _ = lax.optimization_barrier((columns, rows[1]))
+    columns, *_ = lax.optimization_barrier((columns, *rows[1:5]))
     order = member_order()
     tall = 16 * points
     prepared = on_chip(
@@ -209,10 +210,10 @@
         [columns, other_core(columns)],
     )
     kept, weighted = [], []
-    for two in rows:
+    for at in range(0, 8, 2):
         piece = ((2 * points, tall), jnp.bfloat16)
         out = ((2, points + SIDE, CLUSTER_COUNT), jnp.float32)
-        high, low, part = on_chip(pair_kernel, "pairs", [piece, piece, out], [two, *prepared])
+        high, low, part = on_chip(pair_kernel, "pairs", [piece, piece, out], [*rows[at : at + 2], *prepared])
         kept += [high, low]
         weighted.append(part)
     exchange = [((8, points + SIDE, CLUSTER_COUNT), jnp.float32)]

time: 111 us -> 108 us (0.973)
  waiting for transfers between devices: 30.5 us -> 23.3 us
  starting transfers between devices: 24.2 us -> 26.9 us
  blocking collectives: 37.7 us -> 39.6 us
    ppermute x4 -> x7, waiting for transfers between devices: 15 us -> 6.69 us  [moved(): return lax.ppermute(x, EVERY, pairs)]
    ppermute x4 -> x7, starting transfers between devices: 6.34 us -> 8.91 us  [moved(): return lax.ppermute(x, EVERY, pairs)]
    all_to_all x1, blocking collectives: 12 us -> 13.3 us  [exchange_rows(): return lax.all_to_all(blocks, ('y_lo', 'x'), 0, 0, tiled=True)]
  transfers between devices with their start and end apart: 8 -> 11, of which waited for: 7 -> 6; matrix products, arithmetic and copies ran while one was open for 0% -> 0% of each run, Pallas kernels for 5% -> 5%
where the time goes in v6:
time: 108 us
  blocking collectives  39.6 us (37%)
  starting transfers between devices  26.9 us (25%)
  waiting for transfers between devices  23.3 us (22%)
  Pallas kernels  13 us (12%)
  other arithmetic  4.14 us (4%)
  local copies, waits for them, and re-layouts  1.11 us (1%)
    all_to_all x1, blocking collectives, exchange_rows(): return lax.all_to_all(blocks, ('y_lo', 'x'), 0, 0, tiled=True)  13.3 us
    all_to_all x1, blocking collectives, shards(): lax.all_to_all(copies(jnp.sum(own * attraction, axis=0, keepdims=True), 1...  13.2 us
    all_to_all x1, blocking collectives, exchange_columns(): lax.all_to_all(blocks, EVERY, 0, 0, axis_index_groups=COLUMN_GROUPS, tile...  13 us
    pallas_call x9, Pallas kernels, on_chip(): pl.pallas_call(kernel, out_shape=shapes, in_specs=specs, out_specs=[vmem]...  13 us
    all_to_all x1, waiting for transfers between devices, exchange_rows(): return lax.all_to_all(blocks, ('y_lo', 'x'), 0, 0, tiled=True)  10.2 us
    ppermute x7, starting transfers between devices, moved(): return lax.ppermute(x, EVERY, pairs)  8.91 us
    all_to_all x1, starting transfers between devices, exchange_columns(): lax.all_to_all(blocks, EVERY, 0, 0, axis_index_groups=COLUMN_GROUPS, tile...  8.31 us
    ppermute x7, waiting for transfers between devices, moved(): return lax.ppermute(x, EVERY, pairs)  6.69 us
  transfers between devices with their start and end apart: 11, of which 6 were waited for; matrix products, arithmetic and copies ran while one was open for 0% of the time, Pallas kernels for 5%

profile of v6, /device:TPU:1, one launch (start us, length us, event | category | flops | bytes accessed | tf_op | source)
XLA Modules:
  0.0 108.1 jit_solution(2833316257388632789)
XLA Ops:
  0.7 1.0 multiply_reduce_fusion
  2.6 1.1 broadcast_in_dim.7
  3.7 8.3 %all-to-all-start = ((f32[8,136,256]{2,1,0:T(8,128)}), f32[8,136,256]{2,1,0:T(8,128)S(1)}, u32[]{:S(2)}, u32[]{:S(2)}) async-start(f32[8,136,256]{2,1,0:T(8,128)} %broadcast_in_dim.7), calls=%async_computation | async-start | bytes 2228224 | tf_op jit(solution)/shard_map/all_to_all | solution.py:38
  12.0 2.5 %collective-permute-start = (f32[136,256]{1,0:T(8,128)S(1)}, f32[136,256]{1,0:T(8,128)S(1)}, u32[]{:S(2)}, u32[]{:S(2)}) collective-permute-start(f32[136,256]{1,0:T(8,128)S(1)} %pad_maximum_fusion.first), channel_id=1, source_target_pairs={{2,0},{3,1},{4,2},{5,3},{6,4},{7,5},{0,6},{1,7},{10,8},{11,9},{12,... | collective-permute-start | bytes 417800 | tf_op jit(solution)/shard_map/ppermute | solution.py:45
  14.5 1.7 %collective-permute-start.2 = (f32[136,256]{1,0:T(8,128)S(1)}, f32[136,256]{1,0:T(8,128)S(1)}, u32[]{:S(2)}, u32[]{:S(2)}) collective-permute-start(f32[136,256]{1,0:T(8,128)S(1)} %pad_maximum_fusion.first), channel_id=1, source_target_pairs={{4,0},{5,1},{6,2},{7,3},{0,4},{1,5},{2,6},{3,7},{12,8},{13,9},{14,... | collective-permute-start | bytes 417800 | tf_op jit(solution)/shard_map/ppermute | solution.py:45
  16.5 5.3 %collective-permute-done.1.first = f32[136,256]{1,0:T(8,128)S(1)} collective-permute-done((f32[136,256]{1,0:T(8,128)S(1)}, f32[136,256]{1,0:T(8,128)S(1)}, u32[]{:S(2)}, u32[]{:S(2)}) %collective-permute-start.1) | collective-permute-done | bytes 139296 | tf_op jit(solution)/shard_map/ppermute | solution.py:45
  21.8 4.8 %all-to-all-done.own = f32[8,136,256]{2,1,0:T(8,128)S(1)} async-done(((f32[8,136,256]{2,1,0:T(8,128)}), f32[8,136,256]{2,1,0:T(8,128)S(1)}, u32[]{:S(2)}, u32[]{:S(2)}) %all-to-all-start) | async-done | bytes 1114144 | tf_op jit(solution)/shard_map/all_to_all | solution.py:38
  26.6 2.5 %collective-permute-start.4 = (f32[8,136,256]{2,1,0:T(8,128)S(1)}, f32[8,136,256]{2,1,0:T(8,128)S(1)}, u32[]{:S(2)}, u32[]{:S(2)}) collective-permute-start(f32[8,136,256]{2,1,0:T(8,128)S(1)} %all-to-all-done.own), channel_id=1, source_target_pairs={{0,1},{1,0},{2,3},{3,2},{4,5},{5,4},{6,7},{7,6},{8,9},{9,8},{10,11... | collective-permute-start | bytes 3342344 | tf_op jit(solution)/shard_map/ppermute | solution.py:187
  29.1 1.4 %collective-permute-start.5 = (f32[136,256]{1,0:T(8,128)S(1)}, f32[136,256]{1,0:T(8,128)S(1)}, u32[]{:S(2)}, u32[]{:S(2)}) collective-permute-start(f32[136,256]{1,0:T(8,128)S(1)} %pad_maximum_fusion.first), channel_id=1, source_target_pairs={{66,0},{67,1},{68,2},{69,3},{70,4},{71,5},{64,6},{65,7},{74,8},{75... | collective-permute-start | bytes 417800 | tf_op jit(solution)/shard_map/ppermute | solution.py:45
  30.5 0.9 collective-permute-start.6
  31.4 2.2 %collective-permute-start.7 = (f32[136,256]{1,0:T(8,128)S(1)}, f32[136,256]{1,0:T(8,128)S(1)}, u32[]{:S(2)}, u32[]{:S(2)}) collective-permute-start(f32[136,256]{1,0:T(8,128)S(1)} %pad_maximum_fusion.first), channel_id=1, source_target_pairs={{68,0},{69,1},{70,2},{71,3},{64,4},{65,5},{66,6},{67,7},{76,8},{77... | collective-permute-start | bytes 417800 | tf_op jit(solution)/shard_map/ppermute | solution.py:45
  34.2 1.8 %pairs.5 = (bf16[256,2048]{1,0:T(8,128)(2,1)S(1)}, bf16[256,2048]{1,0:T(8,128)(2,1)S(1)}, f32[2,136,128]{2,1,0:T(8,128)S(1)}) custom-call(f32[136,256]{1,0:T(8,128)S(1)} %collective-permute-done.1.first, f32[136,256]{1,0:T(8,128)S(1)} %collective-permute-done.2.second, bf16[2048,768]{1,0:T(8,128)(2,1)S(1)} %get-tuple-element.24.right, ...), custom_call_target="tpu_custom_call" | custom-call | tf_op jit(solution)/shard_map/pairs/pallas_call | solution.py:171
  36.0 1.8 %pairs.4 = (bf16[256,2048]{1,0:T(8,128)(2,1)S(1)}, bf16[256,2048]{1,0:T(8,128)(2,1)S(1)}, f32[2,136,128]{2,1,0:T(8,128)S(1)}) custom-call(f32[136,256]{1,0:T(8,128)S(1)} %pad_maximum_fusion.first, f32[136,256]{1,0:T(8,128)S(1)} %collective-permute-done.second, bf16[2048,768]{1,0:T(8,128)(2,1)S(1)} %get-tuple-element.24.right, ...), custom_call_target="tpu_custom_call" | custom-call | tf_op jit(solution)/shard_map/pairs/pallas_call | solution.py:171
  37.8 1.8 %pairs.6 = (bf16[256,2048]{1,0:T(8,128)(2,1)S(1)}, bf16[256,2048]{1,0:T(8,128)(2,1)S(1)}, f32[2,136,128]{2,1,0:T(8,128)S(1)}) custom-call(f32[136,256]{1,0:T(8,128)S(1)} %collective-permute-done.3.first, f32[136,256]{1,0:T(8,128)S(1)} %collective-permute-done.5.second, bf16[2048,768]{1,0:T(8,128)(2,1)S(1)} %get-tuple-element.24.right, ...), custom_call_target="tpu_custom_call" | custom-call | tf_op jit(solution)/shard_map/pairs/pallas_call | solution.py:171
  39.6 1.2 %collective-permute-done.7.second = f32[136,256]{1,0:T(8,128)S(1)} collective-permute-done((f32[136,256]{1,0:T(8,128)S(1)}, f32[136,256]{1,0:T(8,128)S(1)}, u32[]{:S(2)}, u32[]{:S(2)}) %collective-permute-start.7) | collective-permute-done | bytes 139296 | tf_op jit(solution)/shard_map/ppermute | solution.py:45
  40.8 1.8 %pairs.7 = (bf16[256,2048]{1,0:T(8,128)(2,1)S(1)}, bf16[256,2048]{1,0:T(8,128)(2,1)S(1)}, f32[2,136,128]{2,1,0:T(8,128)S(1)}) custom-call(f32[136,256]{1,0:T(8,128)S(1)} %collective-permute-done.6.first, f32[136,256]{1,0:T(8,128)S(1)} %collective-permute-done.7.second, bf16[2048,768]{1,0:T(8,128)(2,1)S(1)} %get-tuple-element.24.right, ...), custom_call_target="tpu_custom_call" | custom-call | tf_op jit(solution)/shard_map/pairs/pallas_call | solution.py:171
  43.2 13.3 %all_to_all.25.blocks = f32[8,136,128]{2,1,0:T(8,128)S(1)} all-to-all(f32[8,136,128]{2,1,0:T(8,128)S(1)} %place.1), channel_id=1, replica_groups=mesh['y_lo'=2,'z'=4,'y_hi'=2,'x'=4,'core'=2] {'y_lo','x'}, dimensions={0} | all-to-all | bytes 1114112 | tf_op jit(solution)/shard_map/all_to_all | solution.py:34
  56.6 13.0 %all_to_all.26.own = f32[8,136,128]{2,1,0:T(8,128)S(1)} all-to-all(f32[8,136,128]{2,1,0:T(8,128)S(1)} %get-tuple-element.31), channel_id=1, replica_groups={{0,16,32,48,72,88,104,120},{1,17,33,49,73,89,105,121},{2,18,34,50,74,90..., dimensions={0} | all-to-all | bytes 1114112 | tf_op jit(solution)/shard_map/all_to_all | solution.py:38
  69.6 3.7 %collective-permute-start.8 = (f32[8,136,128]{2,1,0:T(8,128)S(1)}, f32[8,136,128]{2,1,0:T(8,128)S(1)}, u32[]{:S(2)}, u32[]{:S(2)}) collective-permute-start(f32[8,136,128]{2,1,0:T(8,128)S(1)} %all_to_all.26.own), channel_id=1, source_target_pairs={{0,1},{1,0},{2,3},{3,2},{4,5},{5,4},{6,7},{7,6},{8,9},{9,8},{10,11... | collective-permute-start | bytes 1671176 | tf_op jit(solution)/shard_map/ppermute | solution.py:187
  73.3 1.6 %collective-permute-done.8.other = f32[8,136,128]{2,1,0:T(8,128)S(1)} collective-permute-done((f32[8,136,128]{2,1,0:T(8,128)S(1)}, f32[8,136,128]{2,1,0:T(8,128)S(1)}, u32[]{:S(2)}, u32[]{:S(2)}) %collective-permute-start.8) | collective-permute-done | bytes 557088 | tf_op jit(solution)/shard_map/ppermute | solution.py:187
  74.9 4.6 %members.1 = f32[8,136,128]{2,1,0:T(8,128)} custom-call(s32[8]{0:T(128)S(1)} %fusion.1.order, f32[8,136,128]{2,1,0:T(8,128)S(1)} %all_to_all.26.own, f32[8,136,128]{2,1,0:T(8,128)S(1)} %collective-permute-done.8.other, bf16[256,2048]{1,0:T(8,128)(2,1)S(1)} %get-tuple-element.32.rest_0_, bf16[256,2048]{1,0:T(8,128)(2,1)S(1)} %get-tuple-element.33.rest_1_, ...), custom_call_target="tpu_custom_call" | custom-call | tf_op jit(solution)/shard_map/members/pallas_call | solution.py:171
  79.4 3.5 %all-to-all-start.3 = ((f32[8,136,128]{2,1,0:T(8,128)}), f32[8,136,128]{2,1,0:T(8,128)S(1)}, u32[]{:S(2)}, u32[]{:S(2)}) async-start(f32[8,136,128]{2,1,0:T(8,128)} %members.1), calls=%async_computation.3 | async-start | bytes 1114112 | tf_op jit(solution)/shard_map/all_to_all | solution.py:34
  83.3 10.2 %all-to-all-done.3.blocks = f32[8,136,128]{2,1,0:T(8,128)S(1)} async-done(((f32[8,136,128]{2,1,0:T(8,128)}), f32[8,136,128]{2,1,0:T(8,128)S(1)}, u32[]{:S(2)}, u32[]{:S(2)}) %all-to-all-start.3) | async-done | bytes 557088 | tf_op jit(solution)/shard_map/all_to_all | solution.py:34
  93.8 13.2 %all_to_all.27 = f32[128,1,128]{2,1,0:T(1,128)S(1)} all-to-all(f32[128,1,128]{2,1,0:T(1,128)S(1)} %broadcast_in_dim.8), channel_id=1, replica_groups=mesh['y_lo'=2,'z'=4,'y_hi'=2,'x'=4,'core'=2] {'y_lo','z','y_hi','x','core'}, dimensions={0} | all-to-all | bytes 131072 | tf_op jit(solution)/shard_map/all_to_all | solution.py:239
  (30 shorter events, 4.7 us)
Async XLA Ops:
  3.7 22.9 %all-to-all-start = ((f32[8,136,256]{2,1,0:T(8,128)}), f32[8,136,256]{2,1,0:T(8,128)S(1)}, u32[]{:S(2)}, u32[]{:S(2)}) async-start(f32[8,136,256]{2,1,0:T(8,128)} %broadcast_in_dim.7), calls=%async_computation | async-start | bytes 2228224 | tf_op jit(solution)/shard_map/all_to_all | solution.py:38
  12.0 4.5 %collective-permute-start = (f32[136,256]{1,0:T(8,128)S(1)}, f32[136,256]{1,0:T(8,128)S(1)}, u32[]{:S(2)}, u32[]{:S(2)}) collective-permute-start(f32[136,256]{1,0:T(8,128)S(1)} %pad_maximum_fusion.first), channel_id=1, source_target_pairs={{2,0},{3,1},{4,2},{5,3},{6,4},{7,5},{0,6},{1,7},{10,8},{11,9},{12,... | collective-permute-start | bytes 417800 | tf_op jit(solution)/shard_map/ppermute | solution.py:45
  14.5 7.3 %collective-permute-start.1 = (f32[136,256]{1,0:T(8,128)S(1)}, f32[136,256]{1,0:T(8,128)S(1)}, u32[]{:S(2)}, u32[]{:S(2)}) collective-permute-start(f32[136,256]{1,0:T(8,128)S(1)} %pad_maximum_fusion.first), channel_id=1, source_target_pairs={{6,0},{7,1},{0,2},{1,3},{2,4},{3,5},{4,6},{5,7},{14,8},{15,9},{8,1... | collective-permute-start | bytes 417800 | tf_op jit(solution)/shard_map/ppermute | solution.py:45
  14.5 7.3 %collective-permute-start.2 = (f32[136,256]{1,0:T(8,128)S(1)}, f32[136,256]{1,0:T(8,128)S(1)}, u32[]{:S(2)}, u32[]{:S(2)}) collective-permute-start(f32[136,256]{1,0:T(8,128)S(1)} %pad_maximum_fusion.first), channel_id=1, source_target_pairs={{4,0},{5,1},{6,2},{7,3},{0,4},{1,5},{2,6},{3,7},{12,8},{13,9},{14,... | collective-permute-start | bytes 417800 | tf_op jit(solution)/shard_map/ppermute | solution.py:45
  16.2 5.6 %collective-permute-start.3 = (f32[136,256]{1,0:T(8,128)S(1)}, f32[136,256]{1,0:T(8,128)S(1)}, u32[]{:S(2)}, u32[]{:S(2)}) collective-permute-start(f32[136,256]{1,0:T(8,128)S(1)} %pad_maximum_fusion.first), channel_id=1, source_target_pairs={{64,0},{65,1},{66,2},{67,3},{68,4},{69,5},{70,6},{71,7},{72,8},{73... | collective-permute-start | bytes 417800 | tf_op jit(solution)/shard_map/ppermute | solution.py:45
  26.6 7.0 %collective-permute-start.4 = (f32[8,136,256]{2,1,0:T(8,128)S(1)}, f32[8,136,256]{2,1,0:T(8,128)S(1)}, u32[]{:S(2)}, u32[]{:S(2)}) collective-permute-start(f32[8,136,256]{2,1,0:T(8,128)S(1)} %all-to-all-done.own), channel_id=1, source_target_pairs={{0,1},{1,0},{2,3},{3,2},{4,5},{5,4},{6,7},{7,6},{8,9},{9,8},{10,11... | collective-permute-start | bytes 3342344 | tf_op jit(solution)/shard_map/ppermute | solution.py:187
  29.1 8.7 %collective-permute-start.5 = (f32[136,256]{1,0:T(8,128)S(1)}, f32[136,256]{1,0:T(8,128)S(1)}, u32[]{:S(2)}, u32[]{:S(2)}) collective-permute-start(f32[136,256]{1,0:T(8,128)S(1)} %pad_maximum_fusion.first), channel_id=1, source_target_pairs={{66,0},{67,1},{68,2},{69,3},{70,4},{71,5},{64,6},{65,7},{74,8},{75... | collective-permute-start | bytes 417800 | tf_op jit(solution)/shard_map/ppermute | solution.py:45
  30.5 9.1 %collective-permute-start.6 = (f32[136,256]{1,0:T(8,128)S(1)}, f32[136,256]{1,0:T(8,128)S(1)}, u32[]{:S(2)}, u32[]{:S(2)}) collective-permute-start(f32[136,256]{1,0:T(8,128)S(1)} %pad_maximum_fusion.first), channel_id=1, source_target_pairs={{70,0},{71,1},{64,2},{65,3},{66,4},{67,5},{68,6},{69,7},{78,8},{79... | collective-permute-start | bytes 417800 | tf_op jit(solution)/shard_map/ppermute | solution.py:45
  31.4 9.4 %collective-permute-start.7 = (f32[136,256]{1,0:T(8,128)S(1)}, f32[136,256]{1,0:T(8,128)S(1)}, u32[]{:S(2)}, u32[]{:S(2)}) collective-permute-start(f32[136,256]{1,0:T(8,128)S(1)} %pad_maximum_fusion.first), channel_id=1, source_target_pairs={{68,0},{69,1},{70,2},{71,3},{64,4},{65,5},{66,6},{67,7},{76,8},{77... | collective-permute-start | bytes 417800 | tf_op jit(solution)/shard_map/ppermute | solution.py:45
  69.6 5.3 %collective-permute-start.8 = (f32[8,136,128]{2,1,0:T(8,128)S(1)}, f32[8,136,128]{2,1,0:T(8,128)S(1)}, u32[]{:S(2)}, u32[]{:S(2)}) collective-permute-start(f32[8,136,128]{2,1,0:T(8,128)S(1)} %all_to_all.26.own), channel_id=1, source_target_pairs={{0,1},{1,0},{2,3},{3,2},{4,5},{5,4},{6,7},{7,6},{8,9},{9,8},{10,11... | collective-permute-start | bytes 1671176 | tf_op jit(solution)/shard_map/ppermute | solution.py:187
  79.4 14.1 %all-to-all-start.3 = ((f32[8,136,128]{2,1,0:T(8,128)}), f32[8,136,128]{2,1,0:T(8,128)S(1)}, u32[]{:S(2)}, u32[]{:S(2)}) async-start(f32[8,136,128]{2,1,0:T(8,128)} %members.1), calls=%async_computation.3 | async-start | bytes 1114112 | tf_op jit(solution)/shard_map/all_to_all | solution.py:34

commit v7 on v6

v7 whole, which is shorter than its diff:
```python
import functools
import itertools

import jax
import jax.numpy as jnp
from jax import lax
from jax.experimental import pallas as pl
from jax.experimental.pallas import tpu as pltpu
from jax.sharding import Mesh
from jax.sharding import PartitionSpec as P

CLUSTER_COUNT = 128
ANNEAL_TEMP_VALUE = 0.02
SIDE = 8

EVERY = ("y_lo", "z", "y_hi", "x", "core")
SIZES = (2, 4, 2, 4, 2)


def place(y_lo, z, y_hi, x, core):
    return (((y_lo * 4 + z) * 2 + y_hi) * 4 + x) * 2 + core


def column_groups():
    groups = []
    for pair, x, core in itertools.product(range(2), range(4), range(2)):
        groups.append([place(lo, z, lo ^ pair, x, core) for lo in range(2) for z in range(4)])
    return groups


COLUMN_GROUPS = column_groups()


def exchange_rows(blocks):
    return lax.all_to_all(blocks, ("y_lo", "x"), 0, 0, tiled=True)


def exchange_columns(blocks):
    return lax.all_to_all(blocks, EVERY, 0, 0, axis_index_groups=COLUMN_GROUPS, tiled=True)


def moved(x, flip, step):
    pairs = []
    for lo, z, hi, at, core in itertools.product(*map(range, SIZES)):
        pairs.append((place(lo ^ flip, z, hi, (at + step) % 4, core), place(lo, z, hi, at, core)))
    return lax.ppermute(x, EVERY, pairs)


def row_peers(x):
    return [moved(x, flip, step) if flip or step else x for flip in range(2) for step in (0, 1, 3, 2)]


def member_order():
    y_lo, x = lax.axis_index("y_lo"), lax.axis_index("x")
    offset = jnp.arange(8, dtype=jnp.int32)
    step = offset % 4
    step = jnp.where(step < 2, step, 5 - step)
    return (y_lo ^ (offset // 4)) * 4 + (x + step) % 4


def halves(x):
    high = x.astype(jnp.bfloat16)
    return high, (x - high.astype(jnp.float32)).astype(jnp.bfloat16)


def product(a, b):
    return jnp.dot(a, b, preferred_element_type=jnp.float32)


def seed_member(seeds):
    labels = lax.broadcasted_iota(jnp.int32, (CLUSTER_COUNT, seeds.shape[1]), 0).astype(jnp.float32)
    return 0.5 * (labels == seeds).astype(jnp.float32).T + 0.5 / CLUSTER_COUNT


def tail_rows(*lines):
    at = lax.broadcasted_iota(jnp.int32, (SIDE, CLUSTER_COUNT), 0)
    tail = jnp.zeros((SIDE, CLUSTER_COUNT), jnp.float32)
    for index, line in enumerate(lines):
        tail = jnp.where(at == index, line, tail)
    return tail


def column_kernel(own, other, right, squares, member):
    points, width = own.shape[1] - SIDE, own.shape[2]
    for source, start in ((own, 0), (other, 8)):
        for block in range(8):
            at = pl.ds((start + block) * points, points)
            high, low = halves(source[block, pl.ds(0, points)])
            right[at, pl.ds(0, width)] = high
            right[at, pl.ds(width, width)] = low
            right[at, pl.ds(2 * width, width)] = high
            line = source[block, pl.ds(points, 1)]
            squares[:, at] = jnp.broadcast_to(line[:, points:], (SIDE, points))
            member[at] = seed_member(line[:, :points]).astype(jnp.bfloat16)


def prepare_kernel(embedding, seeds, block, spread):
    points, width = embedding.shape
    x = embedding[...]
    side = jnp.concatenate([seeds[...].astype(jnp.float32), jnp.sum((x * x).T, axis=0, keepdims=True)], axis=1)
    side = jnp.broadcast_to(side, (SIDE, width))
    block[pl.ds(0, points)] = x
    block[pl.ds(points, SIDE)] = side
    for copy in range(spread.shape[0]):
        spread[copy, pl.ds(0, points)] = x
        spread[copy, pl.ds(points, SIDE)] = side


def pair_kernel(piece, order, first, second, right, squares, member, *rest):
    *_, high_out, low_out, out = rest
    points, width = first.shape[0] - SIDE, first.shape[1]
    at = pl.ds(piece * 2 * points, 2 * points)
    x = jnp.concatenate([first[pl.ds(0, points)], second[pl.ds(0, points)]], axis=0)
    square = jnp.sum(x * x, axis=1, keepdims=True) + 1.0
    high, low = halves(-2.0 * x)
    left = jnp.concatenate([high, high, low], axis=1)
    inner = lax.dot_general(left, right[...], (((1,), (1,)), ((), ())), preferred_element_type=jnp.float32)
    squared = inner + square + squares[pl.ds(0, 1)]
    high, low = halves(squared * lax.rsqrt(squared))
    high_out[at] = high
    low_out[at] = low
    total = product(high, member[...]) + product(low, member[...])
    if piece:
        tail = rest[2][order[0], pl.ds(points, SIDE)]
        cohesion, counts = tail[0:1], tail[1:2]
    else:
        cohesion = jnp.zeros((1, CLUSTER_COUNT), jnp.float32)
        counts = jnp.sum(seed_member(first[pl.ds(points, 1)][:, :points]), axis=0, keepdims=True)
    for index, block in enumerate((first, second)):
        own = seed_member(block[pl.ds(points, 1)][:, :points])
        part = total[index * points : (index + 1) * points]
        out[order[2 * piece + index], pl.ds(0, points)] = part
        cohesion += jnp.sum(own * part, axis=0, keepdims=True)
    tail = tail_rows(cohesion, counts)
    for target in range(8 if piece == 3 else 1):
        out[order[target], pl.ds(points, SIDE)] = tail


def member_kernel(order, own, other, high, low, first, out, own_member, both):
    points = own.shape[1] - SIDE
    sums = jnp.zeros((SIDE, CLUSTER_COUNT), jnp.float32)
    for block in range(8):
        sums += own[block, pl.ds(points, SIDE)] + other[block, pl.ds(points, SIDE)]
    cohesion, counts = sums[0:1], sums[1:2]
    own_member[...] = jnp.exp(log_softmax_energy(first[pl.ds(0, points)], counts, cohesion))
    sizes = jnp.zeros((1, CLUSTER_COUNT), jnp.float32)
    for source, start in ((own, 0), (other, 8)):
        for block in range(8):
            member = jnp.exp(log_softmax_energy(source[block, pl.ds(0, points)], counts, cohesion))
            sizes += jnp.sum(member, axis=0, keepdims=True)
            at = pl.ds((start + block) * points, points)
            both[at, pl.ds(0, CLUSTER_COUNT)], both[at, pl.ds(CLUSTER_COUNT, CLUSTER_COUNT)] = halves(member)
    tail = tail_rows(sizes)
    wide = product(high[...], both[...])
    total = product(low[...], both[:, pl.ds(0, CLUSTER_COUNT)])
    total += wide[:, :CLUSTER_COUNT] + wide[:, CLUSTER_COUNT:]
    for block in range(8):
        out[order[block], pl.ds(0, points)] = total[block * points : (block + 1) * points]
        out[order[block], pl.ds(points, SIDE)] = tail


def summed(blocks):
    total = blocks[0]
    for block in range(1, 8):
        total += blocks[block]
    return total


def sum_kernel(blocks, out, spread):
    out[...] = summed(blocks)
    spread[...] = jnp.broadcast_to(out[...], spread.shape)


def own_kernel(blocks, own, out, part):
    points = own.shape[0]
    out[...] = summed(blocks)
    part[...] = jnp.sum(own[...] * out[pl.ds(0, points)], axis=0, keepdims=True)


def final_kernel(second, cohesion, out):
    points = out.shape[0]
    out[...] = log_softmax_energy(second[pl.ds(0, points)], second[pl.ds(points, 1)], cohesion[...])


def on_chip(kernel, name, shapes, inputs, order_at=None, scratch=(), aliases={}):
    vmem = pl.BlockSpec(memory_space=pltpu.VMEM)
    specs = [vmem] * len(inputs)
    if order_at is not None:
        specs[order_at] = pl.BlockSpec(memory_space=pltpu.SMEM)
    shapes = [jax.ShapeDtypeStruct(*shape) for shape in shapes]
    return pl.pallas_call(
        kernel,
        out_shape=shapes,
        in_specs=specs,
        out_specs=[vmem] * len(shapes),
        scratch_shapes=scratch,
        input_output_aliases=aliases,
        compiler_params=pltpu.CompilerParams(vmem_limit_bytes=12 << 20),
        name=name,
    )(*inputs)


def copies(x, count):
    return jnp.broadcast_to(x, (count, *x.shape))


def other_core(x):
    return lax.ppermute(x, "core", [(0, 1), (1, 0)])


def log_softmax_energy(attraction, counts, cohesion):
    energy = attraction / counts - cohesion / (2.0 * counts**2)
    logits = -energy / ANNEAL_TEMP_VALUE
    highest = jnp.max(logits, axis=1, keepdims=True)
    return logits - highest - jnp.log(jnp.sum(jnp.exp(logits - highest), axis=1, keepdims=True))


def shards(embedding, seed_cluster):
    points, width = embedding.shape
    lines, tall = points + SIDE, 16 * points
    block, spread = on_chip(
        prepare_kernel,
        "prepare",
        [((lines, width), jnp.float32), ((8, lines, width), jnp.float32)],
        [embedding, seed_cluster.reshape(1, points)],
    )
    columns = exchange_columns(spread)
    rows = row_peers(block)
    columns, *_ = lax.optimization_barrier((columns, *rows[1:7]))
    order = member_order()
    prepared = on_chip(
        column_kernel,
        "columns",
        [((tall, 3 * width), jnp.bfloat16), ((SIDE, tall), jnp.float32), ((tall, CLUSTER_COUNT), jnp.bfloat16)],
        [columns, other_core(columns)],
    )
    kept = ((8 * points, tall), jnp.bfloat16)
    exchange = ((8, lines, CLUSTER_COUNT), jnp.float32)
    state = []
    for piece in range(4):
        state = on_chip(
            functools.partial(pair_kernel, piece),
            f"pairs_{piece}",
            [kept, kept, exchange],
            [order, *rows[2 * piece : 2 * piece + 2], *prepared, *state],
            order_at=0,
            aliases={6: 0, 7: 1, 8: 2} if state else {},
        )
    high, low, weighted = state

    line = ((lines, CLUSTER_COUNT), jnp.float32)
    first, spread = on_chip(sum_kernel, "sum_spread", [line, exchange], [exchange_rows(weighted)])
    firsts = exchange_columns(spread)
    weighted, own = on_chip(
        member_kernel,
        "members",
        [exchange, ((points, CLUSTER_COUNT), jnp.float32)],
        [order, firsts, other_core(firsts), high, low, first],
        order_at=0,
        scratch=[pltpu.VMEM((tall, 2 * CLUSTER_COUNT), jnp.bfloat16)],
    )

    part = ((1, CLUSTER_COUNT), jnp.float32)
    second, part = on_chip(own_kernel, "own_sums", [line, part], [exchange_rows(weighted), own])
    parts = lax.all_to_all(copies(part, 128), EVERY, 0, 0, tiled=True)
    (out,) = on_chip(
        final_kernel,
        "final",
        [((points, CLUSTER_COUNT), jnp.float32)],
        [second, jnp.sum(parts, axis=0)],
    )
    return out


def solution(mesh):
    finer = Mesh(mesh.devices.reshape(SIZES), EVERY)
    return jax.shard_map(
        shards, mesh=finer, in_specs=(P(EVERY, None), P(EVERY)), out_specs=P(EVERY, None), check_vma=False
    )
```

time: 108 us -> 107 us (level)
  blocking collectives: 39.6 us -> 57.5 us
  waiting for transfers between devices: 23.3 us -> 10.3 us
  starting transfers between devices: 26.9 us -> 22.1 us
  other arithmetic: 4.14 us -> 0.05 us
  Pallas kernels: 13 us -> 15.1 us
    all_to_all x1 -> x2, blocking collectives: 13.3 us -> 27.9 us  [exchange_rows(): return lax.all_to_all(blocks, ('y_lo', 'x'), 0, 0, tiled=True)]
    all_to_all x1 -> x0, waiting for transfers between devices: 10.2 us -> none  [exchange_rows(): return lax.all_to_all(blocks, ('y_lo', 'x'), 0, 0, tiled=True)]
    all_to_all x1, waiting for transfers between devices: 4.81 us -> 0.01 us  [exchange_columns(): lax.all_to_all(blocks, EVERY, 0, 0, axis_index_groups=COLUMN_GROUPS, tile...]
    all_to_all x1 -> x0, starting transfers between devices: 3.54 us -> none  [exchange_rows(): return lax.all_to_all(blocks, ('y_lo', 'x'), 0, 0, tiled=True)]
    all_to_all x1, blocking collectives: 13 us -> 16.1 us  [exchange_columns(): lax.all_to_all(blocks, EVERY, 0, 0, axis_index_groups=COLUMN_GROUPS, tile...]
    pallas_call x9 -> x10, Pallas kernels: 13 us -> 15.1 us  [on_chip(): pl.pallas_call(kernel, out_shape=shapes, in_specs=specs, out_specs=[vmem]...]
    ppermute x7, waiting for transfers between devices: 6.69 us -> 8.7 us  [moved(): return lax.ppermute(x, EVERY, pairs)]
    ppermute x2, starting transfers between devices: 6.13 us -> 4.13 us  [other_core(): return lax.ppermute(x, 'core', [(0, 1), (1, 0)])]
  transfers between devices with their start and end apart: 11 -> 10, of which waited for: 6 -> 5; matrix products, arithmetic and copies ran while one was open for 0% -> 0% of each run, Pallas kernels for 5% -> 7%
where the time goes in v7:
time: 107 us
  blocking collectives  57.5 us (54%)
  starting transfers between devices  22.1 us (21%)
  Pallas kernels  15.1 us (14%)
  waiting for transfers between devices  10.3 us (10%)
  local copies, waits for them, and re-layouts  1.6 us (1%)
    all_to_all x2, blocking collectives, exchange_rows(): return lax.all_to_all(blocks, ('y_lo', 'x'), 0, 0, tiled=True)  27.9 us
    all_to_all x1, blocking collectives, exchange_columns(): lax.all_to_all(blocks, EVERY, 0, 0, axis_index_groups=COLUMN_GROUPS, tile...  16.1 us
    pallas_call x10, Pallas kernels, on_chip(): pl.pallas_call(kernel, out_shape=shapes, in_specs=specs, out_specs=[vmem]...  15.1 us
    all_to_all x1, blocking collectives, shards(): parts = lax.all_to_all(copies(part, 128), EVERY, 0, 0, tiled=True)  13.5 us
    ppermute x7, starting transfers between devices, moved(): return lax.ppermute(x, EVERY, pairs)  9.69 us
    ppermute x7, waiting for transfers between devices, moved(): return lax.ppermute(x, EVERY, pairs)  8.7 us
    all_to_all x1, starting transfers between devices, exchange_columns(): lax.all_to_all(blocks, EVERY, 0, 0, axis_index_groups=COLUMN_GROUPS, tile...  8.31 us
    ppermute x2, starting transfers between devices, other_core(): return lax.ppermute(x, 'core', [(0, 1), (1, 0)])  4.13 us
  transfers between devices with their start and end apart: 10, of which 5 were waited for; matrix products, arithmetic and copies ran while one was open for 0% of the time, Pallas kernels for 7%

profile of v7, /device:TPU:1, one launch (start us, length us, event | category | flops | bytes accessed | tf_op | source)
XLA Modules:
  0.0 106.7 jit_solution(14504113630063959255)
XLA Ops:
  0.0 0.9 copy-done
  0.9 0.7 copy-done.1
  1.6 1.2 %prepare.1 = (f32[136,256]{1,0:T(8,128)S(1)}, f32[8,136,256]{2,1,0:T(8,128)}) custom-call(f32[128,256]{1,0:T(8,128)S(1)} %copy-done, s32[1,128]{1,0:T(1,128)S(1)} %bitcast.5), custom_call_target="tpu_custom_call" | custom-call | tf_op jit(solution)/shard_map/prepare/pallas_call | solution.py:191
  2.8 8.3 %all-to-all-start = ((f32[8,136,256]{2,1,0:T(8,128)}), f32[8,136,256]{2,1,0:T(8,128)S(1)}, u32[]{:S(2)}, u32[]{:S(2)}) async-start(f32[8,136,256]{2,1,0:T(8,128)} %get-tuple-element.30), calls=%async_computation | async-start | bytes 2228224 | tf_op jit(solution)/shard_map/all_to_all | solution.py:39
  11.1 2.3 %collective-permute-start.6 = (f32[136,256]{1,0:T(8,128)S(1)}, f32[136,256]{1,0:T(8,128)S(1)}, u32[]{:S(2)}, u32[]{:S(2)}) collective-permute-start(f32[136,256]{1,0:T(8,128)S(1)} %get-tuple-element.29.first), channel_id=1, source_target_pairs={{66,0},{67,1},{68,2},{69,3},{70,4},{71,5},{64,6},{65,7},{74,8},{75... | collective-permute-start | bytes 417800 | tf_op jit(solution)/shard_map/ppermute | solution.py:46
  13.4 1.3 %collective-permute-start.5 = (f32[136,256]{1,0:T(8,128)S(1)}, f32[136,256]{1,0:T(8,128)S(1)}, u32[]{:S(2)}, u32[]{:S(2)}) collective-permute-start(f32[136,256]{1,0:T(8,128)S(1)} %get-tuple-element.29.first), channel_id=1, source_target_pairs={{64,0},{65,1},{66,2},{67,3},{68,4},{69,5},{70,6},{71,7},{72,8},{73... | collective-permute-start | bytes 417800 | tf_op jit(solution)/shard_map/ppermute | solution.py:46
  15.9 2.1 %collective-permute-start.2 = (f32[136,256]{1,0:T(8,128)S(1)}, f32[136,256]{1,0:T(8,128)S(1)}, u32[]{:S(2)}, u32[]{:S(2)}) collective-permute-start(f32[136,256]{1,0:T(8,128)S(1)} %get-tuple-element.29.first), channel_id=1, source_target_pairs={{2,0},{3,1},{4,2},{5,3},{6,4},{7,5},{0,6},{1,7},{10,8},{11,9},{12,... | collective-permute-start | bytes 417800 | tf_op jit(solution)/shard_map/ppermute | solution.py:46
  18.0 2.1 %collective-permute-done.5.first = f32[136,256]{1,0:T(8,128)S(1)} collective-permute-done((f32[136,256]{1,0:T(8,128)S(1)}, f32[136,256]{1,0:T(8,128)S(1)}, u32[]{:S(2)}, u32[]{:S(2)}) %collective-permute-start.5) | collective-permute-done | bytes 139296 | tf_op jit(solution)/shard_map/ppermute | solution.py:46
  20.5 3.6 %collective-permute-done.3.first = f32[136,256]{1,0:T(8,128)S(1)} collective-permute-done((f32[136,256]{1,0:T(8,128)S(1)}, f32[136,256]{1,0:T(8,128)S(1)}, u32[]{:S(2)}, u32[]{:S(2)}) %collective-permute-start.3) | collective-permute-done | bytes 139296 | tf_op jit(solution)/shard_map/ppermute | solution.py:46
  24.1 2.6 %collective-permute-done.first = f32[136,256]{1,0:T(8,128)S(1)} collective-permute-done((f32[136,256]{1,0:T(8,128)S(1)}, f32[136,256]{1,0:T(8,128)S(1)}, u32[]{:S(2)}, u32[]{:S(2)}) %collective-permute-start) | collective-permute-done | bytes 139296 | tf_op jit(solution)/shard_map/ppermute | solution.py:46
  26.7 1.5 %collective-permute-start.7 = (f32[8,136,256]{2,1,0:T(8,128)S(1)}, f32[8,136,256]{2,1,0:T(8,128)S(1)}, u32[]{:S(2)}, u32[]{:S(2)}) collective-permute-start(f32[8,136,256]{2,1,0:T(8,128)S(1)} %all-to-all-done.own), channel_id=1, source_target_pairs={{0,1},{1,0},{2,3},{3,2},{4,5},{5,4},{6,7},{7,6},{8,9},{9,8},{10,11... | collective-permute-start | bytes 3342344 | tf_op jit(solution)/shard_map/ppermute | solution.py:208
  28.2 2.8 %collective-permute-start.1 = (f32[136,256]{1,0:T(8,128)S(1)}, f32[136,256]{1,0:T(8,128)S(1)}, u32[]{:S(2)}, u32[]{:S(2)}) collective-permute-start(f32[136,256]{1,0:T(8,128)S(1)} %get-tuple-element.29.first), channel_id=1, source_target_pairs={{68,0},{69,1},{70,2},{71,3},{64,4},{65,5},{66,6},{67,7},{76,8},{77... | collective-permute-start | bytes 417800 | tf_op jit(solution)/shard_map/ppermute | solution.py:46
  31.6 2.3 %pairs_0.1 = (bf16[1024,2048]{1,0:T(8,128)(2,1)S(1)}, bf16[1024,2048]{1,0:T(8,128)(2,1)S(1)}, f32[8,136,128]{2,1,0:T(8,128)S(1)}) custom-call(s32[8]{0:T(128)S(1)} %fusion.order, f32[136,256]{1,0:T(8,128)S(1)} %get-tuple-element.29.first, f32[136,256]{1,0:T(8,128)S(1)} %collective-permute-done.2.second, bf16[2048,768]{1,0:T(8,128)(2,1)S(1)} %get-tuple-element.32.right, ...), custom_call_target="tpu_custom_call" | custom-call | tf_op jit(solution)/shard_map/pairs_0/pallas_call | solution.py:191
  33.9 2.3 %pairs_1.1 = (bf16[1024,2048]{1,0:T(8,128)(2,1)S(1)}, bf16[1024,2048]{1,0:T(8,128)(2,1)S(1)}, f32[8,136,128]{2,1,0:T(8,128)S(1)}) custom-call(s32[8]{0:T(128)S(1)} %fusion.order, f32[136,256]{1,0:T(8,128)S(1)} %collective-permute-done.3.first, ...), custom_call_target="tpu_custom_call", output_to_operand_aliasing={{0}: (6, {}), {1}: (7, {}), {2}: (8, {})} | custom-call | tf_op jit(solution)/shard_map/pairs_1/pallas_call | solution.py:191
  36.1 2.3 %pairs_2.1 = (bf16[1024,2048]{1,0:T(8,128)(2,1)S(1)}, bf16[1024,2048]{1,0:T(8,128)(2,1)S(1)}, f32[8,136,128]{2,1,0:T(8,128)S(1)}) custom-call(s32[8]{0:T(128)S(1)} %fusion.order, f32[136,256]{1,0:T(8,128)S(1)} %collective-permute-done.5.first, ...), custom_call_target="tpu_custom_call", output_to_operand_aliasing={{0}: (6, {}), {1}: (7, {}), {2}: (8, {})} | custom-call | tf_op jit(solution)/shard_map/pairs_2/pallas_call | solution.py:191
  38.4 2.3 %pairs_3.1 = (bf16[1024,2048]{1,0:T(8,128)(2,1)S(1)}, bf16[1024,2048]{1,0:T(8,128)(2,1)S(1)}, f32[8,136,128]{2,1,0:T(8,128)S(1)}) custom-call(s32[8]{0:T(128)S(1)} %fusion.order, f32[136,256]{1,0:T(8,128)S(1)} %collective-permute-done.first, ...), custom_call_target="tpu_custom_call", output_to_operand_aliasing={{0}: (6, {}), {1}: (7, {}), {2}: (8, {})} | custom-call | tf_op jit(solution)/shard_map/pairs_3/pallas_call | solution.py:191
  40.7 14.9 %all_to_all.25.blocks = f32[8,136,128]{2,1,0:T(8,128)S(1)} all-to-all(f32[8,136,128]{2,1,0:T(8,128)S(1)} %get-tuple-element.44), channel_id=1, replica_groups=mesh['y_lo'=2,'z'=4,'y_hi'=2,'x'=4,'core'=2] {'y_lo','x'}, dimensions={0} | all-to-all | bytes 1114112 | tf_op jit(solution)/shard_map/all_to_all | solution.py:35
  55.7 16.1 %all_to_all.26.own = f32[8,136,128]{2,1,0:T(8,128)S(1)} all-to-all(f32[8,136,128]{2,1,0:T(8,128)S(1)} %get-tuple-element.45), channel_id=1, replica_groups={{0,16,32,48,72,88,104,120},{1,17,33,49,73,89,105,121},{2,18,34,50,74,90..., dimensions={0} | all-to-all | bytes 1114112 | tf_op jit(solution)/shard_map/all_to_all | solution.py:39
  71.9 2.6 %collective-permute-start.8 = (f32[8,136,128]{2,1,0:T(8,128)S(1)}, f32[8,136,128]{2,1,0:T(8,128)S(1)}, u32[]{:S(2)}, u32[]{:S(2)}) collective-permute-start(f32[8,136,128]{2,1,0:T(8,128)S(1)} %all_to_all.26.own), channel_id=1, source_target_pairs={{0,1},{1,0},{2,3},{3,2},{4,5},{5,4},{6,7},{7,6},{8,9},{9,8},{10,11... | collective-permute-start | bytes 1671176 | tf_op jit(solution)/shard_map/ppermute | solution.py:208
  74.5 1.6 %collective-permute-done.8.other = f32[8,136,128]{2,1,0:T(8,128)S(1)} collective-permute-done((f32[8,136,128]{2,1,0:T(8,128)S(1)}, f32[8,136,128]{2,1,0:T(8,128)S(1)}, u32[]{:S(2)}, u32[]{:S(2)}) %collective-permute-start.8) | collective-permute-done | bytes 557088 | tf_op jit(solution)/shard_map/ppermute | solution.py:208
  76.1 3.2 %members.1 = (f32[8,136,128]{2,1,0:T(8,128)S(1)}, f32[128,128]{1,0:T(8,128)S(1)}) custom-call(s32[8]{0:T(128)S(1)} %fusion.order, f32[8,136,128]{2,1,0:T(8,128)S(1)} %all_to_all.26.own, f32[8,136,128]{2,1,0:T(8,128)S(1)} %collective-permute-done.8.other, bf16[1024,2048]{1,0:T(8,128)(2,1)S(1)} %get-tuple-element.46.high, ...), custom_call_target="tpu_custom_call" | custom-call | tf_op jit(solution)/shard_map/members/pallas_call | solution.py:191
  79.3 12.9 %all_to_all.27.blocks = f32[8,136,128]{2,1,0:T(8,128)S(1)} all-to-all(f32[8,136,128]{2,1,0:T(8,128)S(1)} %get-tuple-element.49), channel_id=1, replica_groups=mesh['y_lo'=2,'z'=4,'y_hi'=2,'x'=4,'core'=2] {'y_lo','x'}, dimensions={0} | all-to-all | bytes 1114112 | tf_op jit(solution)/shard_map/all_to_all | solution.py:35
  92.3 13.5 %all_to_all.28 = f32[128,1,128]{2,1,0:T(1,128)S(1)} all-to-all(f32[128,1,128]{2,1,0:T(1,128)S(1)} %broadcast_in_dim.3), channel_id=1, replica_groups=mesh['y_lo'=2,'z'=4,'y_hi'=2,'x'=4,'core'=2] {'y_lo','z','y_hi','x','core'}, dimensions={0} | all-to-all | bytes 131072 | tf_op jit(solution)/shard_map/all_to_all | solution.py:265
  105.9 0.8 final.1
  (17 shorter events, 2.3 us)
Async XLA Ops:
  0.0 0.9 copy-start
  0.9 0.7 copy-start.1
  2.8 23.9 %all-to-all-start = ((f32[8,136,256]{2,1,0:T(8,128)}), f32[8,136,256]{2,1,0:T(8,128)S(1)}, u32[]{:S(2)}, u32[]{:S(2)}) async-start(f32[8,136,256]{2,1,0:T(8,128)} %get-tuple-element.30), calls=%async_computation | async-start | bytes 2228224 | tf_op jit(solution)/shard_map/all_to_all | solution.py:39
  11.1 6.9 %collective-permute-start.6 = (f32[136,256]{1,0:T(8,128)S(1)}, f32[136,256]{1,0:T(8,128)S(1)}, u32[]{:S(2)}, u32[]{:S(2)}) collective-permute-start(f32[136,256]{1,0:T(8,128)S(1)} %get-tuple-element.29.first), channel_id=1, source_target_pairs={{66,0},{67,1},{68,2},{69,3},{70,4},{71,5},{64,6},{65,7},{74,8},{75... | collective-permute-start | bytes 417800 | tf_op jit(solution)/shard_map/ppermute | solution.py:46
  13.4 6.6 %collective-permute-start.5 = (f32[136,256]{1,0:T(8,128)S(1)}, f32[136,256]{1,0:T(8,128)S(1)}, u32[]{:S(2)}, u32[]{:S(2)}) collective-permute-start(f32[136,256]{1,0:T(8,128)S(1)} %get-tuple-element.29.first), channel_id=1, source_target_pairs={{64,0},{65,1},{66,2},{67,3},{68,4},{69,5},{70,6},{71,7},{72,8},{73... | collective-permute-start | bytes 417800 | tf_op jit(solution)/shard_map/ppermute | solution.py:46
  14.8 5.7 %collective-permute-start.4 = (f32[136,256]{1,0:T(8,128)S(1)}, f32[136,256]{1,0:T(8,128)S(1)}, u32[]{:S(2)}, u32[]{:S(2)}) collective-permute-start(f32[136,256]{1,0:T(8,128)S(1)} %get-tuple-element.29.first), channel_id=1, source_target_pairs={{4,0},{5,1},{6,2},{7,3},{0,4},{1,5},{2,6},{3,7},{12,8},{13,9},{14,... | collective-permute-start | bytes 417800 | tf_op jit(solution)/shard_map/ppermute | solution.py:46
  15.3 8.8 %collective-permute-start.3 = (f32[136,256]{1,0:T(8,128)S(1)}, f32[136,256]{1,0:T(8,128)S(1)}, u32[]{:S(2)}, u32[]{:S(2)}) collective-permute-start(f32[136,256]{1,0:T(8,128)S(1)} %get-tuple-element.29.first), channel_id=1, source_target_pairs={{6,0},{7,1},{0,2},{1,3},{2,4},{3,5},{4,6},{5,7},{14,8},{15,9},{8,1... | collective-permute-start | bytes 417800 | tf_op jit(solution)/shard_map/ppermute | solution.py:46
  15.9 8.2 %collective-permute-start.2 = (f32[136,256]{1,0:T(8,128)S(1)}, f32[136,256]{1,0:T(8,128)S(1)}, u32[]{:S(2)}, u32[]{:S(2)}) collective-permute-start(f32[136,256]{1,0:T(8,128)S(1)} %get-tuple-element.29.first), channel_id=1, source_target_pairs={{2,0},{3,1},{4,2},{5,3},{6,4},{7,5},{0,6},{1,7},{10,8},{11,9},{12,... | collective-permute-start | bytes 417800 | tf_op jit(solution)/shard_map/ppermute | solution.py:46
  18.0 8.7 %collective-permute-start = (f32[136,256]{1,0:T(8,128)S(1)}, f32[136,256]{1,0:T(8,128)S(1)}, u32[]{:S(2)}, u32[]{:S(2)}) collective-permute-start(f32[136,256]{1,0:T(8,128)S(1)} %get-tuple-element.29.first), channel_id=1, source_target_pairs={{70,0},{71,1},{64,2},{65,3},{66,4},{67,5},{68,6},{69,7},{78,8},{79... | collective-permute-start | bytes 417800 | tf_op jit(solution)/shard_map/ppermute | solution.py:46
  26.7 4.4 %collective-permute-start.7 = (f32[8,136,256]{2,1,0:T(8,128)S(1)}, f32[8,136,256]{2,1,0:T(8,128)S(1)}, u32[]{:S(2)}, u32[]{:S(2)}) collective-permute-start(f32[8,136,256]{2,1,0:T(8,128)S(1)} %all-to-all-done.own), channel_id=1, source_target_pairs={{0,1},{1,0},{2,3},{3,2},{4,5},{5,4},{6,7},{7,6},{8,9},{9,8},{10,11... | collective-permute-start | bytes 3342344 | tf_op jit(solution)/shard_map/ppermute | solution.py:208
  28.2 10.2 %collective-permute-start.1 = (f32[136,256]{1,0:T(8,128)S(1)}, f32[136,256]{1,0:T(8,128)S(1)}, u32[]{:S(2)}, u32[]{:S(2)}) collective-permute-start(f32[136,256]{1,0:T(8,128)S(1)} %get-tuple-element.29.first), channel_id=1, source_target_pairs={{68,0},{69,1},{70,2},{71,3},{64,4},{65,5},{66,6},{67,7},{76,8},{77... | collective-permute-start | bytes 417800 | tf_op jit(solution)/shard_map/ppermute | solution.py:46
  71.9 4.2 %collective-permute-start.8 = (f32[8,136,128]{2,1,0:T(8,128)S(1)}, f32[8,136,128]{2,1,0:T(8,128)S(1)}, u32[]{:S(2)}, u32[]{:S(2)}) collective-permute-start(f32[8,136,128]{2,1,0:T(8,128)S(1)} %all_to_all.26.own), channel_id=1, source_target_pairs={{0,1},{1,0},{2,3},{3,2},{4,5},{5,4},{6,7},{7,6},{8,9},{9,8},{10,11... | collective-permute-start | bytes 1671176 | tf_op jit(solution)/shard_map/ppermute | solution.py:208

commit v8 on v7

--- a/solution.py
+++ b/solution.py
@@ -21,41 +21,47 @@
     return (((y_lo * 4 + z) * 2 + y_hi) * 4 + x) * 2 + core
 
 
-def column_groups():
+NEAR = ((0, 1), (2, 3))
+FAR = ((0, 3), (1, 2))
+
+
+def cubes(pairs):
     groups = []
-    for pair, x, core in itertools.product(range(2), range(4), range(2)):
-        groups.append([place(lo, z, lo ^ pair, x, core) for lo in range(2) for z in range(4)])
+    for along_y, along_z, along_x, core in itertools.product(pairs, pairs, pairs, range(2)):
+        groups.append([place(y % 2, z, y // 2, x, core) for y in along_y for z in along_z for x in along_x])
     return groups
 
 
-COLUMN_GROUPS = column_groups()
+ROW_GROUPS, COLUMN_GROUPS = cubes(NEAR), cubes(FAR)
+ROW_ORDER = (0, 1, 2, 4, 3, 5, 6, 7)
 
 
 def exchange_rows(blocks):
-    return lax.all_to_all(blocks, ("y_lo", "x"), 0, 0, tiled=True)
+    return lax.all_to_all(blocks, EVERY, 0, 0, axis_index_groups=ROW_GROUPS, tiled=True)
 
 
 def exchange_columns(blocks):
     return lax.all_to_all(blocks, EVERY, 0, 0, axis_index_groups=COLUMN_GROUPS, tiled=True)
 
 
-def moved(x, flip, step):
+def moved(x, flips):
+    along_y, along_z, along_x = flips // 4, flips // 2 % 2, flips % 2
     pairs = []
     for lo, z, hi, at, core in itertools.product(*map(range, SIZES)):
-        pairs.append((place(lo ^ flip, z, hi, (at + step) % 4, core), place(lo, z, hi, at, core)))
+        pairs.append((place(lo ^ along_y, z ^ along_z, hi, at ^ along_x, core), place(lo, z, hi, at, core)))
     return lax.ppermute(x, EVERY, pairs)
 
 
 def row_peers(x):
-    return [moved(x, flip, step) if flip or step else x for flip in range(2) for step in (0, 1, 3, 2)]
-
-
-def member_order():
-    y_lo, x = lax.axis_index("y_lo"), lax.axis_index("x")
-    offset = jnp.arange(8, dtype=jnp.int32)
-    step = offset % 4
-    step = jnp.where(step < 2, step, 5 - step)
-    return (y_lo ^ (offset // 4)) * 4 + (x + step) % 4
+    return [moved(x, flips) if flips else x for flips in ROW_ORDER]
+
+
+def member_at(offset):
+    member = 0
+    for name, bit in (("y_lo", 4), ("z", 2), ("x", 1)):
+        own = lax.axis_index(name) % 2
+        member += bit * ((1 - own) if ROW_ORDER[offset] & bit else own)
+    return member
 
 
 def halves(x):
@@ -94,19 +100,31 @@
             member[at] = seed_member(line[:, :points]).astype(jnp.bfloat16)
 
 
-def prepare_kernel(embedding, seeds, block, spread):
+def prepare_kernel(embedding, seeds, block, spread, labels, arrived, sent, tails):
     points, width = embedding.shape
-    x = embedding[...]
-    side = jnp.concatenate([seeds[...].astype(jnp.float32), jnp.sum((x * x).T, axis=0, keepdims=True)], axis=1)
-    side = jnp.broadcast_to(side, (SIDE, width))
-    block[pl.ds(0, points)] = x
-    block[pl.ds(points, SIDE)] = side
-    for copy in range(spread.shape[0]):
-        spread[copy, pl.ds(0, points)] = x
-        spread[copy, pl.ds(points, SIDE)] = side
-
-
-def pair_kernel(piece, order, first, second, right, squares, member, *rest):
+    body, end = pl.ds(0, points), pl.ds(points, SIDE)
+    loads = [
+        pltpu.make_async_copy(embedding, block.at[body], arrived.at[0]),
+        pltpu.make_async_copy(seeds, labels, arrived.at[1]),
+    ]
+    bodies = [pltpu.make_async_copy(embedding, spread.at[copy, body], sent.at[copy]) for copy in range(8)]
+    for load in loads:
+        load.start()
+    for copy in bodies:
+        copy.start()
+    for load in loads:
+        load.wait()
+    x = block[body]
+    side = jnp.concatenate([labels[...].astype(jnp.float32), jnp.sum((x * x).T, axis=0, keepdims=True)], axis=1)
+    block[end] = jnp.broadcast_to(side, (SIDE, width))
+    ends = [pltpu.make_async_copy(block.at[end], spread.at[copy, end], tails.at[copy]) for copy in range(8)]
+    for copy in ends:
+        copy.start()
+    for copy in bodies + ends:
+        copy.wait()
+
+
+def pair_kernel(piece, first, second, right, squares, member, *rest):
     *_, high_out, low_out, out = rest
     points, width = first.shape[0] - SIDE, first.shape[1]
     at = pl.ds(piece * 2 * points, 2 * points)
@@ -121,7 +139,7 @@
     low_out[at] = low
     total = product(high, member[...]) + product(low, member[...])
     if piece:
-        tail = rest[2][order[0], pl.ds(points, SIDE)]
+        tail = rest[2][member_at(0), pl.ds(points, SIDE)]
         cohesion, counts = tail[0:1], tail[1:2]
     else:
         cohesion = jnp.zeros((1, CLUSTER_COUNT), jnp.float32)
@@ -129,14 +147,14 @@
     for index, block in enumerate((first, second)):
         own = seed_member(block[pl.ds(points, 1)][:, :points])
         part = total[index * points : (index + 1) * points]
-        out[order[2 * piece + index], pl.ds(0, points)] = part
+        out[member_at(2 * piece + index), pl.ds(0, points)] = part
         cohesion += jnp.sum(own * part, axis=0, keepdims=True)
     tail = tail_rows(cohesion, counts)
     for target in range(8 if piece == 3 else 1):
-        out[order[target], pl.ds(points, SIDE)] = tail
-
-
-def member_kernel(order, own, other, high, low, first, out, own_member, both):
+        out[member_at(target), pl.ds(points, SIDE)] = tail
+
+
+def member_kernel(own, other, high, low, first, out, own_member, both):
     points = own.shape[1] - SIDE
     sums = jnp.zeros((SIDE, CLUSTER_COUNT), jnp.float32)
     for block in range(8):
@@ -155,8 +173,8 @@
     total = product(low[...], both[:, pl.ds(0, CLUSTER_COUNT)])
     total += wide[:, :CLUSTER_COUNT] + wide[:, CLUSTER_COUNT:]
     for block in range(8):
-        out[order[block], pl.ds(0, points)] = total[block * points : (block + 1) * points]
-        out[order[block], pl.ds(points, SIDE)] = tail
+        out[member_at(block), pl.ds(0, points)] = total[block * points : (block + 1) * points]
+        out[member_at(block), pl.ds(points, SIDE)] = tail
 
 
 def summed(blocks):
@@ -182,11 +200,9 @@
     out[...] = log_softmax_energy(second[pl.ds(0, points)], second[pl.ds(points, 1)], cohesion[...])
 
 
-def on_chip(kernel, name, shapes, inputs, order_at=None, scratch=(), aliases={}):
+def on_chip(kernel, name, shapes, inputs, scratch=(), aliases={}):
     vmem = pl.BlockSpec(memory_space=pltpu.VMEM)
     specs = [vmem] * len(inputs)
-    if order_at is not None:
-        specs[order_at] = pl.BlockSpec(memory_space=pltpu.SMEM)
     shapes = [jax.ShapeDtypeStruct(*shape) for shape in shapes]
     return pl.pallas_call(
         kernel,
@@ -218,16 +234,23 @@
 def shards(embedding, seed_cluster):
     points, width = embedding.shape
     lines, tall = points + SIDE, 16 * points
-    block, spread = on_chip(
+    anywhere = pl.BlockSpec(memory_space=pl.ANY)
+    block, spread = pl.pallas_call(
         prepare_kernel,
-        "prepare",
-        [((lines, width), jnp.float32), ((8, lines, width), jnp.float32)],
-        [embedding, seed_cluster.reshape(1, points)],
-    )
+        out_shape=[jax.ShapeDtypeStruct((lines, width), jnp.float32), jax.ShapeDtypeStruct((8, lines, width), jnp.float32)],
+        in_specs=[anywhere, anywhere],
+        out_specs=[pl.BlockSpec(memory_space=pltpu.VMEM), anywhere],
+        scratch_shapes=[
+            pltpu.VMEM((1, points), jnp.int32),
+            pltpu.SemaphoreType.DMA((2,)),
+            pltpu.SemaphoreType.DMA((8,)),
+            pltpu.SemaphoreType.DMA((8,)),
+        ],
+        name="prepare",
+    )(embedding, seed_cluster.reshape(1, points))
     columns = exchange_columns(spread)
     rows = row_peers(block)
     columns, *_ = lax.optimization_barrier((columns, *rows[1:7]))
-    order = member_order()
     prepared = on_chip(
         column_kernel,
         "columns",
@@ -242,9 +265,8 @@
             functools.partial(pair_kernel, piece),
             f"pairs_{piece}",
             [kept, kept, exchange],
-            [order, *rows[2 * piece : 2 * piece + 2], *prepared, *state],
-            order_at=0,
-            aliases={6: 0, 7: 1, 8: 2} if state else {},
+            [*rows[2 * piece : 2 * piece + 2], *prepared, *state],
+            aliases={5: 0, 6: 1, 7: 2} if state else {},
         )
     high, low, weighted = state
 
@@ -255,8 +277,7 @@
         member_kernel,
         "members",
         [exchange, ((points, CLUSTER_COUNT), jnp.float32)],
-        [order, firsts, other_core(firsts), high, low, first],
-        order_at=0,
+        [firsts, other_core(firsts), high, low, first],
         scratch=[pltpu.VMEM((tall, 2 * CLUSTER_COUNT), jnp.bfloat16)],
     )
 

time: 107 us -> 136 us (1.27)
  Pallas kernels: 15.1 us -> 45.1 us
  waiting for transfers between devices: 10.3 us -> 18.9 us
  blocking collectives: 57.5 us -> 52.3 us
  starting transfers between devices: 22.1 us -> 19.1 us
  local copies, waits for them, and re-layouts: 1.6 us -> 0.04 us
    pallas_call x0 -> x1, Pallas kernels: none -> 33.7 us  [shards(): pl.pallas_call(prepare_kernel, out_shape=[jax.ShapeDtypeStruct((lines, wi...]
    all_to_all x1, waiting for transfers between devices: 0.01 us -> 7.17 us  [exchange_columns(): lax.all_to_all(blocks, EVERY, 0, 0, axis_index_groups=COLUMN_GROUPS, tile...]
    ppermute x7, starting transfers between devices: 9.69 us -> 3.83 us  [moved(): return lax.ppermute(x, EVERY, pairs)]
    all_to_all x2, blocking collectives: 27.9 us -> 23.9 us  [exchange_rows(): lax.all_to_all(blocks, EVERY, 0, 0, axis_index_groups=ROW_GROUPS, tiled=T...]
    pallas_call x10 -> x9, Pallas kernels: 15.1 us -> 11.4 us  [on_chip(): pl.pallas_call(kernel, out_shape=shapes, in_specs=specs, out_specs=[vmem]...]
    ppermute x2, waiting for transfers between devices: 1.59 us -> 3.96 us  [other_core(): return lax.ppermute(x, 'core', [(0, 1), (1, 0)])]
    all_to_all x1, starting transfers between devices: 8.31 us -> 10.7 us  [exchange_columns(): lax.all_to_all(blocks, EVERY, 0, 0, axis_index_groups=COLUMN_GROUPS, tile...]
    all_to_all x1, blocking collectives: 16.1 us -> 14.4 us  [exchange_columns(): lax.all_to_all(blocks, EVERY, 0, 0, axis_index_groups=COLUMN_GROUPS, tile...]
  transfers between devices with their start and end apart: 10 -> 10, of which waited for: 5 -> 7; matrix products, arithmetic and copies ran while one was open for 0% -> 0% of each run, Pallas kernels for 7% -> 4%
where the time goes in v8:
time: 136 us
  blocking collectives  52.3 us (38%)
  Pallas kernels  45.1 us (33%)
  starting transfers between devices  19.1 us (14%)
  waiting for transfers between devices  18.9 us (14%)
    pallas_call x1, Pallas kernels, shards(): pl.pallas_call(prepare_kernel, out_shape=[jax.ShapeDtypeStruct((lines, wi...  33.7 us
    all_to_all x2, blocking collectives, exchange_rows(): lax.all_to_all(blocks, EVERY, 0, 0, axis_index_groups=ROW_GROUPS, tiled=T...  23.9 us
    all_to_all x1, blocking collectives, exchange_columns(): lax.all_to_all(blocks, EVERY, 0, 0, axis_index_groups=COLUMN_GROUPS, tile...  14.4 us
    all_to_all x1, blocking collectives, shards(): parts = lax.all_to_all(copies(part, 128), EVERY, 0, 0, tiled=True)  14 us
    pallas_call x9, Pallas kernels, on_chip(): pl.pallas_call(kernel, out_shape=shapes, in_specs=specs, out_specs=[vmem]...  11.4 us
    all_to_all x1, starting transfers between devices, exchange_columns(): lax.all_to_all(blocks, EVERY, 0, 0, axis_index_groups=COLUMN_GROUPS, tile...  10.7 us
    ppermute x7, waiting for transfers between devices, moved(): return lax.ppermute(x, EVERY, pairs)  7.8 us
    all_to_all x1, waiting for transfers between devices, exchange_columns(): lax.all_to_all(blocks, EVERY, 0, 0, axis_index_groups=COLUMN_GROUPS, tile...  7.17 us
  transfers between devices with their start and end apart: 10, of which 7 were waited for; matrix products, arithmetic and copies ran while one was open for 0% of the time, Pallas kernels for 4%

profile of v8, /device:TPU:1, one launch (start us, length us, event | category | flops | bytes accessed | tf_op | source)
XLA Modules:
  0.0 135.6 jit_solution(13406453548815292928)
XLA Ops:
  0.0 33.7 %prepare.1 = (f32[136,256]{1,0:T(8,128)}, f32[8,136,256]{2,1,0:T(8,128)}) custom-call(f32[128,256]{1,0:T(8,128)} %embedding.1, s32[1,128]{1,0:T(1,128)} %bitcast.7), custom_call_target="tpu_custom_call" | custom-call | tf_op jit(solution)/shard_map/prepare/pallas_call | solution.py:238
  33.7 10.7 %all-to-all-start = ((f32[8,136,256]{2,1,0:T(8,128)}), f32[8,136,256]{2,1,0:T(8,128)S(1)}, u32[]{:S(2)}, u32[]{:S(2)}) async-start(f32[8,136,256]{2,1,0:T(8,128)} %get-tuple-element.30), calls=%async_computation | async-start | bytes 2228224 | tf_op jit(solution)/shard_map/all_to_all | solution.py:44
  44.6 1.6 %collective-permute-start.4 = (f32[136,256]{1,0:T(8,128)}, f32[136,256]{1,0:T(8,128)S(1)}, u32[]{:S(2)}, u32[]{:S(2)}) collective-permute-start(f32[136,256]{1,0:T(8,128)} %get-tuple-element.29.first), channel_id=1, source_target_pairs={{64,0},{65,1},{66,2},{67,3},{68,4},{69,5},{70,6},{71,7},{72,8},{73... | collective-permute-start | bytes 417800 | tf_op jit(solution)/shard_map/ppermute | solution.py:52
  46.3 1.9 %collective-permute-start.3 = (f32[136,256]{1,0:T(8,128)}, f32[136,256]{1,0:T(8,128)S(1)}, u32[]{:S(2)}, u32[]{:S(2)}) collective-permute-start(f32[136,256]{1,0:T(8,128)} %get-tuple-element.29.first), channel_id=1, source_target_pairs={{16,0},{17,1},{18,2},{19,3},{20,4},{21,5},{22,6},{23,7},{24,8},{25... | collective-permute-start | bytes 417800 | tf_op jit(solution)/shard_map/ppermute | solution.py:52
  48.2 1.6 %collective-permute-done.6.second = f32[136,256]{1,0:T(8,128)S(1)} collective-permute-done((f32[136,256]{1,0:T(8,128)}, f32[136,256]{1,0:T(8,128)S(1)}, u32[]{:S(2)}, u32[]{:S(2)}) %collective-permute-start.6) | collective-permute-done | bytes 139296 | tf_op jit(solution)/shard_map/ppermute | solution.py:52
  49.8 1.5 %collective-permute-done.5.first = f32[136,256]{1,0:T(8,128)S(1)} collective-permute-done((f32[136,256]{1,0:T(8,128)}, f32[136,256]{1,0:T(8,128)S(1)}, u32[]{:S(2)}, u32[]{:S(2)}) %collective-permute-start.5) | collective-permute-done | bytes 139296 | tf_op jit(solution)/shard_map/ppermute | solution.py:52
  51.3 1.8 %collective-permute-done.4.second = f32[136,256]{1,0:T(8,128)S(1)} collective-permute-done((f32[136,256]{1,0:T(8,128)}, f32[136,256]{1,0:T(8,128)S(1)}, u32[]{:S(2)}, u32[]{:S(2)}) %collective-permute-start.4) | collective-permute-done | bytes 139296 | tf_op jit(solution)/shard_map/ppermute | solution.py:52
  53.1 2.9 %collective-permute-done.3.first = f32[136,256]{1,0:T(8,128)S(1)} collective-permute-done((f32[136,256]{1,0:T(8,128)}, f32[136,256]{1,0:T(8,128)S(1)}, u32[]{:S(2)}, u32[]{:S(2)}) %collective-permute-start.3) | collective-permute-done | bytes 139296 | tf_op jit(solution)/shard_map/ppermute | solution.py:52
  56.0 7.2 %all-to-all-done.own = f32[8,136,256]{2,1,0:T(8,128)S(1)} async-done(((f32[8,136,256]{2,1,0:T(8,128)}), f32[8,136,256]{2,1,0:T(8,128)S(1)}, u32[]{:S(2)}, u32[]{:S(2)}) %all-to-all-start) | async-done | bytes 1114144 | tf_op jit(solution)/shard_map/all_to_all | solution.py:44
  63.2 1.9 %collective-permute-start.7 = (f32[8,136,256]{2,1,0:T(8,128)S(1)}, f32[8,136,256]{2,1,0:T(8,128)S(1)}, u32[]{:S(2)}, u32[]{:S(2)}) collective-permute-start(f32[8,136,256]{2,1,0:T(8,128)S(1)} %all-to-all-done.own), channel_id=1, source_target_pairs={{0,1},{1,0},{2,3},{3,2},{4,5},{5,4},{6,7},{7,6},{8,9},{9,8},{10,11... | collective-permute-start | bytes 3342344 | tf_op jit(solution)/shard_map/ppermute | solution.py:224
  65.0 2.4 %collective-permute-done.7.other = f32[8,136,256]{2,1,0:T(8,128)S(1)} collective-permute-done((f32[8,136,256]{2,1,0:T(8,128)S(1)}, f32[8,136,256]{2,1,0:T(8,128)S(1)}, u32[]{:S(2)}, u32[]{:S(2)}) %collective-permute-start.7) | collective-permute-done | bytes 1114144 | tf_op jit(solution)/shard_map/ppermute | solution.py:224
  67.4 0.6 columns.1
  68.0 1.8 %pairs_0.1 = (bf16[1024,2048]{1,0:T(8,128)(2,1)S(1)}, bf16[1024,2048]{1,0:T(8,128)(2,1)S(1)}, f32[8,136,128]{2,1,0:T(8,128)S(1)}) custom-call(f32[136,256]{1,0:T(8,128)S(1)} %copy-done, f32[136,256]{1,0:T(8,128)S(1)} %collective-permute-done.2.second, bf16[2048,768]{1,0:T(8,128)(2,1)S(1)} %get-tuple-element.32.right, ...), custom_call_target="tpu_custom_call" | custom-call | tf_op jit(solution)/shard_map/pairs_0/pallas_call | solution.py:207
  69.8 1.8 %pairs_1.1 = (bf16[1024,2048]{1,0:T(8,128)(2,1)S(1)}, bf16[1024,2048]{1,0:T(8,128)(2,1)S(1)}, f32[8,136,128]{2,1,0:T(8,128)S(1)}) custom-call(f32[136,256]{1,0:T(8,128)S(1)} %collective-permute-done.3.first, f32[136,256]{1,0:T(8,128)S(1)} %collective-permute-done.4.second, ...), custom_call_target="tpu_custom_call", output_to_operand_aliasing={{0}: (5, {}), {1}: (6, {}), {2}: (7, {})} | custom-call | tf_op jit(solution)/shard_map/pairs_1/pallas_call | solution.py:207
  71.6 1.8 %pairs_2.1 = (bf16[1024,2048]{1,0:T(8,128)(2,1)S(1)}, bf16[1024,2048]{1,0:T(8,128)(2,1)S(1)}, f32[8,136,128]{2,1,0:T(8,128)S(1)}) custom-call(f32[136,256]{1,0:T(8,128)S(1)} %collective-permute-done.5.first, f32[136,256]{1,0:T(8,128)S(1)} %collective-permute-done.6.second, ...), custom_call_target="tpu_custom_call", output_to_operand_aliasing={{0}: (5, {}), {1}: (6, {}), {2}: (7, {})} | custom-call | tf_op jit(solution)/shard_map/pairs_2/pallas_call | solution.py:207
  73.5 1.8 %pairs_3.1 = (bf16[1024,2048]{1,0:T(8,128)(2,1)S(1)}, bf16[1024,2048]{1,0:T(8,128)(2,1)S(1)}, f32[8,136,128]{2,1,0:T(8,128)S(1)}) custom-call(f32[136,256]{1,0:T(8,128)S(1)} %collective-permute-done.first, f32[136,256]{1,0:T(8,128)S(1)} %collective-permute-done.1.second, ...), custom_call_target="tpu_custom_call", output_to_operand_aliasing={{0}: (5, {}), {1}: (6, {}), {2}: (7, {})} | custom-call | tf_op jit(solution)/shard_map/pairs_3/pallas_call | solution.py:207
  75.3 12.0 %all_to_all.25.blocks = f32[8,136,128]{2,1,0:T(8,128)S(1)} all-to-all(f32[8,136,128]{2,1,0:T(8,128)S(1)} %get-tuple-element.44), channel_id=1, replica_groups={{0,2,16,18,64,66,80,82},{1,3,17,19,65,67,81,83},{4,6,20,22,68,70,84,86}..., dimensions={0} | all-to-all | bytes 1114112 | tf_op jit(solution)/shard_map/all_to_all | solution.py:40
  87.3 14.4 %all_to_all.26.own = f32[8,136,128]{2,1,0:T(8,128)S(1)} all-to-all(f32[8,136,128]{2,1,0:T(8,128)S(1)} %get-tuple-element.45), channel_id=1, replica_groups={{0,6,48,54,72,78,120,126},{1,7,49,55,73,79,121,127},{2,4,50,52,74,76,12..., dimensions={0} | all-to-all | bytes 1114112 | tf_op jit(solution)/shard_map/all_to_all | solution.py:44
  101.7 2.7 %collective-permute-start.8 = (f32[8,136,128]{2,1,0:T(8,128)S(1)}, f32[8,136,128]{2,1,0:T(8,128)S(1)}, u32[]{:S(2)}, u32[]{:S(2)}) collective-permute-start(f32[8,136,128]{2,1,0:T(8,128)S(1)} %all_to_all.26.own), channel_id=1, source_target_pairs={{0,1},{1,0},{2,3},{3,2},{4,5},{5,4},{6,7},{7,6},{8,9},{9,8},{10,11... | collective-permute-start | bytes 1671176 | tf_op jit(solution)/shard_map/ppermute | solution.py:224
  104.4 1.6 %collective-permute-done.8.other = f32[8,136,128]{2,1,0:T(8,128)S(1)} collective-permute-done((f32[8,136,128]{2,1,0:T(8,128)S(1)}, f32[8,136,128]{2,1,0:T(8,128)S(1)}, u32[]{:S(2)}, u32[]{:S(2)}) %collective-permute-start.8) | collective-permute-done | bytes 557088 | tf_op jit(solution)/shard_map/ppermute | solution.py:224
  106.0 2.7 %members.1 = (f32[8,136,128]{2,1,0:T(8,128)S(1)}, f32[128,128]{1,0:T(8,128)S(1)}) custom-call(f32[8,136,128]{2,1,0:T(8,128)S(1)} %all_to_all.26.own, f32[8,136,128]{2,1,0:T(8,128)S(1)} %collective-permute-done.8.other, bf16[1024,2048]{1,0:T(8,128)(2,1)S(1)} %get-tuple-element.46.high, bf16[1024,2048]{1,0:T(8,128)(2,1)S(1)} %get-tuple-element.47.low, ...), custom_call_target="tpu_custom_call" | custom-call | tf_op jit(solution)/shard_map/members/pallas_call | solution.py:207
  108.7 12.0 %all_to_all.27.blocks = f32[8,136,128]{2,1,0:T(8,128)S(1)} all-to-all(f32[8,136,128]{2,1,0:T(8,128)S(1)} %get-tuple-element.49), channel_id=1, replica_groups={{0,2,16,18,64,66,80,82},{1,3,17,19,65,67,81,83},{4,6,20,22,68,70,84,86}..., dimensions={0} | all-to-all | bytes 1114112 | tf_op jit(solution)/shard_map/all_to_all | solution.py:40
  120.7 14.0 %all_to_all.28 = f32[128,1,128]{2,1,0:T(1,128)S(1)} all-to-all(f32[128,1,128]{2,1,0:T(1,128)S(1)} %broadcast_in_dim.3), channel_id=1, replica_groups=mesh['y_lo'=2,'z'=4,'y_hi'=2,'x'=4,'core'=2] {'y_lo','z','y_hi','x','core'}, dimensions={0} | all-to-all | bytes 131072 | tf_op jit(solution)/shard_map/all_to_all | solution.py:286
  134.8 0.8 final.1
  (14 shorter events, 0.5 us)
Async XLA Ops:
  33.7 34.3 %copy-start = (f32[136,256]{1,0:T(8,128)S(1)}, f32[136,256]{1,0:T(8,128)}, u32[]{:S(2)}) copy-start(f32[136,256]{1,0:T(8,128)} %get-tuple-element.29.first) | copy-start | bytes 417796
  33.7 29.5 %all-to-all-start = ((f32[8,136,256]{2,1,0:T(8,128)}), f32[8,136,256]{2,1,0:T(8,128)S(1)}, u32[]{:S(2)}, u32[]{:S(2)}) async-start(f32[8,136,256]{2,1,0:T(8,128)} %get-tuple-element.30), calls=%async_computation | async-start | bytes 2228224 | tf_op jit(solution)/shard_map/all_to_all | solution.py:44
  44.4 5.4 %collective-permute-start.6 = (f32[136,256]{1,0:T(8,128)}, f32[136,256]{1,0:T(8,128)S(1)}, u32[]{:S(2)}, u32[]{:S(2)}) collective-permute-start(f32[136,256]{1,0:T(8,128)} %get-tuple-element.29.first), channel_id=1, source_target_pairs={{66,0},{67,1},{64,2},{65,3},{70,4},{71,5},{68,6},{69,7},{74,8},{75... | collective-permute-start | bytes 417800 | tf_op jit(solution)/shard_map/ppermute | solution.py:52
  44.4 6.9 %collective-permute-start.5 = (f32[136,256]{1,0:T(8,128)}, f32[136,256]{1,0:T(8,128)S(1)}, u32[]{:S(2)}, u32[]{:S(2)}) collective-permute-start(f32[136,256]{1,0:T(8,128)} %get-tuple-element.29.first), channel_id=1, source_target_pairs={{18,0},{19,1},{16,2},{17,3},{22,4},{23,5},{20,6},{21,7},{26,8},{27... | collective-permute-start | bytes 417800 | tf_op jit(solution)/shard_map/ppermute | solution.py:52
  44.6 8.5 %collective-permute-start.4 = (f32[136,256]{1,0:T(8,128)}, f32[136,256]{1,0:T(8,128)S(1)}, u32[]{:S(2)}, u32[]{:S(2)}) collective-permute-start(f32[136,256]{1,0:T(8,128)} %get-tuple-element.29.first), channel_id=1, source_target_pairs={{64,0},{65,1},{66,2},{67,3},{68,4},{69,5},{70,6},{71,7},{72,8},{73... | collective-permute-start | bytes 417800 | tf_op jit(solution)/shard_map/ppermute | solution.py:52
  46.3 9.8 %collective-permute-start.3 = (f32[136,256]{1,0:T(8,128)}, f32[136,256]{1,0:T(8,128)S(1)}, u32[]{:S(2)}, u32[]{:S(2)}) collective-permute-start(f32[136,256]{1,0:T(8,128)} %get-tuple-element.29.first), channel_id=1, source_target_pairs={{16,0},{17,1},{18,2},{19,3},{20,4},{21,5},{22,6},{23,7},{24,8},{25... | collective-permute-start | bytes 417800 | tf_op jit(solution)/shard_map/ppermute | solution.py:52
  48.2 7.8 %collective-permute-start.2 = (f32[136,256]{1,0:T(8,128)}, f32[136,256]{1,0:T(8,128)S(1)}, u32[]{:S(2)}, u32[]{:S(2)}) collective-permute-start(f32[136,256]{1,0:T(8,128)} %get-tuple-element.29.first), channel_id=1, source_target_pairs={{2,0},{3,1},{0,2},{1,3},{6,4},{7,5},{4,6},{5,7},{10,8},{11,9},{8,1... | collective-permute-start | bytes 417800 | tf_op jit(solution)/shard_map/ppermute | solution.py:52
  49.8 6.2 %collective-permute-start = (f32[136,256]{1,0:T(8,128)}, f32[136,256]{1,0:T(8,128)S(1)}, u32[]{:S(2)}, u32[]{:S(2)}) collective-permute-start(f32[136,256]{1,0:T(8,128)} %get-tuple-element.29.first), channel_id=1, source_target_pairs={{80,0},{81,1},{82,2},{83,3},{84,4},{85,5},{86,6},{87,7},{88,8},{89... | collective-permute-start | bytes 417800 | tf_op jit(solution)/shard_map/ppermute | solution.py:52
  63.2 4.2 %collective-permute-start.7 = (f32[8,136,256]{2,1,0:T(8,128)S(1)}, f32[8,136,256]{2,1,0:T(8,128)S(1)}, u32[]{:S(2)}, u32[]{:S(2)}) collective-permute-start(f32[8,136,256]{2,1,0:T(8,128)S(1)} %all-to-all-done.own), channel_id=1, source_target_pairs={{0,1},{1,0},{2,3},{3,2},{4,5},{5,4},{6,7},{7,6},{8,9},{9,8},{10,11... | collective-permute-start | bytes 3342344 | tf_op jit(solution)/shard_map/ppermute | solution.py:224
  65.0 8.4 %collective-permute-start.1 = (f32[136,256]{1,0:T(8,128)}, f32[136,256]{1,0:T(8,128)S(1)}, u32[]{:S(2)}, u32[]{:S(2)}) collective-permute-start(f32[136,256]{1,0:T(8,128)} %get-tuple-element.29.first), channel_id=1, source_target_pairs={{82,0},{83,1},{80,2},{81,3},{86,4},{87,5},{84,6},{85,7},{90,8},{91... | collective-permute-start | bytes 417800 | tf_op jit(solution)/shard_map/ppermute | solution.py:52
  101.7 4.3 %collective-permute-start.8 = (f32[8,136,128]{2,1,0:T(8,128)S(1)}, f32[8,136,128]{2,1,0:T(8,128)S(1)}, u32[]{:S(2)}, u32[]{:S(2)}) collective-permute-start(f32[8,136,128]{2,1,0:T(8,128)S(1)} %all_to_all.26.own), channel_id=1, source_target_pairs={{0,1},{1,0},{2,3},{3,2},{4,5},{5,4},{6,7},{7,6},{8,9},{9,8},{10,11... | collective-permute-start | bytes 1671176 | tf_op jit(solution)/shard_map/ppermute | solution.py:224

commit v9 on v8

--- a/solution.py
+++ b/solution.py
@@ -100,27 +100,24 @@
             member[at] = seed_member(line[:, :points]).astype(jnp.bfloat16)
 
 
-def prepare_kernel(embedding, seeds, block, spread, labels, arrived, sent, tails):
+def prepare_kernel(embedding, seeds, block, spread, labels, arrived, sent):
     points, width = embedding.shape
     body, end = pl.ds(0, points), pl.ds(points, SIDE)
     loads = [
         pltpu.make_async_copy(embedding, block.at[body], arrived.at[0]),
         pltpu.make_async_copy(seeds, labels, arrived.at[1]),
     ]
-    bodies = [pltpu.make_async_copy(embedding, spread.at[copy, body], sent.at[copy]) for copy in range(8)]
     for load in loads:
         load.start()
-    for copy in bodies:
-        copy.start()
     for load in loads:
         load.wait()
     x = block[body]
     side = jnp.concatenate([labels[...].astype(jnp.float32), jnp.sum((x * x).T, axis=0, keepdims=True)], axis=1)
     block[end] = jnp.broadcast_to(side, (SIDE, width))
-    ends = [pltpu.make_async_copy(block.at[end], spread.at[copy, end], tails.at[copy]) for copy in range(8)]
-    for copy in ends:
+    sends = [pltpu.make_async_copy(block, spread.at[copy], sent.at[copy]) for copy in range(8)]
+    for copy in sends:
         copy.start()
-    for copy in bodies + ends:
+    for copy in sends:
         copy.wait()
 
 
@@ -244,7 +241,6 @@
             pltpu.VMEM((1, points), jnp.int32),
             pltpu.SemaphoreType.DMA((2,)),
             pltpu.SemaphoreType.DMA((8,)),
-            pltpu.SemaphoreType.DMA((8,)),
         ],
         name="prepare",
     )(embedding, seed_cluster.reshape(1, points))

time: 136 us -> 105 us (0.77)
  Pallas kernels: 45.1 us -> 14.3 us
    pallas_call x1, Pallas kernels: 33.7 us -> 2.8 us  [shards(): pl.pallas_call(prepare_kernel, out_shape=[jax.ShapeDtypeStruct((lines, wi...]
  transfers between devices with their start and end apart: 10 -> 10, of which waited for: 7 -> 7; matrix products, arithmetic and copies ran while one was open for 0% -> 0% of each run, Pallas kernels for 4% -> 6%
where the time goes in v9:
time: 105 us
  blocking collectives  52.3 us (50%)
  starting transfers between devices  19.1 us (18%)
  waiting for transfers between devices  18.9 us (18%)
  Pallas kernels  14.3 us (14%)
    all_to_all x2, blocking collectives, exchange_rows(): lax.all_to_all(blocks, EVERY, 0, 0, axis_index_groups=ROW_GROUPS, tiled=T...  23.9 us
    all_to_all x1, blocking collectives, exchange_columns(): lax.all_to_all(blocks, EVERY, 0, 0, axis_index_groups=COLUMN_GROUPS, tile...  14.4 us
    all_to_all x1, blocking collectives, shards(): parts = lax.all_to_all(copies(part, 128), EVERY, 0, 0, tiled=True)  14 us
    pallas_call x9, Pallas kernels, on_chip(): pl.pallas_call(kernel, out_shape=shapes, in_specs=specs, out_specs=[vmem]...  11.5 us
    all_to_all x1, starting transfers between devices, exchange_columns(): lax.all_to_all(blocks, EVERY, 0, 0, axis_index_groups=COLUMN_GROUPS, tile...  10.7 us
    ppermute x7, waiting for transfers between devices, moved(): return lax.ppermute(x, EVERY, pairs)  7.8 us
    all_to_all x1, waiting for transfers between devices, exchange_columns(): lax.all_to_all(blocks, EVERY, 0, 0, axis_index_groups=COLUMN_GROUPS, tile...  7.17 us
    ppermute x2, starting transfers between devices, other_core(): return lax.ppermute(x, 'core', [(0, 1), (1, 0)])  4.57 us
  transfers between devices with their start and end apart: 10, of which 7 were waited for; matrix products, arithmetic and copies ran while one was open for 0% of the time, Pallas kernels for 6%

profile of v9, /device:TPU:1, one launch (start us, length us, event | category | flops | bytes accessed | tf_op | source)
XLA Modules:
  0.0 104.7 jit_solution(1517691400059968899)
XLA Ops:
  0.0 2.8 %prepare.1 = (f32[136,256]{1,0:T(8,128)}, f32[8,136,256]{2,1,0:T(8,128)}) custom-call(f32[128,256]{1,0:T(8,128)} %embedding.1, s32[1,128]{1,0:T(1,128)} %bitcast.7), custom_call_target="tpu_custom_call" | custom-call | tf_op jit(solution)/shard_map/prepare/pallas_call | solution.py:235
  2.8 10.7 %all-to-all-start = ((f32[8,136,256]{2,1,0:T(8,128)}), f32[8,136,256]{2,1,0:T(8,128)S(1)}, u32[]{:S(2)}, u32[]{:S(2)}) async-start(f32[8,136,256]{2,1,0:T(8,128)} %get-tuple-element.30), calls=%async_computation | async-start | bytes 2228224 | tf_op jit(solution)/shard_map/all_to_all | solution.py:44
  13.7 1.6 %collective-permute-start.4 = (f32[136,256]{1,0:T(8,128)}, f32[136,256]{1,0:T(8,128)S(1)}, u32[]{:S(2)}, u32[]{:S(2)}) collective-permute-start(f32[136,256]{1,0:T(8,128)} %get-tuple-element.29.first), channel_id=1, source_target_pairs={{64,0},{65,1},{66,2},{67,3},{68,4},{69,5},{70,6},{71,7},{72,8},{73... | collective-permute-start | bytes 417800 | tf_op jit(solution)/shard_map/ppermute | solution.py:52
  15.4 1.9 %collective-permute-start.3 = (f32[136,256]{1,0:T(8,128)}, f32[136,256]{1,0:T(8,128)S(1)}, u32[]{:S(2)}, u32[]{:S(2)}) collective-permute-start(f32[136,256]{1,0:T(8,128)} %get-tuple-element.29.first), channel_id=1, source_target_pairs={{16,0},{17,1},{18,2},{19,3},{20,4},{21,5},{22,6},{23,7},{24,8},{25... | collective-permute-start | bytes 417800 | tf_op jit(solution)/shard_map/ppermute | solution.py:52
  17.3 1.6 %collective-permute-done.6.second = f32[136,256]{1,0:T(8,128)S(1)} collective-permute-done((f32[136,256]{1,0:T(8,128)}, f32[136,256]{1,0:T(8,128)S(1)}, u32[]{:S(2)}, u32[]{:S(2)}) %collective-permute-start.6) | collective-permute-done | bytes 139296 | tf_op jit(solution)/shard_map/ppermute | solution.py:52
  18.9 1.5 %collective-permute-done.5.first = f32[136,256]{1,0:T(8,128)S(1)} collective-permute-done((f32[136,256]{1,0:T(8,128)}, f32[136,256]{1,0:T(8,128)S(1)}, u32[]{:S(2)}, u32[]{:S(2)}) %collective-permute-start.5) | collective-permute-done | bytes 139296 | tf_op jit(solution)/shard_map/ppermute | solution.py:52
  20.4 1.8 %collective-permute-done.4.second = f32[136,256]{1,0:T(8,128)S(1)} collective-permute-done((f32[136,256]{1,0:T(8,128)}, f32[136,256]{1,0:T(8,128)S(1)}, u32[]{:S(2)}, u32[]{:S(2)}) %collective-permute-start.4) | collective-permute-done | bytes 139296 | tf_op jit(solution)/shard_map/ppermute | solution.py:52
  22.2 2.9 %collective-permute-done.3.first = f32[136,256]{1,0:T(8,128)S(1)} collective-permute-done((f32[136,256]{1,0:T(8,128)}, f32[136,256]{1,0:T(8,128)S(1)}, u32[]{:S(2)}, u32[]{:S(2)}) %collective-permute-start.3) | collective-permute-done | bytes 139296 | tf_op jit(solution)/shard_map/ppermute | solution.py:52
  25.1 7.2 %all-to-all-done.own = f32[8,136,256]{2,1,0:T(8,128)S(1)} async-done(((f32[8,136,256]{2,1,0:T(8,128)}), f32[8,136,256]{2,1,0:T(8,128)S(1)}, u32[]{:S(2)}, u32[]{:S(2)}) %all-to-all-start) | async-done | bytes 1114144 | tf_op jit(solution)/shard_map/all_to_all | solution.py:44
  32.3 1.9 %collective-permute-start.7 = (f32[8,136,256]{2,1,0:T(8,128)S(1)}, f32[8,136,256]{2,1,0:T(8,128)S(1)}, u32[]{:S(2)}, u32[]{:S(2)}) collective-permute-start(f32[8,136,256]{2,1,0:T(8,128)S(1)} %all-to-all-done.own), channel_id=1, source_target_pairs={{0,1},{1,0},{2,3},{3,2},{4,5},{5,4},{6,7},{7,6},{8,9},{9,8},{10,11... | collective-permute-start | bytes 3342344 | tf_op jit(solution)/shard_map/ppermute | solution.py:221
  34.1 2.4 %collective-permute-done.7.other = f32[8,136,256]{2,1,0:T(8,128)S(1)} collective-permute-done((f32[8,136,256]{2,1,0:T(8,128)S(1)}, f32[8,136,256]{2,1,0:T(8,128)S(1)}, u32[]{:S(2)}, u32[]{:S(2)}) %collective-permute-start.7) | collective-permute-done | bytes 1114144 | tf_op jit(solution)/shard_map/ppermute | solution.py:221
  36.5 0.6 columns.1
  37.1 1.8 %pairs_0.1 = (bf16[1024,2048]{1,0:T(8,128)(2,1)S(1)}, bf16[1024,2048]{1,0:T(8,128)(2,1)S(1)}, f32[8,136,128]{2,1,0:T(8,128)S(1)}) custom-call(f32[136,256]{1,0:T(8,128)S(1)} %copy-done, f32[136,256]{1,0:T(8,128)S(1)} %collective-permute-done.2.second, bf16[2048,768]{1,0:T(8,128)(2,1)S(1)} %get-tuple-element.32.right, ...), custom_call_target="tpu_custom_call" | custom-call | tf_op jit(solution)/shard_map/pairs_0/pallas_call | solution.py:204
  38.9 1.8 %pairs_1.1 = (bf16[1024,2048]{1,0:T(8,128)(2,1)S(1)}, bf16[1024,2048]{1,0:T(8,128)(2,1)S(1)}, f32[8,136,128]{2,1,0:T(8,128)S(1)}) custom-call(f32[136,256]{1,0:T(8,128)S(1)} %collective-permute-done.3.first, f32[136,256]{1,0:T(8,128)S(1)} %collective-permute-done.4.second, ...), custom_call_target="tpu_custom_call", output_to_operand_aliasing={{0}: (5, {}), {1}: (6, {}), {2}: (7, {})} | custom-call | tf_op jit(solution)/shard_map/pairs_1/pallas_call | solution.py:204
  40.8 1.8 %pairs_2.1 = (bf16[1024,2048]{1,0:T(8,128)(2,1)S(1)}, bf16[1024,2048]{1,0:T(8,128)(2,1)S(1)}, f32[8,136,128]{2,1,0:T(8,128)S(1)}) custom-call(f32[136,256]{1,0:T(8,128)S(1)} %collective-permute-done.5.first, f32[136,256]{1,0:T(8,128)S(1)} %collective-permute-done.6.second, ...), custom_call_target="tpu_custom_call", output_to_operand_aliasing={{0}: (5, {}), {1}: (6, {}), {2}: (7, {})} | custom-call | tf_op jit(solution)/shard_map/pairs_2/pallas_call | solution.py:204
  42.6 1.8 %pairs_3.1 = (bf16[1024,2048]{1,0:T(8,128)(2,1)S(1)}, bf16[1024,2048]{1,0:T(8,128)(2,1)S(1)}, f32[8,136,128]{2,1,0:T(8,128)S(1)}) custom-call(f32[136,256]{1,0:T(8,128)S(1)} %collective-permute-done.first, f32[136,256]{1,0:T(8,128)S(1)} %collective-permute-done.1.second, ...), custom_call_target="tpu_custom_call", output_to_operand_aliasing={{0}: (5, {}), {1}: (6, {}), {2}: (7, {})} | custom-call | tf_op jit(solution)/shard_map/pairs_3/pallas_call | solution.py:204
  44.4 12.0 %all_to_all.25.blocks = f32[8,136,128]{2,1,0:T(8,128)S(1)} all-to-all(f32[8,136,128]{2,1,0:T(8,128)S(1)} %get-tuple-element.44), channel_id=1, replica_groups={{0,2,16,18,64,66,80,82},{1,3,17,19,65,67,81,83},{4,6,20,22,68,70,84,86}..., dimensions={0} | all-to-all | bytes 1114112 | tf_op jit(solution)/shard_map/all_to_all | solution.py:40
  56.5 14.4 %all_to_all.26.own = f32[8,136,128]{2,1,0:T(8,128)S(1)} all-to-all(f32[8,136,128]{2,1,0:T(8,128)S(1)} %get-tuple-element.45), channel_id=1, replica_groups={{0,6,48,54,72,78,120,126},{1,7,49,55,73,79,121,127},{2,4,50,52,74,76,12..., dimensions={0} | all-to-all | bytes 1114112 | tf_op jit(solution)/shard_map/all_to_all | solution.py:44
  70.8 2.7 %collective-permute-start.8 = (f32[8,136,128]{2,1,0:T(8,128)S(1)}, f32[8,136,128]{2,1,0:T(8,128)S(1)}, u32[]{:S(2)}, u32[]{:S(2)}) collective-permute-start(f32[8,136,128]{2,1,0:T(8,128)S(1)} %all_to_all.26.own), channel_id=1, source_target_pairs={{0,1},{1,0},{2,3},{3,2},{4,5},{5,4},{6,7},{7,6},{8,9},{9,8},{10,11... | collective-permute-start | bytes 1671176 | tf_op jit(solution)/shard_map/ppermute | solution.py:221
  73.5 1.6 %collective-permute-done.8.other = f32[8,136,128]{2,1,0:T(8,128)S(1)} collective-permute-done((f32[8,136,128]{2,1,0:T(8,128)S(1)}, f32[8,136,128]{2,1,0:T(8,128)S(1)}, u32[]{:S(2)}, u32[]{:S(2)}) %collective-permute-start.8) | collective-permute-done | bytes 557088 | tf_op jit(solution)/shard_map/ppermute | solution.py:221
  75.1 2.7 %members.1 = (f32[8,136,128]{2,1,0:T(8,128)S(1)}, f32[128,128]{1,0:T(8,128)S(1)}) custom-call(f32[8,136,128]{2,1,0:T(8,128)S(1)} %all_to_all.26.own, f32[8,136,128]{2,1,0:T(8,128)S(1)} %collective-permute-done.8.other, bf16[1024,2048]{1,0:T(8,128)(2,1)S(1)} %get-tuple-element.46.high, bf16[1024,2048]{1,0:T(8,128)(2,1)S(1)} %get-tuple-element.47.low, ...), custom_call_target="tpu_custom_call" | custom-call | tf_op jit(solution)/shard_map/members/pallas_call | solution.py:204
  77.8 12.0 %all_to_all.27.blocks = f32[8,136,128]{2,1,0:T(8,128)S(1)} all-to-all(f32[8,136,128]{2,1,0:T(8,128)S(1)} %get-tuple-element.49), channel_id=1, replica_groups={{0,2,16,18,64,66,80,82},{1,3,17,19,65,67,81,83},{4,6,20,22,68,70,84,86}..., dimensions={0} | all-to-all | bytes 1114112 | tf_op jit(solution)/shard_map/all_to_all | solution.py:40
  89.9 14.0 %all_to_all.28 = f32[128,1,128]{2,1,0:T(1,128)S(1)} all-to-all(f32[128,1,128]{2,1,0:T(1,128)S(1)} %broadcast_in_dim.3), channel_id=1, replica_groups=mesh['y_lo'=2,'z'=4,'y_hi'=2,'x'=4,'core'=2] {'y_lo','z','y_hi','x','core'}, dimensions={0} | all-to-all | bytes 131072 | tf_op jit(solution)/shard_map/all_to_all | solution.py:282
  103.9 0.8 final.1
  (14 shorter events, 0.5 us)
Async XLA Ops:
  2.8 34.3 %copy-start = (f32[136,256]{1,0:T(8,128)S(1)}, f32[136,256]{1,0:T(8,128)}, u32[]{:S(2)}) copy-start(f32[136,256]{1,0:T(8,128)} %get-tuple-element.29.first) | copy-start | bytes 417796
  2.8 29.5 %all-to-all-start = ((f32[8,136,256]{2,1,0:T(8,128)}), f32[8,136,256]{2,1,0:T(8,128)S(1)}, u32[]{:S(2)}, u32[]{:S(2)}) async-start(f32[8,136,256]{2,1,0:T(8,128)} %get-tuple-element.30), calls=%async_computation | async-start | bytes 2228224 | tf_op jit(solution)/shard_map/all_to_all | solution.py:44
  13.5 5.4 %collective-permute-start.6 = (f32[136,256]{1,0:T(8,128)}, f32[136,256]{1,0:T(8,128)S(1)}, u32[]{:S(2)}, u32[]{:S(2)}) collective-permute-start(f32[136,256]{1,0:T(8,128)} %get-tuple-element.29.first), channel_id=1, source_target_pairs={{66,0},{67,1},{64,2},{65,3},{70,4},{71,5},{68,6},{69,7},{74,8},{75... | collective-permute-start | bytes 417800 | tf_op jit(solution)/shard_map/ppermute | solution.py:52
  13.5 6.9 %collective-permute-start.5 = (f32[136,256]{1,0:T(8,128)}, f32[136,256]{1,0:T(8,128)S(1)}, u32[]{:S(2)}, u32[]{:S(2)}) collective-permute-start(f32[136,256]{1,0:T(8,128)} %get-tuple-element.29.first), channel_id=1, source_target_pairs={{18,0},{19,1},{16,2},{17,3},{22,4},{23,5},{20,6},{21,7},{26,8},{27... | collective-permute-start | bytes 417800 | tf_op jit(solution)/shard_map/ppermute | solution.py:52
  13.7 8.5 %collective-permute-start.4 = (f32[136,256]{1,0:T(8,128)}, f32[136,256]{1,0:T(8,128)S(1)}, u32[]{:S(2)}, u32[]{:S(2)}) collective-permute-start(f32[136,256]{1,0:T(8,128)} %get-tuple-element.29.first), channel_id=1, source_target_pairs={{64,0},{65,1},{66,2},{67,3},{68,4},{69,5},{70,6},{71,7},{72,8},{73... | collective-permute-start | bytes 417800 | tf_op jit(solution)/shard_map/ppermute | solution.py:52
  15.4 9.8 %collective-permute-start.3 = (f32[136,256]{1,0:T(8,128)}, f32[136,256]{1,0:T(8,128)S(1)}, u32[]{:S(2)}, u32[]{:S(2)}) collective-permute-start(f32[136,256]{1,0:T(8,128)} %get-tuple-element.29.first), channel_id=1, source_target_pairs={{16,0},{17,1},{18,2},{19,3},{20,4},{21,5},{22,6},{23,7},{24,8},{25... | collective-permute-start | bytes 417800 | tf_op jit(solution)/shard_map/ppermute | solution.py:52
  17.3 7.8 %collective-permute-start.2 = (f32[136,256]{1,0:T(8,128)}, f32[136,256]{1,0:T(8,128)S(1)}, u32[]{:S(2)}, u32[]{:S(2)}) collective-permute-start(f32[136,256]{1,0:T(8,128)} %get-tuple-element.29.first), channel_id=1, source_target_pairs={{2,0},{3,1},{0,2},{1,3},{6,4},{7,5},{4,6},{5,7},{10,8},{11,9},{8,1... | collective-permute-start | bytes 417800 | tf_op jit(solution)/shard_map/ppermute | solution.py:52
  18.9 6.2 %collective-permute-start = (f32[136,256]{1,0:T(8,128)}, f32[136,256]{1,0:T(8,128)S(1)}, u32[]{:S(2)}, u32[]{:S(2)}) collective-permute-start(f32[136,256]{1,0:T(8,128)} %get-tuple-element.29.first), channel_id=1, source_target_pairs={{80,0},{81,1},{82,2},{83,3},{84,4},{85,5},{86,6},{87,7},{88,8},{89... | collective-permute-start | bytes 417800 | tf_op jit(solution)/shard_map/ppermute | solution.py:52
  32.3 4.2 %collective-permute-start.7 = (f32[8,136,256]{2,1,0:T(8,128)S(1)}, f32[8,136,256]{2,1,0:T(8,128)S(1)}, u32[]{:S(2)}, u32[]{:S(2)}) collective-permute-start(f32[8,136,256]{2,1,0:T(8,128)S(1)} %all-to-all-done.own), channel_id=1, source_target_pairs={{0,1},{1,0},{2,3},{3,2},{4,5},{5,4},{6,7},{7,6},{8,9},{9,8},{10,11... | collective-permute-start | bytes 3342344 | tf_op jit(solution)/shard_map/ppermute | solution.py:221
  34.1 8.4 %collective-permute-start.1 = (f32[136,256]{1,0:T(8,128)}, f32[136,256]{1,0:T(8,128)S(1)}, u32[]{:S(2)}, u32[]{:S(2)}) collective-permute-start(f32[136,256]{1,0:T(8,128)} %get-tuple-element.29.first), channel_id=1, source_target_pairs={{82,0},{83,1},{80,2},{81,3},{86,4},{87,5},{84,6},{85,7},{90,8},{91... | collective-permute-start | bytes 417800 | tf_op jit(solution)/shard_map/ppermute | solution.py:52
  70.8 4.3 %collective-permute-start.8 = (f32[8,136,128]{2,1,0:T(8,128)S(1)}, f32[8,136,128]{2,1,0:T(8,128)S(1)}, u32[]{:S(2)}, u32[]{:S(2)}) collective-permute-start(f32[8,136,128]{2,1,0:T(8,128)S(1)} %all_to_all.26.own), channel_id=1, source_target_pairs={{0,1},{1,0},{2,3},{3,2},{4,5},{5,4},{6,7},{7,6},{8,9},{9,8},{10,11... | collective-permute-start | bytes 1671176 | tf_op jit(solution)/shard_map/ppermute | solution.py:221

commit v10 on v9

v10 whole, which is shorter than its diff:
```python
import functools
import itertools

import jax
import jax.numpy as jnp
from jax import lax
from jax.experimental import pallas as pl
from jax.experimental.pallas import tpu as pltpu
from jax.sharding import Mesh
from jax.sharding import PartitionSpec as P

CLUSTER_COUNT = 128
ANNEAL_TEMP_VALUE = 0.02
SIDE = 8

EVERY = ("y_lo", "z", "y_hi", "x", "core")
SIZES = (2, 4, 2, 4, 2)


def place(y_lo, z, y_hi, x, core):
    return (((y_lo * 4 + z) * 2 + y_hi) * 4 + x) * 2 + core


NEAR = ((0, 1), (2, 3))
FAR = ((0, 3), (1, 2))


def cubes(pairs):
    groups = []
    for along_y, along_z, along_x, core in itertools.product(pairs, pairs, pairs, range(2)):
        groups.append([place(y % 2, z, y // 2, x, core) for y in along_y for z in along_z for x in along_x])
    return groups


ROW_GROUPS, COLUMN_GROUPS = cubes(NEAR), cubes(FAR)
ROW_ORDER = (0, 1, 2, 4, 3, 5, 6, 7)


def exchange_rows(blocks):
    return lax.all_to_all(blocks, EVERY, 0, 0, axis_index_groups=ROW_GROUPS, tiled=True)


def exchange_columns(blocks):
    return lax.all_to_all(blocks, EVERY, 0, 0, axis_index_groups=COLUMN_GROUPS, tiled=True)


def moved(x, flips):
    along_y, along_z, along_x = flips // 4, flips // 2 % 2, flips % 2
    pairs = []
    for lo, z, hi, at, core in itertools.product(*map(range, SIZES)):
        pairs.append((place(lo ^ along_y, z ^ along_z, hi, at ^ along_x, core), place(lo, z, hi, at, core)))
    return lax.ppermute(x, EVERY, pairs)


def row_peers(x):
    return [moved(x, flips) if flips else x for flips in ROW_ORDER]


def member_at(offset):
    member = 0
    for name, bit in (("y_lo", 4), ("z", 2), ("x", 1)):
        own = lax.axis_index(name) % 2
        member += bit * ((1 - own) if ROW_ORDER[offset] & bit else own)
    return member


def halves(x):
    high = x.astype(jnp.bfloat16)
    return high, (x - high.astype(jnp.float32)).astype(jnp.bfloat16)


def product(a, b):
    return jnp.dot(a, b, preferred_element_type=jnp.float32)


def seed_member(seeds):
    labels = lax.broadcasted_iota(jnp.int32, (CLUSTER_COUNT, seeds.shape[1]), 0).astype(jnp.float32)
    return 0.5 * (labels == seeds).astype(jnp.float32).T + 0.5 / CLUSTER_COUNT


def tail_rows(*lines):
    at = lax.broadcasted_iota(jnp.int32, (SIDE, CLUSTER_COUNT), 0)
    tail = jnp.zeros((SIDE, CLUSTER_COUNT), jnp.float32)
    for index, line in enumerate(lines):
        tail = jnp.where(at == index, line, tail)
    return tail


def prepare_kernel(embedding, seeds, block, spread, labels, arrived):
    points, width = embedding.shape
    body, end = pl.ds(0, points), pl.ds(points, SIDE)
    loads = [
        pltpu.make_async_copy(embedding, block.at[body], arrived.at[0]),
        pltpu.make_async_copy(seeds, labels, arrived.at[1]),
    ]
    for load in loads:
        load.start()
    for load in loads:
        load.wait()
    x = block[body]
    side = jnp.concatenate([labels[...].astype(jnp.float32), jnp.sum((x * x).T, axis=0, keepdims=True)], axis=1)
    side = jnp.broadcast_to(side, (SIDE, width))
    block[end] = side
    for copy in range(spread.shape[0]):
        spread[copy, body] = x
        spread[copy, end] = side


CHUNK = 256


def weigh(columns, left, squares, high_out, low_out, right, line, member, chunks, keep):
    points, width = columns.shape[1] - SIDE, columns.shape[2]
    for block in range(8):
        at = pl.ds(block * points, points)
        high, low = halves(columns[block, pl.ds(0, points)])
        right[at, pl.ds(0, width)] = high
        right[at, pl.ds(width, width)] = low
        right[at, pl.ds(2 * width, width)] = high
        side = columns[block, pl.ds(points, 1)]
        line[:, at] = jnp.broadcast_to(side[:, points:], (SIDE, points))
        member[at] = seed_member(side[:, :points]).astype(jnp.bfloat16)
    for chunk in range(chunks):
        at = pl.ds(chunk * CHUNK, CHUNK)
        inner = lax.dot_general(left[at], right[...], (((1,), (1,)), ((), ())), preferred_element_type=jnp.float32)
        squared = inner + squares[at] + line[pl.ds(0, 1)]
        high, low = halves(squared * lax.rsqrt(squared))
        high_out[at] = high
        low_out[at] = low
        keep(chunk, product(high, member[...]) + product(low, member[...]))


def own_pair_kernel(*refs):
    rows, (columns, left, squares, high_out, low_out, out, right, line, member) = refs[:8], refs[8:]
    points, width = rows[0].shape[0] - SIDE, rows[0].shape[1]
    for offset, block in enumerate(rows):
        x = block[pl.ds(0, points)]
        at = pl.ds(offset * points, points)
        squares[at] = jnp.sum(x * x, axis=1, keepdims=True) + 1.0
        high, low = halves(-2.0 * x)
        left[at, pl.ds(0, width)] = high
        left[at, pl.ds(width, width)] = high
        left[at, pl.ds(2 * width, width)] = low

    def keep(chunk, total):
        out[pl.ds(chunk * CHUNK, CHUNK)] = total

    weigh(columns, left, squares, high_out, low_out, right, line, member, out.shape[0] // CHUNK, keep)


def other_pair_kernel(*refs):
    rows, (columns, left, squares, weighted, high_out, low_out, out, right, line, member) = refs[:8], refs[8:]
    points = rows[0].shape[0] - SIDE
    cohesion = [jnp.zeros((1, CLUSTER_COUNT), jnp.float32)]

    def keep(chunk, total):
        total += weighted[pl.ds(chunk * CHUNK, CHUNK)]
        for index in range(CHUNK // points):
            offset = chunk * (CHUNK // points) + index
            part = total[index * points : (index + 1) * points]
            out[member_at(offset), pl.ds(0, points)] = part
            own = seed_member(rows[offset][pl.ds(points, 1)][:, :points])
            cohesion[0] += jnp.sum(own * part, axis=0, keepdims=True)

    weigh(columns, left, squares, high_out, low_out, right, line, member, weighted.shape[0] // CHUNK, keep)
    counts = jnp.sum(seed_member(rows[0][pl.ds(points, 1)][:, :points]), axis=0, keepdims=True)
    tail = tail_rows(cohesion[0], counts)
    for target in range(8):
        out[target, pl.ds(points, SIDE)] = tail


def member_kernel(own, other, own_high, own_low, other_high, other_low, first, out, own_member, both):
    points = own.shape[1] - SIDE
    sums = jnp.zeros((SIDE, CLUSTER_COUNT), jnp.float32)
    for block in range(8):
        sums += own[block, pl.ds(points, SIDE)] + other[block, pl.ds(points, SIDE)]
    cohesion, counts = sums[0:1], sums[1:2]
    own_member[...] = jnp.exp(log_softmax_energy(first[pl.ds(0, points)], counts, cohesion))
    sizes = jnp.zeros((1, CLUSTER_COUNT), jnp.float32)
    total = 0.0
    for source, high, low in ((own, own_high, own_low), (other, other_high, other_low)):
        for block in range(8):
            member = jnp.exp(log_softmax_energy(source[block, pl.ds(0, points)], counts, cohesion))
            sizes += jnp.sum(member, axis=0, keepdims=True)
            at = pl.ds(block * points, points)
            both[at, pl.ds(0, CLUSTER_COUNT)], both[at, pl.ds(CLUSTER_COUNT, CLUSTER_COUNT)] = halves(member)
        wide = product(high[...], both[...])
        total += product(low[...], both[:, pl.ds(0, CLUSTER_COUNT)])
        total += wide[:, :CLUSTER_COUNT] + wide[:, CLUSTER_COUNT:]
    tail = tail_rows(sizes)
    for block in range(8):
        out[member_at(block), pl.ds(0, points)] = total[block * points : (block + 1) * points]
        out[member_at(block), pl.ds(points, SIDE)] = tail


def summed(blocks):
    total = blocks[0]
    for block in range(1, 8):
        total += blocks[block]
    return total


def sum_kernel(blocks, out, spread):
    out[...] = summed(blocks)
    spread[...] = jnp.broadcast_to(out[...], spread.shape)


def own_kernel(blocks, own, out, part):
    points = own.shape[0]
    out[...] = summed(blocks)
    part[...] = jnp.sum(own[...] * out[pl.ds(0, points)], axis=0, keepdims=True)


def final_kernel(second, cohesion, out):
    points = out.shape[0]
    out[...] = log_softmax_energy(second[pl.ds(0, points)], second[pl.ds(points, 1)], cohesion[...])


PARAMS = pltpu.CompilerParams(vmem_limit_bytes=12 << 20)


def on_chip(kernel, name, shapes, inputs, scratch=()):
    vmem = pl.BlockSpec(memory_space=pltpu.VMEM)
    specs = [vmem] * len(inputs)
    shapes = [jax.ShapeDtypeStruct(*shape) for shape in shapes]
    return pl.pallas_call(
        kernel,
        out_shape=shapes,
        in_specs=specs,
        out_specs=[vmem] * len(shapes),
        scratch_shapes=scratch,
        compiler_params=PARAMS,
        name=name,
    )(*inputs)


def copies(x, count):
    return jnp.broadcast_to(x, (count, *x.shape))


def other_core(x):
    return lax.ppermute(x, "core", [(0, 1), (1, 0)])


def log_softmax_energy(attraction, counts, cohesion):
    energy = attraction / counts - cohesion / (2.0 * counts**2)
    logits = -energy / ANNEAL_TEMP_VALUE
    highest = jnp.max(logits, axis=1, keepdims=True)
    return logits - highest - jnp.log(jnp.sum(jnp.exp(logits - highest), axis=1, keepdims=True))


def shards(embedding, seed_cluster):
    points, width = embedding.shape
    lines, tall = points + SIDE, 8 * points
    anywhere, vmem = pl.BlockSpec(memory_space=pl.ANY), pl.BlockSpec(memory_space=pltpu.VMEM)
    block, spread = pl.pallas_call(
        prepare_kernel,
        out_shape=[jax.ShapeDtypeStruct((lines, width), jnp.float32), jax.ShapeDtypeStruct((8, lines, width), jnp.float32)],
        in_specs=[anywhere, anywhere],
        out_specs=[vmem, vmem],
        scratch_shapes=[pltpu.VMEM((1, points), jnp.int32), pltpu.SemaphoreType.DMA((2,))],
        compiler_params=PARAMS,
        name="prepare",
    )(embedding, seed_cluster.reshape(1, points))
    columns = exchange_columns(spread)
    columns, *rows = lax.optimization_barrier((columns, *row_peers(block)))
    kept = ((tall, tall), jnp.bfloat16)
    exchange = ((8, lines, CLUSTER_COUNT), jnp.float32)
    scratch = [
        pltpu.VMEM((tall, 3 * width), jnp.bfloat16),
        pltpu.VMEM((SIDE, tall), jnp.float32),
        pltpu.VMEM((tall, CLUSTER_COUNT), jnp.bfloat16),
    ]
    left, squares, own_high, own_low, weighted = on_chip(
        own_pair_kernel,
        "own_pairs",
        [((tall, 3 * width), jnp.bfloat16), ((tall, 1), jnp.float32), kept, kept, ((tall, CLUSTER_COUNT), jnp.float32)],
        [*rows, columns],
        scratch=scratch,
    )
    other_high, other_low, weighted = on_chip(
        other_pair_kernel,
        "other_pairs",
        [kept, kept, exchange],
        [*rows, other_core(columns), left, squares, weighted],
        scratch=scratch,
    )

    line = ((lines, CLUSTER_COUNT), jnp.float32)
    first, spread = on_chip(sum_kernel, "sum_spread", [line, exchange], [exchange_rows(weighted)])
    firsts = exchange_columns(spread)
    weighted, own = on_chip(
        member_kernel,
        "members",
        [exchange, ((points, CLUSTER_COUNT), jnp.float32)],
        [firsts, other_core(firsts), own_high, own_low, other_high, other_low, first],
        scratch=[pltpu.VMEM((tall, 2 * CLUSTER_COUNT), jnp.bfloat16)],
    )

    part = ((1, CLUSTER_COUNT), jnp.float32)
    second, part = on_chip(own_kernel, "own_sums", [line, part], [exchange_rows(weighted), own])
    parts = lax.all_to_all(copies(part, 128), EVERY, 0, 0, tiled=True)
    (out,) = on_chip(
        final_kernel,
        "final",
        [((points, CLUSTER_COUNT), jnp.float32)],
        [second, jnp.sum(parts, axis=0)],
    )
    return out


def solution(mesh):
    finer = Mesh(mesh.devices.reshape(SIZES), EVERY)
    return jax.shard_map(
        shards, mesh=finer, in_specs=(P(EVERY, None), P(EVERY)), out_specs=P(EVERY, None), check_vma=False
    )
```

time: 105 us -> 105 us (level)
  waiting for transfers between devices: 18.9 us -> 13 us
  blocking collectives: 52.3 us -> 56.5 us
  starting transfers between devices: 19.1 us -> 21.9 us
  Pallas kernels: 14.3 us -> 11.8 us
  local copies, waits for them, and re-layouts: 0.04 us -> 1.6 us
    all_to_all x1, waiting for transfers between devices: 7.17 us -> 2.09 us  [exchange_columns(): lax.all_to_all(blocks, EVERY, 0, 0, axis_index_groups=COLUMN_GROUPS, tile...]
    ppermute x7, starting transfers between devices: 3.83 us -> 7.39 us  [moved(): return lax.ppermute(x, EVERY, pairs)]
    all_to_all x1, blocking collectives: 14.4 us -> 17.9 us  [exchange_columns(): lax.all_to_all(blocks, EVERY, 0, 0, axis_index_groups=COLUMN_GROUPS, tile...]
    ppermute x2, waiting for transfers between devices: 3.96 us -> 1.59 us  [other_core(): return lax.ppermute(x, 'core', [(0, 1), (1, 0)])]
    unnamed x2 -> x4, local copies, waits for them, and re-layouts: 0.01 us -> 1.56 us
    ppermute x7, waiting for transfers between devices: 7.8 us -> 9.33 us  [moved(): return lax.ppermute(x, EVERY, pairs)]
    pallas_call x1, Pallas kernels: 2.8 us -> 1.3 us  [shards(): pl.pallas_call(prepare_kernel, out_shape=[jax.ShapeDtypeStruct((lines, wi...]
    pallas_call x9 -> x6, Pallas kernels: 11.5 us -> 10.5 us  [on_chip(): pl.pallas_call(kernel, out_shape=shapes, in_specs=specs, out_specs=[vmem]...]
  transfers between devices with their start and end apart: 10 -> 10, of which waited for: 7 -> 7; matrix products, arithmetic and copies ran while one was open for 0% -> 0% of each run, Pallas kernels for 6% -> 3%
where the time goes in v10:
time: 105 us
  blocking collectives  56.5 us (54%)
  starting transfers between devices  21.9 us (21%)
  waiting for transfers between devices  13 us (12%)
  Pallas kernels  11.8 us (11%)
  local copies, waits for them, and re-layouts  1.6 us (2%)
    all_to_all x2, blocking collectives, exchange_rows(): lax.all_to_all(blocks, EVERY, 0, 0, axis_index_groups=ROW_GROUPS, tiled=T...  24.6 us
    all_to_all x1, blocking collectives, exchange_columns(): lax.all_to_all(blocks, EVERY, 0, 0, axis_index_groups=COLUMN_GROUPS, tile...  17.9 us
    all_to_all x1, blocking collectives, shards(): parts = lax.all_to_all(copies(part, 128), EVERY, 0, 0, tiled=True)  14 us
    all_to_all x1, starting transfers between devices, exchange_columns(): lax.all_to_all(blocks, EVERY, 0, 0, axis_index_groups=COLUMN_GROUPS, tile...  10.5 us
    pallas_call x6, Pallas kernels, on_chip(): pl.pallas_call(kernel, out_shape=shapes, in_specs=specs, out_specs=[vmem]...  10.5 us
    ppermute x7, waiting for transfers between devices, moved(): return lax.ppermute(x, EVERY, pairs)  9.33 us
    ppermute x7, starting transfers between devices, moved(): return lax.ppermute(x, EVERY, pairs)  7.39 us
    ppermute x2, starting transfers between devices, other_core(): return lax.ppermute(x, 'core', [(0, 1), (1, 0)])  3.95 us
  transfers between devices with their start and end apart: 10, of which 7 were waited for; matrix products, arithmetic and copies ran while one was open for 0% of the time, Pallas kernels for 3%

profile of v10, /device:TPU:1, one launch (start us, length us, event | category | flops | bytes accessed | tf_op | source)
XLA Modules:
  0.0 104.8 jit_solution(17460148261327033725)
XLA Ops:
  0.0 0.9 copy-done
  0.9 0.7 copy-done.1
  1.6 1.3 %prepare.1 = (f32[136,256]{1,0:T(8,128)S(1)}, f32[8,136,256]{2,1,0:T(8,128)}) custom-call(f32[128,256]{1,0:T(8,128)S(1)} %copy-done, s32[1,128]{1,0:T(1,128)S(1)} %bitcast.5), custom_call_target="tpu_custom_call" | custom-call | tf_op jit(solution)/shard_map/prepare/pallas_call | solution.py:256
  2.9 10.5 %all-to-all-start = ((f32[8,136,256]{2,1,0:T(8,128)}), f32[8,136,256]{2,1,0:T(8,128)S(1)}, u32[]{:S(2)}, u32[]{:S(2)}) async-start(f32[8,136,256]{2,1,0:T(8,128)} %get-tuple-element.30), calls=%async_computation | async-start | bytes 2228224 | tf_op jit(solution)/shard_map/all_to_all | solution.py:44
  13.4 2.0 %collective-permute-start.5 = (f32[136,256]{1,0:T(8,128)S(1)}, f32[136,256]{1,0:T(8,128)S(1)}, u32[]{:S(2)}, u32[]{:S(2)}) collective-permute-start(f32[136,256]{1,0:T(8,128)S(1)} %get-tuple-element.32.refs_0_), channel_id=1, source_target_pairs={{80,0},{81,1},{82,2},{83,3},{84,4},{85,5},{86,6},{87,7},{88,8},{89... | collective-permute-start | bytes 417800 | tf_op jit(solution)/shard_map/ppermute | solution.py:52
  15.4 1.1 %collective-permute-start.4 = (f32[136,256]{1,0:T(8,128)S(1)}, f32[136,256]{1,0:T(8,128)S(1)}, u32[]{:S(2)}, u32[]{:S(2)}) collective-permute-start(f32[136,256]{1,0:T(8,128)S(1)} %get-tuple-element.32.refs_0_), channel_id=1, source_target_pairs={{66,0},{67,1},{64,2},{65,3},{70,4},{71,5},{68,6},{69,7},{74,8},{75... | collective-permute-start | bytes 417800 | tf_op jit(solution)/shard_map/ppermute | solution.py:52
  17.0 1.1 %collective-permute-start.2 = (f32[136,256]{1,0:T(8,128)S(1)}, f32[136,256]{1,0:T(8,128)S(1)}, u32[]{:S(2)}, u32[]{:S(2)}) collective-permute-start(f32[136,256]{1,0:T(8,128)S(1)} %get-tuple-element.32.refs_0_), channel_id=1, source_target_pairs={{64,0},{65,1},{66,2},{67,3},{68,4},{69,5},{70,6},{71,7},{72,8},{73... | collective-permute-start | bytes 417800 | tf_op jit(solution)/shard_map/ppermute | solution.py:52
  18.1 1.4 %collective-permute-done.6.refs_7_ = f32[136,256]{1,0:T(8,128)S(1)} collective-permute-done((f32[136,256]{1,0:T(8,128)S(1)}, f32[136,256]{1,0:T(8,128)S(1)}, u32[]{:S(2)}, u32[]{:S(2)}) %collective-permute-start.6) | collective-permute-done | bytes 139296 | tf_op jit(solution)/shard_map/ppermute | solution.py:52
  19.5 5.5 %collective-permute-done.5.refs_6_ = f32[136,256]{1,0:T(8,128)S(1)} collective-permute-done((f32[136,256]{1,0:T(8,128)S(1)}, f32[136,256]{1,0:T(8,128)S(1)}, u32[]{:S(2)}, u32[]{:S(2)}) %collective-permute-start.5) | collective-permute-done | bytes 139296 | tf_op jit(solution)/shard_map/ppermute | solution.py:52
  25.0 2.7 %collective-permute-start = (f32[136,256]{1,0:T(8,128)S(1)}, f32[136,256]{1,0:T(8,128)S(1)}, u32[]{:S(2)}, u32[]{:S(2)}) collective-permute-start(f32[136,256]{1,0:T(8,128)S(1)} %get-tuple-element.32.refs_0_), channel_id=1, source_target_pairs={{2,0},{3,1},{0,2},{1,3},{6,4},{7,5},{4,6},{5,7},{10,8},{11,9},{8,1... | collective-permute-start | bytes 417800 | tf_op jit(solution)/shard_map/ppermute | solution.py:52
  27.7 1.0 collective-permute-done.2.refs_3_
  28.7 1.0 collective-permute-done.1.refs_2_
  30.1 2.1 %all-to-all-done.refs_8_ = f32[8,136,256]{2,1,0:T(8,128)S(1)} async-done(((f32[8,136,256]{2,1,0:T(8,128)}), f32[8,136,256]{2,1,0:T(8,128)S(1)}, u32[]{:S(2)}, u32[]{:S(2)}) %all-to-all-start) | async-done | bytes 1114144 | tf_op jit(solution)/shard_map/all_to_all | solution.py:44
  32.2 1.9 %collective-permute-start.7 = (f32[8,136,256]{2,1,0:T(8,128)S(1)}, f32[8,136,256]{2,1,0:T(8,128)S(1)}, u32[]{:S(2)}, u32[]{:S(2)}) collective-permute-start(f32[8,136,256]{2,1,0:T(8,128)S(1)} %all-to-all-done.refs_8_), channel_id=1, source_target_pairs={{0,1},{1,0},{2,3},{3,2},{4,5},{5,4},{6,7},{7,6},{8,9},{9,8},{10,11... | collective-permute-start | bytes 3342344 | tf_op jit(solution)/shard_map/ppermute | solution.py:242
  34.1 3.5 %own_pairs.1 = (bf16[1024,768]{1,0:T(8,128)(2,1)S(1)}, f32[1024,1]{1,0:T(8,128)S(1)}, bf16[1024,1024]{1,0:T(8,128)(2,1)S(1)}, bf16[1024,1024]{1,0:T(8,128)(2,1)S(1)}, f32[1024,128]{1,0:T(8,128)S(1)}) custom-call(f32[136,256]{1,0:T(8,128)S(1)} %get-tuple-element.32.refs_0_, f32[136,256]{1,0:T(8,128)S(1)} %collective-permute-done.refs_1_, ...), custom_call_target="tpu_custom_call" | custom-call | tf_op jit(solution)/shard_map/own_pairs/pallas_call | solution.py:226
  37.6 3.3 %other_pairs.1 = (bf16[1024,1024]{1,0:T(8,128)(2,1)S(1)}, bf16[1024,1024]{1,0:T(8,128)(2,1)S(1)}, f32[8,136,128]{2,1,0:T(8,128)S(1)}) custom-call(f32[136,256]{1,0:T(8,128)S(1)} %get-tuple-element.32.refs_0_, f32[136,256]{1,0:T(8,128)S(1)} %collective-permute-done.refs_1_, f32[136,256]{1,0:T(8,128)S(1)} %collective-permute-done.1.refs_2_, ...), custom_call_target="tpu_custom_call" | custom-call | tf_op jit(solution)/shard_map/other_pairs/pallas_call | solution.py:226
  40.9 12.7 %all_to_all.25.blocks = f32[8,136,128]{2,1,0:T(8,128)S(1)} all-to-all(f32[8,136,128]{2,1,0:T(8,128)S(1)} %get-tuple-element.44), channel_id=1, replica_groups={{0,2,16,18,64,66,80,82},{1,3,17,19,65,67,81,83},{4,6,20,22,68,70,84,86}..., dimensions={0} | all-to-all | bytes 1114112 | tf_op jit(solution)/shard_map/all_to_all | solution.py:40
  53.7 17.9 %all_to_all.26.own = f32[8,136,128]{2,1,0:T(8,128)S(1)} all-to-all(f32[8,136,128]{2,1,0:T(8,128)S(1)} %get-tuple-element.45), channel_id=1, replica_groups={{0,6,48,54,72,78,120,126},{1,7,49,55,73,79,121,127},{2,4,50,52,74,76,12..., dimensions={0} | all-to-all | bytes 1114112 | tf_op jit(solution)/shard_map/all_to_all | solution.py:44
  71.5 2.1 %collective-permute-start.8 = (f32[8,136,128]{2,1,0:T(8,128)S(1)}, f32[8,136,128]{2,1,0:T(8,128)S(1)}, u32[]{:S(2)}, u32[]{:S(2)}) collective-permute-start(f32[8,136,128]{2,1,0:T(8,128)S(1)} %all_to_all.26.own), channel_id=1, source_target_pairs={{0,1},{1,0},{2,3},{3,2},{4,5},{5,4},{6,7},{7,6},{8,9},{9,8},{10,11... | collective-permute-start | bytes 1671176 | tf_op jit(solution)/shard_map/ppermute | solution.py:242
  73.6 1.6 %collective-permute-done.8.other = f32[8,136,128]{2,1,0:T(8,128)S(1)} collective-permute-done((f32[8,136,128]{2,1,0:T(8,128)S(1)}, f32[8,136,128]{2,1,0:T(8,128)S(1)}, u32[]{:S(2)}, u32[]{:S(2)}) %collective-permute-start.8) | collective-permute-done | bytes 557088 | tf_op jit(solution)/shard_map/ppermute | solution.py:242
  75.2 2.7 %members.1 = (f32[8,136,128]{2,1,0:T(8,128)S(1)}, f32[128,128]{1,0:T(8,128)S(1)}) custom-call(f32[8,136,128]{2,1,0:T(8,128)S(1)} %all_to_all.26.own, f32[8,136,128]{2,1,0:T(8,128)S(1)} %collective-permute-done.8.other, bf16[1024,1024]{1,0:T(8,128)(2,1)S(1)} %get-tuple-element.46.own_high, bf16[1024,1024]{1,0:T(8,128)(2,1)S(1)} %get-tuple-element.47.own_low, ...), custom_call_target="tpu_custom_call" | custom-call | tf_op jit(solution)/shard_map/members/pallas_call | solution.py:226
  77.9 12.0 %all_to_all.27.blocks = f32[8,136,128]{2,1,0:T(8,128)S(1)} all-to-all(f32[8,136,128]{2,1,0:T(8,128)S(1)} %get-tuple-element.51), channel_id=1, replica_groups={{0,2,16,18,64,66,80,82},{1,3,17,19,65,67,81,83},{4,6,20,22,68,70,84,86}..., dimensions={0} | all-to-all | bytes 1114112 | tf_op jit(solution)/shard_map/all_to_all | solution.py:40
  90.0 14.0 %all_to_all.28 = f32[128,1,128]{2,1,0:T(1,128)S(1)} all-to-all(f32[128,1,128]{2,1,0:T(1,128)S(1)} %broadcast_in_dim.3), channel_id=1, replica_groups=mesh['y_lo'=2,'z'=4,'y_hi'=2,'x'=4,'core'=2] {'y_lo','z','y_hi','x','core'}, dimensions={0} | all-to-all | bytes 131072 | tf_op jit(solution)/shard_map/all_to_all | solution.py:302
  104.0 0.8 final.1
  (13 shorter events, 1.1 us)
Async XLA Ops:
  0.0 0.9 copy-start
  0.9 0.7 copy-start.1
  2.9 29.3 %all-to-all-start = ((f32[8,136,256]{2,1,0:T(8,128)}), f32[8,136,256]{2,1,0:T(8,128)S(1)}, u32[]{:S(2)}, u32[]{:S(2)}) async-start(f32[8,136,256]{2,1,0:T(8,128)} %get-tuple-element.30), calls=%async_computation | async-start | bytes 2228224 | tf_op jit(solution)/shard_map/all_to_all | solution.py:44
  13.4 6.1 %collective-permute-start.6 = (f32[136,256]{1,0:T(8,128)S(1)}, f32[136,256]{1,0:T(8,128)S(1)}, u32[]{:S(2)}, u32[]{:S(2)}) collective-permute-start(f32[136,256]{1,0:T(8,128)S(1)} %get-tuple-element.32.refs_0_), channel_id=1, source_target_pairs={{82,0},{83,1},{80,2},{81,3},{86,4},{87,5},{84,6},{85,7},{90,8},{91... | collective-permute-start | bytes 417800 | tf_op jit(solution)/shard_map/ppermute | solution.py:52
  13.4 11.6 %collective-permute-start.5 = (f32[136,256]{1,0:T(8,128)S(1)}, f32[136,256]{1,0:T(8,128)S(1)}, u32[]{:S(2)}, u32[]{:S(2)}) collective-permute-start(f32[136,256]{1,0:T(8,128)S(1)} %get-tuple-element.32.refs_0_), channel_id=1, source_target_pairs={{80,0},{81,1},{82,2},{83,3},{84,4},{85,5},{86,6},{87,7},{88,8},{89... | collective-permute-start | bytes 417800 | tf_op jit(solution)/shard_map/ppermute | solution.py:52
  15.4 12.3 %collective-permute-start.4 = (f32[136,256]{1,0:T(8,128)S(1)}, f32[136,256]{1,0:T(8,128)S(1)}, u32[]{:S(2)}, u32[]{:S(2)}) collective-permute-start(f32[136,256]{1,0:T(8,128)S(1)} %get-tuple-element.32.refs_0_), channel_id=1, source_target_pairs={{66,0},{67,1},{64,2},{65,3},{70,4},{71,5},{68,6},{69,7},{74,8},{75... | collective-permute-start | bytes 417800 | tf_op jit(solution)/shard_map/ppermute | solution.py:52
  16.5 11.2 %collective-permute-start.3 = (f32[136,256]{1,0:T(8,128)S(1)}, f32[136,256]{1,0:T(8,128)S(1)}, u32[]{:S(2)}, u32[]{:S(2)}) collective-permute-start(f32[136,256]{1,0:T(8,128)S(1)} %get-tuple-element.32.refs_0_), channel_id=1, source_target_pairs={{18,0},{19,1},{16,2},{17,3},{22,4},{23,5},{20,6},{21,7},{26,8},{27... | collective-permute-start | bytes 417800 | tf_op jit(solution)/shard_map/ppermute | solution.py:52
  17.0 11.7 %collective-permute-start.2 = (f32[136,256]{1,0:T(8,128)S(1)}, f32[136,256]{1,0:T(8,128)S(1)}, u32[]{:S(2)}, u32[]{:S(2)}) collective-permute-start(f32[136,256]{1,0:T(8,128)S(1)} %get-tuple-element.32.refs_0_), channel_id=1, source_target_pairs={{64,0},{65,1},{66,2},{67,3},{68,4},{69,5},{70,6},{71,7},{72,8},{73... | collective-permute-start | bytes 417800 | tf_op jit(solution)/shard_map/ppermute | solution.py:52
  19.5 10.2 %collective-permute-start.1 = (f32[136,256]{1,0:T(8,128)S(1)}, f32[136,256]{1,0:T(8,128)S(1)}, u32[]{:S(2)}, u32[]{:S(2)}) collective-permute-start(f32[136,256]{1,0:T(8,128)S(1)} %get-tuple-element.32.refs_0_), channel_id=1, source_target_pairs={{16,0},{17,1},{18,2},{19,3},{20,4},{21,5},{22,6},{23,7},{24,8},{25... | collective-permute-start | bytes 417800 | tf_op jit(solution)/shard_map/ppermute | solution.py:52
  25.0 5.1 %collective-permute-start = (f32[136,256]{1,0:T(8,128)S(1)}, f32[136,256]{1,0:T(8,128)S(1)}, u32[]{:S(2)}, u32[]{:S(2)}) collective-permute-start(f32[136,256]{1,0:T(8,128)S(1)} %get-tuple-element.32.refs_0_), channel_id=1, source_target_pairs={{2,0},{3,1},{0,2},{1,3},{6,4},{7,5},{4,6},{5,7},{10,8},{11,9},{8,1... | collective-permute-start | bytes 417800 | tf_op jit(solution)/shard_map/ppermute | solution.py:52
  32.2 5.4 %collective-permute-start.7 = (f32[8,136,256]{2,1,0:T(8,128)S(1)}, f32[8,136,256]{2,1,0:T(8,128)S(1)}, u32[]{:S(2)}, u32[]{:S(2)}) collective-permute-start(f32[8,136,256]{2,1,0:T(8,128)S(1)} %all-to-all-done.refs_8_), channel_id=1, source_target_pairs={{0,1},{1,0},{2,3},{3,2},{4,5},{5,4},{6,7},{7,6},{8,9},{9,8},{10,11... | collective-permute-start | bytes 3342344 | tf_op jit(solution)/shard_map/ppermute | solution.py:242
  71.5 3.7 %collective-permute-start.8 = (f32[8,136,128]{2,1,0:T(8,128)S(1)}, f32[8,136,128]{2,1,0:T(8,128)S(1)}, u32[]{:S(2)}, u32[]{:S(2)}) collective-permute-start(f32[8,136,128]{2,1,0:T(8,128)S(1)} %all_to_all.26.own), channel_id=1, source_target_pairs={{0,1},{1,0},{2,3},{3,2},{4,5},{5,4},{6,7},{7,6},{8,9},{9,8},{10,11... | collective-permute-start | bytes 1671176 | tf_op jit(solution)/shard_map/ppermute | solution.py:242

commit v11 on v10

--- a/solution.py
+++ b/solution.py
@@ -107,9 +107,10 @@
 
 
 CHUNK = 256
-
-
-def weigh(columns, left, squares, high_out, low_out, right, line, member, chunks, keep):
+EARLY = 3
+
+
+def set_columns(columns, right, line, member):
     points, width = columns.shape[1] - SIDE, columns.shape[2]
     for block in range(8):
         at = pl.ds(block * points, points)
@@ -120,74 +121,91 @@
         side = columns[block, pl.ds(points, 1)]
         line[:, at] = jnp.broadcast_to(side[:, points:], (SIDE, points))
         member[at] = seed_member(side[:, :points]).astype(jnp.bfloat16)
-    for chunk in range(chunks):
+
+
+def left_rows(x):
+    high, low = halves(-2.0 * x)
+    return jnp.concatenate([high, high, low], axis=1), jnp.sum(x * x, axis=1, keepdims=True) + 1.0
+
+
+def weigh(left, square, right, line, member, high_out, low_out, at):
+    inner = lax.dot_general(left, right[...], (((1,), (1,)), ((), ())), preferred_element_type=jnp.float32)
+    squared = inner + square + line[pl.ds(0, 1)]
+    high, low = halves(squared * lax.rsqrt(squared))
+    high_out[at] = high
+    low_out[at] = low
+    return product(high, member[...]) + product(low, member[...])
+
+
+def own_pair_kernel(*refs):
+    rows, (columns, left, squares, right, line, member, high_out, low_out, out) = refs[:6], refs[6:]
+    points = rows[0].shape[0] - SIDE
+    set_columns(columns, right, line, member)
+    for chunk in range(EARLY):
         at = pl.ds(chunk * CHUNK, CHUNK)
-        inner = lax.dot_general(left[at], right[...], (((1,), (1,)), ((), ())), preferred_element_type=jnp.float32)
-        squared = inner + squares[at] + line[pl.ds(0, 1)]
-        high, low = halves(squared * lax.rsqrt(squared))
-        high_out[at] = high
-        low_out[at] = low
-        keep(chunk, product(high, member[...]) + product(low, member[...]))
-
-
-def own_pair_kernel(*refs):
-    rows, (columns, left, squares, high_out, low_out, out, right, line, member) = refs[:8], refs[8:]
-    points, width = rows[0].shape[0] - SIDE, rows[0].shape[1]
-    for offset, block in enumerate(rows):
-        x = block[pl.ds(0, points)]
-        at = pl.ds(offset * points, points)
-        squares[at] = jnp.sum(x * x, axis=1, keepdims=True) + 1.0
-        high, low = halves(-2.0 * x)
-        left[at, pl.ds(0, width)] = high
-        left[at, pl.ds(width, width)] = high
-        left[at, pl.ds(2 * width, width)] = low
-
-    def keep(chunk, total):
-        out[pl.ds(chunk * CHUNK, CHUNK)] = total
-
-    weigh(columns, left, squares, high_out, low_out, right, line, member, out.shape[0] // CHUNK, keep)
+        x = jnp.concatenate([block[pl.ds(0, points)] for block in rows[2 * chunk : 2 * chunk + 2]], axis=0)
+        left[at], squares[at] = left_rows(x)
+        out[at] = weigh(left[at], squares[at], right, line, member, high_out, low_out, at)
 
 
 def other_pair_kernel(*refs):
-    rows, (columns, left, squares, weighted, high_out, low_out, out, right, line, member) = refs[:8], refs[8:]
+    rows, refs = refs[:8], refs[8:]
+    columns, left, squares, own_right, own_line, own_member, _, _, weighted, *refs = refs
+    own_high, own_low, high_out, low_out, out, right, line, member = refs
     points = rows[0].shape[0] - SIDE
-    cohesion = [jnp.zeros((1, CLUSTER_COUNT), jnp.float32)]
-
-    def keep(chunk, total):
-        total += weighted[pl.ds(chunk * CHUNK, CHUNK)]
-        for index in range(CHUNK // points):
-            offset = chunk * (CHUNK // points) + index
+    cohesion = jnp.zeros((1, CLUSTER_COUNT), jnp.float32)
+    set_columns(columns, right, line, member)
+    for chunk in range(EARLY + 1):
+        at = pl.ds(chunk * CHUNK, CHUNK)
+        if chunk < EARLY:
+            lefts, square, total = left[at], squares[at], weighted[at]
+        else:
+            lefts, square = left_rows(jnp.concatenate([block[pl.ds(0, points)] for block in rows[6:]], axis=0))
+            total = weigh(lefts, square, own_right, own_line, own_member, own_high, own_low, at)
+        total += weigh(lefts, square, right, line, member, high_out, low_out, at)
+        for index in range(2):
+            offset = 2 * chunk + index
             part = total[index * points : (index + 1) * points]
             out[member_at(offset), pl.ds(0, points)] = part
             own = seed_member(rows[offset][pl.ds(points, 1)][:, :points])
-            cohesion[0] += jnp.sum(own * part, axis=0, keepdims=True)
-
-    weigh(columns, left, squares, high_out, low_out, right, line, member, weighted.shape[0] // CHUNK, keep)
+            cohesion += jnp.sum(own * part, axis=0, keepdims=True)
     counts = jnp.sum(seed_member(rows[0][pl.ds(points, 1)][:, :points]), axis=0, keepdims=True)
-    tail = tail_rows(cohesion[0], counts)
+    tail = tail_rows(cohesion, counts)
     for target in range(8):
         out[target, pl.ds(points, SIDE)] = tail
 
 
-def member_kernel(own, other, own_high, own_low, other_high, other_low, first, out, own_member, both):
-    points = own.shape[1] - SIDE
-    sums = jnp.zeros((SIDE, CLUSTER_COUNT), jnp.float32)
+def tail_kernel(blocks, out):
+    points = blocks.shape[1] - SIDE
+    out[...] = sum(blocks[block, pl.ds(points, SIDE)] for block in range(8))
+
+
+def half_product(source, sums, high, low, both):
+    points = source.shape[1] - SIDE
+    sizes = jnp.zeros((1, CLUSTER_COUNT), jnp.float32)
     for block in range(8):
-        sums += own[block, pl.ds(points, SIDE)] + other[block, pl.ds(points, SIDE)]
-    cohesion, counts = sums[0:1], sums[1:2]
-    own_member[...] = jnp.exp(log_softmax_energy(first[pl.ds(0, points)], counts, cohesion))
-    sizes = jnp.zeros((1, CLUSTER_COUNT), jnp.float32)
-    total = 0.0
-    for source, high, low in ((own, own_high, own_low), (other, other_high, other_low)):
-        for block in range(8):
-            member = jnp.exp(log_softmax_energy(source[block, pl.ds(0, points)], counts, cohesion))
-            sizes += jnp.sum(member, axis=0, keepdims=True)
-            at = pl.ds(block * points, points)
-            both[at, pl.ds(0, CLUSTER_COUNT)], both[at, pl.ds(CLUSTER_COUNT, CLUSTER_COUNT)] = halves(member)
-        wide = product(high[...], both[...])
-        total += product(low[...], both[:, pl.ds(0, CLUSTER_COUNT)])
-        total += wide[:, :CLUSTER_COUNT] + wide[:, CLUSTER_COUNT:]
-    tail = tail_rows(sizes)
+        member = jnp.exp(log_softmax_energy(source[block, pl.ds(0, points)], sums[1:2], sums[0:1]))
+        sizes += jnp.sum(member, axis=0, keepdims=True)
+        at = pl.ds(block * points, points)
+        both[at, pl.ds(0, CLUSTER_COUNT)], both[at, pl.ds(CLUSTER_COUNT, CLUSTER_COUNT)] = halves(member)
+    wide = product(high[...], both[...])
+    total = product(low[...], both[:, pl.ds(0, CLUSTER_COUNT)])
+    return total + wide[:, :CLUSTER_COUNT] + wide[:, CLUSTER_COUNT:], sizes
+
+
+def own_member_kernel(blocks, tail, far_tail, high, low, first, out, sums, own_member, both):
+    points = own_member.shape[0]
+    both_tails = tail[...] + far_tail[...]
+    own_member[...] = jnp.exp(log_softmax_energy(first[pl.ds(0, points)], both_tails[1:2], both_tails[0:1]))
+    out[...], sizes = half_product(blocks, both_tails, high, low, both)
+    sums[...] = tail_rows(both_tails[0:1], both_tails[1:2], sizes)
+
+
+def other_member_kernel(blocks, sums, high, low, weighted, out, both):
+    points = blocks.shape[1] - SIDE
+    total, sizes = half_product(blocks, sums[...], high, low, both)
+    total += weighted[...]
+    tail = tail_rows(sums[pl.ds(2, 1)] + sizes)
     for block in range(8):
         out[member_at(block), pl.ds(0, points)] = total[block * points : (block + 1) * points]
         out[member_at(block), pl.ds(points, SIDE)] = tail
@@ -219,7 +237,7 @@
 PARAMS = pltpu.CompilerParams(vmem_limit_bytes=12 << 20)
 
 
-def on_chip(kernel, name, shapes, inputs, scratch=()):
+def on_chip(kernel, name, shapes, inputs, scratch=(), aliases={}):
     vmem = pl.BlockSpec(memory_space=pltpu.VMEM)
     specs = [vmem] * len(inputs)
     shapes = [jax.ShapeDtypeStruct(*shape) for shape in shapes]
@@ -229,6 +247,7 @@
         in_specs=specs,
         out_specs=[vmem] * len(shapes),
         scratch_shapes=scratch,
+        input_output_aliases=aliases,
         compiler_params=PARAMS,
         name=name,
     )(*inputs)
@@ -252,49 +271,58 @@
 def shards(embedding, seed_cluster):
     points, width = embedding.shape
     lines, tall = points + SIDE, 8 * points
-    anywhere, vmem = pl.BlockSpec(memory_space=pl.ANY), pl.BlockSpec(memory_space=pltpu.VMEM)
+    outside, vmem = pl.BlockSpec(memory_space=pltpu.HBM), pl.BlockSpec(memory_space=pltpu.VMEM)
     block, spread = pl.pallas_call(
         prepare_kernel,
         out_shape=[jax.ShapeDtypeStruct((lines, width), jnp.float32), jax.ShapeDtypeStruct((8, lines, width), jnp.float32)],
-        in_specs=[anywhere, anywhere],
+        in_specs=[outside, outside],
         out_specs=[vmem, vmem],
         scratch_shapes=[pltpu.VMEM((1, points), jnp.int32), pltpu.SemaphoreType.DMA((2,))],
-        compiler_params=PARAMS,
         name="prepare",
     )(embedding, seed_cluster.reshape(1, points))
     columns = exchange_columns(spread)
-    columns, *rows = lax.optimization_barrier((columns, *row_peers(block)))
+    rows = row_peers(block)
+    columns, *rows[:7] = lax.optimization_barrier((columns, *rows[:7]))
     kept = ((tall, tall), jnp.bfloat16)
     exchange = ((8, lines, CLUSTER_COUNT), jnp.float32)
-    scratch = [
-        pltpu.VMEM((tall, 3 * width), jnp.bfloat16),
-        pltpu.VMEM((SIDE, tall), jnp.float32),
-        pltpu.VMEM((tall, CLUSTER_COUNT), jnp.bfloat16),
-    ]
-    left, squares, own_high, own_low, weighted = on_chip(
+    early = EARLY * CHUNK
+    sides = [((tall, 3 * width), jnp.bfloat16), ((SIDE, tall), jnp.float32), ((tall, CLUSTER_COUNT), jnp.bfloat16)]
+    *prepared, own_high, own_low, weighted = on_chip(
         own_pair_kernel,
         "own_pairs",
-        [((tall, 3 * width), jnp.bfloat16), ((tall, 1), jnp.float32), kept, kept, ((tall, CLUSTER_COUNT), jnp.float32)],
-        [*rows, columns],
-        scratch=scratch,
-    )
-    other_high, other_low, weighted = on_chip(
+        [((early, 3 * width), jnp.bfloat16), ((early, 1), jnp.float32), *sides, kept, kept, ((early, CLUSTER_COUNT), jnp.float32)],
+        [*rows[:6], columns],
+    )
+    own_high, own_low, other_high, other_low, weighted = on_chip(
         other_pair_kernel,
         "other_pairs",
-        [kept, kept, exchange],
-        [*rows, other_core(columns), left, squares, weighted],
-        scratch=scratch,
+        [kept, kept, kept, kept, exchange],
+        [*rows, other_core(columns), *prepared, own_high, own_low, weighted],
+        scratch=[pltpu.VMEM(*side) for side in sides],
+        aliases={14: 0, 15: 1},
     )
 
     line = ((lines, CLUSTER_COUNT), jnp.float32)
+    tail = ((SIDE, CLUSTER_COUNT), jnp.float32)
     first, spread = on_chip(sum_kernel, "sum_spread", [line, exchange], [exchange_rows(weighted)])
     firsts = exchange_columns(spread)
-    weighted, own = on_chip(
-        member_kernel,
-        "members",
-        [exchange, ((points, CLUSTER_COUNT), jnp.float32)],
-        [firsts, other_core(firsts), own_high, own_low, other_high, other_low, first],
-        scratch=[pltpu.VMEM((tall, 2 * CLUSTER_COUNT), jnp.bfloat16)],
+    (sums,) = on_chip(tail_kernel, "tails", [tail], [firsts])
+    far_sums = other_core(sums)
+    firsts, far_sums = lax.optimization_barrier((firsts, far_sums))
+    both = [pltpu.VMEM((tall, 2 * CLUSTER_COUNT), jnp.bfloat16)]
+    weighted, sums, own = on_chip(
+        own_member_kernel,
+        "own_members",
+        [((tall, CLUSTER_COUNT), jnp.float32), tail, ((points, CLUSTER_COUNT), jnp.float32)],
+        [firsts, sums, far_sums, own_high, own_low, first],
+        scratch=both,
+    )
+    (weighted,) = on_chip(
+        other_member_kernel,
+        "other_members",
+        [exchange],
+        [other_core(firsts), sums, other_high, other_low, weighted],
+        scratch=both,
     )
 
     part = ((1, CLUSTER_COUNT), jnp.float32)

time: 105 us -> 105 us (level)
  waiting for transfers between devices: 13 us -> 19.9 us
  blocking collectives: 56.5 us -> 51.3 us
  starting transfers between devices: 21.9 us -> 20 us
  local copies, waits for them, and re-layouts: 1.6 us -> 0.04 us
  Pallas kernels: 11.8 us -> 13.3 us
    ppermute x7, waiting for transfers between devices: 9.33 us -> 14.3 us  [moved(): return lax.ppermute(x, EVERY, pairs)]
    all_to_all x1, blocking collectives: 17.9 us -> 13.9 us  [exchange_columns(): lax.all_to_all(blocks, EVERY, 0, 0, axis_index_groups=COLUMN_GROUPS, tile...]
    ppermute x7, starting transfers between devices: 7.39 us -> 4 us  [moved(): return lax.ppermute(x, EVERY, pairs)]
    all_to_all x1, waiting for transfers between devices: 2.09 us -> 4.74 us  [exchange_columns(): lax.all_to_all(blocks, EVERY, 0, 0, axis_index_groups=COLUMN_GROUPS, tile...]
    unnamed x4 -> x2, local copies, waits for them, and re-layouts: 1.56 us -> 0.01 us
    ppermute x2 -> x3, starting transfers between devices: 3.95 us -> 5.38 us  [other_core(): return lax.ppermute(x, 'core', [(0, 1), (1, 0)])]
    all_to_all x2, blocking collectives: 24.6 us -> 23.5 us  [exchange_rows(): lax.all_to_all(blocks, EVERY, 0, 0, axis_index_groups=ROW_GROUPS, tiled=T...]
    pallas_call x6 -> x8, Pallas kernels: 10.5 us -> 11.2 us  [on_chip(): pl.pallas_call(kernel, out_shape=shapes, in_specs=specs, out_specs=[vmem]...]
  transfers between devices with their start and end apart: 10 -> 11, of which waited for: 7 -> 8; matrix products, arithmetic and copies ran while one was open for 0% -> 0% of each run, Pallas kernels for 3% -> 4%
where the time goes in v11:
time: 105 us
  blocking collectives  51.3 us (49%)
  starting transfers between devices  20 us (19%)
  waiting for transfers between devices  19.9 us (19%)
  Pallas kernels  13.3 us (13%)
    all_to_all x2, blocking collectives, exchange_rows(): lax.all_to_all(blocks, EVERY, 0, 0, axis_index_groups=ROW_GROUPS, tiled=T...  23.5 us
    ppermute x7, waiting for transfers between devices, moved(): return lax.ppermute(x, EVERY, pairs)  14.3 us
    all_to_all x1, blocking collectives, shards(): parts = lax.all_to_all(copies(part, 128), EVERY, 0, 0, tiled=True)  14 us
    all_to_all x1, blocking collectives, exchange_columns(): lax.all_to_all(blocks, EVERY, 0, 0, axis_index_groups=COLUMN_GROUPS, tile...  13.9 us
    pallas_call x8, Pallas kernels, on_chip(): pl.pallas_call(kernel, out_shape=shapes, in_specs=specs, out_specs=[vmem]...  11.2 us
    all_to_all x1, starting transfers between devices, exchange_columns(): lax.all_to_all(blocks, EVERY, 0, 0, axis_index_groups=COLUMN_GROUPS, tile...  10.7 us
    ppermute x3, starting transfers between devices, other_core(): return lax.ppermute(x, 'core', [(0, 1), (1, 0)])  5.38 us
    all_to_all x1, waiting for transfers between devices, exchange_columns(): lax.all_to_all(blocks, EVERY, 0, 0, axis_index_groups=COLUMN_GROUPS, tile...  4.74 us
  transfers between devices with their start and end apart: 11, of which 8 were waited for; matrix products, arithmetic and copies ran while one was open for 0% of the time, Pallas kernels for 4%

profile of v11, /device:TPU:1, one launch (start us, length us, event | category | flops | bytes accessed | tf_op | source)
XLA Modules:
  0.0 104.8 jit_solution(7325622509612142536)
XLA Ops:
  0.0 2.1 %prepare.1 = (f32[136,256]{1,0:T(8,128)}, f32[8,136,256]{2,1,0:T(8,128)}) custom-call(f32[128,256]{1,0:T(8,128)} %embedding.1, s32[1,128]{1,0:T(1,128)} %bitcast.7), custom_call_target="tpu_custom_call" | custom-call | tf_op jit(solution)/shard_map/prepare/pallas_call | solution.py:275
  2.1 10.7 %all-to-all-start = ((f32[8,136,256]{2,1,0:T(8,128)}), f32[8,136,256]{2,1,0:T(8,128)S(1)}, u32[]{:S(2)}, u32[]{:S(2)}) async-start(f32[8,136,256]{2,1,0:T(8,128)} %get-tuple-element.37), calls=%async_computation | async-start | bytes 2228224 | tf_op jit(solution)/shard_map/all_to_all | solution.py:44
  12.9 0.3 collective-permute-start.4
  13.2 3.2 %collective-permute-start.3 = (f32[136,256]{1,0:T(8,128)S(1)}, f32[136,256]{1,0:T(8,128)S(1)}, u32[]{:S(2)}, u32[]{:S(2)}) collective-permute-start(f32[136,256]{1,0:T(8,128)S(1)} %copy-done), channel_id=1, source_target_pairs={{18,0},{19,1},{16,2},{17,3},{22,4},{23,5},{20,6},{21,7},{26,8},{27... | collective-permute-start | bytes 417800 | tf_op jit(solution)/shard_map/ppermute | solution.py:52
  16.4 0.4 collective-permute-start.1
  16.8 4.3 %collective-permute-done.5.refs_6_ = f32[136,256]{1,0:T(8,128)S(1)} collective-permute-done((f32[136,256]{1,0:T(8,128)S(1)}, f32[136,256]{1,0:T(8,128)S(1)}, u32[]{:S(2)}, u32[]{:S(2)}) %collective-permute-start.5) | collective-permute-done | bytes 139296 | tf_op jit(solution)/shard_map/ppermute | solution.py:52
  21.1 0.9 collective-permute-done.3.refs_4_
  22.0 1.2 %collective-permute-done.2.refs_3_ = f32[136,256]{1,0:T(8,128)S(1)} collective-permute-done((f32[136,256]{1,0:T(8,128)S(1)}, f32[136,256]{1,0:T(8,128)S(1)}, u32[]{:S(2)}, u32[]{:S(2)}) %collective-permute-start.2) | collective-permute-done | bytes 139296 | tf_op jit(solution)/shard_map/ppermute | solution.py:52
  23.1 3.7 %collective-permute-done.1.refs_2_ = f32[136,256]{1,0:T(8,128)S(1)} collective-permute-done((f32[136,256]{1,0:T(8,128)S(1)}, f32[136,256]{1,0:T(8,128)S(1)}, u32[]{:S(2)}, u32[]{:S(2)}) %collective-permute-start.1) | collective-permute-done | bytes 139296 | tf_op jit(solution)/shard_map/ppermute | solution.py:52
  26.9 4.7 %all-to-all-done.refs_6_ = f32[8,136,256]{2,1,0:T(8,128)S(1)} async-done(((f32[8,136,256]{2,1,0:T(8,128)}), f32[8,136,256]{2,1,0:T(8,128)S(1)}, u32[]{:S(2)}, u32[]{:S(2)}) %all-to-all-start) | async-done | bytes 1114144 | tf_op jit(solution)/shard_map/all_to_all | solution.py:44
  31.6 1.9 %collective-permute-start.7 = (f32[8,136,256]{2,1,0:T(8,128)S(1)}, f32[8,136,256]{2,1,0:T(8,128)S(1)}, u32[]{:S(2)}, u32[]{:S(2)}) collective-permute-start(f32[8,136,256]{2,1,0:T(8,128)S(1)} %all-to-all-done.refs_6_), channel_id=1, source_target_pairs={{0,1},{1,0},{2,3},{3,2},{4,5},{5,4},{6,7},{7,6},{8,9},{9,8},{10,11... | collective-permute-start | bytes 3342344 | tf_op jit(solution)/shard_map/ppermute | solution.py:261
  33.5 2.9 %own_pairs.1 = (bf16[768,768]{1,0:T(8,128)(2,1)S(1)}, f32[768,1]{1,0:T(8,128)S(1)}, bf16[1024,768]{1,0:T(8,128)(2,1)S(1)}, f32[8,1024]{1,0:T(8,128)S(1)}, bf16[1...) custom-call(f32[136,256]{1,0:T(8,128)S(1)} %copy-done, ...), custom_call_target="tpu_custom_call" | custom-call | tf_op jit(solution)/shard_map/own_pairs/pallas_call | solution.py:244
  36.3 4.2 %collective-permute-done.6.refs_7_ = f32[136,256]{1,0:T(8,128)S(1)} collective-permute-done((f32[136,256]{1,0:T(8,128)S(1)}, f32[136,256]{1,0:T(8,128)S(1)}, u32[]{:S(2)}, u32[]{:S(2)}) %collective-permute-start.6) | collective-permute-done | bytes 139296 | tf_op jit(solution)/shard_map/ppermute | solution.py:52
  40.6 4.3 %other_pairs.1 = (bf16[1024,1024]{1,0:T(8,128)(2,1)S(1)}, bf16[1024,1024]{1,0:T(8,128)(2,1)S(1)}, bf16[1024,1024]{1,0:T(8,128)(2,1)S(1)}, bf16[1024,1024]{1,0:T(8,128)(2,1)S(1)}, f32[8,136,128]{2,1,0:T(8,128)S(1)}) custom-call(f32[136,256]{1,0:T(8,128)S(1)} %copy-done, ...), custom_call_target="tpu_custom_call", output_to_operand_aliasing={{0}: (14, {}), {1}: (15, {})} | custom-call | tf_op jit(solution)/shard_map/other_pairs/pallas_call | solution.py:244
  44.9 11.5 %all_to_all.25.blocks = f32[8,136,128]{2,1,0:T(8,128)S(1)} all-to-all(f32[8,136,128]{2,1,0:T(8,128)S(1)} %get-tuple-element.55), channel_id=1, replica_groups={{0,2,16,18,64,66,80,82},{1,3,17,19,65,67,81,83},{4,6,20,22,68,70,84,86}..., dimensions={0} | all-to-all | bytes 1114112 | tf_op jit(solution)/shard_map/all_to_all | solution.py:40
  56.4 13.9 %all_to_all.26.blocks = f32[8,136,128]{2,1,0:T(8,128)S(1)} all-to-all(f32[8,136,128]{2,1,0:T(8,128)S(1)} %get-tuple-element.56), channel_id=1, replica_groups={{0,6,48,54,72,78,120,126},{1,7,49,55,73,79,121,127},{2,4,50,52,74,76,12..., dimensions={0} | all-to-all | bytes 1114112 | tf_op jit(solution)/shard_map/all_to_all | solution.py:44
  70.4 3.2 %collective-permute-start.8 = (f32[8,128]{1,0:T(8,128)S(1)}, f32[8,128]{1,0:T(8,128)S(1)}, u32[]{:S(2)}, u32[]{:S(2)}) collective-permute-start(f32[8,128]{1,0:T(8,128)S(1)} %tails.1.tail), channel_id=1, source_target_pairs={{0,1},{1,0},{2,3},{3,2},{4,5},{5,4},{6,7},{7,6},{8,9},{9,8},{10,11... | collective-permute-start | bytes 12296 | tf_op jit(solution)/shard_map/ppermute | solution.py:261
  73.5 0.8 collective-permute-done.8.far_tail
  74.4 0.3 collective-permute-start.9
  74.7 1.5 %own_members.1 = (f32[1024,128]{1,0:T(8,128)S(1)}, f32[8,128]{1,0:T(8,128)S(1)}, f32[128,128]{1,0:T(8,128)S(1)}) custom-call(f32[8,136,128]{2,1,0:T(8,128)S(1)} %all_to_all.26.blocks, f32[8,128]{1,0:T(8,128)S(1)} %tails.1.tail, f32[8,128]{1,0:T(8,128)S(1)} %collective-permute-done.8.far_tail, bf16[1024,1024]{1,0:T(8,128)(2,1)S(1)} %get-tuple-element.59.high, ...), custom_call_target="tpu_custom_call" | custom-call | tf_op jit(solution)/shard_map/own_members/pallas_call | solution.py:244
  76.3 1.6 %other_members.1 = f32[8,136,128]{2,1,0:T(8,128)S(1)} custom-call(f32[8,136,128]{2,1,0:T(8,128)S(1)} %collective-permute-done.9.blocks, f32[8,128]{1,0:T(8,128)S(1)} %get-tuple-element.62.sums, bf16[1024,1024]{1,0:T(8,128)(2,1)S(1)} %get-tuple-element.63.high, bf16[1024,1024]{1,0:T(8,128)(2,1)S(1)} %get-tuple-element.64.low, ...), custom_call_target="tpu_custom_call" | custom-call | tf_op jit(solution)/shard_map/other_members/pallas_call | solution.py:244
  77.9 12.0 %all_to_all.27.blocks = f32[8,136,128]{2,1,0:T(8,128)S(1)} all-to-all(f32[8,136,128]{2,1,0:T(8,128)S(1)} %other_members.1), channel_id=1, replica_groups={{0,2,16,18,64,66,80,82},{1,3,17,19,65,67,81,83},{4,6,20,22,68,70,84,86}..., dimensions={0} | all-to-all | bytes 1114112 | tf_op jit(solution)/shard_map/all_to_all | solution.py:40
  90.0 14.0 %all_to_all.28 = f32[128,1,128]{2,1,0:T(1,128)S(1)} all-to-all(f32[128,1,128]{2,1,0:T(1,128)S(1)} %broadcast_in_dim.3), channel_id=1, replica_groups=mesh['y_lo'=2,'z'=4,'y_hi'=2,'x'=4,'core'=2] {'y_lo','z','y_hi','x','core'}, dimensions={0} | all-to-all | bytes 131072 | tf_op jit(solution)/shard_map/all_to_all | solution.py:330
  104.0 0.8 final.1
  (15 shorter events, 0.4 us)
Async XLA Ops:
  2.1 10.7 %copy-start = (f32[136,256]{1,0:T(8,128)S(1)}, f32[136,256]{1,0:T(8,128)}, u32[]{:S(2)}) copy-start(f32[136,256]{1,0:T(8,128)} %get-tuple-element.39.refs_0_) | copy-start | bytes 417796
  2.1 29.5 %all-to-all-start = ((f32[8,136,256]{2,1,0:T(8,128)}), f32[8,136,256]{2,1,0:T(8,128)S(1)}, u32[]{:S(2)}, u32[]{:S(2)}) async-start(f32[8,136,256]{2,1,0:T(8,128)} %get-tuple-element.37), calls=%async_computation | async-start | bytes 2228224 | tf_op jit(solution)/shard_map/all_to_all | solution.py:44
  12.8 8.3 %collective-permute-start.5 = (f32[136,256]{1,0:T(8,128)S(1)}, f32[136,256]{1,0:T(8,128)S(1)}, u32[]{:S(2)}, u32[]{:S(2)}) collective-permute-start(f32[136,256]{1,0:T(8,128)S(1)} %copy-done), channel_id=1, source_target_pairs={{80,0},{81,1},{82,2},{83,3},{84,4},{85,5},{86,6},{87,7},{88,8},{89... | collective-permute-start | bytes 417800 | tf_op jit(solution)/shard_map/ppermute | solution.py:52
  12.9 8.2 %collective-permute-start.4 = (f32[136,256]{1,0:T(8,128)S(1)}, f32[136,256]{1,0:T(8,128)S(1)}, u32[]{:S(2)}, u32[]{:S(2)}) collective-permute-start(f32[136,256]{1,0:T(8,128)S(1)} %copy-done), channel_id=1, source_target_pairs={{66,0},{67,1},{64,2},{65,3},{70,4},{71,5},{68,6},{69,7},{74,8},{75... | collective-permute-start | bytes 417800 | tf_op jit(solution)/shard_map/ppermute | solution.py:52
  13.2 8.7 %collective-permute-start.3 = (f32[136,256]{1,0:T(8,128)S(1)}, f32[136,256]{1,0:T(8,128)S(1)}, u32[]{:S(2)}, u32[]{:S(2)}) collective-permute-start(f32[136,256]{1,0:T(8,128)S(1)} %copy-done), channel_id=1, source_target_pairs={{18,0},{19,1},{16,2},{17,3},{22,4},{23,5},{20,6},{21,7},{26,8},{27... | collective-permute-start | bytes 417800 | tf_op jit(solution)/shard_map/ppermute | solution.py:52
  16.4 6.7 %collective-permute-start.2 = (f32[136,256]{1,0:T(8,128)S(1)}, f32[136,256]{1,0:T(8,128)S(1)}, u32[]{:S(2)}, u32[]{:S(2)}) collective-permute-start(f32[136,256]{1,0:T(8,128)S(1)} %copy-done), channel_id=1, source_target_pairs={{64,0},{65,1},{66,2},{67,3},{68,4},{69,5},{70,6},{71,7},{72,8},{73... | collective-permute-start | bytes 417800 | tf_op jit(solution)/shard_map/ppermute | solution.py:52
  16.4 10.4 %collective-permute-start.1 = (f32[136,256]{1,0:T(8,128)S(1)}, f32[136,256]{1,0:T(8,128)S(1)}, u32[]{:S(2)}, u32[]{:S(2)}) collective-permute-start(f32[136,256]{1,0:T(8,128)S(1)} %copy-done), channel_id=1, source_target_pairs={{16,0},{17,1},{18,2},{19,3},{20,4},{21,5},{22,6},{23,7},{24,8},{25... | collective-permute-start | bytes 417800 | tf_op jit(solution)/shard_map/ppermute | solution.py:52
  21.1 5.8 %collective-permute-start = (f32[136,256]{1,0:T(8,128)S(1)}, f32[136,256]{1,0:T(8,128)S(1)}, u32[]{:S(2)}, u32[]{:S(2)}) collective-permute-start(f32[136,256]{1,0:T(8,128)S(1)} %copy-done), channel_id=1, source_target_pairs={{2,0},{3,1},{0,2},{1,3},{6,4},{7,5},{4,6},{5,7},{10,8},{11,9},{8,1... | collective-permute-start | bytes 417800 | tf_op jit(solution)/shard_map/ppermute | solution.py:52
  31.6 9.0 %collective-permute-start.7 = (f32[8,136,256]{2,1,0:T(8,128)S(1)}, f32[8,136,256]{2,1,0:T(8,128)S(1)}, u32[]{:S(2)}, u32[]{:S(2)}) collective-permute-start(f32[8,136,256]{2,1,0:T(8,128)S(1)} %all-to-all-done.refs_6_), channel_id=1, source_target_pairs={{0,1},{1,0},{2,3},{3,2},{4,5},{5,4},{6,7},{7,6},{8,9},{9,8},{10,11... | collective-permute-start | bytes 3342344 | tf_op jit(solution)/shard_map/ppermute | solution.py:261
  33.5 7.1 %collective-permute-start.6 = (f32[136,256]{1,0:T(8,128)S(1)}, f32[136,256]{1,0:T(8,128)S(1)}, u32[]{:S(2)}, u32[]{:S(2)}) collective-permute-start(f32[136,256]{1,0:T(8,128)S(1)} %copy-done), channel_id=1, source_target_pairs={{82,0},{83,1},{80,2},{81,3},{86,4},{87,5},{84,6},{85,7},{90,8},{91... | collective-permute-start | bytes 417800 | tf_op jit(solution)/shard_map/ppermute | solution.py:52
  70.4 4.0 %collective-permute-start.8 = (f32[8,128]{1,0:T(8,128)S(1)}, f32[8,128]{1,0:T(8,128)S(1)}, u32[]{:S(2)}, u32[]{:S(2)}) collective-permute-start(f32[8,128]{1,0:T(8,128)S(1)} %tails.1.tail), channel_id=1, source_target_pairs={{0,1},{1,0},{2,3},{3,2},{4,5},{5,4},{6,7},{7,6},{8,9},{9,8},{10,11... | collective-permute-start | bytes 12296 | tf_op jit(solution)/shard_map/ppermute | solution.py:261
  74.4 2.0 %collective-permute-start.9 = (f32[8,136,128]{2,1,0:T(8,128)S(1)}, f32[8,136,128]{2,1,0:T(8,128)S(1)}, u32[]{:S(2)}, u32[]{:S(2)}) collective-permute-start(f32[8,136,128]{2,1,0:T(8,128)S(1)} %all_to_all.26.blocks), channel_id=1, source_target_pairs={{0,1},{1,0},{2,3},{3,2},{4,5},{5,4},{6,7},{7,6},{8,9},{9,8},{10,11... | collective-permute-start | bytes 1671176 | tf_op jit(solution)/shard_map/ppermute | solution.py:261

commit v12 on v10

--- a/solution.py
+++ b/solution.py
@@ -33,7 +33,7 @@
 
 
 ROW_GROUPS, COLUMN_GROUPS = cubes(NEAR), cubes(FAR)
-ROW_ORDER = (0, 1, 2, 4, 3, 5, 6, 7)
+ROW_ORDER = (0, 7, 6, 5, 3, 4, 2, 1)
 
 
 def exchange_rows(blocks):
@@ -252,14 +252,13 @@
 def shards(embedding, seed_cluster):
     points, width = embedding.shape
     lines, tall = points + SIDE, 8 * points
-    anywhere, vmem = pl.BlockSpec(memory_space=pl.ANY), pl.BlockSpec(memory_space=pltpu.VMEM)
+    outside, vmem = pl.BlockSpec(memory_space=pltpu.HBM), pl.BlockSpec(memory_space=pltpu.VMEM)
     block, spread = pl.pallas_call(
         prepare_kernel,
         out_shape=[jax.ShapeDtypeStruct((lines, width), jnp.float32), jax.ShapeDtypeStruct((8, lines, width), jnp.float32)],
-        in_specs=[anywhere, anywhere],
+        in_specs=[outside, outside],
         out_specs=[vmem, vmem],
         scratch_shapes=[pltpu.VMEM((1, points), jnp.int32), pltpu.SemaphoreType.DMA((2,))],
-        compiler_params=PARAMS,
         name="prepare",
     )(embedding, seed_cluster.reshape(1, points))
     columns = exchange_columns(spread)

time: 105 us -> 103 us (0.981)
  blocking collectives: 56.5 us -> 54.7 us
  local copies, waits for them, and re-layouts: 1.6 us -> 0.04 us
    all_to_all x1, waiting for transfers between devices: 2.09 us -> 4.93 us  [exchange_columns(): lax.all_to_all(blocks, EVERY, 0, 0, axis_index_groups=COLUMN_GROUPS, tile...]
    ppermute x7, waiting for transfers between devices: 9.33 us -> 7.5 us  [moved(): return lax.ppermute(x, EVERY, pairs)]
    all_to_all x1, blocking collectives: 17.9 us -> 16.1 us  [exchange_columns(): lax.all_to_all(blocks, EVERY, 0, 0, axis_index_groups=COLUMN_GROUPS, tile...]
    unnamed x4 -> x2, local copies, waits for them, and re-layouts: 1.56 us -> 0.01 us
  transfers between devices with their start and end apart: 10 -> 10, of which waited for: 7 -> 6; matrix products, arithmetic and copies ran while one was open for 0% -> 0% of each run, Pallas kernels for 3% -> 3%
where the time goes in v12:
time: 103 us; the launch traced here: 102 us
  blocking collectives  54.7 us (53%)
  starting transfers between devices  20.9 us (20%)
  waiting for transfers between devices  14 us (14%)
  Pallas kernels  12.6 us (12%)
    all_to_all x2, blocking collectives, exchange_rows(): lax.all_to_all(blocks, EVERY, 0, 0, axis_index_groups=ROW_GROUPS, tiled=T...  24.6 us
    all_to_all x1, blocking collectives, exchange_columns(): lax.all_to_all(blocks, EVERY, 0, 0, axis_index_groups=COLUMN_GROUPS, tile...  16.1 us
    all_to_all x1, blocking collectives, shards(): parts = lax.all_to_all(copies(part, 128), EVERY, 0, 0, tiled=True)  14 us
    all_to_all x1, starting transfers between devices, exchange_columns(): lax.all_to_all(blocks, EVERY, 0, 0, axis_index_groups=COLUMN_GROUPS, tile...  10.7 us
    pallas_call x6, Pallas kernels, on_chip(): pl.pallas_call(kernel, out_shape=shapes, in_specs=specs, out_specs=[vmem]...  10.5 us
    ppermute x7, waiting for transfers between devices, moved(): return lax.ppermute(x, EVERY, pairs)  7.5 us
    ppermute x7, starting transfers between devices, moved(): return lax.ppermute(x, EVERY, pairs)  6.35 us
    all_to_all x1, waiting for transfers between devices, exchange_columns(): lax.all_to_all(blocks, EVERY, 0, 0, axis_index_groups=COLUMN_GROUPS, tile...  4.93 us
  transfers between devices with their start and end apart: 10, of which 6 were waited for; matrix products, arithmetic and copies ran while one was open for 0% of the time, Pallas kernels for 3%

profile of v12, /device:TPU:1, one launch (start us, length us, event | category | flops | bytes accessed | tf_op | source)
XLA Modules:
  0.0 102.4 jit_solution(211146553801267972)
XLA Ops:
  0.0 2.1 %prepare.1 = (f32[136,256]{1,0:T(8,128)}, f32[8,136,256]{2,1,0:T(8,128)}) custom-call(f32[128,256]{1,0:T(8,128)} %embedding.1, s32[1,128]{1,0:T(1,128)} %bitcast.7), custom_call_target="tpu_custom_call" | custom-call | tf_op jit(solution)/shard_map/prepare/pallas_call | solution.py:256
  2.1 10.7 %all-to-all-start = ((f32[8,136,256]{2,1,0:T(8,128)}), f32[8,136,256]{2,1,0:T(8,128)S(1)}, u32[]{:S(2)}, u32[]{:S(2)}) async-start(f32[8,136,256]{2,1,0:T(8,128)} %get-tuple-element.30), calls=%async_computation | async-start | bytes 2228224 | tf_op jit(solution)/shard_map/all_to_all | solution.py:44
  12.8 0.1 collective-permute-start.6
  12.9 0.1 collective-permute-start.5
  13.0 0.1 collective-permute-start.4
  13.1 2.5 %collective-permute-start.3 = (f32[136,256]{1,0:T(8,128)S(1)}, f32[136,256]{1,0:T(8,128)S(1)}, u32[]{:S(2)}, u32[]{:S(2)}) collective-permute-start(f32[136,256]{1,0:T(8,128)S(1)} %copy-done), channel_id=1, source_target_pairs={{18,0},{19,1},{16,2},{17,3},{22,4},{23,5},{20,6},{21,7},{26,8},{27... | collective-permute-start | bytes 417800 | tf_op jit(solution)/shard_map/ppermute | solution.py:52
  15.5 1.3 %collective-permute-start.2 = (f32[136,256]{1,0:T(8,128)S(1)}, f32[136,256]{1,0:T(8,128)S(1)}, u32[]{:S(2)}, u32[]{:S(2)}) collective-permute-start(f32[136,256]{1,0:T(8,128)S(1)} %copy-done), channel_id=1, source_target_pairs={{66,0},{67,1},{64,2},{65,3},{70,4},{71,5},{68,6},{69,7},{74,8},{75... | collective-permute-start | bytes 417800 | tf_op jit(solution)/shard_map/ppermute | solution.py:52
  16.8 0.3 collective-permute-done.6.refs_7_
  17.1 0.8 collective-permute-done.5.refs_6_
  17.9 2.4 %collective-permute-start = (f32[136,256]{1,0:T(8,128)S(1)}, f32[136,256]{1,0:T(8,128)S(1)}, u32[]{:S(2)}, u32[]{:S(2)}) collective-permute-start(f32[136,256]{1,0:T(8,128)S(1)} %copy-done), channel_id=1, source_target_pairs={{82,0},{83,1},{80,2},{81,3},{86,4},{87,5},{84,6},{85,7},{90,8},{91... | collective-permute-start | bytes 417800 | tf_op jit(solution)/shard_map/ppermute | solution.py:52
  20.3 1.8 %collective-permute-done.2.refs_3_ = f32[136,256]{1,0:T(8,128)S(1)} collective-permute-done((f32[136,256]{1,0:T(8,128)S(1)}, f32[136,256]{1,0:T(8,128)S(1)}, u32[]{:S(2)}, u32[]{:S(2)}) %collective-permute-start.2) | collective-permute-done | bytes 139296 | tf_op jit(solution)/shard_map/ppermute | solution.py:52
  22.0 4.6 %collective-permute-done.1.refs_2_ = f32[136,256]{1,0:T(8,128)S(1)} collective-permute-done((f32[136,256]{1,0:T(8,128)S(1)}, f32[136,256]{1,0:T(8,128)S(1)}, u32[]{:S(2)}, u32[]{:S(2)}) %collective-permute-start.1) | collective-permute-done | bytes 139296 | tf_op jit(solution)/shard_map/ppermute | solution.py:52
  26.7 4.9 %all-to-all-done.refs_8_ = f32[8,136,256]{2,1,0:T(8,128)S(1)} async-done(((f32[8,136,256]{2,1,0:T(8,128)}), f32[8,136,256]{2,1,0:T(8,128)S(1)}, u32[]{:S(2)}, u32[]{:S(2)}) %all-to-all-start) | async-done | bytes 1114144 | tf_op jit(solution)/shard_map/all_to_all | solution.py:44
  31.6 1.9 %collective-permute-start.7 = (f32[8,136,256]{2,1,0:T(8,128)S(1)}, f32[8,136,256]{2,1,0:T(8,128)S(1)}, u32[]{:S(2)}, u32[]{:S(2)}) collective-permute-start(f32[8,136,256]{2,1,0:T(8,128)S(1)} %all-to-all-done.refs_8_), channel_id=1, source_target_pairs={{0,1},{1,0},{2,3},{3,2},{4,5},{5,4},{6,7},{7,6},{8,9},{9,8},{10,11... | collective-permute-start | bytes 3342344 | tf_op jit(solution)/shard_map/ppermute | solution.py:242
  33.5 3.5 %own_pairs.1 = (bf16[1024,768]{1,0:T(8,128)(2,1)S(1)}, f32[1024,1]{1,0:T(8,128)S(1)}, bf16[1024,1024]{1,0:T(8,128)(2,1)S(1)}, bf16[1024,1024]{1,0:T(8,128)(2,1)S(1)}, f32[1024,128]{1,0:T(8,128)S(1)}) custom-call(f32[136,256]{1,0:T(8,128)S(1)} %copy-done, f32[136,256]{1,0:T(8,128)S(1)} %collective-permute-done.refs_1_, ...), custom_call_target="tpu_custom_call" | custom-call | tf_op jit(solution)/shard_map/own_pairs/pallas_call | solution.py:226
  37.0 3.3 %other_pairs.1 = (bf16[1024,1024]{1,0:T(8,128)(2,1)S(1)}, bf16[1024,1024]{1,0:T(8,128)(2,1)S(1)}, f32[8,136,128]{2,1,0:T(8,128)S(1)}) custom-call(f32[136,256]{1,0:T(8,128)S(1)} %copy-done, f32[136,256]{1,0:T(8,128)S(1)} %collective-permute-done.refs_1_, f32[136,256]{1,0:T(8,128)S(1)} %collective-permute-done.1.refs_2_, ...), custom_call_target="tpu_custom_call" | custom-call | tf_op jit(solution)/shard_map/other_pairs/pallas_call | solution.py:226
  40.4 12.7 %all_to_all.25.blocks = f32[8,136,128]{2,1,0:T(8,128)S(1)} all-to-all(f32[8,136,128]{2,1,0:T(8,128)S(1)} %get-tuple-element.44), channel_id=1, replica_groups={{0,2,16,18,64,66,80,82},{1,3,17,19,65,67,81,83},{4,6,20,22,68,70,84,86}..., dimensions={0} | all-to-all | bytes 1114112 | tf_op jit(solution)/shard_map/all_to_all | solution.py:40
  53.1 16.1 %all_to_all.26.own = f32[8,136,128]{2,1,0:T(8,128)S(1)} all-to-all(f32[8,136,128]{2,1,0:T(8,128)S(1)} %get-tuple-element.45), channel_id=1, replica_groups={{0,6,48,54,72,78,120,126},{1,7,49,55,73,79,121,127},{2,4,50,52,74,76,12..., dimensions={0} | all-to-all | bytes 1114112 | tf_op jit(solution)/shard_map/all_to_all | solution.py:44
  69.2 2.1 %collective-permute-start.8 = (f32[8,136,128]{2,1,0:T(8,128)S(1)}, f32[8,136,128]{2,1,0:T(8,128)S(1)}, u32[]{:S(2)}, u32[]{:S(2)}) collective-permute-start(f32[8,136,128]{2,1,0:T(8,128)S(1)} %all_to_all.26.own), channel_id=1, source_target_pairs={{0,1},{1,0},{2,3},{3,2},{4,5},{5,4},{6,7},{7,6},{8,9},{9,8},{10,11... | collective-permute-start | bytes 1671176 | tf_op jit(solution)/shard_map/ppermute | solution.py:242
  71.3 1.6 %collective-permute-done.8.other = f32[8,136,128]{2,1,0:T(8,128)S(1)} collective-permute-done((f32[8,136,128]{2,1,0:T(8,128)S(1)}, f32[8,136,128]{2,1,0:T(8,128)S(1)}, u32[]{:S(2)}, u32[]{:S(2)}) %collective-permute-start.8) | collective-permute-done | bytes 557088 | tf_op jit(solution)/shard_map/ppermute | solution.py:242
  72.8 2.7 %members.1 = (f32[8,136,128]{2,1,0:T(8,128)S(1)}, f32[128,128]{1,0:T(8,128)S(1)}) custom-call(f32[8,136,128]{2,1,0:T(8,128)S(1)} %all_to_all.26.own, f32[8,136,128]{2,1,0:T(8,128)S(1)} %collective-permute-done.8.other, bf16[1024,1024]{1,0:T(8,128)(2,1)S(1)} %get-tuple-element.46.own_high, bf16[1024,1024]{1,0:T(8,128)(2,1)S(1)} %get-tuple-element.47.own_low, ...), custom_call_target="tpu_custom_call" | custom-call | tf_op jit(solution)/shard_map/members/pallas_call | solution.py:226
  75.5 12.0 %all_to_all.27.blocks = f32[8,136,128]{2,1,0:T(8,128)S(1)} all-to-all(f32[8,136,128]{2,1,0:T(8,128)S(1)} %get-tuple-element.51), channel_id=1, replica_groups={{0,2,16,18,64,66,80,82},{1,3,17,19,65,67,81,83},{4,6,20,22,68,70,84,86}..., dimensions={0} | all-to-all | bytes 1114112 | tf_op jit(solution)/shard_map/all_to_all | solution.py:40
  87.6 14.0 %all_to_all.28 = f32[128,1,128]{2,1,0:T(1,128)S(1)} all-to-all(f32[128,1,128]{2,1,0:T(1,128)S(1)} %broadcast_in_dim.3), channel_id=1, replica_groups=mesh['y_lo'=2,'z'=4,'y_hi'=2,'x'=4,'core'=2] {'y_lo','z','y_hi','x','core'}, dimensions={0} | all-to-all | bytes 131072 | tf_op jit(solution)/shard_map/all_to_all | solution.py:301
  101.6 0.8 final.1
  (11 shorter events, 0.2 us)
Async XLA Ops:
  2.1 10.7 %copy-start = (f32[136,256]{1,0:T(8,128)S(1)}, f32[136,256]{1,0:T(8,128)}, u32[]{:S(2)}) copy-start(f32[136,256]{1,0:T(8,128)} %get-tuple-element.32.refs_0_) | copy-start | bytes 417796
  2.1 29.5 %all-to-all-start = ((f32[8,136,256]{2,1,0:T(8,128)}), f32[8,136,256]{2,1,0:T(8,128)S(1)}, u32[]{:S(2)}, u32[]{:S(2)}) async-start(f32[8,136,256]{2,1,0:T(8,128)} %get-tuple-element.30), calls=%async_computation | async-start | bytes 2228224 | tf_op jit(solution)/shard_map/all_to_all | solution.py:44
  12.8 4.3 %collective-permute-start.6 = (f32[136,256]{1,0:T(8,128)S(1)}, f32[136,256]{1,0:T(8,128)S(1)}, u32[]{:S(2)}, u32[]{:S(2)}) collective-permute-start(f32[136,256]{1,0:T(8,128)S(1)} %copy-done), channel_id=1, source_target_pairs={{2,0},{3,1},{0,2},{1,3},{6,4},{7,5},{4,6},{5,7},{10,8},{11,9},{8,1... | collective-permute-start | bytes 417800 | tf_op jit(solution)/shard_map/ppermute | solution.py:52
  12.9 5.0 %collective-permute-start.5 = (f32[136,256]{1,0:T(8,128)S(1)}, f32[136,256]{1,0:T(8,128)S(1)}, u32[]{:S(2)}, u32[]{:S(2)}) collective-permute-start(f32[136,256]{1,0:T(8,128)S(1)} %copy-done), channel_id=1, source_target_pairs={{16,0},{17,1},{18,2},{19,3},{20,4},{21,5},{22,6},{23,7},{24,8},{25... | collective-permute-start | bytes 417800 | tf_op jit(solution)/shard_map/ppermute | solution.py:52
  13.0 7.3 %collective-permute-start.4 = (f32[136,256]{1,0:T(8,128)S(1)}, f32[136,256]{1,0:T(8,128)S(1)}, u32[]{:S(2)}, u32[]{:S(2)}) collective-permute-start(f32[136,256]{1,0:T(8,128)S(1)} %copy-done), channel_id=1, source_target_pairs={{64,0},{65,1},{66,2},{67,3},{68,4},{69,5},{70,6},{71,7},{72,8},{73... | collective-permute-start | bytes 417800 | tf_op jit(solution)/shard_map/ppermute | solution.py:52
  13.1 7.2 %collective-permute-start.3 = (f32[136,256]{1,0:T(8,128)S(1)}, f32[136,256]{1,0:T(8,128)S(1)}, u32[]{:S(2)}, u32[]{:S(2)}) collective-permute-start(f32[136,256]{1,0:T(8,128)S(1)} %copy-done), channel_id=1, source_target_pairs={{18,0},{19,1},{16,2},{17,3},{22,4},{23,5},{20,6},{21,7},{26,8},{27... | collective-permute-start | bytes 417800 | tf_op jit(solution)/shard_map/ppermute | solution.py:52
  15.5 6.5 %collective-permute-start.2 = (f32[136,256]{1,0:T(8,128)S(1)}, f32[136,256]{1,0:T(8,128)S(1)}, u32[]{:S(2)}, u32[]{:S(2)}) collective-permute-start(f32[136,256]{1,0:T(8,128)S(1)} %copy-done), channel_id=1, source_target_pairs={{66,0},{67,1},{64,2},{65,3},{70,4},{71,5},{68,6},{69,7},{74,8},{75... | collective-permute-start | bytes 417800 | tf_op jit(solution)/shard_map/ppermute | solution.py:52
  17.1 9.6 %collective-permute-start.1 = (f32[136,256]{1,0:T(8,128)S(1)}, f32[136,256]{1,0:T(8,128)S(1)}, u32[]{:S(2)}, u32[]{:S(2)}) collective-permute-start(f32[136,256]{1,0:T(8,128)S(1)} %copy-done), channel_id=1, source_target_pairs={{80,0},{81,1},{82,2},{83,3},{84,4},{85,5},{86,6},{87,7},{88,8},{89... | collective-permute-start | bytes 417800 | tf_op jit(solution)/shard_map/ppermute | solution.py:52
  17.9 8.8 %collective-permute-start = (f32[136,256]{1,0:T(8,128)S(1)}, f32[136,256]{1,0:T(8,128)S(1)}, u32[]{:S(2)}, u32[]{:S(2)}) collective-permute-start(f32[136,256]{1,0:T(8,128)S(1)} %copy-done), channel_id=1, source_target_pairs={{82,0},{83,1},{80,2},{81,3},{86,4},{87,5},{84,6},{85,7},{90,8},{91... | collective-permute-start | bytes 417800 | tf_op jit(solution)/shard_map/ppermute | solution.py:52
  31.6 5.4 %collective-permute-start.7 = (f32[8,136,256]{2,1,0:T(8,128)S(1)}, f32[8,136,256]{2,1,0:T(8,128)S(1)}, u32[]{:S(2)}, u32[]{:S(2)}) collective-permute-start(f32[8,136,256]{2,1,0:T(8,128)S(1)} %all-to-all-done.refs_8_), channel_id=1, source_target_pairs={{0,1},{1,0},{2,3},{3,2},{4,5},{5,4},{6,7},{7,6},{8,9},{9,8},{10,11... | collective-permute-start | bytes 3342344 | tf_op jit(solution)/shard_map/ppermute | solution.py:242
  69.2 3.7 %collective-permute-start.8 = (f32[8,136,128]{2,1,0:T(8,128)S(1)}, f32[8,136,128]{2,1,0:T(8,128)S(1)}, u32[]{:S(2)}, u32[]{:S(2)}) collective-permute-start(f32[8,136,128]{2,1,0:T(8,128)S(1)} %all_to_all.26.own), channel_id=1, source_target_pairs={{0,1},{1,0},{2,3},{3,2},{4,5},{5,4},{6,7},{7,6},{8,9},{9,8},{10,11... | collective-permute-start | bytes 1671176 | tf_op jit(solution)/shard_map/ppermute | solution.py:242

commit v13 on v11

--- a/solution.py
+++ b/solution.py
@@ -33,7 +33,7 @@
 
 
 ROW_GROUPS, COLUMN_GROUPS = cubes(NEAR), cubes(FAR)
-ROW_ORDER = (0, 1, 2, 4, 3, 5, 6, 7)
+ROW_ORDER = (0, 7, 6, 5, 3, 4, 2, 1)
 
 
 def exchange_rows(blocks):

time: 105 us -> 104 us (level)
  waiting for transfers between devices: 19.9 us -> 18.2 us
    ppermute x7, waiting for transfers between devices: 14.3 us -> 12.2 us  [moved(): return lax.ppermute(x, EVERY, pairs)]
  transfers between devices with their start and end apart: 11 -> 11, of which waited for: 8 -> 7; matrix products, arithmetic and copies ran while one was open for 0% -> 0% of each run, Pallas kernels for 4% -> 4%
where the time goes in v13:
time: 104 us; the launch traced here: 103 us
  blocking collectives  51.5 us (50%)
  starting transfers between devices  20.3 us (20%)
  waiting for transfers between devices  18.2 us (18%)
  Pallas kernels  13.4 us (13%)
    all_to_all x2, blocking collectives, exchange_rows(): lax.all_to_all(blocks, EVERY, 0, 0, axis_index_groups=ROW_GROUPS, tiled=T...  23.5 us
    all_to_all x1, blocking collectives, exchange_columns(): lax.all_to_all(blocks, EVERY, 0, 0, axis_index_groups=COLUMN_GROUPS, tile...  14 us
    all_to_all x1, blocking collectives, shards(): parts = lax.all_to_all(copies(part, 128), EVERY, 0, 0, tiled=True)  14 us
    ppermute x7, waiting for transfers between devices, moved(): return lax.ppermute(x, EVERY, pairs)  12.2 us
    pallas_call x8, Pallas kernels, on_chip(): pl.pallas_call(kernel, out_shape=shapes, in_specs=specs, out_specs=[vmem]...  11.2 us
    all_to_all x1, starting transfers between devices, exchange_columns(): lax.all_to_all(blocks, EVERY, 0, 0, axis_index_groups=COLUMN_GROUPS, tile...  10.7 us
    ppermute x3, starting transfers between devices, other_core(): return lax.ppermute(x, 'core', [(0, 1), (1, 0)])  5.72 us
    all_to_all x1, waiting for transfers between devices, exchange_columns(): lax.all_to_all(blocks, EVERY, 0, 0, axis_index_groups=COLUMN_GROUPS, tile...  5.08 us
  transfers between devices with their start and end apart: 11, of which 7 were waited for; matrix products, arithmetic and copies ran while one was open for 0% of the time, Pallas kernels for 4%

profile of v13, /device:TPU:1, one launch (start us, length us, event | category | flops | bytes accessed | tf_op | source)
XLA Modules:
  0.0 103.5 jit_solution(15192309742073857558)
XLA Ops:
  0.0 2.1 %prepare.1 = (f32[136,256]{1,0:T(8,128)}, f32[8,136,256]{2,1,0:T(8,128)}) custom-call(f32[128,256]{1,0:T(8,128)} %embedding.1, s32[1,128]{1,0:T(1,128)} %bitcast.7), custom_call_target="tpu_custom_call" | custom-call | tf_op jit(solution)/shard_map/prepare/pallas_call | solution.py:275
  2.1 10.7 %all-to-all-start = ((f32[8,136,256]{2,1,0:T(8,128)}), f32[8,136,256]{2,1,0:T(8,128)S(1)}, u32[]{:S(2)}, u32[]{:S(2)}) async-start(f32[8,136,256]{2,1,0:T(8,128)} %get-tuple-element.37), calls=%async_computation | async-start | bytes 2228224 | tf_op jit(solution)/shard_map/all_to_all | solution.py:44
  12.8 0.1 collective-permute-start.5
  12.9 0.1 collective-permute-start.4
  13.0 1.0 collective-permute-start.3
  14.0 2.7 %collective-permute-start.2 = (f32[136,256]{1,0:T(8,128)S(1)}, f32[136,256]{1,0:T(8,128)S(1)}, u32[]{:S(2)}, u32[]{:S(2)}) collective-permute-start(f32[136,256]{1,0:T(8,128)S(1)} %copy-done), channel_id=1, source_target_pairs={{66,0},{67,1},{64,2},{65,3},{70,4},{71,5},{68,6},{69,7},{74,8},{75... | collective-permute-start | bytes 417800 | tf_op jit(solution)/shard_map/ppermute | solution.py:52
  16.7 2.7 %collective-permute-done.5.refs_6_ = f32[136,256]{1,0:T(8,128)S(1)} collective-permute-done((f32[136,256]{1,0:T(8,128)S(1)}, f32[136,256]{1,0:T(8,128)S(1)}, u32[]{:S(2)}, u32[]{:S(2)}) %collective-permute-start.5) | collective-permute-done | bytes 139296 | tf_op jit(solution)/shard_map/ppermute | solution.py:52
  19.5 2.4 %collective-permute-done.2.refs_3_ = f32[136,256]{1,0:T(8,128)S(1)} collective-permute-done((f32[136,256]{1,0:T(8,128)S(1)}, f32[136,256]{1,0:T(8,128)S(1)}, u32[]{:S(2)}, u32[]{:S(2)}) %collective-permute-start.2) | collective-permute-done | bytes 139296 | tf_op jit(solution)/shard_map/ppermute | solution.py:52
  21.9 4.6 %collective-permute-done.1.refs_2_ = f32[136,256]{1,0:T(8,128)S(1)} collective-permute-done((f32[136,256]{1,0:T(8,128)S(1)}, f32[136,256]{1,0:T(8,128)S(1)}, u32[]{:S(2)}, u32[]{:S(2)}) %collective-permute-start.1) | collective-permute-done | bytes 139296 | tf_op jit(solution)/shard_map/ppermute | solution.py:52
  26.5 5.1 %all-to-all-done.refs_6_ = f32[8,136,256]{2,1,0:T(8,128)S(1)} async-done(((f32[8,136,256]{2,1,0:T(8,128)}), f32[8,136,256]{2,1,0:T(8,128)S(1)}, u32[]{:S(2)}, u32[]{:S(2)}) %all-to-all-start) | async-done | bytes 1114144 | tf_op jit(solution)/shard_map/all_to_all | solution.py:44
  31.6 1.9 %collective-permute-start.7 = (f32[8,136,256]{2,1,0:T(8,128)S(1)}, f32[8,136,256]{2,1,0:T(8,128)S(1)}, u32[]{:S(2)}, u32[]{:S(2)}) collective-permute-start(f32[8,136,256]{2,1,0:T(8,128)S(1)} %all-to-all-done.refs_6_), channel_id=1, source_target_pairs={{0,1},{1,0},{2,3},{3,2},{4,5},{5,4},{6,7},{7,6},{8,9},{9,8},{10,11... | collective-permute-start | bytes 3342344 | tf_op jit(solution)/shard_map/ppermute | solution.py:261
  33.5 2.9 %own_pairs.1 = (bf16[768,768]{1,0:T(8,128)(2,1)S(1)}, f32[768,1]{1,0:T(8,128)S(1)}, bf16[1024,768]{1,0:T(8,128)(2,1)S(1)}, f32[8,1024]{1,0:T(8,128)S(1)}, bf16[1...) custom-call(f32[136,256]{1,0:T(8,128)S(1)} %copy-done, ...), custom_call_target="tpu_custom_call" | custom-call | tf_op jit(solution)/shard_map/own_pairs/pallas_call | solution.py:244
  36.3 2.4 %collective-permute-done.6.refs_7_ = f32[136,256]{1,0:T(8,128)S(1)} collective-permute-done((f32[136,256]{1,0:T(8,128)S(1)}, f32[136,256]{1,0:T(8,128)S(1)}, u32[]{:S(2)}, u32[]{:S(2)}) %collective-permute-start.6) | collective-permute-done | bytes 139296 | tf_op jit(solution)/shard_map/ppermute | solution.py:52
  38.8 4.3 %other_pairs.1 = (bf16[1024,1024]{1,0:T(8,128)(2,1)S(1)}, bf16[1024,1024]{1,0:T(8,128)(2,1)S(1)}, bf16[1024,1024]{1,0:T(8,128)(2,1)S(1)}, bf16[1024,1024]{1,0:T(8,128)(2,1)S(1)}, f32[8,136,128]{2,1,0:T(8,128)S(1)}) custom-call(f32[136,256]{1,0:T(8,128)S(1)} %copy-done, ...), custom_call_target="tpu_custom_call", output_to_operand_aliasing={{0}: (14, {}), {1}: (15, {})} | custom-call | tf_op jit(solution)/shard_map/other_pairs/pallas_call | solution.py:244
  43.1 11.5 %all_to_all.25.blocks = f32[8,136,128]{2,1,0:T(8,128)S(1)} all-to-all(f32[8,136,128]{2,1,0:T(8,128)S(1)} %get-tuple-element.55), channel_id=1, replica_groups={{0,2,16,18,64,66,80,82},{1,3,17,19,65,67,81,83},{4,6,20,22,68,70,84,86}..., dimensions={0} | all-to-all | bytes 1114112 | tf_op jit(solution)/shard_map/all_to_all | solution.py:40
  54.7 14.0 %all_to_all.26.blocks = f32[8,136,128]{2,1,0:T(8,128)S(1)} all-to-all(f32[8,136,128]{2,1,0:T(8,128)S(1)} %get-tuple-element.56), channel_id=1, replica_groups={{0,6,48,54,72,78,120,126},{1,7,49,55,73,79,121,127},{2,4,50,52,74,76,12..., dimensions={0} | all-to-all | bytes 1114112 | tf_op jit(solution)/shard_map/all_to_all | solution.py:44
  68.7 3.5 %collective-permute-start.8 = (f32[8,128]{1,0:T(8,128)S(1)}, f32[8,128]{1,0:T(8,128)S(1)}, u32[]{:S(2)}, u32[]{:S(2)}) collective-permute-start(f32[8,128]{1,0:T(8,128)S(1)} %tails.1.tail), channel_id=1, source_target_pairs={{0,1},{1,0},{2,3},{3,2},{4,5},{5,4},{6,7},{7,6},{8,9},{9,8},{10,11... | collective-permute-start | bytes 12296 | tf_op jit(solution)/shard_map/ppermute | solution.py:261
  72.2 0.8 collective-permute-done.8.far_tail
  73.0 0.3 collective-permute-start.9
  73.4 1.5 %own_members.1 = (f32[1024,128]{1,0:T(8,128)S(1)}, f32[8,128]{1,0:T(8,128)S(1)}, f32[128,128]{1,0:T(8,128)S(1)}) custom-call(f32[8,136,128]{2,1,0:T(8,128)S(1)} %all_to_all.26.blocks, f32[8,128]{1,0:T(8,128)S(1)} %tails.1.tail, f32[8,128]{1,0:T(8,128)S(1)} %collective-permute-done.8.far_tail, bf16[1024,1024]{1,0:T(8,128)(2,1)S(1)} %get-tuple-element.59.high, ...), custom_call_target="tpu_custom_call" | custom-call | tf_op jit(solution)/shard_map/own_members/pallas_call | solution.py:244
  75.0 1.6 %other_members.1 = f32[8,136,128]{2,1,0:T(8,128)S(1)} custom-call(f32[8,136,128]{2,1,0:T(8,128)S(1)} %collective-permute-done.9.blocks, f32[8,128]{1,0:T(8,128)S(1)} %get-tuple-element.62.sums, bf16[1024,1024]{1,0:T(8,128)(2,1)S(1)} %get-tuple-element.63.high, bf16[1024,1024]{1,0:T(8,128)(2,1)S(1)} %get-tuple-element.64.low, ...), custom_call_target="tpu_custom_call" | custom-call | tf_op jit(solution)/shard_map/other_members/pallas_call | solution.py:244
  76.6 12.0 %all_to_all.27.blocks = f32[8,136,128]{2,1,0:T(8,128)S(1)} all-to-all(f32[8,136,128]{2,1,0:T(8,128)S(1)} %other_members.1), channel_id=1, replica_groups={{0,2,16,18,64,66,80,82},{1,3,17,19,65,67,81,83},{4,6,20,22,68,70,84,86}..., dimensions={0} | all-to-all | bytes 1114112 | tf_op jit(solution)/shard_map/all_to_all | solution.py:40
  88.6 14.0 %all_to_all.28 = f32[128,1,128]{2,1,0:T(1,128)S(1)} all-to-all(f32[128,1,128]{2,1,0:T(1,128)S(1)} %broadcast_in_dim.3), channel_id=1, replica_groups=mesh['y_lo'=2,'z'=4,'y_hi'=2,'x'=4,'core'=2] {'y_lo','z','y_hi','x','core'}, dimensions={0} | all-to-all | bytes 131072 | tf_op jit(solution)/shard_map/all_to_all | solution.py:330
  102.6 0.8 final.1
  (15 shorter events, 0.3 us)
Async XLA Ops:
  2.1 10.7 %copy-start = (f32[136,256]{1,0:T(8,128)S(1)}, f32[136,256]{1,0:T(8,128)}, u32[]{:S(2)}) copy-start(f32[136,256]{1,0:T(8,128)} %get-tuple-element.39.refs_0_) | copy-start | bytes 417796
  2.1 29.5 %all-to-all-start = ((f32[8,136,256]{2,1,0:T(8,128)}), f32[8,136,256]{2,1,0:T(8,128)S(1)}, u32[]{:S(2)}, u32[]{:S(2)}) async-start(f32[8,136,256]{2,1,0:T(8,128)} %get-tuple-element.37), calls=%async_computation | async-start | bytes 2228224 | tf_op jit(solution)/shard_map/all_to_all | solution.py:44
  12.8 6.7 %collective-permute-start.5 = (f32[136,256]{1,0:T(8,128)S(1)}, f32[136,256]{1,0:T(8,128)S(1)}, u32[]{:S(2)}, u32[]{:S(2)}) collective-permute-start(f32[136,256]{1,0:T(8,128)S(1)} %copy-done), channel_id=1, source_target_pairs={{16,0},{17,1},{18,2},{19,3},{20,4},{21,5},{22,6},{23,7},{24,8},{25... | collective-permute-start | bytes 417800 | tf_op jit(solution)/shard_map/ppermute | solution.py:52
  12.9 6.6 %collective-permute-start.4 = (f32[136,256]{1,0:T(8,128)S(1)}, f32[136,256]{1,0:T(8,128)S(1)}, u32[]{:S(2)}, u32[]{:S(2)}) collective-permute-start(f32[136,256]{1,0:T(8,128)S(1)} %copy-done), channel_id=1, source_target_pairs={{64,0},{65,1},{66,2},{67,3},{68,4},{69,5},{70,6},{71,7},{72,8},{73... | collective-permute-start | bytes 417800 | tf_op jit(solution)/shard_map/ppermute | solution.py:52
  13.0 6.5 %collective-permute-start.3 = (f32[136,256]{1,0:T(8,128)S(1)}, f32[136,256]{1,0:T(8,128)S(1)}, u32[]{:S(2)}, u32[]{:S(2)}) collective-permute-start(f32[136,256]{1,0:T(8,128)S(1)} %copy-done), channel_id=1, source_target_pairs={{18,0},{19,1},{16,2},{17,3},{22,4},{23,5},{20,6},{21,7},{26,8},{27... | collective-permute-start | bytes 417800 | tf_op jit(solution)/shard_map/ppermute | solution.py:52
  14.0 7.9 %collective-permute-start.2 = (f32[136,256]{1,0:T(8,128)S(1)}, f32[136,256]{1,0:T(8,128)S(1)}, u32[]{:S(2)}, u32[]{:S(2)}) collective-permute-start(f32[136,256]{1,0:T(8,128)S(1)} %copy-done), channel_id=1, source_target_pairs={{66,0},{67,1},{64,2},{65,3},{70,4},{71,5},{68,6},{69,7},{74,8},{75... | collective-permute-start | bytes 417800 | tf_op jit(solution)/shard_map/ppermute | solution.py:52
  16.7 9.8 %collective-permute-start.1 = (f32[136,256]{1,0:T(8,128)S(1)}, f32[136,256]{1,0:T(8,128)S(1)}, u32[]{:S(2)}, u32[]{:S(2)}) collective-permute-start(f32[136,256]{1,0:T(8,128)S(1)} %copy-done), channel_id=1, source_target_pairs={{80,0},{81,1},{82,2},{83,3},{84,4},{85,5},{86,6},{87,7},{88,8},{89... | collective-permute-start | bytes 417800 | tf_op jit(solution)/shard_map/ppermute | solution.py:52
  19.4 7.1 %collective-permute-start = (f32[136,256]{1,0:T(8,128)S(1)}, f32[136,256]{1,0:T(8,128)S(1)}, u32[]{:S(2)}, u32[]{:S(2)}) collective-permute-start(f32[136,256]{1,0:T(8,128)S(1)} %copy-done), channel_id=1, source_target_pairs={{82,0},{83,1},{80,2},{81,3},{86,4},{87,5},{84,6},{85,7},{90,8},{91... | collective-permute-start | bytes 417800 | tf_op jit(solution)/shard_map/ppermute | solution.py:52
  31.6 7.2 %collective-permute-start.7 = (f32[8,136,256]{2,1,0:T(8,128)S(1)}, f32[8,136,256]{2,1,0:T(8,128)S(1)}, u32[]{:S(2)}, u32[]{:S(2)}) collective-permute-start(f32[8,136,256]{2,1,0:T(8,128)S(1)} %all-to-all-done.refs_6_), channel_id=1, source_target_pairs={{0,1},{1,0},{2,3},{3,2},{4,5},{5,4},{6,7},{7,6},{8,9},{9,8},{10,11... | collective-permute-start | bytes 3342344 | tf_op jit(solution)/shard_map/ppermute | solution.py:261
  33.5 5.3 %collective-permute-start.6 = (f32[136,256]{1,0:T(8,128)S(1)}, f32[136,256]{1,0:T(8,128)S(1)}, u32[]{:S(2)}, u32[]{:S(2)}) collective-permute-start(f32[136,256]{1,0:T(8,128)S(1)} %copy-done), channel_id=1, source_target_pairs={{2,0},{3,1},{0,2},{1,3},{6,4},{7,5},{4,6},{5,7},{10,8},{11,9},{8,1... | collective-permute-start | bytes 417800 | tf_op jit(solution)/shard_map/ppermute | solution.py:52
  68.7 4.3 %collective-permute-start.8 = (f32[8,128]{1,0:T(8,128)S(1)}, f32[8,128]{1,0:T(8,128)S(1)}, u32[]{:S(2)}, u32[]{:S(2)}) collective-permute-start(f32[8,128]{1,0:T(8,128)S(1)} %tails.1.tail), channel_id=1, source_target_pairs={{0,1},{1,0},{2,3},{3,2},{4,5},{5,4},{6,7},{7,6},{8,9},{9,8},{10,11... | collective-permute-start | bytes 12296 | tf_op jit(solution)/shard_map/ppermute | solution.py:261
  73.0 2.0 %collective-permute-start.9 = (f32[8,136,128]{2,1,0:T(8,128)S(1)}, f32[8,136,128]{2,1,0:T(8,128)S(1)}, u32[]{:S(2)}, u32[]{:S(2)}) collective-permute-start(f32[8,136,128]{2,1,0:T(8,128)S(1)} %all_to_all.26.blocks), channel_id=1, source_target_pairs={{0,1},{1,0},{2,3},{3,2},{4,5},{5,4},{6,7},{7,6},{8,9},{9,8},{10,11... | collective-permute-start | bytes 1671176 | tf_op jit(solution)/shard_map/ppermute | solution.py:261

commit v14 on v12

--- a/solution.py
+++ b/solution.py
@@ -21,47 +21,40 @@
     return (((y_lo * 4 + z) * 2 + y_hi) * 4 + x) * 2 + core
 
 
-NEAR = ((0, 1), (2, 3))
-FAR = ((0, 3), (1, 2))
-
-
-def cubes(pairs):
+def column_groups():
     groups = []
-    for along_y, along_z, along_x, core in itertools.product(pairs, pairs, pairs, range(2)):
-        groups.append([place(y % 2, z, y // 2, x, core) for y in along_y for z in along_z for x in along_x])
+    for pair, x, core in itertools.product(range(2), range(4), range(2)):
+        groups.append([place(lo, z, lo ^ pair, x, core) for lo in range(2) for z in range(4)])
     return groups
 
 
-ROW_GROUPS, COLUMN_GROUPS = cubes(NEAR), cubes(FAR)
-ROW_ORDER = (0, 7, 6, 5, 3, 4, 2, 1)
+COLUMN_GROUPS = column_groups()
+ROW_ORDER = ((0, 0), (1, 2), (1, 3), (1, 1), (0, 2), (1, 0), (0, 3), (0, 1))
 
 
 def exchange_rows(blocks):
-    return lax.all_to_all(blocks, EVERY, 0, 0, axis_index_groups=ROW_GROUPS, tiled=True)
+    return lax.all_to_all(blocks, ("y_lo", "x"), 0, 0, tiled=True)
 
 
 def exchange_columns(blocks):
     return lax.all_to_all(blocks, EVERY, 0, 0, axis_index_groups=COLUMN_GROUPS, tiled=True)
 
 
-def moved(x, flips):
-    along_y, along_z, along_x = flips // 4, flips // 2 % 2, flips % 2
+def moved(x, flip, step):
     pairs = []
     for lo, z, hi, at, core in itertools.product(*map(range, SIZES)):
-        pairs.append((place(lo ^ along_y, z ^ along_z, hi, at ^ along_x, core), place(lo, z, hi, at, core)))
+        pairs.append((place(lo ^ flip, z, hi, (at + step) % 4, core), place(lo, z, hi, at, core)))
     return lax.ppermute(x, EVERY, pairs)
 
 
 def row_peers(x):
-    return [moved(x, flips) if flips else x for flips in ROW_ORDER]
+    return [moved(x, flip, step) if flip or step else x for flip, step in ROW_ORDER]
 
 
 def member_at(offset):
-    member = 0
-    for name, bit in (("y_lo", 4), ("z", 2), ("x", 1)):
-        own = lax.axis_index(name) % 2
-        member += bit * ((1 - own) if ROW_ORDER[offset] & bit else own)
-    return member
+    y_lo, x = lax.axis_index("y_lo"), lax.axis_index("x")
+    flip, step = ROW_ORDER[offset]
+    return ((1 - y_lo) if flip else y_lo) * 4 + (x + step) % 4
 
 
 def halves(x):

time: 103 us -> 102 us (level)
  waiting for transfers between devices: 14 us -> 12.6 us
    all_to_all x1, waiting for transfers between devices: 4.93 us -> 0.01 us  [exchange_columns(): lax.all_to_all(blocks, EVERY, 0, 0, axis_index_groups=COLUMN_GROUPS, tile...]
    ppermute x7, waiting for transfers between devices: 7.5 us -> 11 us  [moved(): return lax.ppermute(x, EVERY, pairs)]
    all_to_all x1, starting transfers between devices: 10.7 us -> 8.46 us  [exchange_columns(): lax.all_to_all(blocks, EVERY, 0, 0, axis_index_groups=COLUMN_GROUPS, tile...]
    ppermute x2, starting transfers between devices: 3.95 us -> 5.77 us  [other_core(): return lax.ppermute(x, 'core', [(0, 1), (1, 0)])]
    all_to_all x2, blocking collectives: 24.6 us -> 25.8 us  [exchange_rows(): return lax.all_to_all(blocks, ('y_lo', 'x'), 0, 0, tiled=True)]
  transfers between devices with their start and end apart: 10 -> 10, of which waited for: 6 -> 5; matrix products, arithmetic and copies ran while one was open for 0% -> 0% of each run, Pallas kernels for 3% -> 3%
where the time goes in v14:
time: 102 us
  blocking collectives  54.8 us (54%)
  starting transfers between devices  21.4 us (21%)
  Pallas kernels  12.6 us (12%)
  waiting for transfers between devices  12.6 us (12%)
    all_to_all x2, blocking collectives, exchange_rows(): return lax.all_to_all(blocks, ('y_lo', 'x'), 0, 0, tiled=True)  25.8 us
    all_to_all x1, blocking collectives, exchange_columns(): lax.all_to_all(blocks, EVERY, 0, 0, axis_index_groups=COLUMN_GROUPS, tile...  15.3 us
    all_to_all x1, blocking collectives, shards(): parts = lax.all_to_all(copies(part, 128), EVERY, 0, 0, tiled=True)  13.7 us
    ppermute x7, waiting for transfers between devices, moved(): return lax.ppermute(x, EVERY, pairs)  11 us
    pallas_call x6, Pallas kernels, on_chip(): pl.pallas_call(kernel, out_shape=shapes, in_specs=specs, out_specs=[vmem]...  10.5 us
    all_to_all x1, starting transfers between devices, exchange_columns(): lax.all_to_all(blocks, EVERY, 0, 0, axis_index_groups=COLUMN_GROUPS, tile...  8.46 us
    ppermute x7, starting transfers between devices, moved(): return lax.ppermute(x, EVERY, pairs)  7.16 us
    ppermute x2, starting transfers between devices, other_core(): return lax.ppermute(x, 'core', [(0, 1), (1, 0)])  5.77 us
  transfers between devices with their start and end apart: 10, of which 5 were waited for; matrix products, arithmetic and copies ran while one was open for 0% of the time, Pallas kernels for 3%

profile of v14, /device:TPU:1, one launch (start us, length us, event | category | flops | bytes accessed | tf_op | source)
XLA Modules:
  0.0 101.6 jit_solution(12670097493615906827)
XLA Ops:
  0.0 2.1 %prepare.1 = (f32[136,256]{1,0:T(8,128)}, f32[8,136,256]{2,1,0:T(8,128)}) custom-call(f32[128,256]{1,0:T(8,128)} %embedding.1, s32[1,128]{1,0:T(1,128)} %bitcast.7), custom_call_target="tpu_custom_call" | custom-call | tf_op jit(solution)/shard_map/prepare/pallas_call | solution.py:249
  2.1 8.5 %all-to-all-start = ((f32[8,136,256]{2,1,0:T(8,128)}), f32[8,136,256]{2,1,0:T(8,128)S(1)}, u32[]{:S(2)}, u32[]{:S(2)}) async-start(f32[8,136,256]{2,1,0:T(8,128)} %get-tuple-element.30), calls=%async_computation | async-start | bytes 2228224 | tf_op jit(solution)/shard_map/all_to_all | solution.py:40
  10.6 2.5 %collective-permute-start.6 = (f32[136,256]{1,0:T(8,128)S(1)}, f32[136,256]{1,0:T(8,128)S(1)}, u32[]{:S(2)}, u32[]{:S(2)}) collective-permute-start(f32[136,256]{1,0:T(8,128)S(1)} %copy-done), channel_id=1, source_target_pairs={{2,0},{3,1},{4,2},{5,3},{6,4},{7,5},{0,6},{1,7},{10,8},{11,9},{12,... | collective-permute-start | bytes 417800 | tf_op jit(solution)/shard_map/ppermute | solution.py:47
  13.2 0.1 collective-permute-start.4
  13.2 1.7 %collective-permute-start.3 = (f32[136,256]{1,0:T(8,128)S(1)}, f32[136,256]{1,0:T(8,128)S(1)}, u32[]{:S(2)}, u32[]{:S(2)}) collective-permute-start(f32[136,256]{1,0:T(8,128)S(1)} %copy-done), channel_id=1, source_target_pairs={{4,0},{5,1},{6,2},{7,3},{0,4},{1,5},{2,6},{3,7},{12,8},{13,9},{14,... | collective-permute-start | bytes 417800 | tf_op jit(solution)/shard_map/ppermute | solution.py:47
  15.0 2.1 %collective-permute-start.2 = (f32[136,256]{1,0:T(8,128)S(1)}, f32[136,256]{1,0:T(8,128)S(1)}, u32[]{:S(2)}, u32[]{:S(2)}) collective-permute-start(f32[136,256]{1,0:T(8,128)S(1)} %copy-done), channel_id=1, source_target_pairs={{66,0},{67,1},{68,2},{69,3},{70,4},{71,5},{64,6},{65,7},{74,8},{75... | collective-permute-start | bytes 417800 | tf_op jit(solution)/shard_map/ppermute | solution.py:47
  17.0 0.6 collective-permute-start.1
  17.6 2.9 %collective-permute-done.5.refs_6_ = f32[136,256]{1,0:T(8,128)S(1)} collective-permute-done((f32[136,256]{1,0:T(8,128)S(1)}, f32[136,256]{1,0:T(8,128)S(1)}, u32[]{:S(2)}, u32[]{:S(2)}) %collective-permute-start.5) | collective-permute-done | bytes 139296 | tf_op jit(solution)/shard_map/ppermute | solution.py:47
  20.5 0.2 collective-permute-start
  20.7 1.9 %collective-permute-done.2.refs_3_ = f32[136,256]{1,0:T(8,128)S(1)} collective-permute-done((f32[136,256]{1,0:T(8,128)S(1)}, f32[136,256]{1,0:T(8,128)S(1)}, u32[]{:S(2)}, u32[]{:S(2)}) %collective-permute-start.2) | collective-permute-done | bytes 139296 | tf_op jit(solution)/shard_map/ppermute | solution.py:47
  22.6 2.1 %collective-permute-done.1.refs_2_ = f32[136,256]{1,0:T(8,128)S(1)} collective-permute-done((f32[136,256]{1,0:T(8,128)S(1)}, f32[136,256]{1,0:T(8,128)S(1)}, u32[]{:S(2)}, u32[]{:S(2)}) %collective-permute-start.1) | collective-permute-done | bytes 139296 | tf_op jit(solution)/shard_map/ppermute | solution.py:47
  24.6 4.2 %collective-permute-done.refs_1_ = f32[136,256]{1,0:T(8,128)S(1)} collective-permute-done((f32[136,256]{1,0:T(8,128)S(1)}, f32[136,256]{1,0:T(8,128)S(1)}, u32[]{:S(2)}, u32[]{:S(2)}) %collective-permute-start) | collective-permute-done | bytes 139296 | tf_op jit(solution)/shard_map/ppermute | solution.py:47
  28.8 3.2 %collective-permute-start.7 = (f32[8,136,256]{2,1,0:T(8,128)S(1)}, f32[8,136,256]{2,1,0:T(8,128)S(1)}, u32[]{:S(2)}, u32[]{:S(2)}) collective-permute-start(f32[8,136,256]{2,1,0:T(8,128)S(1)} %all-to-all-done.refs_8_), channel_id=1, source_target_pairs={{0,1},{1,0},{2,3},{3,2},{4,5},{5,4},{6,7},{7,6},{8,9},{9,8},{10,11... | collective-permute-start | bytes 3342344 | tf_op jit(solution)/shard_map/ppermute | solution.py:235
  32.0 3.5 %own_pairs.1 = (bf16[1024,768]{1,0:T(8,128)(2,1)S(1)}, f32[1024,1]{1,0:T(8,128)S(1)}, bf16[1024,1024]{1,0:T(8,128)(2,1)S(1)}, bf16[1024,1024]{1,0:T(8,128)(2,1)S(1)}, f32[1024,128]{1,0:T(8,128)S(1)}) custom-call(f32[136,256]{1,0:T(8,128)S(1)} %copy-done, f32[136,256]{1,0:T(8,128)S(1)} %collective-permute-done.refs_1_, ...), custom_call_target="tpu_custom_call" | custom-call | tf_op jit(solution)/shard_map/own_pairs/pallas_call | solution.py:219
  35.5 3.3 %other_pairs.1 = (bf16[1024,1024]{1,0:T(8,128)(2,1)S(1)}, bf16[1024,1024]{1,0:T(8,128)(2,1)S(1)}, f32[8,136,128]{2,1,0:T(8,128)S(1)}) custom-call(f32[136,256]{1,0:T(8,128)S(1)} %copy-done, f32[136,256]{1,0:T(8,128)S(1)} %collective-permute-done.refs_1_, f32[136,256]{1,0:T(8,128)S(1)} %collective-permute-done.1.refs_2_, ...), custom_call_target="tpu_custom_call" | custom-call | tf_op jit(solution)/shard_map/other_pairs/pallas_call | solution.py:219
  38.9 12.9 %all_to_all.25.blocks = f32[8,136,128]{2,1,0:T(8,128)S(1)} all-to-all(f32[8,136,128]{2,1,0:T(8,128)S(1)} %get-tuple-element.44), channel_id=1, replica_groups=mesh['y_lo'=2,'z'=4,'y_hi'=2,'x'=4,'core'=2] {'y_lo','x'}, dimensions={0} | all-to-all | bytes 1114112 | tf_op jit(solution)/shard_map/all_to_all | solution.py:36
  51.8 0.1 sum_spread.1
  51.8 15.3 %all_to_all.26.own = f32[8,136,128]{2,1,0:T(8,128)S(1)} all-to-all(f32[8,136,128]{2,1,0:T(8,128)S(1)} %get-tuple-element.45), channel_id=1, replica_groups={{0,16,32,48,72,88,104,120},{1,17,33,49,73,89,105,121},{2,18,34,50,74,90..., dimensions={0} | all-to-all | bytes 1114112 | tf_op jit(solution)/shard_map/all_to_all | solution.py:40
  67.1 2.6 %collective-permute-start.8 = (f32[8,136,128]{2,1,0:T(8,128)S(1)}, f32[8,136,128]{2,1,0:T(8,128)S(1)}, u32[]{:S(2)}, u32[]{:S(2)}) collective-permute-start(f32[8,136,128]{2,1,0:T(8,128)S(1)} %all_to_all.26.own), channel_id=1, source_target_pairs={{0,1},{1,0},{2,3},{3,2},{4,5},{5,4},{6,7},{7,6},{8,9},{9,8},{10,11... | collective-permute-start | bytes 1671176 | tf_op jit(solution)/shard_map/ppermute | solution.py:235
  69.7 1.6 %collective-permute-done.8.other = f32[8,136,128]{2,1,0:T(8,128)S(1)} collective-permute-done((f32[8,136,128]{2,1,0:T(8,128)S(1)}, f32[8,136,128]{2,1,0:T(8,128)S(1)}, u32[]{:S(2)}, u32[]{:S(2)}) %collective-permute-start.8) | collective-permute-done | bytes 557088 | tf_op jit(solution)/shard_map/ppermute | solution.py:235
  71.3 2.7 %members.1 = (f32[8,136,128]{2,1,0:T(8,128)S(1)}, f32[128,128]{1,0:T(8,128)S(1)}) custom-call(f32[8,136,128]{2,1,0:T(8,128)S(1)} %all_to_all.26.own, f32[8,136,128]{2,1,0:T(8,128)S(1)} %collective-permute-done.8.other, bf16[1024,1024]{1,0:T(8,128)(2,1)S(1)} %get-tuple-element.46.own_high, bf16[1024,1024]{1,0:T(8,128)(2,1)S(1)} %get-tuple-element.47.own_low, ...), custom_call_target="tpu_custom_call" | custom-call | tf_op jit(solution)/shard_map/members/pallas_call | solution.py:219
  74.0 12.9 %all_to_all.27.blocks = f32[8,136,128]{2,1,0:T(8,128)S(1)} all-to-all(f32[8,136,128]{2,1,0:T(8,128)S(1)} %get-tuple-element.51), channel_id=1, replica_groups=mesh['y_lo'=2,'z'=4,'y_hi'=2,'x'=4,'core'=2] {'y_lo','x'}, dimensions={0} | all-to-all | bytes 1114112 | tf_op jit(solution)/shard_map/all_to_all | solution.py:36
  87.0 13.7 %all_to_all.28 = f32[128,1,128]{2,1,0:T(1,128)S(1)} all-to-all(f32[128,1,128]{2,1,0:T(1,128)S(1)} %broadcast_in_dim.3), channel_id=1, replica_groups=mesh['y_lo'=2,'z'=4,'y_hi'=2,'x'=4,'core'=2] {'y_lo','z','y_hi','x','core'}, dimensions={0} | all-to-all | bytes 131072 | tf_op jit(solution)/shard_map/all_to_all | solution.py:294
  100.8 0.8 final.1
  (11 shorter events, 0.1 us)
Async XLA Ops:
  2.1 8.5 %copy-start = (f32[136,256]{1,0:T(8,128)S(1)}, f32[136,256]{1,0:T(8,128)}, u32[]{:S(2)}) copy-start(f32[136,256]{1,0:T(8,128)} %get-tuple-element.32.refs_0_) | copy-start | bytes 417796
  2.1 26.7 %all-to-all-start = ((f32[8,136,256]{2,1,0:T(8,128)}), f32[8,136,256]{2,1,0:T(8,128)S(1)}, u32[]{:S(2)}, u32[]{:S(2)}) async-start(f32[8,136,256]{2,1,0:T(8,128)} %get-tuple-element.30), calls=%async_computation | async-start | bytes 2228224 | tf_op jit(solution)/shard_map/all_to_all | solution.py:40
  10.6 6.4 %collective-permute-start.6 = (f32[136,256]{1,0:T(8,128)S(1)}, f32[136,256]{1,0:T(8,128)S(1)}, u32[]{:S(2)}, u32[]{:S(2)}) collective-permute-start(f32[136,256]{1,0:T(8,128)S(1)} %copy-done), channel_id=1, source_target_pairs={{2,0},{3,1},{4,2},{5,3},{6,4},{7,5},{0,6},{1,7},{10,8},{11,9},{12,... | collective-permute-start | bytes 417800 | tf_op jit(solution)/shard_map/ppermute | solution.py:47
  13.2 7.3 %collective-permute-start.5 = (f32[136,256]{1,0:T(8,128)S(1)}, f32[136,256]{1,0:T(8,128)S(1)}, u32[]{:S(2)}, u32[]{:S(2)}) collective-permute-start(f32[136,256]{1,0:T(8,128)S(1)} %copy-done), channel_id=1, source_target_pairs={{6,0},{7,1},{0,2},{1,3},{2,4},{3,5},{4,6},{5,7},{14,8},{15,9},{8,1... | collective-permute-start | bytes 417800 | tf_op jit(solution)/shard_map/ppermute | solution.py:47
  13.2 7.5 %collective-permute-start.4 = (f32[136,256]{1,0:T(8,128)S(1)}, f32[136,256]{1,0:T(8,128)S(1)}, u32[]{:S(2)}, u32[]{:S(2)}) collective-permute-start(f32[136,256]{1,0:T(8,128)S(1)} %copy-done), channel_id=1, source_target_pairs={{64,0},{65,1},{66,2},{67,3},{68,4},{69,5},{70,6},{71,7},{72,8},{73... | collective-permute-start | bytes 417800 | tf_op jit(solution)/shard_map/ppermute | solution.py:47
  13.2 7.5 %collective-permute-start.3 = (f32[136,256]{1,0:T(8,128)S(1)}, f32[136,256]{1,0:T(8,128)S(1)}, u32[]{:S(2)}, u32[]{:S(2)}) collective-permute-start(f32[136,256]{1,0:T(8,128)S(1)} %copy-done), channel_id=1, source_target_pairs={{4,0},{5,1},{6,2},{7,3},{0,4},{1,5},{2,6},{3,7},{12,8},{13,9},{14,... | collective-permute-start | bytes 417800 | tf_op jit(solution)/shard_map/ppermute | solution.py:47
  15.0 7.6 %collective-permute-start.2 = (f32[136,256]{1,0:T(8,128)S(1)}, f32[136,256]{1,0:T(8,128)S(1)}, u32[]{:S(2)}, u32[]{:S(2)}) collective-permute-start(f32[136,256]{1,0:T(8,128)S(1)} %copy-done), channel_id=1, source_target_pairs={{66,0},{67,1},{68,2},{69,3},{70,4},{71,5},{64,6},{65,7},{74,8},{75... | collective-permute-start | bytes 417800 | tf_op jit(solution)/shard_map/ppermute | solution.py:47
  17.0 7.6 %collective-permute-start.1 = (f32[136,256]{1,0:T(8,128)S(1)}, f32[136,256]{1,0:T(8,128)S(1)}, u32[]{:S(2)}, u32[]{:S(2)}) collective-permute-start(f32[136,256]{1,0:T(8,128)S(1)} %copy-done), channel_id=1, source_target_pairs={{70,0},{71,1},{64,2},{65,3},{66,4},{67,5},{68,6},{69,7},{78,8},{79... | collective-permute-start | bytes 417800 | tf_op jit(solution)/shard_map/ppermute | solution.py:47
  20.5 8.3 %collective-permute-start = (f32[136,256]{1,0:T(8,128)S(1)}, f32[136,256]{1,0:T(8,128)S(1)}, u32[]{:S(2)}, u32[]{:S(2)}) collective-permute-start(f32[136,256]{1,0:T(8,128)S(1)} %copy-done), channel_id=1, source_target_pairs={{68,0},{69,1},{70,2},{71,3},{64,4},{65,5},{66,6},{67,7},{76,8},{77... | collective-permute-start | bytes 417800 | tf_op jit(solution)/shard_map/ppermute | solution.py:47
  28.8 6.7 %collective-permute-start.7 = (f32[8,136,256]{2,1,0:T(8,128)S(1)}, f32[8,136,256]{2,1,0:T(8,128)S(1)}, u32[]{:S(2)}, u32[]{:S(2)}) collective-permute-start(f32[8,136,256]{2,1,0:T(8,128)S(1)} %all-to-all-done.refs_8_), channel_id=1, source_target_pairs={{0,1},{1,0},{2,3},{3,2},{4,5},{5,4},{6,7},{7,6},{8,9},{9,8},{10,11... | collective-permute-start | bytes 3342344 | tf_op jit(solution)/shard_map/ppermute | solution.py:235
  67.1 4.2 %collective-permute-start.8 = (f32[8,136,128]{2,1,0:T(8,128)S(1)}, f32[8,136,128]{2,1,0:T(8,128)S(1)}, u32[]{:S(2)}, u32[]{:S(2)}) collective-permute-start(f32[8,136,128]{2,1,0:T(8,128)S(1)} %all_to_all.26.own), channel_id=1, source_target_pairs={{0,1},{1,0},{2,3},{3,2},{4,5},{5,4},{6,7},{7,6},{8,9},{9,8},{10,11... | collective-permute-start | bytes 1671176 | tf_op jit(solution)/shard_map/ppermute | solution.py:235

commit v15 on v14

--- a/solution.py
+++ b/solution.py
@@ -102,7 +102,7 @@
 CHUNK = 256
 
 
-def weigh(columns, left, squares, high_out, low_out, right, line, member, chunks, keep):
+def weigh(columns, left, squares, high_out, low_out, right, line, member):
     points, width = columns.shape[1] - SIDE, columns.shape[2]
     for block in range(8):
         at = pl.ds(block * points, points)
@@ -113,14 +113,14 @@
         side = columns[block, pl.ds(points, 1)]
         line[:, at] = jnp.broadcast_to(side[:, points:], (SIDE, points))
         member[at] = seed_member(side[:, :points]).astype(jnp.bfloat16)
-    for chunk in range(chunks):
+    for chunk in range(left.shape[0] // CHUNK):
         at = pl.ds(chunk * CHUNK, CHUNK)
         inner = lax.dot_general(left[at], right[...], (((1,), (1,)), ((), ())), preferred_element_type=jnp.float32)
         squared = inner + squares[at] + line[pl.ds(0, 1)]
         high, low = halves(squared * lax.rsqrt(squared))
         high_out[at] = high
         low_out[at] = low
-        keep(chunk, product(high, member[...]) + product(low, member[...]))
+    return product(high_out[...], member[...]) + product(low_out[...], member[...])
 
 
 def own_pair_kernel(*refs):
@@ -134,30 +134,21 @@
         left[at, pl.ds(0, width)] = high
         left[at, pl.ds(width, width)] = high
         left[at, pl.ds(2 * width, width)] = low
-
-    def keep(chunk, total):
-        out[pl.ds(chunk * CHUNK, CHUNK)] = total
-
-    weigh(columns, left, squares, high_out, low_out, right, line, member, out.shape[0] // CHUNK, keep)
+    out[...] = weigh(columns, left, squares, high_out, low_out, right, line, member)
 
 
 def other_pair_kernel(*refs):
     rows, (columns, left, squares, weighted, high_out, low_out, out, right, line, member) = refs[:8], refs[8:]
     points = rows[0].shape[0] - SIDE
-    cohesion = [jnp.zeros((1, CLUSTER_COUNT), jnp.float32)]
-
-    def keep(chunk, total):
-        total += weighted[pl.ds(chunk * CHUNK, CHUNK)]
-        for index in range(CHUNK // points):
-            offset = chunk * (CHUNK // points) + index
-            part = total[index * points : (index + 1) * points]
-            out[member_at(offset), pl.ds(0, points)] = part
-            own = seed_member(rows[offset][pl.ds(points, 1)][:, :points])
-            cohesion[0] += jnp.sum(own * part, axis=0, keepdims=True)
-
-    weigh(columns, left, squares, high_out, low_out, right, line, member, weighted.shape[0] // CHUNK, keep)
+    total = weighted[...] + weigh(columns, left, squares, high_out, low_out, right, line, member)
+    cohesion = jnp.zeros((1, CLUSTER_COUNT), jnp.float32)
+    for offset in range(8):
+        part = total[offset * points : (offset + 1) * points]
+        out[member_at(offset), pl.ds(0, points)] = part
+        own = seed_member(rows[offset][pl.ds(points, 1)][:, :points])
+        cohesion += jnp.sum(own * part, axis=0, keepdims=True)
     counts = jnp.sum(seed_member(rows[0][pl.ds(points, 1)][:, :points]), axis=0, keepdims=True)
-    tail = tail_rows(cohesion[0], counts)
+    tail = tail_rows(cohesion, counts)
     for target in range(8):
         out[target, pl.ds(points, SIDE)] = tail
 

time: 102 us -> 101 us (level)
  no operation moved by 1% of the time
where the time goes in v15:
time: 101 us
  blocking collectives  54.8 us (54%)
  starting transfers between devices  21.4 us (21%)
  waiting for transfers between devices  12.6 us (12%)
  Pallas kernels  11.9 us (12%)
    all_to_all x2, blocking collectives, exchange_rows(): return lax.all_to_all(blocks, ('y_lo', 'x'), 0, 0, tiled=True)  25.8 us
    all_to_all x1, blocking collectives, exchange_columns(): lax.all_to_all(blocks, EVERY, 0, 0, axis_index_groups=COLUMN_GROUPS, tile...  15.3 us
    all_to_all x1, blocking collectives, shards(): parts = lax.all_to_all(copies(part, 128), EVERY, 0, 0, tiled=True)  13.7 us
    ppermute x7, waiting for transfers between devices, moved(): return lax.ppermute(x, EVERY, pairs)  11 us
    pallas_call x6, Pallas kernels, on_chip(): pl.pallas_call(kernel, out_shape=shapes, in_specs=specs, out_specs=[vmem]...  9.77 us
    all_to_all x1, starting transfers between devices, exchange_columns(): lax.all_to_all(blocks, EVERY, 0, 0, axis_index_groups=COLUMN_GROUPS, tile...  8.46 us
    ppermute x7, starting transfers between devices, moved(): return lax.ppermute(x, EVERY, pairs)  7.16 us
    ppermute x2, starting transfers between devices, other_core(): return lax.ppermute(x, 'core', [(0, 1), (1, 0)])  5.77 us
  transfers between devices with their start and end apart: 10, of which 5 were waited for; matrix products, arithmetic and copies ran while one was open for 0% of the time, Pallas kernels for 3%

profile of v15, /device:TPU:1, one launch (start us, length us, event | category | flops | bytes accessed | tf_op | source)
XLA Modules:
  0.0 100.9 jit_solution(6468774752070307054)
XLA Ops:
  0.0 2.1 %prepare.1 = (f32[136,256]{1,0:T(8,128)}, f32[8,136,256]{2,1,0:T(8,128)}) custom-call(f32[128,256]{1,0:T(8,128)} %embedding.1, s32[1,128]{1,0:T(1,128)} %bitcast.7), custom_call_target="tpu_custom_call" | custom-call | tf_op jit(solution)/shard_map/prepare/pallas_call | solution.py:240
  2.1 8.5 %all-to-all-start = ((f32[8,136,256]{2,1,0:T(8,128)}), f32[8,136,256]{2,1,0:T(8,128)S(1)}, u32[]{:S(2)}, u32[]{:S(2)}) async-start(f32[8,136,256]{2,1,0:T(8,128)} %get-tuple-element.30), calls=%async_computation | async-start | bytes 2228224 | tf_op jit(solution)/shard_map/all_to_all | solution.py:40
  10.6 2.5 %collective-permute-start.6 = (f32[136,256]{1,0:T(8,128)S(1)}, f32[136,256]{1,0:T(8,128)S(1)}, u32[]{:S(2)}, u32[]{:S(2)}) collective-permute-start(f32[136,256]{1,0:T(8,128)S(1)} %copy-done), channel_id=1, source_target_pairs={{2,0},{3,1},{4,2},{5,3},{6,4},{7,5},{0,6},{1,7},{10,8},{11,9},{12,... | collective-permute-start | bytes 417800 | tf_op jit(solution)/shard_map/ppermute | solution.py:47
  13.2 0.1 collective-permute-start.4
  13.2 1.7 %collective-permute-start.3 = (f32[136,256]{1,0:T(8,128)S(1)}, f32[136,256]{1,0:T(8,128)S(1)}, u32[]{:S(2)}, u32[]{:S(2)}) collective-permute-start(f32[136,256]{1,0:T(8,128)S(1)} %copy-done), channel_id=1, source_target_pairs={{4,0},{5,1},{6,2},{7,3},{0,4},{1,5},{2,6},{3,7},{12,8},{13,9},{14,... | collective-permute-start | bytes 417800 | tf_op jit(solution)/shard_map/ppermute | solution.py:47
  15.0 2.1 %collective-permute-start.2 = (f32[136,256]{1,0:T(8,128)S(1)}, f32[136,256]{1,0:T(8,128)S(1)}, u32[]{:S(2)}, u32[]{:S(2)}) collective-permute-start(f32[136,256]{1,0:T(8,128)S(1)} %copy-done), channel_id=1, source_target_pairs={{66,0},{67,1},{68,2},{69,3},{70,4},{71,5},{64,6},{65,7},{74,8},{75... | collective-permute-start | bytes 417800 | tf_op jit(solution)/shard_map/ppermute | solution.py:47
  17.0 0.6 collective-permute-start.1
  17.6 2.9 %collective-permute-done.5.refs_6_ = f32[136,256]{1,0:T(8,128)S(1)} collective-permute-done((f32[136,256]{1,0:T(8,128)S(1)}, f32[136,256]{1,0:T(8,128)S(1)}, u32[]{:S(2)}, u32[]{:S(2)}) %collective-permute-start.5) | collective-permute-done | bytes 139296 | tf_op jit(solution)/shard_map/ppermute | solution.py:47
  20.5 0.2 collective-permute-start
  20.7 1.9 %collective-permute-done.2.refs_3_ = f32[136,256]{1,0:T(8,128)S(1)} collective-permute-done((f32[136,256]{1,0:T(8,128)S(1)}, f32[136,256]{1,0:T(8,128)S(1)}, u32[]{:S(2)}, u32[]{:S(2)}) %collective-permute-start.2) | collective-permute-done | bytes 139296 | tf_op jit(solution)/shard_map/ppermute | solution.py:47
  22.6 2.1 %collective-permute-done.1.refs_2_ = f32[136,256]{1,0:T(8,128)S(1)} collective-permute-done((f32[136,256]{1,0:T(8,128)S(1)}, f32[136,256]{1,0:T(8,128)S(1)}, u32[]{:S(2)}, u32[]{:S(2)}) %collective-permute-start.1) | collective-permute-done | bytes 139296 | tf_op jit(solution)/shard_map/ppermute | solution.py:47
  24.6 4.2 %collective-permute-done.refs_1_ = f32[136,256]{1,0:T(8,128)S(1)} collective-permute-done((f32[136,256]{1,0:T(8,128)S(1)}, f32[136,256]{1,0:T(8,128)S(1)}, u32[]{:S(2)}, u32[]{:S(2)}) %collective-permute-start) | collective-permute-done | bytes 139296 | tf_op jit(solution)/shard_map/ppermute | solution.py:47
  28.8 3.2 %collective-permute-start.7 = (f32[8,136,256]{2,1,0:T(8,128)S(1)}, f32[8,136,256]{2,1,0:T(8,128)S(1)}, u32[]{:S(2)}, u32[]{:S(2)}) collective-permute-start(f32[8,136,256]{2,1,0:T(8,128)S(1)} %all-to-all-done.refs_8_), channel_id=1, source_target_pairs={{0,1},{1,0},{2,3},{3,2},{4,5},{5,4},{6,7},{7,6},{8,9},{9,8},{10,11... | collective-permute-start | bytes 3342344 | tf_op jit(solution)/shard_map/ppermute | solution.py:226
  32.0 3.1 %own_pairs.1 = (bf16[1024,768]{1,0:T(8,128)(2,1)S(1)}, f32[1024,1]{1,0:T(8,128)S(1)}, bf16[1024,1024]{1,0:T(8,128)(2,1)S(1)}, bf16[1024,1024]{1,0:T(8,128)(2,1)S(1)}, f32[1024,128]{1,0:T(8,128)S(1)}) custom-call(f32[136,256]{1,0:T(8,128)S(1)} %copy-done, f32[136,256]{1,0:T(8,128)S(1)} %collective-permute-done.refs_1_, ...), custom_call_target="tpu_custom_call" | custom-call | tf_op jit(solution)/shard_map/own_pairs/pallas_call | solution.py:210
  35.1 3.0 %other_pairs.1 = (bf16[1024,1024]{1,0:T(8,128)(2,1)S(1)}, bf16[1024,1024]{1,0:T(8,128)(2,1)S(1)}, f32[8,136,128]{2,1,0:T(8,128)S(1)}) custom-call(f32[136,256]{1,0:T(8,128)S(1)} %copy-done, f32[136,256]{1,0:T(8,128)S(1)} %collective-permute-done.refs_1_, f32[136,256]{1,0:T(8,128)S(1)} %collective-permute-done.1.refs_2_, ...), custom_call_target="tpu_custom_call" | custom-call | tf_op jit(solution)/shard_map/other_pairs/pallas_call | solution.py:210
  38.2 12.9 %all_to_all.25.blocks = f32[8,136,128]{2,1,0:T(8,128)S(1)} all-to-all(f32[8,136,128]{2,1,0:T(8,128)S(1)} %get-tuple-element.44), channel_id=1, replica_groups=mesh['y_lo'=2,'z'=4,'y_hi'=2,'x'=4,'core'=2] {'y_lo','x'}, dimensions={0} | all-to-all | bytes 1114112 | tf_op jit(solution)/shard_map/all_to_all | solution.py:36
  51.1 0.1 sum_spread.1
  51.1 15.3 %all_to_all.26.own = f32[8,136,128]{2,1,0:T(8,128)S(1)} all-to-all(f32[8,136,128]{2,1,0:T(8,128)S(1)} %get-tuple-element.45), channel_id=1, replica_groups={{0,16,32,48,72,88,104,120},{1,17,33,49,73,89,105,121},{2,18,34,50,74,90..., dimensions={0} | all-to-all | bytes 1114112 | tf_op jit(solution)/shard_map/all_to_all | solution.py:40
  66.4 2.6 %collective-permute-start.8 = (f32[8,136,128]{2,1,0:T(8,128)S(1)}, f32[8,136,128]{2,1,0:T(8,128)S(1)}, u32[]{:S(2)}, u32[]{:S(2)}) collective-permute-start(f32[8,136,128]{2,1,0:T(8,128)S(1)} %all_to_all.26.own), channel_id=1, source_target_pairs={{0,1},{1,0},{2,3},{3,2},{4,5},{5,4},{6,7},{7,6},{8,9},{9,8},{10,11... | collective-permute-start | bytes 1671176 | tf_op jit(solution)/shard_map/ppermute | solution.py:226
  69.0 1.6 %collective-permute-done.8.other = f32[8,136,128]{2,1,0:T(8,128)S(1)} collective-permute-done((f32[8,136,128]{2,1,0:T(8,128)S(1)}, f32[8,136,128]{2,1,0:T(8,128)S(1)}, u32[]{:S(2)}, u32[]{:S(2)}) %collective-permute-start.8) | collective-permute-done | bytes 557088 | tf_op jit(solution)/shard_map/ppermute | solution.py:226
  70.6 2.7 %members.1 = (f32[8,136,128]{2,1,0:T(8,128)S(1)}, f32[128,128]{1,0:T(8,128)S(1)}) custom-call(f32[8,136,128]{2,1,0:T(8,128)S(1)} %all_to_all.26.own, f32[8,136,128]{2,1,0:T(8,128)S(1)} %collective-permute-done.8.other, bf16[1024,1024]{1,0:T(8,128)(2,1)S(1)} %get-tuple-element.46.own_high, bf16[1024,1024]{1,0:T(8,128)(2,1)S(1)} %get-tuple-element.47.own_low, ...), custom_call_target="tpu_custom_call" | custom-call | tf_op jit(solution)/shard_map/members/pallas_call | solution.py:210
  73.3 12.9 %all_to_all.27.blocks = f32[8,136,128]{2,1,0:T(8,128)S(1)} all-to-all(f32[8,136,128]{2,1,0:T(8,128)S(1)} %get-tuple-element.51), channel_id=1, replica_groups=mesh['y_lo'=2,'z'=4,'y_hi'=2,'x'=4,'core'=2] {'y_lo','x'}, dimensions={0} | all-to-all | bytes 1114112 | tf_op jit(solution)/shard_map/all_to_all | solution.py:36
  86.3 13.7 %all_to_all.28 = f32[128,1,128]{2,1,0:T(1,128)S(1)} all-to-all(f32[128,1,128]{2,1,0:T(1,128)S(1)} %broadcast_in_dim.3), channel_id=1, replica_groups=mesh['y_lo'=2,'z'=4,'y_hi'=2,'x'=4,'core'=2] {'y_lo','z','y_hi','x','core'}, dimensions={0} | all-to-all | bytes 131072 | tf_op jit(solution)/shard_map/all_to_all | solution.py:285
  100.1 0.8 final.1
  (11 shorter events, 0.1 us)
Async XLA Ops:
  2.1 8.5 %copy-start = (f32[136,256]{1,0:T(8,128)S(1)}, f32[136,256]{1,0:T(8,128)}, u32[]{:S(2)}) copy-start(f32[136,256]{1,0:T(8,128)} %get-tuple-element.32.refs_0_) | copy-start | bytes 417796
  2.1 26.7 %all-to-all-start = ((f32[8,136,256]{2,1,0:T(8,128)}), f32[8,136,256]{2,1,0:T(8,128)S(1)}, u32[]{:S(2)}, u32[]{:S(2)}) async-start(f32[8,136,256]{2,1,0:T(8,128)} %get-tuple-element.30), calls=%async_computation | async-start | bytes 2228224 | tf_op jit(solution)/shard_map/all_to_all | solution.py:40
  10.6 6.4 %collective-permute-start.6 = (f32[136,256]{1,0:T(8,128)S(1)}, f32[136,256]{1,0:T(8,128)S(1)}, u32[]{:S(2)}, u32[]{:S(2)}) collective-permute-start(f32[136,256]{1,0:T(8,128)S(1)} %copy-done), channel_id=1, source_target_pairs={{2,0},{3,1},{4,2},{5,3},{6,4},{7,5},{0,6},{1,7},{10,8},{11,9},{12,... | collective-permute-start | bytes 417800 | tf_op jit(solution)/shard_map/ppermute | solution.py:47
  13.2 7.3 %collective-permute-start.5 = (f32[136,256]{1,0:T(8,128)S(1)}, f32[136,256]{1,0:T(8,128)S(1)}, u32[]{:S(2)}, u32[]{:S(2)}) collective-permute-start(f32[136,256]{1,0:T(8,128)S(1)} %copy-done), channel_id=1, source_target_pairs={{6,0},{7,1},{0,2},{1,3},{2,4},{3,5},{4,6},{5,7},{14,8},{15,9},{8,1... | collective-permute-start | bytes 417800 | tf_op jit(solution)/shard_map/ppermute | solution.py:47
  13.2 7.5 %collective-permute-start.4 = (f32[136,256]{1,0:T(8,128)S(1)}, f32[136,256]{1,0:T(8,128)S(1)}, u32[]{:S(2)}, u32[]{:S(2)}) collective-permute-start(f32[136,256]{1,0:T(8,128)S(1)} %copy-done), channel_id=1, source_target_pairs={{64,0},{65,1},{66,2},{67,3},{68,4},{69,5},{70,6},{71,7},{72,8},{73... | collective-permute-start | bytes 417800 | tf_op jit(solution)/shard_map/ppermute | solution.py:47
  13.2 7.5 %collective-permute-start.3 = (f32[136,256]{1,0:T(8,128)S(1)}, f32[136,256]{1,0:T(8,128)S(1)}, u32[]{:S(2)}, u32[]{:S(2)}) collective-permute-start(f32[136,256]{1,0:T(8,128)S(1)} %copy-done), channel_id=1, source_target_pairs={{4,0},{5,1},{6,2},{7,3},{0,4},{1,5},{2,6},{3,7},{12,8},{13,9},{14,... | collective-permute-start | bytes 417800 | tf_op jit(solution)/shard_map/ppermute | solution.py:47
  15.0 7.6 %collective-permute-start.2 = (f32[136,256]{1,0:T(8,128)S(1)}, f32[136,256]{1,0:T(8,128)S(1)}, u32[]{:S(2)}, u32[]{:S(2)}) collective-permute-start(f32[136,256]{1,0:T(8,128)S(1)} %copy-done), channel_id=1, source_target_pairs={{66,0},{67,1},{68,2},{69,3},{70,4},{71,5},{64,6},{65,7},{74,8},{75... | collective-permute-start | bytes 417800 | tf_op jit(solution)/shard_map/ppermute | solution.py:47
  17.0 7.6 %collective-permute-start.1 = (f32[136,256]{1,0:T(8,128)S(1)}, f32[136,256]{1,0:T(8,128)S(1)}, u32[]{:S(2)}, u32[]{:S(2)}) collective-permute-start(f32[136,256]{1,0:T(8,128)S(1)} %copy-done), channel_id=1, source_target_pairs={{70,0},{71,1},{64,2},{65,3},{66,4},{67,5},{68,6},{69,7},{78,8},{79... | collective-permute-start | bytes 417800 | tf_op jit(solution)/shard_map/ppermute | solution.py:47
  20.5 8.3 %collective-permute-start = (f32[136,256]{1,0:T(8,128)S(1)}, f32[136,256]{1,0:T(8,128)S(1)}, u32[]{:S(2)}, u32[]{:S(2)}) collective-permute-start(f32[136,256]{1,0:T(8,128)S(1)} %copy-done), channel_id=1, source_target_pairs={{68,0},{69,1},{70,2},{71,3},{64,4},{65,5},{66,6},{67,7},{76,8},{77... | collective-permute-start | bytes 417800 | tf_op jit(solution)/shard_map/ppermute | solution.py:47
  28.8 6.3 %collective-permute-start.7 = (f32[8,136,256]{2,1,0:T(8,128)S(1)}, f32[8,136,256]{2,1,0:T(8,128)S(1)}, u32[]{:S(2)}, u32[]{:S(2)}) collective-permute-start(f32[8,136,256]{2,1,0:T(8,128)S(1)} %all-to-all-done.refs_8_), channel_id=1, source_target_pairs={{0,1},{1,0},{2,3},{3,2},{4,5},{5,4},{6,7},{7,6},{8,9},{9,8},{10,11... | collective-permute-start | bytes 3342344 | tf_op jit(solution)/shard_map/ppermute | solution.py:226
  66.4 4.2 %collective-permute-start.8 = (f32[8,136,128]{2,1,0:T(8,128)S(1)}, f32[8,136,128]{2,1,0:T(8,128)S(1)}, u32[]{:S(2)}, u32[]{:S(2)}) collective-permute-start(f32[8,136,128]{2,1,0:T(8,128)S(1)} %all_to_all.26.own), channel_id=1, source_target_pairs={{0,1},{1,0},{2,3},{3,2},{4,5},{5,4},{6,7},{7,6},{8,9},{9,8},{10,11... | collective-permute-start | bytes 1671176 | tf_op jit(solution)/shard_map/ppermute | solution.py:226

commit v16 on v15

--- a/solution.py
+++ b/solution.py
@@ -29,7 +29,7 @@
 
 
 COLUMN_GROUPS = column_groups()
-ROW_ORDER = ((0, 0), (1, 2), (1, 3), (1, 1), (0, 2), (1, 0), (0, 3), (0, 1))
+ROW_ORDER = ((0, 0), (1, 0), (0, 2), (1, 3), (1, 1), (1, 2), (0, 3), (0, 1))
 
 
 def exchange_rows(blocks):

time: 101 us -> 102 us (level)
  starting transfers between devices: 21.4 us -> 20.1 us
  blocking collectives: 54.8 us -> 56 us
    ppermute x2, starting transfers between devices: 5.77 us -> 3.11 us  [other_core(): return lax.ppermute(x, 'core', [(0, 1), (1, 0)])]
    ppermute x7, starting transfers between devices: 7.16 us -> 8.49 us  [moved(): return lax.ppermute(x, EVERY, pairs)]
  transfers between devices with their start and end apart: 10 -> 10, of which waited for: 5 -> 7; matrix products, arithmetic and copies ran while one was open for 0% -> 0% of each run, Pallas kernels for 3% -> 3%
where the time goes in v16:
time: 102 us
  blocking collectives  56 us (55%)
  starting transfers between devices  20.1 us (20%)
  waiting for transfers between devices  13.5 us (13%)
  Pallas kernels  11.9 us (12%)
    all_to_all x2, blocking collectives, exchange_rows(): return lax.all_to_all(blocks, ('y_lo', 'x'), 0, 0, tiled=True)  26.2 us
    all_to_all x1, blocking collectives, exchange_columns(): lax.all_to_all(blocks, EVERY, 0, 0, axis_index_groups=COLUMN_GROUPS, tile...  16.1 us
    all_to_all x1, blocking collectives, shards(): parts = lax.all_to_all(copies(part, 128), EVERY, 0, 0, tiled=True)  13.7 us
    ppermute x7, waiting for transfers between devices, moved(): return lax.ppermute(x, EVERY, pairs)  11.9 us
    pallas_call x6, Pallas kernels, on_chip(): pl.pallas_call(kernel, out_shape=shapes, in_specs=specs, out_specs=[vmem]...  9.78 us
    ppermute x7, starting transfers between devices, moved(): return lax.ppermute(x, EVERY, pairs)  8.49 us
    all_to_all x1, starting transfers between devices, exchange_columns(): lax.all_to_all(blocks, EVERY, 0, 0, axis_index_groups=COLUMN_GROUPS, tile...  8.46 us
    ppermute x2, starting transfers between devices, other_core(): return lax.ppermute(x, 'core', [(0, 1), (1, 0)])  3.11 us
  transfers between devices with their start and end apart: 10, of which 7 were waited for; matrix products, arithmetic and copies ran while one was open for 0% of the time, Pallas kernels for 3%

profile of v16, /device:TPU:1, one launch (start us, length us, event | category | flops | bytes accessed | tf_op | source)
XLA Modules:
  0.0 101.6 jit_solution(8530011563429244654)
XLA Ops:
  0.0 2.1 %prepare.1 = (f32[136,256]{1,0:T(8,128)}, f32[8,136,256]{2,1,0:T(8,128)}) custom-call(f32[128,256]{1,0:T(8,128)} %embedding.1, s32[1,128]{1,0:T(1,128)} %bitcast.7), custom_call_target="tpu_custom_call" | custom-call | tf_op jit(solution)/shard_map/prepare/pallas_call | solution.py:240
  2.1 8.5 %all-to-all-start = ((f32[8,136,256]{2,1,0:T(8,128)}), f32[8,136,256]{2,1,0:T(8,128)S(1)}, u32[]{:S(2)}, u32[]{:S(2)}) async-start(f32[8,136,256]{2,1,0:T(8,128)} %get-tuple-element.30), calls=%async_computation | async-start | bytes 2228224 | tf_op jit(solution)/shard_map/all_to_all | solution.py:40
  10.6 2.5 %collective-permute-start.6 = (f32[136,256]{1,0:T(8,128)S(1)}, f32[136,256]{1,0:T(8,128)S(1)}, u32[]{:S(2)}, u32[]{:S(2)}) collective-permute-start(f32[136,256]{1,0:T(8,128)S(1)} %copy-done), channel_id=1, source_target_pairs={{2,0},{3,1},{4,2},{5,3},{6,4},{7,5},{0,6},{1,7},{10,8},{11,9},{12,... | collective-permute-start | bytes 417800 | tf_op jit(solution)/shard_map/ppermute | solution.py:47
  13.2 1.5 %collective-permute-start.4 = (f32[136,256]{1,0:T(8,128)S(1)}, f32[136,256]{1,0:T(8,128)S(1)}, u32[]{:S(2)}, u32[]{:S(2)}) collective-permute-start(f32[136,256]{1,0:T(8,128)S(1)} %copy-done), channel_id=1, source_target_pairs={{68,0},{69,1},{70,2},{71,3},{64,4},{65,5},{66,6},{67,7},{76,8},{77... | collective-permute-start | bytes 417800 | tf_op jit(solution)/shard_map/ppermute | solution.py:47
  14.7 2.0 %collective-permute-start.3 = (f32[136,256]{1,0:T(8,128)S(1)}, f32[136,256]{1,0:T(8,128)S(1)}, u32[]{:S(2)}, u32[]{:S(2)}) collective-permute-start(f32[136,256]{1,0:T(8,128)S(1)} %copy-done), channel_id=1, source_target_pairs={{66,0},{67,1},{68,2},{69,3},{70,4},{71,5},{64,6},{65,7},{74,8},{75... | collective-permute-start | bytes 417800 | tf_op jit(solution)/shard_map/ppermute | solution.py:47
  16.6 0.7 collective-permute-start.2
  17.3 1.8 %collective-permute-start.1 = (f32[136,256]{1,0:T(8,128)S(1)}, f32[136,256]{1,0:T(8,128)S(1)}, u32[]{:S(2)}, u32[]{:S(2)}) collective-permute-start(f32[136,256]{1,0:T(8,128)S(1)} %copy-done), channel_id=1, source_target_pairs={{4,0},{5,1},{6,2},{7,3},{0,4},{1,5},{2,6},{3,7},{12,8},{13,9},{14,... | collective-permute-start | bytes 417800 | tf_op jit(solution)/shard_map/ppermute | solution.py:47
  19.1 1.4 %collective-permute-done.5.refs_6_ = f32[136,256]{1,0:T(8,128)S(1)} collective-permute-done((f32[136,256]{1,0:T(8,128)S(1)}, f32[136,256]{1,0:T(8,128)S(1)}, u32[]{:S(2)}, u32[]{:S(2)}) %collective-permute-start.5) | collective-permute-done | bytes 139296 | tf_op jit(solution)/shard_map/ppermute | solution.py:47
  20.5 0.9 collective-permute-done.4.refs_5_
  21.4 1.6 %collective-permute-done.3.refs_4_ = f32[136,256]{1,0:T(8,128)S(1)} collective-permute-done((f32[136,256]{1,0:T(8,128)S(1)}, f32[136,256]{1,0:T(8,128)S(1)}, u32[]{:S(2)}, u32[]{:S(2)}) %collective-permute-start.3) | collective-permute-done | bytes 139296 | tf_op jit(solution)/shard_map/ppermute | solution.py:47
  23.1 3.2 %collective-permute-done.2.refs_3_ = f32[136,256]{1,0:T(8,128)S(1)} collective-permute-done((f32[136,256]{1,0:T(8,128)S(1)}, f32[136,256]{1,0:T(8,128)S(1)}, u32[]{:S(2)}, u32[]{:S(2)}) %collective-permute-start.2) | collective-permute-done | bytes 139296 | tf_op jit(solution)/shard_map/ppermute | solution.py:47
  26.2 0.3 collective-permute-done.1.refs_2_
  26.6 4.4 %collective-permute-done.refs_1_ = f32[136,256]{1,0:T(8,128)S(1)} collective-permute-done((f32[136,256]{1,0:T(8,128)S(1)}, f32[136,256]{1,0:T(8,128)S(1)}, u32[]{:S(2)}, u32[]{:S(2)}) %collective-permute-start) | collective-permute-done | bytes 139296 | tf_op jit(solution)/shard_map/ppermute | solution.py:47
  31.0 0.5 collective-permute-start.7
  31.5 3.1 %own_pairs.1 = (bf16[1024,768]{1,0:T(8,128)(2,1)S(1)}, f32[1024,1]{1,0:T(8,128)S(1)}, bf16[1024,1024]{1,0:T(8,128)(2,1)S(1)}, bf16[1024,1024]{1,0:T(8,128)(2,1)S(1)}, f32[1024,128]{1,0:T(8,128)S(1)}) custom-call(f32[136,256]{1,0:T(8,128)S(1)} %copy-done, f32[136,256]{1,0:T(8,128)S(1)} %collective-permute-done.refs_1_, ...), custom_call_target="tpu_custom_call" | custom-call | tf_op jit(solution)/shard_map/own_pairs/pallas_call | solution.py:210
  34.6 3.0 %other_pairs.1 = (bf16[1024,1024]{1,0:T(8,128)(2,1)S(1)}, bf16[1024,1024]{1,0:T(8,128)(2,1)S(1)}, f32[8,136,128]{2,1,0:T(8,128)S(1)}) custom-call(f32[136,256]{1,0:T(8,128)S(1)} %copy-done, f32[136,256]{1,0:T(8,128)S(1)} %collective-permute-done.refs_1_, f32[136,256]{1,0:T(8,128)S(1)} %collective-permute-done.1.refs_2_, ...), custom_call_target="tpu_custom_call" | custom-call | tf_op jit(solution)/shard_map/other_pairs/pallas_call | solution.py:210
  37.7 13.3 %all_to_all.25.blocks = f32[8,136,128]{2,1,0:T(8,128)S(1)} all-to-all(f32[8,136,128]{2,1,0:T(8,128)S(1)} %get-tuple-element.44), channel_id=1, replica_groups=mesh['y_lo'=2,'z'=4,'y_hi'=2,'x'=4,'core'=2] {'y_lo','x'}, dimensions={0} | all-to-all | bytes 1114112 | tf_op jit(solution)/shard_map/all_to_all | solution.py:36
  51.0 16.1 %all_to_all.26.own = f32[8,136,128]{2,1,0:T(8,128)S(1)} all-to-all(f32[8,136,128]{2,1,0:T(8,128)S(1)} %get-tuple-element.45), channel_id=1, replica_groups={{0,16,32,48,72,88,104,120},{1,17,33,49,73,89,105,121},{2,18,34,50,74,90..., dimensions={0} | all-to-all | bytes 1114112 | tf_op jit(solution)/shard_map/all_to_all | solution.py:40
  67.1 2.6 %collective-permute-start.8 = (f32[8,136,128]{2,1,0:T(8,128)S(1)}, f32[8,136,128]{2,1,0:T(8,128)S(1)}, u32[]{:S(2)}, u32[]{:S(2)}) collective-permute-start(f32[8,136,128]{2,1,0:T(8,128)S(1)} %all_to_all.26.own), channel_id=1, source_target_pairs={{0,1},{1,0},{2,3},{3,2},{4,5},{5,4},{6,7},{7,6},{8,9},{9,8},{10,11... | collective-permute-start | bytes 1671176 | tf_op jit(solution)/shard_map/ppermute | solution.py:226
  69.7 1.6 %collective-permute-done.8.other = f32[8,136,128]{2,1,0:T(8,128)S(1)} collective-permute-done((f32[8,136,128]{2,1,0:T(8,128)S(1)}, f32[8,136,128]{2,1,0:T(8,128)S(1)}, u32[]{:S(2)}, u32[]{:S(2)}) %collective-permute-start.8) | collective-permute-done | bytes 557088 | tf_op jit(solution)/shard_map/ppermute | solution.py:226
  71.3 2.7 %members.1 = (f32[8,136,128]{2,1,0:T(8,128)S(1)}, f32[128,128]{1,0:T(8,128)S(1)}) custom-call(f32[8,136,128]{2,1,0:T(8,128)S(1)} %all_to_all.26.own, f32[8,136,128]{2,1,0:T(8,128)S(1)} %collective-permute-done.8.other, bf16[1024,1024]{1,0:T(8,128)(2,1)S(1)} %get-tuple-element.46.own_high, bf16[1024,1024]{1,0:T(8,128)(2,1)S(1)} %get-tuple-element.47.own_low, ...), custom_call_target="tpu_custom_call" | custom-call | tf_op jit(solution)/shard_map/members/pallas_call | solution.py:210
  74.0 12.9 %all_to_all.27.blocks = f32[8,136,128]{2,1,0:T(8,128)S(1)} all-to-all(f32[8,136,128]{2,1,0:T(8,128)S(1)} %get-tuple-element.51), channel_id=1, replica_groups=mesh['y_lo'=2,'z'=4,'y_hi'=2,'x'=4,'core'=2] {'y_lo','x'}, dimensions={0} | all-to-all | bytes 1114112 | tf_op jit(solution)/shard_map/all_to_all | solution.py:36
  87.0 13.7 %all_to_all.28 = f32[128,1,128]{2,1,0:T(1,128)S(1)} all-to-all(f32[128,1,128]{2,1,0:T(1,128)S(1)} %broadcast_in_dim.3), channel_id=1, replica_groups=mesh['y_lo'=2,'z'=4,'y_hi'=2,'x'=4,'core'=2] {'y_lo','z','y_hi','x','core'}, dimensions={0} | all-to-all | bytes 131072 | tf_op jit(solution)/shard_map/all_to_all | solution.py:285
  100.8 0.8 final.1
  (11 shorter events, 0.2 us)
Async XLA Ops:
  2.1 8.5 %copy-start = (f32[136,256]{1,0:T(8,128)S(1)}, f32[136,256]{1,0:T(8,128)}, u32[]{:S(2)}) copy-start(f32[136,256]{1,0:T(8,128)} %get-tuple-element.32.refs_0_) | copy-start | bytes 417796
  2.1 28.8 %all-to-all-start = ((f32[8,136,256]{2,1,0:T(8,128)}), f32[8,136,256]{2,1,0:T(8,128)S(1)}, u32[]{:S(2)}, u32[]{:S(2)}) async-start(f32[8,136,256]{2,1,0:T(8,128)} %get-tuple-element.30), calls=%async_computation | async-start | bytes 2228224 | tf_op jit(solution)/shard_map/all_to_all | solution.py:40
  10.6 6.7 %collective-permute-start.6 = (f32[136,256]{1,0:T(8,128)S(1)}, f32[136,256]{1,0:T(8,128)S(1)}, u32[]{:S(2)}, u32[]{:S(2)}) collective-permute-start(f32[136,256]{1,0:T(8,128)S(1)} %copy-done), channel_id=1, source_target_pairs={{2,0},{3,1},{4,2},{5,3},{6,4},{7,5},{0,6},{1,7},{10,8},{11,9},{12,... | collective-permute-start | bytes 417800 | tf_op jit(solution)/shard_map/ppermute | solution.py:47
  13.2 7.3 %collective-permute-start.5 = (f32[136,256]{1,0:T(8,128)S(1)}, f32[136,256]{1,0:T(8,128)S(1)}, u32[]{:S(2)}, u32[]{:S(2)}) collective-permute-start(f32[136,256]{1,0:T(8,128)S(1)} %copy-done), channel_id=1, source_target_pairs={{6,0},{7,1},{0,2},{1,3},{2,4},{3,5},{4,6},{5,7},{14,8},{15,9},{8,1... | collective-permute-start | bytes 417800 | tf_op jit(solution)/shard_map/ppermute | solution.py:47
  13.2 8.3 %collective-permute-start.4 = (f32[136,256]{1,0:T(8,128)S(1)}, f32[136,256]{1,0:T(8,128)S(1)}, u32[]{:S(2)}, u32[]{:S(2)}) collective-permute-start(f32[136,256]{1,0:T(8,128)S(1)} %copy-done), channel_id=1, source_target_pairs={{68,0},{69,1},{70,2},{71,3},{64,4},{65,5},{66,6},{67,7},{76,8},{77... | collective-permute-start | bytes 417800 | tf_op jit(solution)/shard_map/ppermute | solution.py:47
  14.7 8.4 %collective-permute-start.3 = (f32[136,256]{1,0:T(8,128)S(1)}, f32[136,256]{1,0:T(8,128)S(1)}, u32[]{:S(2)}, u32[]{:S(2)}) collective-permute-start(f32[136,256]{1,0:T(8,128)S(1)} %copy-done), channel_id=1, source_target_pairs={{66,0},{67,1},{68,2},{69,3},{70,4},{71,5},{64,6},{65,7},{74,8},{75... | collective-permute-start | bytes 417800 | tf_op jit(solution)/shard_map/ppermute | solution.py:47
  16.6 9.6 %collective-permute-start.2 = (f32[136,256]{1,0:T(8,128)S(1)}, f32[136,256]{1,0:T(8,128)S(1)}, u32[]{:S(2)}, u32[]{:S(2)}) collective-permute-start(f32[136,256]{1,0:T(8,128)S(1)} %copy-done), channel_id=1, source_target_pairs={{70,0},{71,1},{64,2},{65,3},{66,4},{67,5},{68,6},{69,7},{78,8},{79... | collective-permute-start | bytes 417800 | tf_op jit(solution)/shard_map/ppermute | solution.py:47
  17.3 9.2 %collective-permute-start.1 = (f32[136,256]{1,0:T(8,128)S(1)}, f32[136,256]{1,0:T(8,128)S(1)}, u32[]{:S(2)}, u32[]{:S(2)}) collective-permute-start(f32[136,256]{1,0:T(8,128)S(1)} %copy-done), channel_id=1, source_target_pairs={{4,0},{5,1},{6,2},{7,3},{0,4},{1,5},{2,6},{3,7},{12,8},{13,9},{14,... | collective-permute-start | bytes 417800 | tf_op jit(solution)/shard_map/ppermute | solution.py:47
  20.5 10.5 %collective-permute-start = (f32[136,256]{1,0:T(8,128)S(1)}, f32[136,256]{1,0:T(8,128)S(1)}, u32[]{:S(2)}, u32[]{:S(2)}) collective-permute-start(f32[136,256]{1,0:T(8,128)S(1)} %copy-done), channel_id=1, source_target_pairs={{64,0},{65,1},{66,2},{67,3},{68,4},{69,5},{70,6},{71,7},{72,8},{73... | collective-permute-start | bytes 417800 | tf_op jit(solution)/shard_map/ppermute | solution.py:47
  31.0 3.6 %collective-permute-start.7 = (f32[8,136,256]{2,1,0:T(8,128)S(1)}, f32[8,136,256]{2,1,0:T(8,128)S(1)}, u32[]{:S(2)}, u32[]{:S(2)}) collective-permute-start(f32[8,136,256]{2,1,0:T(8,128)S(1)} %all-to-all-done.refs_8_), channel_id=1, source_target_pairs={{0,1},{1,0},{2,3},{3,2},{4,5},{5,4},{6,7},{7,6},{8,9},{9,8},{10,11... | collective-permute-start | bytes 3342344 | tf_op jit(solution)/shard_map/ppermute | solution.py:226
  67.1 4.2 %collective-permute-start.8 = (f32[8,136,128]{2,1,0:T(8,128)S(1)}, f32[8,136,128]{2,1,0:T(8,128)S(1)}, u32[]{:S(2)}, u32[]{:S(2)}) collective-permute-start(f32[8,136,128]{2,1,0:T(8,128)S(1)} %all_to_all.26.own), channel_id=1, source_target_pairs={{0,1},{1,0},{2,3},{3,2},{4,5},{5,4},{6,7},{7,6},{8,9},{9,8},{10,11... | collective-permute-start | bytes 1671176 | tf_op jit(solution)/shard_map/ppermute | solution.py:226

commit v17 on v16

--- a/solution.py
+++ b/solution.py
@@ -29,7 +29,7 @@
 
 
 COLUMN_GROUPS = column_groups()
-ROW_ORDER = ((0, 0), (1, 0), (0, 2), (1, 3), (1, 1), (1, 2), (0, 3), (0, 1))
+ROW_ORDER = ((0, 0), (1, 2), (1, 3), (1, 1), (0, 2), (0, 3), (0, 1), (1, 0))
 
 
 def exchange_rows(blocks):
@@ -102,7 +102,7 @@
 CHUNK = 256
 
 
-def weigh(columns, left, squares, high_out, low_out, right, line, member):
+def set_columns(columns, right, line, member):
     points, width = columns.shape[1] - SIDE, columns.shape[2]
     for block in range(8):
         at = pl.ds(block * points, points)
@@ -113,37 +113,62 @@
         side = columns[block, pl.ds(points, 1)]
         line[:, at] = jnp.broadcast_to(side[:, points:], (SIDE, points))
         member[at] = seed_member(side[:, :points]).astype(jnp.bfloat16)
-    for chunk in range(left.shape[0] // CHUNK):
-        at = pl.ds(chunk * CHUNK, CHUNK)
-        inner = lax.dot_general(left[at], right[...], (((1,), (1,)), ((), ())), preferred_element_type=jnp.float32)
-        squared = inner + squares[at] + line[pl.ds(0, 1)]
-        high, low = halves(squared * lax.rsqrt(squared))
-        high_out[at] = high
-        low_out[at] = low
-    return product(high_out[...], member[...]) + product(low_out[...], member[...])
+
+
+def left_rows(x):
+    high, low = halves(-2.0 * x)
+    return jnp.concatenate([high, high, low], axis=1), jnp.sum(x * x, axis=1, keepdims=True) + 1.0
+
+
+def distances(left, square, right, line, high_out, low_out, at):
+    inner = lax.dot_general(left, right[...], (((1,), (1,)), ((), ())), preferred_element_type=jnp.float32)
+    squared = inner + square + line[pl.ds(0, 1)]
+    high_out[at], low_out[at] = halves(squared * lax.rsqrt(squared))
+
+
+def weights(high, low, member, at):
+    return product(high[at], member[...]) + product(low[at], member[...])
+
+
+EARLY = 768
 
 
 def own_pair_kernel(*refs):
-    rows, (columns, left, squares, high_out, low_out, out, right, line, member) = refs[:8], refs[8:]
-    points, width = rows[0].shape[0] - SIDE, rows[0].shape[1]
+    rows, (columns, left, squares, right, line, member, high, low, out) = refs[:6], refs[6:]
+    points = rows[0].shape[0] - SIDE
+    set_columns(columns, right, line, member)
     for offset, block in enumerate(rows):
-        x = block[pl.ds(0, points)]
         at = pl.ds(offset * points, points)
-        squares[at] = jnp.sum(x * x, axis=1, keepdims=True) + 1.0
-        high, low = halves(-2.0 * x)
-        left[at, pl.ds(0, width)] = high
-        left[at, pl.ds(width, width)] = high
-        left[at, pl.ds(2 * width, width)] = low
-    out[...] = weigh(columns, left, squares, high_out, low_out, right, line, member)
-
-
-def other_pair_kernel(*refs):
-    rows, (columns, left, squares, weighted, high_out, low_out, out, right, line, member) = refs[:8], refs[8:]
+        left[at], squares[at] = left_rows(block[pl.ds(0, points)])
+    for start in range(0, EARLY, CHUNK):
+        at = pl.ds(start, CHUNK)
+        distances(left[at], squares[at], right, line, high, low, at)
+    out[...] = weights(high, low, member, pl.ds(0, EARLY))
+
+
+def other_pair_kernel(columns, left, squares, weighted, right, line, member, high, low, out):
+    set_columns(columns, right, line, member)
+    for start in range(0, EARLY, CHUNK):
+        at = pl.ds(start, CHUNK)
+        distances(left[at], squares[at], right, line, high, low, at)
+    out[...] = weighted[...] + weights(high, low, member, pl.ds(0, EARLY))
+
+
+def late_pair_kernel(*refs):
+    rows, sides, weighted, refs = refs[:8], (refs[8:11], refs[11:14]), refs[14], refs[19:]
+    (*kept, out) = refs
     points = rows[0].shape[0] - SIDE
-    total = weighted[...] + weigh(columns, left, squares, high_out, low_out, right, line, member)
+    at = pl.ds(EARLY, CHUNK)
+    left, square = left_rows(jnp.concatenate([block[pl.ds(0, points)] for block in rows[6:]], axis=0))
+    late = 0.0
+    for half, (right, line, member) in enumerate(sides):
+        high, low = kept[2 * half : 2 * half + 2]
+        distances(left, square, right, line, high, low, at)
+        late += weights(high, low, member, at)
     cohesion = jnp.zeros((1, CLUSTER_COUNT), jnp.float32)
     for offset in range(8):
-        part = total[offset * points : (offset + 1) * points]
+        start = offset * points
+        part = weighted[pl.ds(start, points)] if start < EARLY else late[start - EARLY : start - EARLY + points]
         out[member_at(offset), pl.ds(0, points)] = part
         own = seed_member(rows[offset][pl.ds(points, 1)][:, :points])
         cohesion += jnp.sum(own * part, axis=0, keepdims=True)
@@ -203,7 +228,7 @@
 PARAMS = pltpu.CompilerParams(vmem_limit_bytes=12 << 20)
 
 
-def on_chip(kernel, name, shapes, inputs, scratch=()):
+def on_chip(kernel, name, shapes, inputs, scratch=(), aliases={}):
     vmem = pl.BlockSpec(memory_space=pltpu.VMEM)
     specs = [vmem] * len(inputs)
     shapes = [jax.ShapeDtypeStruct(*shape) for shape in shapes]
@@ -213,6 +238,7 @@
         in_specs=specs,
         out_specs=[vmem] * len(shapes),
         scratch_shapes=scratch,
+        input_output_aliases=aliases,
         compiler_params=PARAMS,
         name=name,
     )(*inputs)
@@ -246,27 +272,28 @@
         name="prepare",
     )(embedding, seed_cluster.reshape(1, points))
     columns = exchange_columns(spread)
-    columns, *rows = lax.optimization_barrier((columns, *row_peers(block)))
+    rows = row_peers(block)
+    columns, *rows[:7] = lax.optimization_barrier((columns, *rows[:7]))
     kept = ((tall, tall), jnp.bfloat16)
     exchange = ((8, lines, CLUSTER_COUNT), jnp.float32)
-    scratch = [
-        pltpu.VMEM((tall, 3 * width), jnp.bfloat16),
-        pltpu.VMEM((SIDE, tall), jnp.float32),
-        pltpu.VMEM((tall, CLUSTER_COUNT), jnp.bfloat16),
-    ]
-    left, squares, own_high, own_low, weighted = on_chip(
-        own_pair_kernel,
-        "own_pairs",
-        [((tall, 3 * width), jnp.bfloat16), ((tall, 1), jnp.float32), kept, kept, ((tall, CLUSTER_COUNT), jnp.float32)],
-        [*rows, columns],
-        scratch=scratch,
-    )
-    other_high, other_low, weighted = on_chip(
+    sides = [((tall, 3 * width), jnp.bfloat16), ((SIDE, tall), jnp.float32), ((tall, CLUSTER_COUNT), jnp.bfloat16)]
+    lefts = [((EARLY, 3 * width), jnp.bfloat16), ((EARLY, 1), jnp.float32)]
+    early = ((EARLY, CLUSTER_COUNT), jnp.float32)
+    left, squares, *own_sides, own_high, own_low, weighted = on_chip(
+        own_pair_kernel, "own_pairs", [*lefts, *sides, kept, kept, early], [*rows[:6], columns]
+    )
+    *other_sides, other_high, other_low, weighted = on_chip(
         other_pair_kernel,
         "other_pairs",
-        [kept, kept, exchange],
-        [*rows, other_core(columns), left, squares, weighted],
-        scratch=scratch,
+        [*sides, kept, kept, early],
+        [other_core(columns), left, squares, weighted],
+    )
+    own_high, own_low, other_high, other_low, weighted = on_chip(
+        late_pair_kernel,
+        "late_pairs",
+        [kept] * 4 + [exchange],
+        [*rows, *own_sides, *other_sides, weighted, own_high, own_low, other_high, other_low],
+        aliases={15: 0, 16: 1, 17: 2, 18: 3},
     )
 
     line = ((lines, CLUSTER_COUNT), jnp.float32)

time: 102 us -> 103 us (level)
  starting transfers between devices: 20.1 us -> 23.6 us
  waiting for transfers between devices: 13.5 us -> 10.9 us
  blocking collectives: 56 us -> 54.9 us
    ppermute x7, waiting for transfers between devices: 11.9 us -> 9.28 us  [moved(): return lax.ppermute(x, EVERY, pairs)]
    ppermute x2, starting transfers between devices: 3.11 us -> 4.98 us  [other_core(): return lax.ppermute(x, 'core', [(0, 1), (1, 0)])]
    ppermute x7, starting transfers between devices: 8.49 us -> 10.2 us  [moved(): return lax.ppermute(x, EVERY, pairs)]
    pallas_call x6 -> x7, Pallas kernels: 9.78 us -> 10.6 us  [on_chip(): pl.pallas_call(kernel, out_shape=shapes, in_specs=specs, out_specs=[vmem]...]
  transfers between devices with their start and end apart: 10 -> 10, of which waited for: 7 -> 4; matrix products, arithmetic and copies ran while one was open for 0% -> 0% of each run, Pallas kernels for 3% -> 5%
where the time goes in v17:
time: 103 us; the launch traced here: 102 us
  blocking collectives  54.9 us (53%)
  starting transfers between devices  23.6 us (23%)
  Pallas kernels  12.7 us (12%)
  waiting for transfers between devices  10.9 us (11%)
    all_to_all x2, blocking collectives, exchange_rows(): return lax.all_to_all(blocks, ('y_lo', 'x'), 0, 0, tiled=True)  25.8 us
    all_to_all x1, blocking collectives, exchange_columns(): lax.all_to_all(blocks, EVERY, 0, 0, axis_index_groups=COLUMN_GROUPS, tile...  15.1 us
    all_to_all x1, blocking collectives, shards(): parts = lax.all_to_all(copies(part, 128), EVERY, 0, 0, tiled=True)  14 us
    pallas_call x7, Pallas kernels, on_chip(): pl.pallas_call(kernel, out_shape=shapes, in_specs=specs, out_specs=[vmem]...  10.6 us
    ppermute x7, starting transfers between devices, moved(): return lax.ppermute(x, EVERY, pairs)  10.2 us
    ppermute x7, waiting for transfers between devices, moved(): return lax.ppermute(x, EVERY, pairs)  9.28 us
    all_to_all x1, starting transfers between devices, exchange_columns(): lax.all_to_all(blocks, EVERY, 0, 0, axis_index_groups=COLUMN_GROUPS, tile...  8.46 us
    ppermute x2, starting transfers between devices, other_core(): return lax.ppermute(x, 'core', [(0, 1), (1, 0)])  4.98 us
  transfers between devices with their start and end apart: 10, of which 4 were waited for; matrix products, arithmetic and copies ran while one was open for 0% of the time, Pallas kernels for 5%

profile of v17, /device:TPU:1, one launch (start us, length us, event | category | flops | bytes accessed | tf_op | source)
XLA Modules:
  0.0 102.2 jit_solution(11214240867640332961)
XLA Ops:
  0.0 2.1 %prepare.1 = (f32[136,256]{1,0:T(8,128)}, f32[8,136,256]{2,1,0:T(8,128)}) custom-call(f32[128,256]{1,0:T(8,128)} %embedding.1, s32[1,128]{1,0:T(1,128)} %bitcast.7), custom_call_target="tpu_custom_call" | custom-call | tf_op jit(solution)/shard_map/prepare/pallas_call | solution.py:266
  2.1 8.5 %all-to-all-start = ((f32[8,136,256]{2,1,0:T(8,128)}), f32[8,136,256]{2,1,0:T(8,128)S(1)}, u32[]{:S(2)}, u32[]{:S(2)}) async-start(f32[8,136,256]{2,1,0:T(8,128)} %get-tuple-element.40), calls=%async_computation | async-start | bytes 2228224 | tf_op jit(solution)/shard_map/all_to_all | solution.py:40
  10.6 2.5 %collective-permute-start.5 = (f32[136,256]{1,0:T(8,128)S(1)}, f32[136,256]{1,0:T(8,128)S(1)}, u32[]{:S(2)}, u32[]{:S(2)}) collective-permute-start(f32[136,256]{1,0:T(8,128)S(1)} %copy-done), channel_id=1, source_target_pairs={{2,0},{3,1},{4,2},{5,3},{6,4},{7,5},{0,6},{1,7},{10,8},{11,9},{12,... | collective-permute-start | bytes 417800 | tf_op jit(solution)/shard_map/ppermute | solution.py:47
  13.2 1.7 %collective-permute-start.3 = (f32[136,256]{1,0:T(8,128)S(1)}, f32[136,256]{1,0:T(8,128)S(1)}, u32[]{:S(2)}, u32[]{:S(2)}) collective-permute-start(f32[136,256]{1,0:T(8,128)S(1)} %copy-done), channel_id=1, source_target_pairs={{4,0},{5,1},{6,2},{7,3},{0,4},{1,5},{2,6},{3,7},{12,8},{13,9},{14,... | collective-permute-start | bytes 417800 | tf_op jit(solution)/shard_map/ppermute | solution.py:47
  14.9 0.7 collective-permute-start.2
  15.6 1.6 %collective-permute-start.1 = (f32[136,256]{1,0:T(8,128)S(1)}, f32[136,256]{1,0:T(8,128)S(1)}, u32[]{:S(2)}, u32[]{:S(2)}) collective-permute-start(f32[136,256]{1,0:T(8,128)S(1)} %copy-done), channel_id=1, source_target_pairs={{70,0},{71,1},{64,2},{65,3},{66,4},{67,5},{68,6},{69,7},{78,8},{79... | collective-permute-start | bytes 417800 | tf_op jit(solution)/shard_map/ppermute | solution.py:47
  17.2 1.8 %collective-permute-start = (f32[136,256]{1,0:T(8,128)S(1)}, f32[136,256]{1,0:T(8,128)S(1)}, u32[]{:S(2)}, u32[]{:S(2)}) collective-permute-start(f32[136,256]{1,0:T(8,128)S(1)} %copy-done), channel_id=1, source_target_pairs={{68,0},{69,1},{70,2},{71,3},{64,4},{65,5},{66,6},{67,7},{76,8},{77... | collective-permute-start | bytes 417800 | tf_op jit(solution)/shard_map/ppermute | solution.py:47
  19.1 1.4 %collective-permute-done.4.refs_5_ = f32[136,256]{1,0:T(8,128)S(1)} collective-permute-done((f32[136,256]{1,0:T(8,128)S(1)}, f32[136,256]{1,0:T(8,128)S(1)}, u32[]{:S(2)}, u32[]{:S(2)}) %collective-permute-start.4) | collective-permute-done | bytes 139296 | tf_op jit(solution)/shard_map/ppermute | solution.py:47
  20.5 2.5 %collective-permute-done.2.refs_3_ = f32[136,256]{1,0:T(8,128)S(1)} collective-permute-done((f32[136,256]{1,0:T(8,128)S(1)}, f32[136,256]{1,0:T(8,128)S(1)}, u32[]{:S(2)}, u32[]{:S(2)}) %collective-permute-start.2) | collective-permute-done | bytes 139296 | tf_op jit(solution)/shard_map/ppermute | solution.py:47
  23.0 5.3 %collective-permute-done.1.refs_2_ = f32[136,256]{1,0:T(8,128)S(1)} collective-permute-done((f32[136,256]{1,0:T(8,128)S(1)}, f32[136,256]{1,0:T(8,128)S(1)}, u32[]{:S(2)}, u32[]{:S(2)}) %collective-permute-start.1) | collective-permute-done | bytes 139296 | tf_op jit(solution)/shard_map/ppermute | solution.py:47
  28.4 1.3 %collective-permute-start.7 = (f32[8,136,256]{2,1,0:T(8,128)S(1)}, f32[8,136,256]{2,1,0:T(8,128)S(1)}, u32[]{:S(2)}, u32[]{:S(2)}) collective-permute-start(f32[8,136,256]{2,1,0:T(8,128)S(1)} %all-to-all-done.refs_6_), channel_id=1, source_target_pairs={{0,1},{1,0},{2,3},{3,2},{4,5},{5,4},{6,7},{7,6},{8,9},{9,8},{10,11... | collective-permute-start | bytes 3342344 | tf_op jit(solution)/shard_map/ppermute | solution.py:252
  29.7 1.7 %collective-permute-start.6 = (f32[136,256]{1,0:T(8,128)S(1)}, f32[136,256]{1,0:T(8,128)S(1)}, u32[]{:S(2)}, u32[]{:S(2)}) collective-permute-start(f32[136,256]{1,0:T(8,128)S(1)} %copy-done), channel_id=1, source_target_pairs={{64,0},{65,1},{66,2},{67,3},{68,4},{69,5},{70,6},{71,7},{72,8},{73... | collective-permute-start | bytes 417800 | tf_op jit(solution)/shard_map/ppermute | solution.py:47
  31.4 2.5 %own_pairs.1 = (bf16[768,768]{1,0:T(8,128)(2,1)S(1)}, f32[768,1]{1,0:T(8,128)S(1)}, bf16[1024,768]{1,0:T(8,128)(2,1)S(1)}, f32[8,1024]{1,0:T(8,128)S(1)}, bf16[1...) custom-call(f32[136,256]{1,0:T(8,128)S(1)} %copy-done, ...), custom_call_target="tpu_custom_call" | custom-call | tf_op jit(solution)/shard_map/own_pairs/pallas_call | solution.py:235
  33.9 2.5 %other_pairs.1 = (bf16[1024,768]{1,0:T(8,128)(2,1)S(1)}, f32[8,1024]{1,0:T(8,128)S(1)}, bf16[1024,128]{1,0:T(8,128)(2,1)S(1)}, bf16[1024,1024]{1,0:T(8,128)(2,1)...) custom-call(f32[8,136,256]{2,1,0:T(8,128)S(1)} %collective-permute-done.7.columns, ...), custom_call_target="tpu_custom_call" | custom-call | tf_op jit(solution)/shard_map/other_pairs/pallas_call | solution.py:235
  36.5 1.9 %late_pairs.1 = (bf16[1024,1024]{1,0:T(8,128)(2,1)S(1)}, bf16[1024,1024]{1,0:T(8,128)(2,1)S(1)}, bf16[1024,1024]{1,0:T(8,128)(2,1)S(1)}, bf16[1024,1024]{1,0:T(8,128)(2,1)S(1)}, f32[8,136,128]{2,1,0:T(8,128)S(1)}) custom-call(f32[136,256]{1,0:T(8,128)S(1)} %copy-done, ...), custom_call_target="tpu_custom_call", output_to_operand_aliasing={{0}: (15, {}), {1}: (16, {}), {2}: (17, {}), {3}: (18, {})} | custom-call | tf_op jit(solution)/shard_map/late_pairs/pallas_call | solution.py:235
  38.4 12.9 %all_to_all.25.blocks = f32[8,136,128]{2,1,0:T(8,128)S(1)} all-to-all(f32[8,136,128]{2,1,0:T(8,128)S(1)} %get-tuple-element.64), channel_id=1, replica_groups=mesh['y_lo'=2,'z'=4,'y_hi'=2,'x'=4,'core'=2] {'y_lo','x'}, dimensions={0} | all-to-all | bytes 1114112 | tf_op jit(solution)/shard_map/all_to_all | solution.py:36
  51.3 0.1 sum_spread.1
  51.4 15.1 %all_to_all.26.own = f32[8,136,128]{2,1,0:T(8,128)S(1)} all-to-all(f32[8,136,128]{2,1,0:T(8,128)S(1)} %get-tuple-element.65), channel_id=1, replica_groups={{0,16,32,48,72,88,104,120},{1,17,33,49,73,89,105,121},{2,18,34,50,74,90..., dimensions={0} | all-to-all | bytes 1114112 | tf_op jit(solution)/shard_map/all_to_all | solution.py:40
  66.4 3.7 %collective-permute-start.8 = (f32[8,136,128]{2,1,0:T(8,128)S(1)}, f32[8,136,128]{2,1,0:T(8,128)S(1)}, u32[]{:S(2)}, u32[]{:S(2)}) collective-permute-start(f32[8,136,128]{2,1,0:T(8,128)S(1)} %all_to_all.26.own), channel_id=1, source_target_pairs={{0,1},{1,0},{2,3},{3,2},{4,5},{5,4},{6,7},{7,6},{8,9},{9,8},{10,11... | collective-permute-start | bytes 1671176 | tf_op jit(solution)/shard_map/ppermute | solution.py:252
  70.1 1.6 %collective-permute-done.8.other = f32[8,136,128]{2,1,0:T(8,128)S(1)} collective-permute-done((f32[8,136,128]{2,1,0:T(8,128)S(1)}, f32[8,136,128]{2,1,0:T(8,128)S(1)}, u32[]{:S(2)}, u32[]{:S(2)}) %collective-permute-start.8) | collective-permute-done | bytes 557088 | tf_op jit(solution)/shard_map/ppermute | solution.py:252
  71.7 2.7 %members.1 = (f32[8,136,128]{2,1,0:T(8,128)S(1)}, f32[128,128]{1,0:T(8,128)S(1)}) custom-call(f32[8,136,128]{2,1,0:T(8,128)S(1)} %all_to_all.26.own, f32[8,136,128]{2,1,0:T(8,128)S(1)} %collective-permute-done.8.other, bf16[1024,1024]{1,0:T(8,128)(2,1)S(1)} %get-tuple-element.66.own_high, bf16[1024,1024]{1,0:T(8,128)(2,1)S(1)} %get-tuple-element.67.own_low, ...), custom_call_target="tpu_custom_call" | custom-call | tf_op jit(solution)/shard_map/members/pallas_call | solution.py:235
  74.4 12.9 %all_to_all.27.blocks = f32[8,136,128]{2,1,0:T(8,128)S(1)} all-to-all(f32[8,136,128]{2,1,0:T(8,128)S(1)} %get-tuple-element.71), channel_id=1, replica_groups=mesh['y_lo'=2,'z'=4,'y_hi'=2,'x'=4,'core'=2] {'y_lo','x'}, dimensions={0} | all-to-all | bytes 1114112 | tf_op jit(solution)/shard_map/all_to_all | solution.py:36
  87.4 14.0 %all_to_all.28 = f32[128,1,128]{2,1,0:T(1,128)S(1)} all-to-all(f32[128,1,128]{2,1,0:T(1,128)S(1)} %broadcast_in_dim.3), channel_id=1, replica_groups=mesh['y_lo'=2,'z'=4,'y_hi'=2,'x'=4,'core'=2] {'y_lo','z','y_hi','x','core'}, dimensions={0} | all-to-all | bytes 131072 | tf_op jit(solution)/shard_map/all_to_all | solution.py:312
  101.4 0.8 final.1
  (12 shorter events, 0.1 us)
Async XLA Ops:
  2.1 8.5 %copy-start = (f32[136,256]{1,0:T(8,128)S(1)}, f32[136,256]{1,0:T(8,128)}, u32[]{:S(2)}) copy-start(f32[136,256]{1,0:T(8,128)} %get-tuple-element.42.refs_0_) | copy-start | bytes 417796
  2.1 26.2 %all-to-all-start = ((f32[8,136,256]{2,1,0:T(8,128)}), f32[8,136,256]{2,1,0:T(8,128)S(1)}, u32[]{:S(2)}, u32[]{:S(2)}) async-start(f32[8,136,256]{2,1,0:T(8,128)} %get-tuple-element.40), calls=%async_computation | async-start | bytes 2228224 | tf_op jit(solution)/shard_map/all_to_all | solution.py:40
  10.6 6.6 %collective-permute-start.5 = (f32[136,256]{1,0:T(8,128)S(1)}, f32[136,256]{1,0:T(8,128)S(1)}, u32[]{:S(2)}, u32[]{:S(2)}) collective-permute-start(f32[136,256]{1,0:T(8,128)S(1)} %copy-done), channel_id=1, source_target_pairs={{2,0},{3,1},{4,2},{5,3},{6,4},{7,5},{0,6},{1,7},{10,8},{11,9},{12,... | collective-permute-start | bytes 417800 | tf_op jit(solution)/shard_map/ppermute | solution.py:47
  13.1 7.3 %collective-permute-start.4 = (f32[136,256]{1,0:T(8,128)S(1)}, f32[136,256]{1,0:T(8,128)S(1)}, u32[]{:S(2)}, u32[]{:S(2)}) collective-permute-start(f32[136,256]{1,0:T(8,128)S(1)} %copy-done), channel_id=1, source_target_pairs={{6,0},{7,1},{0,2},{1,3},{2,4},{3,5},{4,6},{5,7},{14,8},{15,9},{8,1... | collective-permute-start | bytes 417800 | tf_op jit(solution)/shard_map/ppermute | solution.py:47
  13.2 7.3 %collective-permute-start.3 = (f32[136,256]{1,0:T(8,128)S(1)}, f32[136,256]{1,0:T(8,128)S(1)}, u32[]{:S(2)}, u32[]{:S(2)}) collective-permute-start(f32[136,256]{1,0:T(8,128)S(1)} %copy-done), channel_id=1, source_target_pairs={{4,0},{5,1},{6,2},{7,3},{0,4},{1,5},{2,6},{3,7},{12,8},{13,9},{14,... | collective-permute-start | bytes 417800 | tf_op jit(solution)/shard_map/ppermute | solution.py:47
  14.9 8.2 %collective-permute-start.2 = (f32[136,256]{1,0:T(8,128)S(1)}, f32[136,256]{1,0:T(8,128)S(1)}, u32[]{:S(2)}, u32[]{:S(2)}) collective-permute-start(f32[136,256]{1,0:T(8,128)S(1)} %copy-done), channel_id=1, source_target_pairs={{66,0},{67,1},{68,2},{69,3},{70,4},{71,5},{64,6},{65,7},{74,8},{75... | collective-permute-start | bytes 417800 | tf_op jit(solution)/shard_map/ppermute | solution.py:47
  15.6 12.8 %collective-permute-start.1 = (f32[136,256]{1,0:T(8,128)S(1)}, f32[136,256]{1,0:T(8,128)S(1)}, u32[]{:S(2)}, u32[]{:S(2)}) collective-permute-start(f32[136,256]{1,0:T(8,128)S(1)} %copy-done), channel_id=1, source_target_pairs={{70,0},{71,1},{64,2},{65,3},{66,4},{67,5},{68,6},{69,7},{78,8},{79... | collective-permute-start | bytes 417800 | tf_op jit(solution)/shard_map/ppermute | solution.py:47
  17.2 11.1 %collective-permute-start = (f32[136,256]{1,0:T(8,128)S(1)}, f32[136,256]{1,0:T(8,128)S(1)}, u32[]{:S(2)}, u32[]{:S(2)}) collective-permute-start(f32[136,256]{1,0:T(8,128)S(1)} %copy-done), channel_id=1, source_target_pairs={{68,0},{69,1},{70,2},{71,3},{64,4},{65,5},{66,6},{67,7},{76,8},{77... | collective-permute-start | bytes 417800 | tf_op jit(solution)/shard_map/ppermute | solution.py:47
  28.4 5.5 %collective-permute-start.7 = (f32[8,136,256]{2,1,0:T(8,128)S(1)}, f32[8,136,256]{2,1,0:T(8,128)S(1)}, u32[]{:S(2)}, u32[]{:S(2)}) collective-permute-start(f32[8,136,256]{2,1,0:T(8,128)S(1)} %all-to-all-done.refs_6_), channel_id=1, source_target_pairs={{0,1},{1,0},{2,3},{3,2},{4,5},{5,4},{6,7},{7,6},{8,9},{9,8},{10,11... | collective-permute-start | bytes 3342344 | tf_op jit(solution)/shard_map/ppermute | solution.py:252
  29.7 6.7 %collective-permute-start.6 = (f32[136,256]{1,0:T(8,128)S(1)}, f32[136,256]{1,0:T(8,128)S(1)}, u32[]{:S(2)}, u32[]{:S(2)}) collective-permute-start(f32[136,256]{1,0:T(8,128)S(1)} %copy-done), channel_id=1, source_target_pairs={{64,0},{65,1},{66,2},{67,3},{68,4},{69,5},{70,6},{71,7},{72,8},{73... | collective-permute-start | bytes 417800 | tf_op jit(solution)/shard_map/ppermute | solution.py:47
  66.4 5.2 %collective-permute-start.8 = (f32[8,136,128]{2,1,0:T(8,128)S(1)}, f32[8,136,128]{2,1,0:T(8,128)S(1)}, u32[]{:S(2)}, u32[]{:S(2)}) collective-permute-start(f32[8,136,128]{2,1,0:T(8,128)S(1)} %all_to_all.26.own), channel_id=1, source_target_pairs={{0,1},{1,0},{2,3},{3,2},{4,5},{5,4},{6,7},{7,6},{8,9},{9,8},{10,11... | collective-permute-start | bytes 1671176 | tf_op jit(solution)/shard_map/ppermute | solution.py:252

commit v18 on v17

--- a/solution.py
+++ b/solution.py
@@ -273,7 +273,7 @@
     )(embedding, seed_cluster.reshape(1, points))
     columns = exchange_columns(spread)
     rows = row_peers(block)
-    columns, *rows[:7] = lax.optimization_barrier((columns, *rows[:7]))
+    columns, *rows[:6] = lax.optimization_barrier((columns, *rows[:6]))
     kept = ((tall, tall), jnp.bfloat16)
     exchange = ((8, lines, CLUSTER_COUNT), jnp.float32)
     sides = [((tall, 3 * width), jnp.bfloat16), ((SIDE, tall), jnp.float32), ((tall, CLUSTER_COUNT), jnp.bfloat16)]

time: 103 us -> 99.7 us (0.968)
  blocking collectives: 54.9 us -> 53.3 us
  waiting for transfers between devices: 10.9 us -> 9.55 us
    ppermute x7, waiting for transfers between devices: 9.28 us -> 7.96 us  [moved(): return lax.ppermute(x, EVERY, pairs)]
    ppermute x2, starting transfers between devices: 4.98 us -> 6.26 us  [other_core(): return lax.ppermute(x, 'core', [(0, 1), (1, 0)])]
where the time goes in v18:
time: 99.7 us; the launch traced here: 99.4 us
  blocking collectives  53.3 us (53%)
  starting transfers between devices  24 us (24%)
  Pallas kernels  12.4 us (12%)
  waiting for transfers between devices  9.55 us (10%)
    all_to_all x2, blocking collectives, exchange_rows(): return lax.all_to_all(blocks, ('y_lo', 'x'), 0, 0, tiled=True)  25.4 us
    all_to_all x1, blocking collectives, exchange_columns(): lax.all_to_all(blocks, EVERY, 0, 0, axis_index_groups=COLUMN_GROUPS, tile...  14.1 us
    all_to_all x1, blocking collectives, shards(): parts = lax.all_to_all(copies(part, 128), EVERY, 0, 0, tiled=True)  13.8 us
    pallas_call x7, Pallas kernels, on_chip(): pl.pallas_call(kernel, out_shape=shapes, in_specs=specs, out_specs=[vmem]...  10.3 us
    ppermute x7, starting transfers between devices, moved(): return lax.ppermute(x, EVERY, pairs)  9.29 us
    all_to_all x1, starting transfers between devices, exchange_columns(): lax.all_to_all(blocks, EVERY, 0, 0, axis_index_groups=COLUMN_GROUPS, tile...  8.46 us
    ppermute x7, waiting for transfers between devices, moved(): return lax.ppermute(x, EVERY, pairs)  7.96 us
    ppermute x2, starting transfers between devices, other_core(): return lax.ppermute(x, 'core', [(0, 1), (1, 0)])  6.26 us
  transfers between devices with their start and end apart: 10, of which 4 were waited for; matrix products, arithmetic and copies ran while one was open for 0% of the time, Pallas kernels for 5%

profile of v18, /device:TPU:1, one launch (start us, length us, event | category | flops | bytes accessed | tf_op | source)
XLA Modules:
  0.0 99.4 jit_solution(4163276416033543753)
XLA Ops:
  0.0 2.1 %prepare.1 = (f32[136,256]{1,0:T(8,128)}, f32[8,136,256]{2,1,0:T(8,128)}) custom-call(f32[128,256]{1,0:T(8,128)} %embedding.1, s32[1,128]{1,0:T(1,128)} %bitcast.7), custom_call_target="tpu_custom_call" | custom-call | tf_op jit(solution)/shard_map/prepare/pallas_call | solution.py:266
  2.1 8.5 %all-to-all-start = ((f32[8,136,256]{2,1,0:T(8,128)}), f32[8,136,256]{2,1,0:T(8,128)S(1)}, u32[]{:S(2)}, u32[]{:S(2)}) async-start(f32[8,136,256]{2,1,0:T(8,128)} %get-tuple-element.39), calls=%async_computation | async-start | bytes 2228224 | tf_op jit(solution)/shard_map/all_to_all | solution.py:40
  10.6 1.3 %collective-permute-start.4 = (f32[136,256]{1,0:T(8,128)S(1)}, f32[136,256]{1,0:T(8,128)S(1)}, u32[]{:S(2)}, u32[]{:S(2)}) collective-permute-start(f32[136,256]{1,0:T(8,128)S(1)} %copy-done), channel_id=1, source_target_pairs={{6,0},{7,1},{0,2},{1,3},{2,4},{3,5},{4,6},{5,7},{14,8},{15,9},{8,1... | collective-permute-start | bytes 417800 | tf_op jit(solution)/shard_map/ppermute | solution.py:47
  11.9 2.5 %collective-permute-start.3 = (f32[136,256]{1,0:T(8,128)S(1)}, f32[136,256]{1,0:T(8,128)S(1)}, u32[]{:S(2)}, u32[]{:S(2)}) collective-permute-start(f32[136,256]{1,0:T(8,128)S(1)} %copy-done), channel_id=1, source_target_pairs={{4,0},{5,1},{6,2},{7,3},{0,4},{1,5},{2,6},{3,7},{12,8},{13,9},{14,... | collective-permute-start | bytes 417800 | tf_op jit(solution)/shard_map/ppermute | solution.py:47
  14.3 0.9 collective-permute-start.2
  15.3 1.4 %collective-permute-start.1 = (f32[136,256]{1,0:T(8,128)S(1)}, f32[136,256]{1,0:T(8,128)S(1)}, u32[]{:S(2)}, u32[]{:S(2)}) collective-permute-start(f32[136,256]{1,0:T(8,128)S(1)} %copy-done), channel_id=1, source_target_pairs={{70,0},{71,1},{64,2},{65,3},{66,4},{67,5},{68,6},{69,7},{78,8},{79... | collective-permute-start | bytes 417800 | tf_op jit(solution)/shard_map/ppermute | solution.py:47
  16.7 0.9 collective-permute-start
  17.6 2.5 %collective-permute-done.3.refs_4_ = f32[136,256]{1,0:T(8,128)S(1)} collective-permute-done((f32[136,256]{1,0:T(8,128)S(1)}, f32[136,256]{1,0:T(8,128)S(1)}, u32[]{:S(2)}, u32[]{:S(2)}) %collective-permute-start.3) | collective-permute-done | bytes 139296 | tf_op jit(solution)/shard_map/ppermute | solution.py:47
  20.1 3.9 %collective-permute-done.1.refs_2_ = f32[136,256]{1,0:T(8,128)S(1)} collective-permute-done((f32[136,256]{1,0:T(8,128)S(1)}, f32[136,256]{1,0:T(8,128)S(1)}, u32[]{:S(2)}, u32[]{:S(2)}) %collective-permute-start.1) | collective-permute-done | bytes 139296 | tf_op jit(solution)/shard_map/ppermute | solution.py:47
  24.0 1.6 %collective-permute-done.refs_1_ = f32[136,256]{1,0:T(8,128)S(1)} collective-permute-done((f32[136,256]{1,0:T(8,128)S(1)}, f32[136,256]{1,0:T(8,128)S(1)}, u32[]{:S(2)}, u32[]{:S(2)}) %collective-permute-start) | collective-permute-done | bytes 139296 | tf_op jit(solution)/shard_map/ppermute | solution.py:47
  25.5 2.4 %collective-permute-start.7 = (f32[8,136,256]{2,1,0:T(8,128)S(1)}, f32[8,136,256]{2,1,0:T(8,128)S(1)}, u32[]{:S(2)}, u32[]{:S(2)}) collective-permute-start(f32[8,136,256]{2,1,0:T(8,128)S(1)} %all-to-all-done.refs_6_), channel_id=1, source_target_pairs={{0,1},{1,0},{2,3},{3,2},{4,5},{5,4},{6,7},{7,6},{8,9},{9,8},{10,11... | collective-permute-start | bytes 3342344 | tf_op jit(solution)/shard_map/ppermute | solution.py:252
  28.0 1.3 %collective-permute-start.6 = (f32[136,256]{1,0:T(8,128)S(1)}, f32[136,256]{1,0:T(8,128)S(1)}, u32[]{:S(2)}, u32[]{:S(2)}) collective-permute-start(f32[136,256]{1,0:T(8,128)S(1)} %copy-done), channel_id=1, source_target_pairs={{64,0},{65,1},{66,2},{67,3},{68,4},{69,5},{70,6},{71,7},{72,8},{73... | collective-permute-start | bytes 417800 | tf_op jit(solution)/shard_map/ppermute | solution.py:47
  29.2 1.1 %collective-permute-start.5 = (f32[136,256]{1,0:T(8,128)S(1)}, f32[136,256]{1,0:T(8,128)S(1)}, u32[]{:S(2)}, u32[]{:S(2)}) collective-permute-start(f32[136,256]{1,0:T(8,128)S(1)} %copy-done), channel_id=1, source_target_pairs={{2,0},{3,1},{4,2},{5,3},{6,4},{7,5},{0,6},{1,7},{10,8},{11,9},{12,... | collective-permute-start | bytes 417800 | tf_op jit(solution)/shard_map/ppermute | solution.py:47
  30.3 2.5 %own_pairs.1 = (bf16[768,768]{1,0:T(8,128)(2,1)S(1)}, f32[768,1]{1,0:T(8,128)S(1)}, bf16[1024,768]{1,0:T(8,128)(2,1)S(1)}, f32[8,1024]{1,0:T(8,128)S(1)}, bf16[1...) custom-call(f32[136,256]{1,0:T(8,128)S(1)} %copy-done, ...), custom_call_target="tpu_custom_call" | custom-call | tf_op jit(solution)/shard_map/own_pairs/pallas_call | solution.py:235
  32.8 2.4 %other_pairs.1 = (bf16[1024,768]{1,0:T(8,128)(2,1)S(1)}, f32[8,1024]{1,0:T(8,128)S(1)}, bf16[1024,128]{1,0:T(8,128)(2,1)S(1)}, bf16[1024,1024]{1,0:T(8,128)(2,1)...) custom-call(f32[8,136,256]{2,1,0:T(8,128)S(1)} %collective-permute-done.7.columns, ...), custom_call_target="tpu_custom_call" | custom-call | tf_op jit(solution)/shard_map/other_pairs/pallas_call | solution.py:235
  35.2 1.9 %late_pairs.1 = (bf16[1024,1024]{1,0:T(8,128)(2,1)S(1)}, bf16[1024,1024]{1,0:T(8,128)(2,1)S(1)}, bf16[1024,1024]{1,0:T(8,128)(2,1)S(1)}, bf16[1024,1024]{1,0:T(8,128)(2,1)S(1)}, f32[8,136,128]{2,1,0:T(8,128)S(1)}) custom-call(f32[136,256]{1,0:T(8,128)S(1)} %copy-done, ...), custom_call_target="tpu_custom_call", output_to_operand_aliasing={{0}: (15, {}), {1}: (16, {}), {2}: (17, {}), {3}: (18, {})} | custom-call | tf_op jit(solution)/shard_map/late_pairs/pallas_call | solution.py:235
  37.0 12.5 %all_to_all.25.blocks = f32[8,136,128]{2,1,0:T(8,128)S(1)} all-to-all(f32[8,136,128]{2,1,0:T(8,128)S(1)} %get-tuple-element.62), channel_id=1, replica_groups=mesh['y_lo'=2,'z'=4,'y_hi'=2,'x'=4,'core'=2] {'y_lo','x'}, dimensions={0} | all-to-all | bytes 1114112 | tf_op jit(solution)/shard_map/all_to_all | solution.py:36
  49.6 14.1 %all_to_all.26.own = f32[8,136,128]{2,1,0:T(8,128)S(1)} all-to-all(f32[8,136,128]{2,1,0:T(8,128)S(1)} %get-tuple-element.63), channel_id=1, replica_groups={{0,16,32,48,72,88,104,120},{1,17,33,49,73,89,105,121},{2,18,34,50,74,90..., dimensions={0} | all-to-all | bytes 1114112 | tf_op jit(solution)/shard_map/all_to_all | solution.py:40
  63.7 3.8 %collective-permute-start.8 = (f32[8,136,128]{2,1,0:T(8,128)S(1)}, f32[8,136,128]{2,1,0:T(8,128)S(1)}, u32[]{:S(2)}, u32[]{:S(2)}) collective-permute-start(f32[8,136,128]{2,1,0:T(8,128)S(1)} %all_to_all.26.own), channel_id=1, source_target_pairs={{0,1},{1,0},{2,3},{3,2},{4,5},{5,4},{6,7},{7,6},{8,9},{9,8},{10,11... | collective-permute-start | bytes 1671176 | tf_op jit(solution)/shard_map/ppermute | solution.py:252
  67.5 1.6 %collective-permute-done.8.other = f32[8,136,128]{2,1,0:T(8,128)S(1)} collective-permute-done((f32[8,136,128]{2,1,0:T(8,128)S(1)}, f32[8,136,128]{2,1,0:T(8,128)S(1)}, u32[]{:S(2)}, u32[]{:S(2)}) %collective-permute-start.8) | collective-permute-done | bytes 557088 | tf_op jit(solution)/shard_map/ppermute | solution.py:252
  69.1 2.7 %members.1 = (f32[8,136,128]{2,1,0:T(8,128)S(1)}, f32[128,128]{1,0:T(8,128)S(1)}) custom-call(f32[8,136,128]{2,1,0:T(8,128)S(1)} %all_to_all.26.own, f32[8,136,128]{2,1,0:T(8,128)S(1)} %collective-permute-done.8.other, bf16[1024,1024]{1,0:T(8,128)(2,1)S(1)} %get-tuple-element.64.own_high, bf16[1024,1024]{1,0:T(8,128)(2,1)S(1)} %get-tuple-element.65.own_low, ...), custom_call_target="tpu_custom_call" | custom-call | tf_op jit(solution)/shard_map/members/pallas_call | solution.py:235
  71.8 12.9 %all_to_all.27.blocks = f32[8,136,128]{2,1,0:T(8,128)S(1)} all-to-all(f32[8,136,128]{2,1,0:T(8,128)S(1)} %get-tuple-element.69), channel_id=1, replica_groups=mesh['y_lo'=2,'z'=4,'y_hi'=2,'x'=4,'core'=2] {'y_lo','x'}, dimensions={0} | all-to-all | bytes 1114112 | tf_op jit(solution)/shard_map/all_to_all | solution.py:36
  84.8 13.8 %all_to_all.28 = f32[128,1,128]{2,1,0:T(1,128)S(1)} all-to-all(f32[128,1,128]{2,1,0:T(1,128)S(1)} %broadcast_in_dim.3), channel_id=1, replica_groups=mesh['y_lo'=2,'z'=4,'y_hi'=2,'x'=4,'core'=2] {'y_lo','z','y_hi','x','core'}, dimensions={0} | all-to-all | bytes 131072 | tf_op jit(solution)/shard_map/all_to_all | solution.py:312
  98.6 0.8 final.1
  (12 shorter events, 0.2 us)
Async XLA Ops:
  2.1 8.5 %copy-start = (f32[136,256]{1,0:T(8,128)S(1)}, f32[136,256]{1,0:T(8,128)}, u32[]{:S(2)}) copy-start(f32[136,256]{1,0:T(8,128)} %get-tuple-element.41.refs_0_) | copy-start | bytes 417796
  2.1 23.4 %all-to-all-start = ((f32[8,136,256]{2,1,0:T(8,128)}), f32[8,136,256]{2,1,0:T(8,128)S(1)}, u32[]{:S(2)}, u32[]{:S(2)}) async-start(f32[8,136,256]{2,1,0:T(8,128)} %get-tuple-element.39), calls=%async_computation | async-start | bytes 2228224 | tf_op jit(solution)/shard_map/all_to_all | solution.py:40
  10.6 7.0 %collective-permute-start.4 = (f32[136,256]{1,0:T(8,128)S(1)}, f32[136,256]{1,0:T(8,128)S(1)}, u32[]{:S(2)}, u32[]{:S(2)}) collective-permute-start(f32[136,256]{1,0:T(8,128)S(1)} %copy-done), channel_id=1, source_target_pairs={{6,0},{7,1},{0,2},{1,3},{2,4},{3,5},{4,6},{5,7},{14,8},{15,9},{8,1... | collective-permute-start | bytes 417800 | tf_op jit(solution)/shard_map/ppermute | solution.py:47
  11.9 8.2 %collective-permute-start.3 = (f32[136,256]{1,0:T(8,128)S(1)}, f32[136,256]{1,0:T(8,128)S(1)}, u32[]{:S(2)}, u32[]{:S(2)}) collective-permute-start(f32[136,256]{1,0:T(8,128)S(1)} %copy-done), channel_id=1, source_target_pairs={{4,0},{5,1},{6,2},{7,3},{0,4},{1,5},{2,6},{3,7},{12,8},{13,9},{14,... | collective-permute-start | bytes 417800 | tf_op jit(solution)/shard_map/ppermute | solution.py:47
  14.3 5.7 %collective-permute-start.2 = (f32[136,256]{1,0:T(8,128)S(1)}, f32[136,256]{1,0:T(8,128)S(1)}, u32[]{:S(2)}, u32[]{:S(2)}) collective-permute-start(f32[136,256]{1,0:T(8,128)S(1)} %copy-done), channel_id=1, source_target_pairs={{66,0},{67,1},{68,2},{69,3},{70,4},{71,5},{64,6},{65,7},{74,8},{75... | collective-permute-start | bytes 417800 | tf_op jit(solution)/shard_map/ppermute | solution.py:47
  15.3 8.7 %collective-permute-start.1 = (f32[136,256]{1,0:T(8,128)S(1)}, f32[136,256]{1,0:T(8,128)S(1)}, u32[]{:S(2)}, u32[]{:S(2)}) collective-permute-start(f32[136,256]{1,0:T(8,128)S(1)} %copy-done), channel_id=1, source_target_pairs={{70,0},{71,1},{64,2},{65,3},{66,4},{67,5},{68,6},{69,7},{78,8},{79... | collective-permute-start | bytes 417800 | tf_op jit(solution)/shard_map/ppermute | solution.py:47
  16.7 8.8 %collective-permute-start = (f32[136,256]{1,0:T(8,128)S(1)}, f32[136,256]{1,0:T(8,128)S(1)}, u32[]{:S(2)}, u32[]{:S(2)}) collective-permute-start(f32[136,256]{1,0:T(8,128)S(1)} %copy-done), channel_id=1, source_target_pairs={{68,0},{69,1},{70,2},{71,3},{64,4},{65,5},{66,6},{67,7},{76,8},{77... | collective-permute-start | bytes 417800 | tf_op jit(solution)/shard_map/ppermute | solution.py:47
  25.5 7.2 %collective-permute-start.7 = (f32[8,136,256]{2,1,0:T(8,128)S(1)}, f32[8,136,256]{2,1,0:T(8,128)S(1)}, u32[]{:S(2)}, u32[]{:S(2)}) collective-permute-start(f32[8,136,256]{2,1,0:T(8,128)S(1)} %all-to-all-done.refs_6_), channel_id=1, source_target_pairs={{0,1},{1,0},{2,3},{3,2},{4,5},{5,4},{6,7},{7,6},{8,9},{9,8},{10,11... | collective-permute-start | bytes 3342344 | tf_op jit(solution)/shard_map/ppermute | solution.py:252
  28.0 7.2 %collective-permute-start.6 = (f32[136,256]{1,0:T(8,128)S(1)}, f32[136,256]{1,0:T(8,128)S(1)}, u32[]{:S(2)}, u32[]{:S(2)}) collective-permute-start(f32[136,256]{1,0:T(8,128)S(1)} %copy-done), channel_id=1, source_target_pairs={{64,0},{65,1},{66,2},{67,3},{68,4},{69,5},{70,6},{71,7},{72,8},{73... | collective-permute-start | bytes 417800 | tf_op jit(solution)/shard_map/ppermute | solution.py:47
  29.2 5.9 %collective-permute-start.5 = (f32[136,256]{1,0:T(8,128)S(1)}, f32[136,256]{1,0:T(8,128)S(1)}, u32[]{:S(2)}, u32[]{:S(2)}) collective-permute-start(f32[136,256]{1,0:T(8,128)S(1)} %copy-done), channel_id=1, source_target_pairs={{2,0},{3,1},{4,2},{5,3},{6,4},{7,5},{0,6},{1,7},{10,8},{11,9},{12,... | collective-permute-start | bytes 417800 | tf_op jit(solution)/shard_map/ppermute | solution.py:47
  63.7 5.4 %collective-permute-start.8 = (f32[8,136,128]{2,1,0:T(8,128)S(1)}, f32[8,136,128]{2,1,0:T(8,128)S(1)}, u32[]{:S(2)}, u32[]{:S(2)}) collective-permute-start(f32[8,136,128]{2,1,0:T(8,128)S(1)} %all_to_all.26.own), channel_id=1, source_target_pairs={{0,1},{1,0},{2,3},{3,2},{4,5},{5,4},{6,7},{7,6},{8,9},{9,8},{10,11... | collective-permute-start | bytes 1671176 | tf_op jit(solution)/shard_map/ppermute | solution.py:252

commit v19 on v18

--- a/solution.py
+++ b/solution.py
@@ -29,7 +29,7 @@
 
 
 COLUMN_GROUPS = column_groups()
-ROW_ORDER = ((0, 0), (1, 2), (1, 3), (1, 1), (0, 2), (0, 3), (0, 1), (1, 0))
+ROW_ORDER = ((0, 0), (0, 3), (0, 2), (1, 1), (1, 3), (1, 2), (0, 1), (1, 0))
 
 
 def exchange_rows(blocks):

time: 99.7 us -> 101 us (1.013)
  starting transfers between devices: 24 us -> 22.5 us
  blocking collectives: 53.3 us -> 54.5 us
  waiting for transfers between devices: 9.55 us -> 10.6 us
    ppermute x2, starting transfers between devices: 6.26 us -> 4.67 us  [other_core(): return lax.ppermute(x, 'core', [(0, 1), (1, 0)])]
    ppermute x7, waiting for transfers between devices: 7.96 us -> 9.05 us  [moved(): return lax.ppermute(x, EVERY, pairs)]
where the time goes in v19:
time: 101 us; the launch traced here: 100 us
  blocking collectives  54.5 us (54%)
  starting transfers between devices  22.5 us (22%)
  Pallas kernels  12.4 us (12%)
  waiting for transfers between devices  10.6 us (10%)
    all_to_all x2, blocking collectives, exchange_rows(): return lax.all_to_all(blocks, ('y_lo', 'x'), 0, 0, tiled=True)  25.5 us
    all_to_all x1, blocking collectives, exchange_columns(): lax.all_to_all(blocks, EVERY, 0, 0, axis_index_groups=COLUMN_GROUPS, tile...  15.1 us
    all_to_all x1, blocking collectives, shards(): parts = lax.all_to_all(copies(part, 128), EVERY, 0, 0, tiled=True)  14 us
    pallas_call x7, Pallas kernels, on_chip(): pl.pallas_call(kernel, out_shape=shapes, in_specs=specs, out_specs=[vmem]...  10.3 us
    ppermute x7, starting transfers between devices, moved(): return lax.ppermute(x, EVERY, pairs)  9.35 us
    ppermute x7, waiting for transfers between devices, moved(): return lax.ppermute(x, EVERY, pairs)  9.05 us
    all_to_all x1, starting transfers between devices, exchange_columns(): lax.all_to_all(blocks, EVERY, 0, 0, axis_index_groups=COLUMN_GROUPS, tile...  8.46 us
    ppermute x2, starting transfers between devices, other_core(): return lax.ppermute(x, 'core', [(0, 1), (1, 0)])  4.67 us
  transfers between devices with their start and end apart: 10, of which 4 were waited for; matrix products, arithmetic and copies ran while one was open for 0% of the time, Pallas kernels for 5%

profile of v19, /device:TPU:1, one launch (start us, length us, event | category | flops | bytes accessed | tf_op | source)
XLA Modules:
  0.0 100.2 jit_solution(8352662422769593268)
XLA Ops:
  0.0 2.1 %prepare.1 = (f32[136,256]{1,0:T(8,128)}, f32[8,136,256]{2,1,0:T(8,128)}) custom-call(f32[128,256]{1,0:T(8,128)} %embedding.1, s32[1,128]{1,0:T(1,128)} %bitcast.7), custom_call_target="tpu_custom_call" | custom-call | tf_op jit(solution)/shard_map/prepare/pallas_call | solution.py:266
  2.1 8.5 %all-to-all-start = ((f32[8,136,256]{2,1,0:T(8,128)}), f32[8,136,256]{2,1,0:T(8,128)S(1)}, u32[]{:S(2)}, u32[]{:S(2)}) async-start(f32[8,136,256]{2,1,0:T(8,128)} %get-tuple-element.39), calls=%async_computation | async-start | bytes 2228224 | tf_op jit(solution)/shard_map/all_to_all | solution.py:40
  10.6 2.6 %collective-permute-start.4 = (f32[136,256]{1,0:T(8,128)S(1)}, f32[136,256]{1,0:T(8,128)S(1)}, u32[]{:S(2)}, u32[]{:S(2)}) collective-permute-start(f32[136,256]{1,0:T(8,128)S(1)} %copy-done), channel_id=1, source_target_pairs={{68,0},{69,1},{70,2},{71,3},{64,4},{65,5},{66,6},{67,7},{76,8},{77... | collective-permute-start | bytes 417800 | tf_op jit(solution)/shard_map/ppermute | solution.py:47
  13.2 1.4 %collective-permute-start.3 = (f32[136,256]{1,0:T(8,128)S(1)}, f32[136,256]{1,0:T(8,128)S(1)}, u32[]{:S(2)}, u32[]{:S(2)}) collective-permute-start(f32[136,256]{1,0:T(8,128)S(1)} %copy-done), channel_id=1, source_target_pairs={{70,0},{71,1},{64,2},{65,3},{66,4},{67,5},{68,6},{69,7},{78,8},{79... | collective-permute-start | bytes 417800 | tf_op jit(solution)/shard_map/ppermute | solution.py:47
  14.6 2.1 %collective-permute-start.2 = (f32[136,256]{1,0:T(8,128)S(1)}, f32[136,256]{1,0:T(8,128)S(1)}, u32[]{:S(2)}, u32[]{:S(2)}) collective-permute-start(f32[136,256]{1,0:T(8,128)S(1)} %copy-done), channel_id=1, source_target_pairs={{66,0},{67,1},{68,2},{69,3},{70,4},{71,5},{64,6},{65,7},{74,8},{75... | collective-permute-start | bytes 417800 | tf_op jit(solution)/shard_map/ppermute | solution.py:47
  16.8 0.8 collective-permute-start
  17.6 4.9 %collective-permute-done.3.refs_4_ = f32[136,256]{1,0:T(8,128)S(1)} collective-permute-done((f32[136,256]{1,0:T(8,128)S(1)}, f32[136,256]{1,0:T(8,128)S(1)}, u32[]{:S(2)}, u32[]{:S(2)}) %collective-permute-start.3) | collective-permute-done | bytes 139296 | tf_op jit(solution)/shard_map/ppermute | solution.py:47
  22.4 1.0 %collective-permute-done.1.refs_2_ = f32[136,256]{1,0:T(8,128)S(1)} collective-permute-done((f32[136,256]{1,0:T(8,128)S(1)}, f32[136,256]{1,0:T(8,128)S(1)}, u32[]{:S(2)}, u32[]{:S(2)}) %collective-permute-start.1) | collective-permute-done | bytes 139296 | tf_op jit(solution)/shard_map/ppermute | solution.py:47
  23.5 3.1 %collective-permute-done.refs_1_ = f32[136,256]{1,0:T(8,128)S(1)} collective-permute-done((f32[136,256]{1,0:T(8,128)S(1)}, f32[136,256]{1,0:T(8,128)S(1)}, u32[]{:S(2)}, u32[]{:S(2)}) %collective-permute-start) | collective-permute-done | bytes 139296 | tf_op jit(solution)/shard_map/ppermute | solution.py:47
  26.6 1.2 %collective-permute-start.7 = (f32[8,136,256]{2,1,0:T(8,128)S(1)}, f32[8,136,256]{2,1,0:T(8,128)S(1)}, u32[]{:S(2)}, u32[]{:S(2)}) collective-permute-start(f32[8,136,256]{2,1,0:T(8,128)S(1)} %all-to-all-done.refs_6_), channel_id=1, source_target_pairs={{0,1},{1,0},{2,3},{3,2},{4,5},{5,4},{6,7},{7,6},{8,9},{9,8},{10,11... | collective-permute-start | bytes 3342344 | tf_op jit(solution)/shard_map/ppermute | solution.py:252
  27.8 1.4 %collective-permute-start.6 = (f32[136,256]{1,0:T(8,128)S(1)}, f32[136,256]{1,0:T(8,128)S(1)}, u32[]{:S(2)}, u32[]{:S(2)}) collective-permute-start(f32[136,256]{1,0:T(8,128)S(1)} %copy-done), channel_id=1, source_target_pairs={{64,0},{65,1},{66,2},{67,3},{68,4},{69,5},{70,6},{71,7},{72,8},{73... | collective-permute-start | bytes 417800 | tf_op jit(solution)/shard_map/ppermute | solution.py:47
  29.2 1.0 collective-permute-start.5
  30.2 2.5 %own_pairs.1 = (bf16[768,768]{1,0:T(8,128)(2,1)S(1)}, f32[768,1]{1,0:T(8,128)S(1)}, bf16[1024,768]{1,0:T(8,128)(2,1)S(1)}, f32[8,1024]{1,0:T(8,128)S(1)}, bf16[1...) custom-call(f32[136,256]{1,0:T(8,128)S(1)} %copy-done, ...), custom_call_target="tpu_custom_call" | custom-call | tf_op jit(solution)/shard_map/own_pairs/pallas_call | solution.py:235
  32.6 2.4 %other_pairs.1 = (bf16[1024,768]{1,0:T(8,128)(2,1)S(1)}, f32[8,1024]{1,0:T(8,128)S(1)}, bf16[1024,128]{1,0:T(8,128)(2,1)S(1)}, bf16[1024,1024]{1,0:T(8,128)(2,1)...) custom-call(f32[8,136,256]{2,1,0:T(8,128)S(1)} %collective-permute-done.7.columns, ...), custom_call_target="tpu_custom_call" | custom-call | tf_op jit(solution)/shard_map/other_pairs/pallas_call | solution.py:235
  35.0 1.9 %late_pairs.1 = (bf16[1024,1024]{1,0:T(8,128)(2,1)S(1)}, bf16[1024,1024]{1,0:T(8,128)(2,1)S(1)}, bf16[1024,1024]{1,0:T(8,128)(2,1)S(1)}, bf16[1024,1024]{1,0:T(8,128)(2,1)S(1)}, f32[8,136,128]{2,1,0:T(8,128)S(1)}) custom-call(f32[136,256]{1,0:T(8,128)S(1)} %copy-done, ...), custom_call_target="tpu_custom_call", output_to_operand_aliasing={{0}: (15, {}), {1}: (16, {}), {2}: (17, {}), {3}: (18, {})} | custom-call | tf_op jit(solution)/shard_map/late_pairs/pallas_call | solution.py:235
  36.9 12.6 %all_to_all.25.blocks = f32[8,136,128]{2,1,0:T(8,128)S(1)} all-to-all(f32[8,136,128]{2,1,0:T(8,128)S(1)} %get-tuple-element.62), channel_id=1, replica_groups=mesh['y_lo'=2,'z'=4,'y_hi'=2,'x'=4,'core'=2] {'y_lo','x'}, dimensions={0} | all-to-all | bytes 1114112 | tf_op jit(solution)/shard_map/all_to_all | solution.py:36
  49.5 0.1 sum_spread.1
  49.6 15.1 %all_to_all.26.own = f32[8,136,128]{2,1,0:T(8,128)S(1)} all-to-all(f32[8,136,128]{2,1,0:T(8,128)S(1)} %get-tuple-element.63), channel_id=1, replica_groups={{0,16,32,48,72,88,104,120},{1,17,33,49,73,89,105,121},{2,18,34,50,74,90..., dimensions={0} | all-to-all | bytes 1114112 | tf_op jit(solution)/shard_map/all_to_all | solution.py:40
  64.6 3.5 %collective-permute-start.8 = (f32[8,136,128]{2,1,0:T(8,128)S(1)}, f32[8,136,128]{2,1,0:T(8,128)S(1)}, u32[]{:S(2)}, u32[]{:S(2)}) collective-permute-start(f32[8,136,128]{2,1,0:T(8,128)S(1)} %all_to_all.26.own), channel_id=1, source_target_pairs={{0,1},{1,0},{2,3},{3,2},{4,5},{5,4},{6,7},{7,6},{8,9},{9,8},{10,11... | collective-permute-start | bytes 1671176 | tf_op jit(solution)/shard_map/ppermute | solution.py:252
  68.1 1.6 %collective-permute-done.8.other = f32[8,136,128]{2,1,0:T(8,128)S(1)} collective-permute-done((f32[8,136,128]{2,1,0:T(8,128)S(1)}, f32[8,136,128]{2,1,0:T(8,128)S(1)}, u32[]{:S(2)}, u32[]{:S(2)}) %collective-permute-start.8) | collective-permute-done | bytes 557088 | tf_op jit(solution)/shard_map/ppermute | solution.py:252
  69.7 2.7 %members.1 = (f32[8,136,128]{2,1,0:T(8,128)S(1)}, f32[128,128]{1,0:T(8,128)S(1)}) custom-call(f32[8,136,128]{2,1,0:T(8,128)S(1)} %all_to_all.26.own, f32[8,136,128]{2,1,0:T(8,128)S(1)} %collective-permute-done.8.other, bf16[1024,1024]{1,0:T(8,128)(2,1)S(1)} %get-tuple-element.64.own_high, bf16[1024,1024]{1,0:T(8,128)(2,1)S(1)} %get-tuple-element.65.own_low, ...), custom_call_target="tpu_custom_call" | custom-call | tf_op jit(solution)/shard_map/members/pallas_call | solution.py:235
  72.4 12.9 %all_to_all.27.blocks = f32[8,136,128]{2,1,0:T(8,128)S(1)} all-to-all(f32[8,136,128]{2,1,0:T(8,128)S(1)} %get-tuple-element.69), channel_id=1, replica_groups=mesh['y_lo'=2,'z'=4,'y_hi'=2,'x'=4,'core'=2] {'y_lo','x'}, dimensions={0} | all-to-all | bytes 1114112 | tf_op jit(solution)/shard_map/all_to_all | solution.py:36
  85.4 14.0 %all_to_all.28 = f32[128,1,128]{2,1,0:T(1,128)S(1)} all-to-all(f32[128,1,128]{2,1,0:T(1,128)S(1)} %broadcast_in_dim.3), channel_id=1, replica_groups=mesh['y_lo'=2,'z'=4,'y_hi'=2,'x'=4,'core'=2] {'y_lo','z','y_hi','x','core'}, dimensions={0} | all-to-all | bytes 131072 | tf_op jit(solution)/shard_map/all_to_all | solution.py:312
  99.4 0.8 final.1
  (12 shorter events, 0.1 us)
Async XLA Ops:
  2.1 8.5 %copy-start = (f32[136,256]{1,0:T(8,128)S(1)}, f32[136,256]{1,0:T(8,128)}, u32[]{:S(2)}) copy-start(f32[136,256]{1,0:T(8,128)} %get-tuple-element.41.refs_0_) | copy-start | bytes 417796
  2.1 24.5 %all-to-all-start = ((f32[8,136,256]{2,1,0:T(8,128)}), f32[8,136,256]{2,1,0:T(8,128)S(1)}, u32[]{:S(2)}, u32[]{:S(2)}) async-start(f32[8,136,256]{2,1,0:T(8,128)} %get-tuple-element.39), calls=%async_computation | async-start | bytes 2228224 | tf_op jit(solution)/shard_map/all_to_all | solution.py:40
  10.6 7.0 %collective-permute-start.4 = (f32[136,256]{1,0:T(8,128)S(1)}, f32[136,256]{1,0:T(8,128)S(1)}, u32[]{:S(2)}, u32[]{:S(2)}) collective-permute-start(f32[136,256]{1,0:T(8,128)S(1)} %copy-done), channel_id=1, source_target_pairs={{68,0},{69,1},{70,2},{71,3},{64,4},{65,5},{66,6},{67,7},{76,8},{77... | collective-permute-start | bytes 417800 | tf_op jit(solution)/shard_map/ppermute | solution.py:47
  13.2 9.2 %collective-permute-start.3 = (f32[136,256]{1,0:T(8,128)S(1)}, f32[136,256]{1,0:T(8,128)S(1)}, u32[]{:S(2)}, u32[]{:S(2)}) collective-permute-start(f32[136,256]{1,0:T(8,128)S(1)} %copy-done), channel_id=1, source_target_pairs={{70,0},{71,1},{64,2},{65,3},{66,4},{67,5},{68,6},{69,7},{78,8},{79... | collective-permute-start | bytes 417800 | tf_op jit(solution)/shard_map/ppermute | solution.py:47
  14.6 7.8 %collective-permute-start.2 = (f32[136,256]{1,0:T(8,128)S(1)}, f32[136,256]{1,0:T(8,128)S(1)}, u32[]{:S(2)}, u32[]{:S(2)}) collective-permute-start(f32[136,256]{1,0:T(8,128)S(1)} %copy-done), channel_id=1, source_target_pairs={{66,0},{67,1},{68,2},{69,3},{70,4},{71,5},{64,6},{65,7},{74,8},{75... | collective-permute-start | bytes 417800 | tf_op jit(solution)/shard_map/ppermute | solution.py:47
  16.8 6.7 %collective-permute-start.1 = (f32[136,256]{1,0:T(8,128)S(1)}, f32[136,256]{1,0:T(8,128)S(1)}, u32[]{:S(2)}, u32[]{:S(2)}) collective-permute-start(f32[136,256]{1,0:T(8,128)S(1)} %copy-done), channel_id=1, source_target_pairs={{4,0},{5,1},{6,2},{7,3},{0,4},{1,5},{2,6},{3,7},{12,8},{13,9},{14,... | collective-permute-start | bytes 417800 | tf_op jit(solution)/shard_map/ppermute | solution.py:47
  16.8 9.8 %collective-permute-start = (f32[136,256]{1,0:T(8,128)S(1)}, f32[136,256]{1,0:T(8,128)S(1)}, u32[]{:S(2)}, u32[]{:S(2)}) collective-permute-start(f32[136,256]{1,0:T(8,128)S(1)} %copy-done), channel_id=1, source_target_pairs={{6,0},{7,1},{0,2},{1,3},{2,4},{3,5},{4,6},{5,7},{14,8},{15,9},{8,1... | collective-permute-start | bytes 417800 | tf_op jit(solution)/shard_map/ppermute | solution.py:47
  26.6 6.0 %collective-permute-start.7 = (f32[8,136,256]{2,1,0:T(8,128)S(1)}, f32[8,136,256]{2,1,0:T(8,128)S(1)}, u32[]{:S(2)}, u32[]{:S(2)}) collective-permute-start(f32[8,136,256]{2,1,0:T(8,128)S(1)} %all-to-all-done.refs_6_), channel_id=1, source_target_pairs={{0,1},{1,0},{2,3},{3,2},{4,5},{5,4},{6,7},{7,6},{8,9},{9,8},{10,11... | collective-permute-start | bytes 3342344 | tf_op jit(solution)/shard_map/ppermute | solution.py:252
  27.8 7.2 %collective-permute-start.6 = (f32[136,256]{1,0:T(8,128)S(1)}, f32[136,256]{1,0:T(8,128)S(1)}, u32[]{:S(2)}, u32[]{:S(2)}) collective-permute-start(f32[136,256]{1,0:T(8,128)S(1)} %copy-done), channel_id=1, source_target_pairs={{64,0},{65,1},{66,2},{67,3},{68,4},{69,5},{70,6},{71,7},{72,8},{73... | collective-permute-start | bytes 417800 | tf_op jit(solution)/shard_map/ppermute | solution.py:47
  29.2 5.8 %collective-permute-start.5 = (f32[136,256]{1,0:T(8,128)S(1)}, f32[136,256]{1,0:T(8,128)S(1)}, u32[]{:S(2)}, u32[]{:S(2)}) collective-permute-start(f32[136,256]{1,0:T(8,128)S(1)} %copy-done), channel_id=1, source_target_pairs={{2,0},{3,1},{4,2},{5,3},{6,4},{7,5},{0,6},{1,7},{10,8},{11,9},{12,... | collective-permute-start | bytes 417800 | tf_op jit(solution)/shard_map/ppermute | solution.py:47
  64.6 5.1 %collective-permute-start.8 = (f32[8,136,128]{2,1,0:T(8,128)S(1)}, f32[8,136,128]{2,1,0:T(8,128)S(1)}, u32[]{:S(2)}, u32[]{:S(2)}) collective-permute-start(f32[8,136,128]{2,1,0:T(8,128)S(1)} %all_to_all.26.own), channel_id=1, source_target_pairs={{0,1},{1,0},{2,3},{3,2},{4,5},{5,4},{6,7},{7,6},{8,9},{9,8},{10,11... | collective-permute-start | bytes 1671176 | tf_op jit(solution)/shard_map/ppermute | solution.py:252

commit v20 on v18

--- a/solution.py
+++ b/solution.py
@@ -178,25 +178,37 @@
         out[target, pl.ds(points, SIDE)] = tail
 
 
-def member_kernel(own, other, own_high, own_low, other_high, other_low, first, out, own_member, both):
-    points = own.shape[1] - SIDE
-    sums = jnp.zeros((SIDE, CLUSTER_COUNT), jnp.float32)
+def tail_kernel(blocks, out):
+    points = blocks.shape[1] - SIDE
+    out[...] = sum(blocks[block, pl.ds(points, SIDE)] for block in range(8))
+
+
+def half_product(source, sums, high, low, both):
+    points = source.shape[1] - SIDE
+    sizes = jnp.zeros((1, CLUSTER_COUNT), jnp.float32)
     for block in range(8):
-        sums += own[block, pl.ds(points, SIDE)] + other[block, pl.ds(points, SIDE)]
-    cohesion, counts = sums[0:1], sums[1:2]
-    own_member[...] = jnp.exp(log_softmax_energy(first[pl.ds(0, points)], counts, cohesion))
-    sizes = jnp.zeros((1, CLUSTER_COUNT), jnp.float32)
-    total = 0.0
-    for source, high, low in ((own, own_high, own_low), (other, other_high, other_low)):
-        for block in range(8):
-            member = jnp.exp(log_softmax_energy(source[block, pl.ds(0, points)], counts, cohesion))
-            sizes += jnp.sum(member, axis=0, keepdims=True)
-            at = pl.ds(block * points, points)
-            both[at, pl.ds(0, CLUSTER_COUNT)], both[at, pl.ds(CLUSTER_COUNT, CLUSTER_COUNT)] = halves(member)
-        wide = product(high[...], both[...])
-        total += product(low[...], both[:, pl.ds(0, CLUSTER_COUNT)])
-        total += wide[:, :CLUSTER_COUNT] + wide[:, CLUSTER_COUNT:]
-    tail = tail_rows(sizes)
+        member = jnp.exp(log_softmax_energy(source[block, pl.ds(0, points)], sums[1:2], sums[0:1]))
+        sizes += jnp.sum(member, axis=0, keepdims=True)
+        at = pl.ds(block * points, points)
+        both[at, pl.ds(0, CLUSTER_COUNT)], both[at, pl.ds(CLUSTER_COUNT, CLUSTER_COUNT)] = halves(member)
+    wide = product(high[...], both[...])
+    total = product(low[...], both[:, pl.ds(0, CLUSTER_COUNT)])
+    return total + wide[:, :CLUSTER_COUNT] + wide[:, CLUSTER_COUNT:], sizes
+
+
+def own_member_kernel(blocks, tail, far_tail, high, low, first, out, sums, own_member, both):
+    points = own_member.shape[0]
+    both_tails = tail[...] + far_tail[...]
+    own_member[...] = jnp.exp(log_softmax_energy(first[pl.ds(0, points)], both_tails[1:2], both_tails[0:1]))
+    out[...], sizes = half_product(blocks, both_tails, high, low, both)
+    sums[...] = tail_rows(both_tails[0:1], both_tails[1:2], sizes)
+
+
+def other_member_kernel(blocks, sums, high, low, weighted, out, both):
+    points = blocks.shape[1] - SIDE
+    total, sizes = half_product(blocks, sums[...], high, low, both)
+    total += weighted[...]
+    tail = tail_rows(sums[pl.ds(2, 1)] + sizes)
     for block in range(8):
         out[member_at(block), pl.ds(0, points)] = total[block * points : (block + 1) * points]
         out[member_at(block), pl.ds(points, SIDE)] = tail
@@ -298,13 +310,25 @@
 
     line = ((lines, CLUSTER_COUNT), jnp.float32)
     first, spread = on_chip(sum_kernel, "sum_spread", [line, exchange], [exchange_rows(weighted)])
+    tail = ((SIDE, CLUSTER_COUNT), jnp.float32)
     firsts = exchange_columns(spread)
-    weighted, own = on_chip(
-        member_kernel,
-        "members",
-        [exchange, ((points, CLUSTER_COUNT), jnp.float32)],
-        [firsts, other_core(firsts), own_high, own_low, other_high, other_low, first],
-        scratch=[pltpu.VMEM((tall, 2 * CLUSTER_COUNT), jnp.bfloat16)],
+    (sums,) = on_chip(tail_kernel, "tails", [tail], [firsts])
+    far_sums = other_core(sums)
+    firsts, far_sums = lax.optimization_barrier((firsts, far_sums))
+    both = [pltpu.VMEM((tall, 2 * CLUSTER_COUNT), jnp.bfloat16)]
+    weighted, sums, own = on_chip(
+        own_member_kernel,
+        "own_members",
+        [((tall, CLUSTER_COUNT), jnp.float32), tail, ((points, CLUSTER_COUNT), jnp.float32)],
+        [firsts, sums, far_sums, own_high, own_low, first],
+        scratch=both,
+    )
+    (weighted,) = on_chip(
+        other_member_kernel,
+        "other_members",
+        [exchange],
+        [other_core(firsts), sums, other_high, other_low, weighted],
+        scratch=both,
     )
 
     part = ((1, CLUSTER_COUNT), jnp.float32)

time: 99.7 us -> 99.8 us (level)
    pallas_call x7 -> x9, Pallas kernels: 10.3 us -> 10.8 us  [on_chip(): pl.pallas_call(kernel, out_shape=shapes, in_specs=specs, out_specs=[vmem]...]
    ppermute x2 -> x3, starting transfers between devices: 6.26 us -> 6.62 us  [other_core(): return lax.ppermute(x, 'core', [(0, 1), (1, 0)])]
  transfers between devices with their start and end apart: 10 -> 11, of which waited for: 4 -> 5; matrix products, arithmetic and copies ran while one was open for 0% -> 0% of each run, Pallas kernels for 5% -> 6%
where the time goes in v20:
time: 99.8 us; the launch traced here: 99.5 us
  blocking collectives  53.3 us (53%)
  starting transfers between devices  24.4 us (24%)
  Pallas kernels  12.9 us (13%)
  waiting for transfers between devices  8.85 us (9%)
    all_to_all x2, blocking collectives, exchange_rows(): return lax.all_to_all(blocks, ('y_lo', 'x'), 0, 0, tiled=True)  25.4 us
    all_to_all x1, blocking collectives, exchange_columns(): lax.all_to_all(blocks, EVERY, 0, 0, axis_index_groups=COLUMN_GROUPS, tile...  14.1 us
    all_to_all x1, blocking collectives, shards(): parts = lax.all_to_all(copies(part, 128), EVERY, 0, 0, tiled=True)  13.8 us
    pallas_call x9, Pallas kernels, on_chip(): pl.pallas_call(kernel, out_shape=shapes, in_specs=specs, out_specs=[vmem]...  10.8 us
    ppermute x7, starting transfers between devices, moved(): return lax.ppermute(x, EVERY, pairs)  9.29 us
    all_to_all x1, starting transfers between devices, exchange_columns(): lax.all_to_all(blocks, EVERY, 0, 0, axis_index_groups=COLUMN_GROUPS, tile...  8.46 us
    ppermute x7, waiting for transfers between devices, moved(): return lax.ppermute(x, EVERY, pairs)  7.96 us
    ppermute x3, starting transfers between devices, other_core(): return lax.ppermute(x, 'core', [(0, 1), (1, 0)])  6.62 us
  transfers between devices with their start and end apart: 11, of which 5 were waited for; matrix products, arithmetic and copies ran while one was open for 0% of the time, Pallas kernels for 6%

profile of v20, /device:TPU:1, one launch (start us, length us, event | category | flops | bytes accessed | tf_op | source)
XLA Modules:
  0.0 99.5 jit_solution(11027471852465399917)
XLA Ops:
  0.0 2.1 %prepare.1 = (f32[136,256]{1,0:T(8,128)}, f32[8,136,256]{2,1,0:T(8,128)}) custom-call(f32[128,256]{1,0:T(8,128)} %embedding.1, s32[1,128]{1,0:T(1,128)} %bitcast.7), custom_call_target="tpu_custom_call" | custom-call | tf_op jit(solution)/shard_map/prepare/pallas_call | solution.py:278
  2.1 8.5 %all-to-all-start = ((f32[8,136,256]{2,1,0:T(8,128)}), f32[8,136,256]{2,1,0:T(8,128)S(1)}, u32[]{:S(2)}, u32[]{:S(2)}) async-start(f32[8,136,256]{2,1,0:T(8,128)} %get-tuple-element.42), calls=%async_computation | async-start | bytes 2228224 | tf_op jit(solution)/shard_map/all_to_all | solution.py:40
  10.6 1.3 %collective-permute-start.4 = (f32[136,256]{1,0:T(8,128)S(1)}, f32[136,256]{1,0:T(8,128)S(1)}, u32[]{:S(2)}, u32[]{:S(2)}) collective-permute-start(f32[136,256]{1,0:T(8,128)S(1)} %copy-done), channel_id=1, source_target_pairs={{6,0},{7,1},{0,2},{1,3},{2,4},{3,5},{4,6},{5,7},{14,8},{15,9},{8,1... | collective-permute-start | bytes 417800 | tf_op jit(solution)/shard_map/ppermute | solution.py:47
  11.9 2.5 %collective-permute-start.3 = (f32[136,256]{1,0:T(8,128)S(1)}, f32[136,256]{1,0:T(8,128)S(1)}, u32[]{:S(2)}, u32[]{:S(2)}) collective-permute-start(f32[136,256]{1,0:T(8,128)S(1)} %copy-done), channel_id=1, source_target_pairs={{4,0},{5,1},{6,2},{7,3},{0,4},{1,5},{2,6},{3,7},{12,8},{13,9},{14,... | collective-permute-start | bytes 417800 | tf_op jit(solution)/shard_map/ppermute | solution.py:47
  14.3 0.9 collective-permute-start.2
  15.3 1.4 %collective-permute-start.1 = (f32[136,256]{1,0:T(8,128)S(1)}, f32[136,256]{1,0:T(8,128)S(1)}, u32[]{:S(2)}, u32[]{:S(2)}) collective-permute-start(f32[136,256]{1,0:T(8,128)S(1)} %copy-done), channel_id=1, source_target_pairs={{70,0},{71,1},{64,2},{65,3},{66,4},{67,5},{68,6},{69,7},{78,8},{79... | collective-permute-start | bytes 417800 | tf_op jit(solution)/shard_map/ppermute | solution.py:47
  16.7 0.9 collective-permute-start
  17.6 2.5 %collective-permute-done.3.refs_4_ = f32[136,256]{1,0:T(8,128)S(1)} collective-permute-done((f32[136,256]{1,0:T(8,128)S(1)}, f32[136,256]{1,0:T(8,128)S(1)}, u32[]{:S(2)}, u32[]{:S(2)}) %collective-permute-start.3) | collective-permute-done | bytes 139296 | tf_op jit(solution)/shard_map/ppermute | solution.py:47
  20.1 3.9 %collective-permute-done.1.refs_2_ = f32[136,256]{1,0:T(8,128)S(1)} collective-permute-done((f32[136,256]{1,0:T(8,128)S(1)}, f32[136,256]{1,0:T(8,128)S(1)}, u32[]{:S(2)}, u32[]{:S(2)}) %collective-permute-start.1) | collective-permute-done | bytes 139296 | tf_op jit(solution)/shard_map/ppermute | solution.py:47
  24.0 1.6 %collective-permute-done.refs_1_ = f32[136,256]{1,0:T(8,128)S(1)} collective-permute-done((f32[136,256]{1,0:T(8,128)S(1)}, f32[136,256]{1,0:T(8,128)S(1)}, u32[]{:S(2)}, u32[]{:S(2)}) %collective-permute-start) | collective-permute-done | bytes 139296 | tf_op jit(solution)/shard_map/ppermute | solution.py:47
  25.5 2.4 %collective-permute-start.7 = (f32[8,136,256]{2,1,0:T(8,128)S(1)}, f32[8,136,256]{2,1,0:T(8,128)S(1)}, u32[]{:S(2)}, u32[]{:S(2)}) collective-permute-start(f32[8,136,256]{2,1,0:T(8,128)S(1)} %all-to-all-done.refs_6_), channel_id=1, source_target_pairs={{0,1},{1,0},{2,3},{3,2},{4,5},{5,4},{6,7},{7,6},{8,9},{9,8},{10,11... | collective-permute-start | bytes 3342344 | tf_op jit(solution)/shard_map/ppermute | solution.py:264
  27.9 1.3 %collective-permute-start.6 = (f32[136,256]{1,0:T(8,128)S(1)}, f32[136,256]{1,0:T(8,128)S(1)}, u32[]{:S(2)}, u32[]{:S(2)}) collective-permute-start(f32[136,256]{1,0:T(8,128)S(1)} %copy-done), channel_id=1, source_target_pairs={{64,0},{65,1},{66,2},{67,3},{68,4},{69,5},{70,6},{71,7},{72,8},{73... | collective-permute-start | bytes 417800 | tf_op jit(solution)/shard_map/ppermute | solution.py:47
  29.2 1.1 %collective-permute-start.5 = (f32[136,256]{1,0:T(8,128)S(1)}, f32[136,256]{1,0:T(8,128)S(1)}, u32[]{:S(2)}, u32[]{:S(2)}) collective-permute-start(f32[136,256]{1,0:T(8,128)S(1)} %copy-done), channel_id=1, source_target_pairs={{2,0},{3,1},{4,2},{5,3},{6,4},{7,5},{0,6},{1,7},{10,8},{11,9},{12,... | collective-permute-start | bytes 417800 | tf_op jit(solution)/shard_map/ppermute | solution.py:47
  30.3 2.5 %own_pairs.1 = (bf16[768,768]{1,0:T(8,128)(2,1)S(1)}, f32[768,1]{1,0:T(8,128)S(1)}, bf16[1024,768]{1,0:T(8,128)(2,1)S(1)}, f32[8,1024]{1,0:T(8,128)S(1)}, bf16[1...) custom-call(f32[136,256]{1,0:T(8,128)S(1)} %copy-done, ...), custom_call_target="tpu_custom_call" | custom-call | tf_op jit(solution)/shard_map/own_pairs/pallas_call | solution.py:247
  32.8 2.4 %other_pairs.1 = (bf16[1024,768]{1,0:T(8,128)(2,1)S(1)}, f32[8,1024]{1,0:T(8,128)S(1)}, bf16[1024,128]{1,0:T(8,128)(2,1)S(1)}, bf16[1024,1024]{1,0:T(8,128)(2,1)...) custom-call(f32[8,136,256]{2,1,0:T(8,128)S(1)} %collective-permute-done.7.columns, ...), custom_call_target="tpu_custom_call" | custom-call | tf_op jit(solution)/shard_map/other_pairs/pallas_call | solution.py:247
  35.2 1.8 %late_pairs.1 = (bf16[1024,1024]{1,0:T(8,128)(2,1)S(1)}, bf16[1024,1024]{1,0:T(8,128)(2,1)S(1)}, bf16[1024,1024]{1,0:T(8,128)(2,1)S(1)}, bf16[1024,1024]{1,0:T(8,128)(2,1)S(1)}, f32[8,136,128]{2,1,0:T(8,128)S(1)}) custom-call(f32[136,256]{1,0:T(8,128)S(1)} %copy-done, ...), custom_call_target="tpu_custom_call", output_to_operand_aliasing={{0}: (15, {}), {1}: (16, {}), {2}: (17, {}), {3}: (18, {})} | custom-call | tf_op jit(solution)/shard_map/late_pairs/pallas_call | solution.py:247
  37.0 12.5 %all_to_all.25.blocks = f32[8,136,128]{2,1,0:T(8,128)S(1)} all-to-all(f32[8,136,128]{2,1,0:T(8,128)S(1)} %get-tuple-element.65), channel_id=1, replica_groups=mesh['y_lo'=2,'z'=4,'y_hi'=2,'x'=4,'core'=2] {'y_lo','x'}, dimensions={0} | all-to-all | bytes 1114112 | tf_op jit(solution)/shard_map/all_to_all | solution.py:36
  49.6 14.1 %all_to_all.26.blocks = f32[8,136,128]{2,1,0:T(8,128)S(1)} all-to-all(f32[8,136,128]{2,1,0:T(8,128)S(1)} %get-tuple-element.66), channel_id=1, replica_groups={{0,16,32,48,72,88,104,120},{1,17,33,49,73,89,105,121},{2,18,34,50,74,90..., dimensions={0} | all-to-all | bytes 1114112 | tf_op jit(solution)/shard_map/all_to_all | solution.py:40
  63.7 3.9 %collective-permute-start.8 = (f32[8,128]{1,0:T(8,128)S(1)}, f32[8,128]{1,0:T(8,128)S(1)}, u32[]{:S(2)}, u32[]{:S(2)}) collective-permute-start(f32[8,128]{1,0:T(8,128)S(1)} %tails.1.tail), channel_id=1, source_target_pairs={{0,1},{1,0},{2,3},{3,2},{4,5},{5,4},{6,7},{7,6},{8,9},{9,8},{10,11... | collective-permute-start | bytes 12296 | tf_op jit(solution)/shard_map/ppermute | solution.py:264
  68.7 1.5 %own_members.1 = (f32[1024,128]{1,0:T(8,128)S(1)}, f32[8,128]{1,0:T(8,128)S(1)}, f32[128,128]{1,0:T(8,128)S(1)}) custom-call(f32[8,136,128]{2,1,0:T(8,128)S(1)} %all_to_all.26.blocks, f32[8,128]{1,0:T(8,128)S(1)} %tails.1.tail, f32[8,128]{1,0:T(8,128)S(1)} %collective-permute-done.8.far_tail, bf16[1024,1024]{1,0:T(8,128)(2,1)S(1)} %get-tuple-element.69.high, ...), custom_call_target="tpu_custom_call" | custom-call | tf_op jit(solution)/shard_map/own_members/pallas_call | solution.py:247
  70.3 1.6 %other_members.1 = f32[8,136,128]{2,1,0:T(8,128)S(1)} custom-call(f32[8,136,128]{2,1,0:T(8,128)S(1)} %collective-permute-done.9.blocks, f32[8,128]{1,0:T(8,128)S(1)} %get-tuple-element.72.sums, bf16[1024,1024]{1,0:T(8,128)(2,1)S(1)} %get-tuple-element.73.high, bf16[1024,1024]{1,0:T(8,128)(2,1)S(1)} %get-tuple-element.74.low, ...), custom_call_target="tpu_custom_call" | custom-call | tf_op jit(solution)/shard_map/other_members/pallas_call | solution.py:247
  71.9 12.9 %all_to_all.27.blocks = f32[8,136,128]{2,1,0:T(8,128)S(1)} all-to-all(f32[8,136,128]{2,1,0:T(8,128)S(1)} %other_members.1), channel_id=1, replica_groups=mesh['y_lo'=2,'z'=4,'y_hi'=2,'x'=4,'core'=2] {'y_lo','x'}, dimensions={0} | all-to-all | bytes 1114112 | tf_op jit(solution)/shard_map/all_to_all | solution.py:36
  84.9 13.8 %all_to_all.28 = f32[128,1,128]{2,1,0:T(1,128)S(1)} all-to-all(f32[128,1,128]{2,1,0:T(1,128)S(1)} %broadcast_in_dim.3), channel_id=1, replica_groups=mesh['y_lo'=2,'z'=4,'y_hi'=2,'x'=4,'core'=2] {'y_lo','z','y_hi','x','core'}, dimensions={0} | all-to-all | bytes 131072 | tf_op jit(solution)/shard_map/all_to_all | solution.py:336
  98.7 0.8 final.1
  (16 shorter events, 1.4 us)
Async XLA Ops:
  2.1 8.5 %copy-start = (f32[136,256]{1,0:T(8,128)S(1)}, f32[136,256]{1,0:T(8,128)}, u32[]{:S(2)}) copy-start(f32[136,256]{1,0:T(8,128)} %get-tuple-element.44.refs_0_) | copy-start | bytes 417796
  2.1 23.4 %all-to-all-start = ((f32[8,136,256]{2,1,0:T(8,128)}), f32[8,136,256]{2,1,0:T(8,128)S(1)}, u32[]{:S(2)}, u32[]{:S(2)}) async-start(f32[8,136,256]{2,1,0:T(8,128)} %get-tuple-element.42), calls=%async_computation | async-start | bytes 2228224 | tf_op jit(solution)/shard_map/all_to_all | solution.py:40
  10.6 7.0 %collective-permute-start.4 = (f32[136,256]{1,0:T(8,128)S(1)}, f32[136,256]{1,0:T(8,128)S(1)}, u32[]{:S(2)}, u32[]{:S(2)}) collective-permute-start(f32[136,256]{1,0:T(8,128)S(1)} %copy-done), channel_id=1, source_target_pairs={{6,0},{7,1},{0,2},{1,3},{2,4},{3,5},{4,6},{5,7},{14,8},{15,9},{8,1... | collective-permute-start | bytes 417800 | tf_op jit(solution)/shard_map/ppermute | solution.py:47
  11.9 8.2 %collective-permute-start.3 = (f32[136,256]{1,0:T(8,128)S(1)}, f32[136,256]{1,0:T(8,128)S(1)}, u32[]{:S(2)}, u32[]{:S(2)}) collective-permute-start(f32[136,256]{1,0:T(8,128)S(1)} %copy-done), channel_id=1, source_target_pairs={{4,0},{5,1},{6,2},{7,3},{0,4},{1,5},{2,6},{3,7},{12,8},{13,9},{14,... | collective-permute-start | bytes 417800 | tf_op jit(solution)/shard_map/ppermute | solution.py:47
  14.3 5.7 %collective-permute-start.2 = (f32[136,256]{1,0:T(8,128)S(1)}, f32[136,256]{1,0:T(8,128)S(1)}, u32[]{:S(2)}, u32[]{:S(2)}) collective-permute-start(f32[136,256]{1,0:T(8,128)S(1)} %copy-done), channel_id=1, source_target_pairs={{66,0},{67,1},{68,2},{69,3},{70,4},{71,5},{64,6},{65,7},{74,8},{75... | collective-permute-start | bytes 417800 | tf_op jit(solution)/shard_map/ppermute | solution.py:47
  15.3 8.7 %collective-permute-start.1 = (f32[136,256]{1,0:T(8,128)S(1)}, f32[136,256]{1,0:T(8,128)S(1)}, u32[]{:S(2)}, u32[]{:S(2)}) collective-permute-start(f32[136,256]{1,0:T(8,128)S(1)} %copy-done), channel_id=1, source_target_pairs={{70,0},{71,1},{64,2},{65,3},{66,4},{67,5},{68,6},{69,7},{78,8},{79... | collective-permute-start | bytes 417800 | tf_op jit(solution)/shard_map/ppermute | solution.py:47
  16.7 8.8 %collective-permute-start = (f32[136,256]{1,0:T(8,128)S(1)}, f32[136,256]{1,0:T(8,128)S(1)}, u32[]{:S(2)}, u32[]{:S(2)}) collective-permute-start(f32[136,256]{1,0:T(8,128)S(1)} %copy-done), channel_id=1, source_target_pairs={{68,0},{69,1},{70,2},{71,3},{64,4},{65,5},{66,6},{67,7},{76,8},{77... | collective-permute-start | bytes 417800 | tf_op jit(solution)/shard_map/ppermute | solution.py:47
  25.5 7.2 %collective-permute-start.7 = (f32[8,136,256]{2,1,0:T(8,128)S(1)}, f32[8,136,256]{2,1,0:T(8,128)S(1)}, u32[]{:S(2)}, u32[]{:S(2)}) collective-permute-start(f32[8,136,256]{2,1,0:T(8,128)S(1)} %all-to-all-done.refs_6_), channel_id=1, source_target_pairs={{0,1},{1,0},{2,3},{3,2},{4,5},{5,4},{6,7},{7,6},{8,9},{9,8},{10,11... | collective-permute-start | bytes 3342344 | tf_op jit(solution)/shard_map/ppermute | solution.py:264
  27.9 7.2 %collective-permute-start.6 = (f32[136,256]{1,0:T(8,128)S(1)}, f32[136,256]{1,0:T(8,128)S(1)}, u32[]{:S(2)}, u32[]{:S(2)}) collective-permute-start(f32[136,256]{1,0:T(8,128)S(1)} %copy-done), channel_id=1, source_target_pairs={{64,0},{65,1},{66,2},{67,3},{68,4},{69,5},{70,6},{71,7},{72,8},{73... | collective-permute-start | bytes 417800 | tf_op jit(solution)/shard_map/ppermute | solution.py:47
  29.2 6.0 %collective-permute-start.5 = (f32[136,256]{1,0:T(8,128)S(1)}, f32[136,256]{1,0:T(8,128)S(1)}, u32[]{:S(2)}, u32[]{:S(2)}) collective-permute-start(f32[136,256]{1,0:T(8,128)S(1)} %copy-done), channel_id=1, source_target_pairs={{2,0},{3,1},{4,2},{5,3},{6,4},{7,5},{0,6},{1,7},{10,8},{11,9},{12,... | collective-permute-start | bytes 417800 | tf_op jit(solution)/shard_map/ppermute | solution.py:47
  63.7 4.7 %collective-permute-start.8 = (f32[8,128]{1,0:T(8,128)S(1)}, f32[8,128]{1,0:T(8,128)S(1)}, u32[]{:S(2)}, u32[]{:S(2)}) collective-permute-start(f32[8,128]{1,0:T(8,128)S(1)} %tails.1.tail), channel_id=1, source_target_pairs={{0,1},{1,0},{2,3},{3,2},{4,5},{5,4},{6,7},{7,6},{8,9},{9,8},{10,11... | collective-permute-start | bytes 12296 | tf_op jit(solution)/shard_map/ppermute | solution.py:264
  68.4 2.0 %collective-permute-start.9 = (f32[8,136,128]{2,1,0:T(8,128)S(1)}, f32[8,136,128]{2,1,0:T(8,128)S(1)}, u32[]{:S(2)}, u32[]{:S(2)}) collective-permute-start(f32[8,136,128]{2,1,0:T(8,128)S(1)} %all_to_all.26.blocks), channel_id=1, source_target_pairs={{0,1},{1,0},{2,3},{3,2},{4,5},{5,4},{6,7},{7,6},{8,9},{9,8},{10,11... | collective-permute-start | bytes 1671176 | tf_op jit(solution)/shard_map/ppermute | solution.py:264

commit v21 on v18

--- a/solution.py
+++ b/solution.py
@@ -133,13 +133,23 @@
 EARLY = 768
 
 
-def own_pair_kernel(*refs):
-    rows, (columns, left, squares, right, line, member, high, low, out) = refs[:6], refs[6:]
+FIRST = (0, 2, 3, 4, 5)
+
+
+def row_kernel(*refs):
+    rows, (left, squares, members) = refs[: len(FIRST)], refs[len(FIRST) :]
     points = rows[0].shape[0] - SIDE
-    set_columns(columns, right, line, member)
-    for offset, block in enumerate(rows):
+    for offset, block in zip(FIRST, rows):
         at = pl.ds(offset * points, points)
         left[at], squares[at] = left_rows(block[pl.ds(0, points)])
+        members[at] = seed_member(block[pl.ds(points, 1)][:, :points])
+
+
+def own_pair_kernel(last, columns, _, __, left, squares, right, line, member, high, low, out):
+    points = last.shape[0] - SIDE
+    set_columns(columns, right, line, member)
+    at = pl.ds(points, points)
+    left[at], squares[at] = left_rows(last[pl.ds(0, points)])
     for start in range(0, EARLY, CHUNK):
         at = pl.ds(start, CHUNK)
         distances(left[at], squares[at], right, line, high, low, at)
@@ -155,11 +165,11 @@
 
 
 def late_pair_kernel(*refs):
-    rows, sides, weighted, refs = refs[:8], (refs[8:11], refs[11:14]), refs[14], refs[19:]
+    rows, members, sides, weighted, refs = refs[:3], refs[3], (refs[4:7], refs[7:10]), refs[10], refs[15:]
     (*kept, out) = refs
     points = rows[0].shape[0] - SIDE
     at = pl.ds(EARLY, CHUNK)
-    left, square = left_rows(jnp.concatenate([block[pl.ds(0, points)] for block in rows[6:]], axis=0))
+    left, square = left_rows(jnp.concatenate([block[pl.ds(0, points)] for block in rows[1:]], axis=0))
     late = 0.0
     for half, (right, line, member) in enumerate(sides):
         high, low = kept[2 * half : 2 * half + 2]
@@ -170,9 +180,12 @@
         start = offset * points
         part = weighted[pl.ds(start, points)] if start < EARLY else late[start - EARLY : start - EARLY + points]
         out[member_at(offset), pl.ds(0, points)] = part
-        own = seed_member(rows[offset][pl.ds(points, 1)][:, :points])
+        if offset in FIRST:
+            own = members[pl.ds(start, points)]
+        else:
+            own = seed_member(rows[{1: 0, 6: 1, 7: 2}[offset]][pl.ds(points, 1)][:, :points])
         cohesion += jnp.sum(own * part, axis=0, keepdims=True)
-    counts = jnp.sum(seed_member(rows[0][pl.ds(points, 1)][:, :points]), axis=0, keepdims=True)
+    counts = jnp.sum(members[pl.ds(0, points)], axis=0, keepdims=True)
     tail = tail_rows(cohesion, counts)
     for target in range(8):
         out[target, pl.ds(points, SIDE)] = tail
@@ -273,14 +286,19 @@
     )(embedding, seed_cluster.reshape(1, points))
     columns = exchange_columns(spread)
     rows = row_peers(block)
-    columns, *rows[:6] = lax.optimization_barrier((columns, *rows[:6]))
+    lefts = [((EARLY, 3 * width), jnp.bfloat16), ((EARLY, 1), jnp.float32)]
+    early = ((EARLY, CLUSTER_COUNT), jnp.float32)
+    *prepared, members = on_chip(row_kernel, "rows", [*lefts, early], [rows[offset] for offset in FIRST])
+    columns, rows[1], *prepared = lax.optimization_barrier((columns, rows[1], *prepared))
     kept = ((tall, tall), jnp.bfloat16)
     exchange = ((8, lines, CLUSTER_COUNT), jnp.float32)
     sides = [((tall, 3 * width), jnp.bfloat16), ((SIDE, tall), jnp.float32), ((tall, CLUSTER_COUNT), jnp.bfloat16)]
-    lefts = [((EARLY, 3 * width), jnp.bfloat16), ((EARLY, 1), jnp.float32)]
-    early = ((EARLY, CLUSTER_COUNT), jnp.float32)
     left, squares, *own_sides, own_high, own_low, weighted = on_chip(
-        own_pair_kernel, "own_pairs", [*lefts, *sides, kept, kept, early], [*rows[:6], columns]
+        own_pair_kernel,
+        "own_pairs",
+        [*lefts, *sides, kept, kept, early],
+        [rows[1], columns, *prepared],
+        aliases={2: 0, 3: 1},
     )
     *other_sides, other_high, other_low, weighted = on_chip(
         other_pair_kernel,
@@ -292,8 +310,8 @@
         late_pair_kernel,
         "late_pairs",
         [kept] * 4 + [exchange],
-        [*rows, *own_sides, *other_sides, weighted, own_high, own_low, other_high, other_low],
-        aliases={15: 0, 16: 1, 17: 2, 18: 3},
+        [rows[1], *rows[6:], members, *own_sides, *other_sides, weighted, own_high, own_low, other_high, other_low],
+        aliases={11: 0, 12: 1, 13: 2, 14: 3},
     )
 
     line = ((lines, CLUSTER_COUNT), jnp.float32)

time: 99.7 us -> 100 us (level)
    pallas_call x7 -> x8, Pallas kernels: 10.3 us -> 10.5 us  [on_chip(): pl.pallas_call(kernel, out_shape=shapes, in_specs=specs, out_specs=[vmem]...]
where the time goes in v21:
time: 100 us; the launch traced here: 99.7 us
  blocking collectives  53.6 us (54%)
  starting transfers between devices  24 us (24%)
  Pallas kernels  12.6 us (13%)
  waiting for transfers between devices  9.29 us (9%)
    all_to_all x2, blocking collectives, exchange_rows(): return lax.all_to_all(blocks, ('y_lo', 'x'), 0, 0, tiled=True)  25.5 us
    all_to_all x1, blocking collectives, exchange_columns(): lax.all_to_all(blocks, EVERY, 0, 0, axis_index_groups=COLUMN_GROUPS, tile...  14.4 us
    all_to_all x1, blocking collectives, shards(): parts = lax.all_to_all(copies(part, 128), EVERY, 0, 0, tiled=True)  13.8 us
    pallas_call x8, Pallas kernels, on_chip(): pl.pallas_call(kernel, out_shape=shapes, in_specs=specs, out_specs=[vmem]...  10.5 us
    ppermute x7, starting transfers between devices, moved(): return lax.ppermute(x, EVERY, pairs)  8.94 us
    all_to_all x1, starting transfers between devices, exchange_columns(): lax.all_to_all(blocks, EVERY, 0, 0, axis_index_groups=COLUMN_GROUPS, tile...  8.46 us
    ppermute x7, waiting for transfers between devices, moved(): return lax.ppermute(x, EVERY, pairs)  7.7 us
    ppermute x2, starting transfers between devices, other_core(): return lax.ppermute(x, 'core', [(0, 1), (1, 0)])  6.62 us
  transfers between devices with their start and end apart: 10, of which 4 were waited for; matrix products, arithmetic and copies ran while one was open for 0% of the time, Pallas kernels for 5%

profile of v21, /device:TPU:1, one launch (start us, length us, event | category | flops | bytes accessed | tf_op | source)
XLA Modules:
  0.0 99.7 jit_solution(8644393814528510239)
XLA Ops:
  0.0 2.1 %prepare.1 = (f32[136,256]{1,0:T(8,128)}, f32[8,136,256]{2,1,0:T(8,128)}) custom-call(f32[128,256]{1,0:T(8,128)} %embedding.1, s32[1,128]{1,0:T(1,128)} %bitcast.7), custom_call_target="tpu_custom_call" | custom-call | tf_op jit(solution)/shard_map/prepare/pallas_call | solution.py:279
  2.1 8.5 %all-to-all-start = ((f32[8,136,256]{2,1,0:T(8,128)}), f32[8,136,256]{2,1,0:T(8,128)S(1)}, u32[]{:S(2)}, u32[]{:S(2)}) async-start(f32[8,136,256]{2,1,0:T(8,128)} %get-tuple-element.39), calls=%async_computation | async-start | bytes 2228224 | tf_op jit(solution)/shard_map/all_to_all | solution.py:40
  10.6 1.3 %collective-permute-start.4 = (f32[136,256]{1,0:T(8,128)S(1)}, f32[136,256]{1,0:T(8,128)S(1)}, u32[]{:S(2)}, u32[]{:S(2)}) collective-permute-start(f32[136,256]{1,0:T(8,128)S(1)} %copy-done), channel_id=1, source_target_pairs={{6,0},{7,1},{0,2},{1,3},{2,4},{3,5},{4,6},{5,7},{14,8},{15,9},{8,1... | collective-permute-start | bytes 417800 | tf_op jit(solution)/shard_map/ppermute | solution.py:47
  11.9 2.5 %collective-permute-start.3 = (f32[136,256]{1,0:T(8,128)S(1)}, f32[136,256]{1,0:T(8,128)S(1)}, u32[]{:S(2)}, u32[]{:S(2)}) collective-permute-start(f32[136,256]{1,0:T(8,128)S(1)} %copy-done), channel_id=1, source_target_pairs={{4,0},{5,1},{6,2},{7,3},{0,4},{1,5},{2,6},{3,7},{12,8},{13,9},{14,... | collective-permute-start | bytes 417800 | tf_op jit(solution)/shard_map/ppermute | solution.py:47
  14.3 0.9 collective-permute-start.2
  15.3 1.4 %collective-permute-start.1 = (f32[136,256]{1,0:T(8,128)S(1)}, f32[136,256]{1,0:T(8,128)S(1)}, u32[]{:S(2)}, u32[]{:S(2)}) collective-permute-start(f32[136,256]{1,0:T(8,128)S(1)} %copy-done), channel_id=1, source_target_pairs={{70,0},{71,1},{64,2},{65,3},{66,4},{67,5},{68,6},{69,7},{78,8},{79... | collective-permute-start | bytes 417800 | tf_op jit(solution)/shard_map/ppermute | solution.py:47
  16.7 0.9 collective-permute-start
  17.6 2.5 %collective-permute-done.3.refs_3_ = f32[136,256]{1,0:T(8,128)S(1)} collective-permute-done((f32[136,256]{1,0:T(8,128)S(1)}, f32[136,256]{1,0:T(8,128)S(1)}, u32[]{:S(2)}, u32[]{:S(2)}) %collective-permute-start.3) | collective-permute-done | bytes 139296 | tf_op jit(solution)/shard_map/ppermute | solution.py:47
  20.1 3.9 %collective-permute-done.1.refs_1_ = f32[136,256]{1,0:T(8,128)S(1)} collective-permute-done((f32[136,256]{1,0:T(8,128)S(1)}, f32[136,256]{1,0:T(8,128)S(1)}, u32[]{:S(2)}, u32[]{:S(2)}) %collective-permute-start.1) | collective-permute-done | bytes 139296 | tf_op jit(solution)/shard_map/ppermute | solution.py:47
  24.2 1.3 %collective-permute-done.last.refs_0_ = f32[136,256]{1,0:T(8,128)S(1)} collective-permute-done((f32[136,256]{1,0:T(8,128)S(1)}, f32[136,256]{1,0:T(8,128)S(1)}, u32[]{:S(2)}, u32[]{:S(2)}) %collective-permute-start) | collective-permute-done | bytes 139296 | tf_op jit(solution)/shard_map/ppermute | solution.py:47
  25.5 2.8 %collective-permute-start.7 = (f32[8,136,256]{2,1,0:T(8,128)S(1)}, f32[8,136,256]{2,1,0:T(8,128)S(1)}, u32[]{:S(2)}, u32[]{:S(2)}) collective-permute-start(f32[8,136,256]{2,1,0:T(8,128)S(1)} %all-to-all-done.columns), channel_id=1, source_target_pairs={{0,1},{1,0},{2,3},{3,2},{4,5},{5,4},{6,7},{7,6},{8,9},{9,8},{10,11... | collective-permute-start | bytes 3342344 | tf_op jit(solution)/shard_map/ppermute | solution.py:265
  28.3 0.9 collective-permute-start.6
  29.2 1.1 %collective-permute-start.5 = (f32[136,256]{1,0:T(8,128)S(1)}, f32[136,256]{1,0:T(8,128)S(1)}, u32[]{:S(2)}, u32[]{:S(2)}) collective-permute-start(f32[136,256]{1,0:T(8,128)S(1)} %copy-done), channel_id=1, source_target_pairs={{2,0},{3,1},{4,2},{5,3},{6,4},{7,5},{0,6},{1,7},{10,8},{11,9},{12,... | collective-permute-start | bytes 417800 | tf_op jit(solution)/shard_map/ppermute | solution.py:47
  30.3 2.4 %own_pairs.1 = (bf16[768,768]{1,0:T(8,128)(2,1)S(1)}, f32[768,1]{1,0:T(8,128)S(1)}, bf16[1024,768]{1,0:T(8,128)(2,1)S(1)}, f32[8,1024]{1,0:T(8,128)S(1)}, bf16[1...) custom-call(f32[136,256]{1,0:T(8,128)S(1)} %collective-permute-done., ...), custom_call_target="tpu_custom_call", output_to_operand_aliasing={{0}: (2, {}), {1}: (3, {})} | custom-call | tf_op jit(solution)/shard_map/own_pairs/pallas_call | solution.py:248
  32.7 2.4 %other_pairs.1 = (bf16[1024,768]{1,0:T(8,128)(2,1)S(1)}, f32[8,1024]{1,0:T(8,128)S(1)}, bf16[1024,128]{1,0:T(8,128)(2,1)S(1)}, bf16[1024,1024]{1,0:T(8,128)(2,1)...) custom-call(f32[8,136,256]{2,1,0:T(8,128)S(1)} %collective-permute-done.7.columns, ...), custom_call_target="tpu_custom_call" | custom-call | tf_op jit(solution)/shard_map/other_pairs/pallas_call | solution.py:248
  35.1 1.8 %late_pairs.1 = (bf16[1024,1024]{1,0:T(8,128)(2,1)S(1)}, bf16[1024,1024]{1,0:T(8,128)(2,1)S(1)}, bf16[1024,1024]{1,0:T(8,128)(2,1)S(1)}, bf16[1024,1024]{1,0:T(8,128)(2,1)S(1)}, f32[8,136,128]{2,1,0:T(8,128)S(1)}) custom-call(f32[136,256]{1,0:T(8,128)S(1)} %collective-permute-done.last.re, ...), custom_call_target="tpu_custom_call", output_to_operand_aliasing={{0}: (11, {}), {1}: (12, {}), {2}: (13, {}), {3}: (14, {})} | custom-call | tf_op jit(solution)/shard_map/late_pairs/pallas_call | solution.py:248
  37.0 12.5 %all_to_all.25.blocks = f32[8,136,128]{2,1,0:T(8,128)S(1)} all-to-all(f32[8,136,128]{2,1,0:T(8,128)S(1)} %get-tuple-element.62), channel_id=1, replica_groups=mesh['y_lo'=2,'z'=4,'y_hi'=2,'x'=4,'core'=2] {'y_lo','x'}, dimensions={0} | all-to-all | bytes 1114112 | tf_op jit(solution)/shard_map/all_to_all | solution.py:36
  49.6 14.4 %all_to_all.26.own = f32[8,136,128]{2,1,0:T(8,128)S(1)} all-to-all(f32[8,136,128]{2,1,0:T(8,128)S(1)} %get-tuple-element.63), channel_id=1, replica_groups={{0,16,32,48,72,88,104,120},{1,17,33,49,73,89,105,121},{2,18,34,50,74,90..., dimensions={0} | all-to-all | bytes 1114112 | tf_op jit(solution)/shard_map/all_to_all | solution.py:40
  63.9 3.8 %collective-permute-start.8 = (f32[8,136,128]{2,1,0:T(8,128)S(1)}, f32[8,136,128]{2,1,0:T(8,128)S(1)}, u32[]{:S(2)}, u32[]{:S(2)}) collective-permute-start(f32[8,136,128]{2,1,0:T(8,128)S(1)} %all_to_all.26.own), channel_id=1, source_target_pairs={{0,1},{1,0},{2,3},{3,2},{4,5},{5,4},{6,7},{7,6},{8,9},{9,8},{10,11... | collective-permute-start | bytes 1671176 | tf_op jit(solution)/shard_map/ppermute | solution.py:265
  67.8 1.6 %collective-permute-done.8.other = f32[8,136,128]{2,1,0:T(8,128)S(1)} collective-permute-done((f32[8,136,128]{2,1,0:T(8,128)S(1)}, f32[8,136,128]{2,1,0:T(8,128)S(1)}, u32[]{:S(2)}, u32[]{:S(2)}) %collective-permute-start.8) | collective-permute-done | bytes 557088 | tf_op jit(solution)/shard_map/ppermute | solution.py:265
  69.4 2.7 %members.1 = (f32[8,136,128]{2,1,0:T(8,128)S(1)}, f32[128,128]{1,0:T(8,128)S(1)}) custom-call(f32[8,136,128]{2,1,0:T(8,128)S(1)} %all_to_all.26.own, f32[8,136,128]{2,1,0:T(8,128)S(1)} %collective-permute-done.8.other, bf16[1024,1024]{1,0:T(8,128)(2,1)S(1)} %get-tuple-element.64.own_high, bf16[1024,1024]{1,0:T(8,128)(2,1)S(1)} %get-tuple-element.65.own_low, ...), custom_call_target="tpu_custom_call" | custom-call | tf_op jit(solution)/shard_map/members/pallas_call | solution.py:248
  72.0 12.9 %all_to_all.27.blocks = f32[8,136,128]{2,1,0:T(8,128)S(1)} all-to-all(f32[8,136,128]{2,1,0:T(8,128)S(1)} %get-tuple-element.69), channel_id=1, replica_groups=mesh['y_lo'=2,'z'=4,'y_hi'=2,'x'=4,'core'=2] {'y_lo','x'}, dimensions={0} | all-to-all | bytes 1114112 | tf_op jit(solution)/shard_map/all_to_all | solution.py:36
  85.1 13.8 %all_to_all.28 = f32[128,1,128]{2,1,0:T(1,128)S(1)} all-to-all(f32[128,1,128]{2,1,0:T(1,128)S(1)} %broadcast_in_dim.3), channel_id=1, replica_groups=mesh['y_lo'=2,'z'=4,'y_hi'=2,'x'=4,'core'=2] {'y_lo','z','y_hi','x','core'}, dimensions={0} | all-to-all | bytes 131072 | tf_op jit(solution)/shard_map/all_to_all | solution.py:330
  98.9 0.8 final.1
  (13 shorter events, 0.5 us)
Async XLA Ops:
  2.1 8.5 %copy-start = (f32[136,256]{1,0:T(8,128)S(1)}, f32[136,256]{1,0:T(8,128)}, u32[]{:S(2)}) copy-start(f32[136,256]{1,0:T(8,128)} %get-tuple-element.40.refs_0_) | copy-start | bytes 417796
  2.1 23.4 %all-to-all-start = ((f32[8,136,256]{2,1,0:T(8,128)}), f32[8,136,256]{2,1,0:T(8,128)S(1)}, u32[]{:S(2)}, u32[]{:S(2)}) async-start(f32[8,136,256]{2,1,0:T(8,128)} %get-tuple-element.39), calls=%async_computation | async-start | bytes 2228224 | tf_op jit(solution)/shard_map/all_to_all | solution.py:40
  10.6 7.0 %collective-permute-start.4 = (f32[136,256]{1,0:T(8,128)S(1)}, f32[136,256]{1,0:T(8,128)S(1)}, u32[]{:S(2)}, u32[]{:S(2)}) collective-permute-start(f32[136,256]{1,0:T(8,128)S(1)} %copy-done), channel_id=1, source_target_pairs={{6,0},{7,1},{0,2},{1,3},{2,4},{3,5},{4,6},{5,7},{14,8},{15,9},{8,1... | collective-permute-start | bytes 417800 | tf_op jit(solution)/shard_map/ppermute | solution.py:47
  11.9 8.2 %collective-permute-start.3 = (f32[136,256]{1,0:T(8,128)S(1)}, f32[136,256]{1,0:T(8,128)S(1)}, u32[]{:S(2)}, u32[]{:S(2)}) collective-permute-start(f32[136,256]{1,0:T(8,128)S(1)} %copy-done), channel_id=1, source_target_pairs={{4,0},{5,1},{6,2},{7,3},{0,4},{1,5},{2,6},{3,7},{12,8},{13,9},{14,... | collective-permute-start | bytes 417800 | tf_op jit(solution)/shard_map/ppermute | solution.py:47
  14.3 5.7 %collective-permute-start.2 = (f32[136,256]{1,0:T(8,128)S(1)}, f32[136,256]{1,0:T(8,128)S(1)}, u32[]{:S(2)}, u32[]{:S(2)}) collective-permute-start(f32[136,256]{1,0:T(8,128)S(1)} %copy-done), channel_id=1, source_target_pairs={{66,0},{67,1},{68,2},{69,3},{70,4},{71,5},{64,6},{65,7},{74,8},{75... | collective-permute-start | bytes 417800 | tf_op jit(solution)/shard_map/ppermute | solution.py:47
  15.3 8.7 %collective-permute-start.1 = (f32[136,256]{1,0:T(8,128)S(1)}, f32[136,256]{1,0:T(8,128)S(1)}, u32[]{:S(2)}, u32[]{:S(2)}) collective-permute-start(f32[136,256]{1,0:T(8,128)S(1)} %copy-done), channel_id=1, source_target_pairs={{70,0},{71,1},{64,2},{65,3},{66,4},{67,5},{68,6},{69,7},{78,8},{79... | collective-permute-start | bytes 417800 | tf_op jit(solution)/shard_map/ppermute | solution.py:47
  16.7 8.8 %collective-permute-start = (f32[136,256]{1,0:T(8,128)S(1)}, f32[136,256]{1,0:T(8,128)S(1)}, u32[]{:S(2)}, u32[]{:S(2)}) collective-permute-start(f32[136,256]{1,0:T(8,128)S(1)} %copy-done), channel_id=1, source_target_pairs={{68,0},{69,1},{70,2},{71,3},{64,4},{65,5},{66,6},{67,7},{76,8},{77... | collective-permute-start | bytes 417800 | tf_op jit(solution)/shard_map/ppermute | solution.py:47
  25.5 7.2 %collective-permute-start.7 = (f32[8,136,256]{2,1,0:T(8,128)S(1)}, f32[8,136,256]{2,1,0:T(8,128)S(1)}, u32[]{:S(2)}, u32[]{:S(2)}) collective-permute-start(f32[8,136,256]{2,1,0:T(8,128)S(1)} %all-to-all-done.columns), channel_id=1, source_target_pairs={{0,1},{1,0},{2,3},{3,2},{4,5},{5,4},{6,7},{7,6},{8,9},{9,8},{10,11... | collective-permute-start | bytes 3342344 | tf_op jit(solution)/shard_map/ppermute | solution.py:265
  28.3 6.8 %collective-permute-start.6 = (f32[136,256]{1,0:T(8,128)S(1)}, f32[136,256]{1,0:T(8,128)S(1)}, u32[]{:S(2)}, u32[]{:S(2)}) collective-permute-start(f32[136,256]{1,0:T(8,128)S(1)} %copy-done), channel_id=1, source_target_pairs={{64,0},{65,1},{66,2},{67,3},{68,4},{69,5},{70,6},{71,7},{72,8},{73... | collective-permute-start | bytes 417800 | tf_op jit(solution)/shard_map/ppermute | solution.py:47
  29.2 5.9 %collective-permute-start.5 = (f32[136,256]{1,0:T(8,128)S(1)}, f32[136,256]{1,0:T(8,128)S(1)}, u32[]{:S(2)}, u32[]{:S(2)}) collective-permute-start(f32[136,256]{1,0:T(8,128)S(1)} %copy-done), channel_id=1, source_target_pairs={{2,0},{3,1},{4,2},{5,3},{6,4},{7,5},{0,6},{1,7},{10,8},{11,9},{12,... | collective-permute-start | bytes 417800 | tf_op jit(solution)/shard_map/ppermute | solution.py:47
  63.9 5.4 %collective-permute-start.8 = (f32[8,136,128]{2,1,0:T(8,128)S(1)}, f32[8,136,128]{2,1,0:T(8,128)S(1)}, u32[]{:S(2)}, u32[]{:S(2)}) collective-permute-start(f32[8,136,128]{2,1,0:T(8,128)S(1)} %all_to_all.26.own), channel_id=1, source_target_pairs={{0,1},{1,0},{2,3},{3,2},{4,5},{5,4},{6,7},{7,6},{8,9},{9,8},{10,11... | collective-permute-start | bytes 1671176 | tf_op jit(solution)/shard_map/ppermute | solution.py:265

commit v22 on v18

--- a/solution.py
+++ b/solution.py
@@ -130,11 +130,11 @@
     return product(high[at], member[...]) + product(low[at], member[...])
 
 
-EARLY = 768
+EARLY = 512
 
 
 def own_pair_kernel(*refs):
-    rows, (columns, left, squares, right, line, member, high, low, out) = refs[:6], refs[6:]
+    rows, (columns, left, squares, right, line, member, high, low, out) = refs[:4], refs[4:]
     points = rows[0].shape[0] - SIDE
     set_columns(columns, right, line, member)
     for offset, block in enumerate(rows):
@@ -158,13 +158,14 @@
     rows, sides, weighted, refs = refs[:8], (refs[8:11], refs[11:14]), refs[14], refs[19:]
     (*kept, out) = refs
     points = rows[0].shape[0] - SIDE
-    at = pl.ds(EARLY, CHUNK)
-    left, square = left_rows(jnp.concatenate([block[pl.ds(0, points)] for block in rows[6:]], axis=0))
     late = 0.0
     for half, (right, line, member) in enumerate(sides):
         high, low = kept[2 * half : 2 * half + 2]
-        distances(left, square, right, line, high, low, at)
-        late += weights(high, low, member, at)
+        for first in (4, 6):
+            pair = rows[first : first + 2]
+            left, square = left_rows(jnp.concatenate([block[pl.ds(0, points)] for block in pair], axis=0))
+            distances(left, square, right, line, high, low, pl.ds(first * points, CHUNK))
+        late += weights(high, low, member, pl.ds(EARLY, EARLY))
     cohesion = jnp.zeros((1, CLUSTER_COUNT), jnp.float32)
     for offset in range(8):
         start = offset * points
@@ -273,14 +274,14 @@
     )(embedding, seed_cluster.reshape(1, points))
     columns = exchange_columns(spread)
     rows = row_peers(block)
-    columns, *rows[:6] = lax.optimization_barrier((columns, *rows[:6]))
+    columns, *rows[:5] = lax.optimization_barrier((columns, *rows[:5]))
     kept = ((tall, tall), jnp.bfloat16)
     exchange = ((8, lines, CLUSTER_COUNT), jnp.float32)
     sides = [((tall, 3 * width), jnp.bfloat16), ((SIDE, tall), jnp.float32), ((tall, CLUSTER_COUNT), jnp.bfloat16)]
     lefts = [((EARLY, 3 * width), jnp.bfloat16), ((EARLY, 1), jnp.float32)]
     early = ((EARLY, CLUSTER_COUNT), jnp.float32)
     left, squares, *own_sides, own_high, own_low, weighted = on_chip(
-        own_pair_kernel, "own_pairs", [*lefts, *sides, kept, kept, early], [*rows[:6], columns]
+        own_pair_kernel, "own_pairs", [*lefts, *sides, kept, kept, early], [*rows[:4], columns]
     )
     *other_sides, other_high, other_low, weighted = on_chip(
         other_pair_kernel,

time: 99.7 us -> 101 us (1.013)
  waiting for transfers between devices: 9.55 us -> 12.8 us
  blocking collectives: 53.3 us -> 51.1 us
    ppermute x7, waiting for transfers between devices: 7.96 us -> 9.78 us  [moved(): return lax.ppermute(x, EVERY, pairs)]
    all_to_all x1, waiting for transfers between devices: 0.01 us -> 1.47 us  [exchange_columns(): lax.all_to_all(blocks, EVERY, 0, 0, axis_index_groups=COLUMN_GROUPS, tile...]
    all_to_all x1, blocking collectives: 14.1 us -> 12.8 us  [exchange_columns(): lax.all_to_all(blocks, EVERY, 0, 0, axis_index_groups=COLUMN_GROUPS, tile...]
    pallas_call x7, Pallas kernels: 10.3 us -> 11.3 us  [on_chip(): pl.pallas_call(kernel, out_shape=shapes, in_specs=specs, out_specs=[vmem]...]
  transfers between devices with their start and end apart: 10 -> 10, of which waited for: 4 -> 6; matrix products, arithmetic and copies ran while one was open for 0% -> 0% of each run, Pallas kernels for 5% -> 4%
where the time goes in v22:
time: 101 us
  blocking collectives  51.1 us (51%)
  starting transfers between devices  23.1 us (23%)
  Pallas kernels  13.4 us (13%)
  waiting for transfers between devices  12.8 us (13%)
    all_to_all x2, blocking collectives, exchange_rows(): return lax.all_to_all(blocks, ('y_lo', 'x'), 0, 0, tiled=True)  24.5 us
    all_to_all x1, blocking collectives, shards(): parts = lax.all_to_all(copies(part, 128), EVERY, 0, 0, tiled=True)  13.8 us
    all_to_all x1, blocking collectives, exchange_columns(): lax.all_to_all(blocks, EVERY, 0, 0, axis_index_groups=COLUMN_GROUPS, tile...  12.8 us
    pallas_call x7, Pallas kernels, on_chip(): pl.pallas_call(kernel, out_shape=shapes, in_specs=specs, out_specs=[vmem]...  11.3 us
    ppermute x7, waiting for transfers between devices, moved(): return lax.ppermute(x, EVERY, pairs)  9.78 us
    all_to_all x1, starting transfers between devices, exchange_columns(): lax.all_to_all(blocks, EVERY, 0, 0, axis_index_groups=COLUMN_GROUPS, tile...  8.46 us
    ppermute x7, starting transfers between devices, moved(): return lax.ppermute(x, EVERY, pairs)  8.31 us
    ppermute x2, starting transfers between devices, other_core(): return lax.ppermute(x, 'core', [(0, 1), (1, 0)])  6.31 us
  transfers between devices with their start and end apart: 10, of which 6 were waited for; matrix products, arithmetic and copies ran while one was open for 0% of the time, Pallas kernels for 4%

profile of v22, /device:TPU:1, one launch (start us, length us, event | category | flops | bytes accessed | tf_op | source)
XLA Modules:
  0.0 100.5 jit_solution(6572877475257288072)
XLA Ops:
  0.0 2.1 %prepare.1 = (f32[136,256]{1,0:T(8,128)}, f32[8,136,256]{2,1,0:T(8,128)}) custom-call(f32[128,256]{1,0:T(8,128)} %embedding.1, s32[1,128]{1,0:T(1,128)} %bitcast.7), custom_call_target="tpu_custom_call" | custom-call | tf_op jit(solution)/shard_map/prepare/pallas_call | solution.py:267
  2.1 8.5 %all-to-all-start = ((f32[8,136,256]{2,1,0:T(8,128)}), f32[8,136,256]{2,1,0:T(8,128)S(1)}, u32[]{:S(2)}, u32[]{:S(2)}) async-start(f32[8,136,256]{2,1,0:T(8,128)} %get-tuple-element.38), calls=%async_computation | async-start | bytes 2228224 | tf_op jit(solution)/shard_map/all_to_all | solution.py:40
  10.6 2.8 %collective-permute-start.3 = (f32[136,256]{1,0:T(8,128)S(1)}, f32[136,256]{1,0:T(8,128)S(1)}, u32[]{:S(2)}, u32[]{:S(2)}) collective-permute-start(f32[136,256]{1,0:T(8,128)S(1)} %copy-done), channel_id=1, source_target_pairs={{4,0},{5,1},{6,2},{7,3},{0,4},{1,5},{2,6},{3,7},{12,8},{13,9},{14,... | collective-permute-start | bytes 417800 | tf_op jit(solution)/shard_map/ppermute | solution.py:47
  13.4 0.6 collective-permute-start.2
  14.1 1.7 %collective-permute-start.1 = (f32[136,256]{1,0:T(8,128)S(1)}, f32[136,256]{1,0:T(8,128)S(1)}, u32[]{:S(2)}, u32[]{:S(2)}) collective-permute-start(f32[136,256]{1,0:T(8,128)S(1)} %copy-done), channel_id=1, source_target_pairs={{70,0},{71,1},{64,2},{65,3},{66,4},{67,5},{68,6},{69,7},{78,8},{79... | collective-permute-start | bytes 417800 | tf_op jit(solution)/shard_map/ppermute | solution.py:47
  15.8 0.6 collective-permute-start
  16.4 4.3 %collective-permute-done.2.refs_3_ = f32[136,256]{1,0:T(8,128)S(1)} collective-permute-done((f32[136,256]{1,0:T(8,128)S(1)}, f32[136,256]{1,0:T(8,128)S(1)}, u32[]{:S(2)}, u32[]{:S(2)}) %collective-permute-start.2) | collective-permute-done | bytes 139296 | tf_op jit(solution)/shard_map/ppermute | solution.py:47
  21.3 2.4 %collective-permute-done.refs_1_ = f32[136,256]{1,0:T(8,128)S(1)} collective-permute-done((f32[136,256]{1,0:T(8,128)S(1)}, f32[136,256]{1,0:T(8,128)S(1)}, u32[]{:S(2)}, u32[]{:S(2)}) %collective-permute-start) | collective-permute-done | bytes 139296 | tf_op jit(solution)/shard_map/ppermute | solution.py:47
  23.8 1.5 %all-to-all-done.refs_4_ = f32[8,136,256]{2,1,0:T(8,128)S(1)} async-done(((f32[8,136,256]{2,1,0:T(8,128)}), f32[8,136,256]{2,1,0:T(8,128)S(1)}, u32[]{:S(2)}, u32[]{:S(2)}) %all-to-all-start) | async-done | bytes 1114144 | tf_op jit(solution)/shard_map/all_to_all | solution.py:40
  25.2 2.5 %collective-permute-start.7 = (f32[8,136,256]{2,1,0:T(8,128)S(1)}, f32[8,136,256]{2,1,0:T(8,128)S(1)}, u32[]{:S(2)}, u32[]{:S(2)}) collective-permute-start(f32[8,136,256]{2,1,0:T(8,128)S(1)} %all-to-all-done.refs_4_), channel_id=1, source_target_pairs={{0,1},{1,0},{2,3},{3,2},{4,5},{5,4},{6,7},{7,6},{8,9},{9,8},{10,11... | collective-permute-start | bytes 3342344 | tf_op jit(solution)/shard_map/ppermute | solution.py:253
  27.7 0.7 collective-permute-start.6
  28.4 1.8 %collective-permute-start.5 = (f32[136,256]{1,0:T(8,128)S(1)}, f32[136,256]{1,0:T(8,128)S(1)}, u32[]{:S(2)}, u32[]{:S(2)}) collective-permute-start(f32[136,256]{1,0:T(8,128)S(1)} %copy-done), channel_id=1, source_target_pairs={{2,0},{3,1},{4,2},{5,3},{6,4},{7,5},{0,6},{1,7},{10,8},{11,9},{12,... | collective-permute-start | bytes 417800 | tf_op jit(solution)/shard_map/ppermute | solution.py:47
  30.2 1.9 %own_pairs.1 = (bf16[512,768]{1,0:T(8,128)(2,1)S(1)}, f32[512,1]{1,0:T(8,128)S(1)}, bf16[1024,768]{1,0:T(8,128)(2,1)S(1)}, f32[8,1024]{1,0:T(8,128)S(1)}, bf16[1...) custom-call(f32[136,256]{1,0:T(8,128)S(1)} %copy-done, ...), custom_call_target="tpu_custom_call" | custom-call | tf_op jit(solution)/shard_map/own_pairs/pallas_call | solution.py:236
  32.1 1.8 %other_pairs.1 = (bf16[1024,768]{1,0:T(8,128)(2,1)S(1)}, f32[8,1024]{1,0:T(8,128)S(1)}, bf16[1024,128]{1,0:T(8,128)(2,1)S(1)}, bf16[1024,1024]{1,0:T(8,128)(2,1)...) custom-call(f32[8,136,256]{2,1,0:T(8,128)S(1)} %collective-permute-done.7.columns, ...), custom_call_target="tpu_custom_call" | custom-call | tf_op jit(solution)/shard_map/other_pairs/pallas_call | solution.py:236
  33.9 2.4 %collective-permute-done.4.refs_5_ = f32[136,256]{1,0:T(8,128)S(1)} collective-permute-done((f32[136,256]{1,0:T(8,128)S(1)}, f32[136,256]{1,0:T(8,128)S(1)}, u32[]{:S(2)}, u32[]{:S(2)}) %collective-permute-start.4) | collective-permute-done | bytes 139296 | tf_op jit(solution)/shard_map/ppermute | solution.py:47
  36.4 4.0 %late_pairs.1 = (bf16[1024,1024]{1,0:T(8,128)(2,1)S(1)}, bf16[1024,1024]{1,0:T(8,128)(2,1)S(1)}, bf16[1024,1024]{1,0:T(8,128)(2,1)S(1)}, bf16[1024,1024]{1,0:T(8,128)(2,1)S(1)}, f32[8,136,128]{2,1,0:T(8,128)S(1)}) custom-call(f32[136,256]{1,0:T(8,128)S(1)} %copy-done, ...), custom_call_target="tpu_custom_call", output_to_operand_aliasing={{0}: (15, {}), {1}: (16, {}), {2}: (17, {}), {3}: (18, {})} | custom-call | tf_op jit(solution)/shard_map/late_pairs/pallas_call | solution.py:236
  40.4 11.6 %all_to_all.25.blocks = f32[8,136,128]{2,1,0:T(8,128)S(1)} all-to-all(f32[8,136,128]{2,1,0:T(8,128)S(1)} %get-tuple-element.60), channel_id=1, replica_groups=mesh['y_lo'=2,'z'=4,'y_hi'=2,'x'=4,'core'=2] {'y_lo','x'}, dimensions={0} | all-to-all | bytes 1114112 | tf_op jit(solution)/shard_map/all_to_all | solution.py:36
  52.0 12.8 %all_to_all.26.own = f32[8,136,128]{2,1,0:T(8,128)S(1)} all-to-all(f32[8,136,128]{2,1,0:T(8,128)S(1)} %get-tuple-element.61), channel_id=1, replica_groups={{0,16,32,48,72,88,104,120},{1,17,33,49,73,89,105,121},{2,18,34,50,74,90..., dimensions={0} | all-to-all | bytes 1114112 | tf_op jit(solution)/shard_map/all_to_all | solution.py:40
  64.8 3.9 %collective-permute-start.8 = (f32[8,136,128]{2,1,0:T(8,128)S(1)}, f32[8,136,128]{2,1,0:T(8,128)S(1)}, u32[]{:S(2)}, u32[]{:S(2)}) collective-permute-start(f32[8,136,128]{2,1,0:T(8,128)S(1)} %all_to_all.26.own), channel_id=1, source_target_pairs={{0,1},{1,0},{2,3},{3,2},{4,5},{5,4},{6,7},{7,6},{8,9},{9,8},{10,11... | collective-permute-start | bytes 1671176 | tf_op jit(solution)/shard_map/ppermute | solution.py:253
  68.6 1.6 %collective-permute-done.8.other = f32[8,136,128]{2,1,0:T(8,128)S(1)} collective-permute-done((f32[8,136,128]{2,1,0:T(8,128)S(1)}, f32[8,136,128]{2,1,0:T(8,128)S(1)}, u32[]{:S(2)}, u32[]{:S(2)}) %collective-permute-start.8) | collective-permute-done | bytes 557088 | tf_op jit(solution)/shard_map/ppermute | solution.py:253
  70.2 2.7 %members.1 = (f32[8,136,128]{2,1,0:T(8,128)S(1)}, f32[128,128]{1,0:T(8,128)S(1)}) custom-call(f32[8,136,128]{2,1,0:T(8,128)S(1)} %all_to_all.26.own, f32[8,136,128]{2,1,0:T(8,128)S(1)} %collective-permute-done.8.other, bf16[1024,1024]{1,0:T(8,128)(2,1)S(1)} %get-tuple-element.62.own_high, bf16[1024,1024]{1,0:T(8,128)(2,1)S(1)} %get-tuple-element.63.own_low, ...), custom_call_target="tpu_custom_call" | custom-call | tf_op jit(solution)/shard_map/members/pallas_call | solution.py:236
  72.9 12.9 %all_to_all.27.blocks = f32[8,136,128]{2,1,0:T(8,128)S(1)} all-to-all(f32[8,136,128]{2,1,0:T(8,128)S(1)} %get-tuple-element.67), channel_id=1, replica_groups=mesh['y_lo'=2,'z'=4,'y_hi'=2,'x'=4,'core'=2] {'y_lo','x'}, dimensions={0} | all-to-all | bytes 1114112 | tf_op jit(solution)/shard_map/all_to_all | solution.py:36
  85.9 13.8 %all_to_all.28 = f32[128,1,128]{2,1,0:T(1,128)S(1)} all-to-all(f32[128,1,128]{2,1,0:T(1,128)S(1)} %broadcast_in_dim.3), channel_id=1, replica_groups=mesh['y_lo'=2,'z'=4,'y_hi'=2,'x'=4,'core'=2] {'y_lo','z','y_hi','x','core'}, dimensions={0} | all-to-all | bytes 131072 | tf_op jit(solution)/shard_map/all_to_all | solution.py:313
  99.7 0.8 final.1
  (12 shorter events, 0.7 us)
Async XLA Ops:
  2.1 8.5 %copy-start = (f32[136,256]{1,0:T(8,128)S(1)}, f32[136,256]{1,0:T(8,128)}, u32[]{:S(2)}) copy-start(f32[136,256]{1,0:T(8,128)} %get-tuple-element.40.refs_0_) | copy-start | bytes 417796
  2.1 23.1 %all-to-all-start = ((f32[8,136,256]{2,1,0:T(8,128)}), f32[8,136,256]{2,1,0:T(8,128)S(1)}, u32[]{:S(2)}, u32[]{:S(2)}) async-start(f32[8,136,256]{2,1,0:T(8,128)} %get-tuple-element.38), calls=%async_computation | async-start | bytes 2228224 | tf_op jit(solution)/shard_map/all_to_all | solution.py:40
  10.6 5.8 %collective-permute-start.3 = (f32[136,256]{1,0:T(8,128)S(1)}, f32[136,256]{1,0:T(8,128)S(1)}, u32[]{:S(2)}, u32[]{:S(2)}) collective-permute-start(f32[136,256]{1,0:T(8,128)S(1)} %copy-done), channel_id=1, source_target_pairs={{4,0},{5,1},{6,2},{7,3},{0,4},{1,5},{2,6},{3,7},{12,8},{13,9},{14,... | collective-permute-start | bytes 417800 | tf_op jit(solution)/shard_map/ppermute | solution.py:47
  13.4 7.3 %collective-permute-start.2 = (f32[136,256]{1,0:T(8,128)S(1)}, f32[136,256]{1,0:T(8,128)S(1)}, u32[]{:S(2)}, u32[]{:S(2)}) collective-permute-start(f32[136,256]{1,0:T(8,128)S(1)} %copy-done), channel_id=1, source_target_pairs={{66,0},{67,1},{68,2},{69,3},{70,4},{71,5},{64,6},{65,7},{74,8},{75... | collective-permute-start | bytes 417800 | tf_op jit(solution)/shard_map/ppermute | solution.py:47
  14.1 7.3 %collective-permute-start.1 = (f32[136,256]{1,0:T(8,128)S(1)}, f32[136,256]{1,0:T(8,128)S(1)}, u32[]{:S(2)}, u32[]{:S(2)}) collective-permute-start(f32[136,256]{1,0:T(8,128)S(1)} %copy-done), channel_id=1, source_target_pairs={{70,0},{71,1},{64,2},{65,3},{66,4},{67,5},{68,6},{69,7},{78,8},{79... | collective-permute-start | bytes 417800 | tf_op jit(solution)/shard_map/ppermute | solution.py:47
  15.8 8.0 %collective-permute-start = (f32[136,256]{1,0:T(8,128)S(1)}, f32[136,256]{1,0:T(8,128)S(1)}, u32[]{:S(2)}, u32[]{:S(2)}) collective-permute-start(f32[136,256]{1,0:T(8,128)S(1)} %copy-done), channel_id=1, source_target_pairs={{68,0},{69,1},{70,2},{71,3},{64,4},{65,5},{66,6},{67,7},{76,8},{77... | collective-permute-start | bytes 417800 | tf_op jit(solution)/shard_map/ppermute | solution.py:47
  25.2 6.8 %collective-permute-start.7 = (f32[8,136,256]{2,1,0:T(8,128)S(1)}, f32[8,136,256]{2,1,0:T(8,128)S(1)}, u32[]{:S(2)}, u32[]{:S(2)}) collective-permute-start(f32[8,136,256]{2,1,0:T(8,128)S(1)} %all-to-all-done.refs_4_), channel_id=1, source_target_pairs={{0,1},{1,0},{2,3},{3,2},{4,5},{5,4},{6,7},{7,6},{8,9},{9,8},{10,11... | collective-permute-start | bytes 3342344 | tf_op jit(solution)/shard_map/ppermute | solution.py:253
  27.7 6.2 %collective-permute-start.6 = (f32[136,256]{1,0:T(8,128)S(1)}, f32[136,256]{1,0:T(8,128)S(1)}, u32[]{:S(2)}, u32[]{:S(2)}) collective-permute-start(f32[136,256]{1,0:T(8,128)S(1)} %copy-done), channel_id=1, source_target_pairs={{64,0},{65,1},{66,2},{67,3},{68,4},{69,5},{70,6},{71,7},{72,8},{73... | collective-permute-start | bytes 417800 | tf_op jit(solution)/shard_map/ppermute | solution.py:47
  28.4 5.6 %collective-permute-start.5 = (f32[136,256]{1,0:T(8,128)S(1)}, f32[136,256]{1,0:T(8,128)S(1)}, u32[]{:S(2)}, u32[]{:S(2)}) collective-permute-start(f32[136,256]{1,0:T(8,128)S(1)} %copy-done), channel_id=1, source_target_pairs={{2,0},{3,1},{4,2},{5,3},{6,4},{7,5},{0,6},{1,7},{10,8},{11,9},{12,... | collective-permute-start | bytes 417800 | tf_op jit(solution)/shard_map/ppermute | solution.py:47
  30.2 6.2 %collective-permute-start.4 = (f32[136,256]{1,0:T(8,128)S(1)}, f32[136,256]{1,0:T(8,128)S(1)}, u32[]{:S(2)}, u32[]{:S(2)}) collective-permute-start(f32[136,256]{1,0:T(8,128)S(1)} %copy-done), channel_id=1, source_target_pairs={{6,0},{7,1},{0,2},{1,3},{2,4},{3,5},{4,6},{5,7},{14,8},{15,9},{8,1... | collective-permute-start | bytes 417800 | tf_op jit(solution)/shard_map/ppermute | solution.py:47
  64.8 5.4 %collective-permute-start.8 = (f32[8,136,128]{2,1,0:T(8,128)S(1)}, f32[8,136,128]{2,1,0:T(8,128)S(1)}, u32[]{:S(2)}, u32[]{:S(2)}) collective-permute-start(f32[8,136,128]{2,1,0:T(8,128)S(1)} %all_to_all.26.own), channel_id=1, source_target_pairs={{0,1},{1,0},{2,3},{3,2},{4,5},{5,4},{6,7},{7,6},{8,9},{9,8},{10,11... | collective-permute-start | bytes 1671176 | tf_op jit(solution)/shard_map/ppermute | solution.py:253

commit v23 on v19

--- a/solution.py
+++ b/solution.py
@@ -29,7 +29,7 @@
 
 
 COLUMN_GROUPS = column_groups()
-ROW_ORDER = ((0, 0), (0, 3), (0, 2), (1, 1), (1, 3), (1, 2), (0, 1), (1, 0))
+ROW_ORDER = ((0, 0), (1, 2), (1, 3), (1, 0), (0, 2), (0, 1), (0, 3), (1, 1))
 
 
 def exchange_rows(blocks):

time: 101 us -> 99.5 us (0.985)
  blocking collectives: 54.5 us -> 53.2 us
    all_to_all x1, blocking collectives: 15.1 us -> 12.4 us  [exchange_columns(): lax.all_to_all(blocks, EVERY, 0, 0, axis_index_groups=COLUMN_GROUPS, tile...]
    ppermute x2, starting transfers between devices: 4.67 us -> 6.06 us  [other_core(): return lax.ppermute(x, 'core', [(0, 1), (1, 0)])]
    all_to_all x2, blocking collectives: 25.5 us -> 26.9 us  [exchange_rows(): return lax.all_to_all(blocks, ('y_lo', 'x'), 0, 0, tiled=True)]
    ppermute x7, starting transfers between devices: 9.35 us -> 8.13 us  [moved(): return lax.ppermute(x, EVERY, pairs)]
    all_to_all x1, waiting for transfers between devices: 0.01 us -> 1.18 us  [exchange_columns(): lax.all_to_all(blocks, EVERY, 0, 0, axis_index_groups=COLUMN_GROUPS, tile...]
  transfers between devices with their start and end apart: 10 -> 10, of which waited for: 4 -> 6; matrix products, arithmetic and copies ran while one was open for 0% -> 0% of each run, Pallas kernels for 5% -> 5%
where the time goes in v23:
time: 99.5 us; the launch traced here: 99.2 us
  blocking collectives  53.2 us (53%)
  starting transfers between devices  22.6 us (23%)
  Pallas kernels  12.4 us (12%)
  waiting for transfers between devices  10.8 us (11%)
    all_to_all x2, blocking collectives, exchange_rows(): return lax.all_to_all(blocks, ('y_lo', 'x'), 0, 0, tiled=True)  26.9 us
    all_to_all x1, blocking collectives, shards(): parts = lax.all_to_all(copies(part, 128), EVERY, 0, 0, tiled=True)  13.9 us
    all_to_all x1, blocking collectives, exchange_columns(): lax.all_to_all(blocks, EVERY, 0, 0, axis_index_groups=COLUMN_GROUPS, tile...  12.4 us
    pallas_call x7, Pallas kernels, on_chip(): pl.pallas_call(kernel, out_shape=shapes, in_specs=specs, out_specs=[vmem]...  10.3 us
    all_to_all x1, starting transfers between devices, exchange_columns(): lax.all_to_all(blocks, EVERY, 0, 0, axis_index_groups=COLUMN_GROUPS, tile...  8.46 us
    ppermute x7, starting transfers between devices, moved(): return lax.ppermute(x, EVERY, pairs)  8.13 us
    ppermute x7, waiting for transfers between devices, moved(): return lax.ppermute(x, EVERY, pairs)  8.07 us
    ppermute x2, starting transfers between devices, other_core(): return lax.ppermute(x, 'core', [(0, 1), (1, 0)])  6.06 us
  transfers between devices with their start and end apart: 10, of which 6 were waited for; matrix products, arithmetic and copies ran while one was open for 0% of the time, Pallas kernels for 5%

profile of v23, /device:TPU:1, one launch (start us, length us, event | category | flops | bytes accessed | tf_op | source)
XLA Modules:
  0.0 99.2 jit_solution(1781226246848665303)
XLA Ops:
  0.0 2.1 %prepare.1 = (f32[136,256]{1,0:T(8,128)}, f32[8,136,256]{2,1,0:T(8,128)}) custom-call(f32[128,256]{1,0:T(8,128)} %embedding.1, s32[1,128]{1,0:T(1,128)} %bitcast.7), custom_call_target="tpu_custom_call" | custom-call | tf_op jit(solution)/shard_map/prepare/pallas_call | solution.py:266
  2.1 8.5 %all-to-all-start = ((f32[8,136,256]{2,1,0:T(8,128)}), f32[8,136,256]{2,1,0:T(8,128)S(1)}, u32[]{:S(2)}, u32[]{:S(2)}) async-start(f32[8,136,256]{2,1,0:T(8,128)} %get-tuple-element.39), calls=%async_computation | async-start | bytes 2228224 | tf_op jit(solution)/shard_map/all_to_all | solution.py:40
  10.6 2.5 %collective-permute-start.4 = (f32[136,256]{1,0:T(8,128)S(1)}, f32[136,256]{1,0:T(8,128)S(1)}, u32[]{:S(2)}, u32[]{:S(2)}) collective-permute-start(f32[136,256]{1,0:T(8,128)S(1)} %copy-done), channel_id=1, source_target_pairs={{2,0},{3,1},{4,2},{5,3},{6,4},{7,5},{0,6},{1,7},{10,8},{11,9},{12,... | collective-permute-start | bytes 417800 | tf_op jit(solution)/shard_map/ppermute | solution.py:47
  13.1 0.5 collective-permute-start.3
  13.7 1.7 %collective-permute-start.1 = (f32[136,256]{1,0:T(8,128)S(1)}, f32[136,256]{1,0:T(8,128)S(1)}, u32[]{:S(2)}, u32[]{:S(2)}) collective-permute-start(f32[136,256]{1,0:T(8,128)S(1)} %copy-done), channel_id=1, source_target_pairs={{70,0},{71,1},{64,2},{65,3},{66,4},{67,5},{68,6},{69,7},{78,8},{79... | collective-permute-start | bytes 417800 | tf_op jit(solution)/shard_map/ppermute | solution.py:47
  15.5 1.8 %collective-permute-start = (f32[136,256]{1,0:T(8,128)S(1)}, f32[136,256]{1,0:T(8,128)S(1)}, u32[]{:S(2)}, u32[]{:S(2)}) collective-permute-start(f32[136,256]{1,0:T(8,128)S(1)} %copy-done), channel_id=1, source_target_pairs={{68,0},{69,1},{70,2},{71,3},{64,4},{65,5},{66,6},{67,7},{76,8},{77... | collective-permute-start | bytes 417800 | tf_op jit(solution)/shard_map/ppermute | solution.py:47
  17.3 1.5 %collective-permute-done.3.refs_4_ = f32[136,256]{1,0:T(8,128)S(1)} collective-permute-done((f32[136,256]{1,0:T(8,128)S(1)}, f32[136,256]{1,0:T(8,128)S(1)}, u32[]{:S(2)}, u32[]{:S(2)}) %collective-permute-start.3) | collective-permute-done | bytes 139296 | tf_op jit(solution)/shard_map/ppermute | solution.py:47
  18.9 2.2 %collective-permute-done.1.refs_2_ = f32[136,256]{1,0:T(8,128)S(1)} collective-permute-done((f32[136,256]{1,0:T(8,128)S(1)}, f32[136,256]{1,0:T(8,128)S(1)}, u32[]{:S(2)}, u32[]{:S(2)}) %collective-permute-start.1) | collective-permute-done | bytes 139296 | tf_op jit(solution)/shard_map/ppermute | solution.py:47
  21.1 3.0 %collective-permute-done.refs_1_ = f32[136,256]{1,0:T(8,128)S(1)} collective-permute-done((f32[136,256]{1,0:T(8,128)S(1)}, f32[136,256]{1,0:T(8,128)S(1)}, u32[]{:S(2)}, u32[]{:S(2)}) %collective-permute-start) | collective-permute-done | bytes 139296 | tf_op jit(solution)/shard_map/ppermute | solution.py:47
  24.1 1.2 %all-to-all-done.refs_6_ = f32[8,136,256]{2,1,0:T(8,128)S(1)} async-done(((f32[8,136,256]{2,1,0:T(8,128)}), f32[8,136,256]{2,1,0:T(8,128)S(1)}, u32[]{:S(2)}, u32[]{:S(2)}) %all-to-all-start) | async-done | bytes 1114144 | tf_op jit(solution)/shard_map/all_to_all | solution.py:40
  25.2 2.5 %collective-permute-start.7 = (f32[8,136,256]{2,1,0:T(8,128)S(1)}, f32[8,136,256]{2,1,0:T(8,128)S(1)}, u32[]{:S(2)}, u32[]{:S(2)}) collective-permute-start(f32[8,136,256]{2,1,0:T(8,128)S(1)} %all-to-all-done.refs_6_), channel_id=1, source_target_pairs={{0,1},{1,0},{2,3},{3,2},{4,5},{5,4},{6,7},{7,6},{8,9},{9,8},{10,11... | collective-permute-start | bytes 3342344 | tf_op jit(solution)/shard_map/ppermute | solution.py:252
  27.7 1.4 %collective-permute-start.6 = (f32[136,256]{1,0:T(8,128)S(1)}, f32[136,256]{1,0:T(8,128)S(1)}, u32[]{:S(2)}, u32[]{:S(2)}) collective-permute-start(f32[136,256]{1,0:T(8,128)S(1)} %copy-done), channel_id=1, source_target_pairs={{66,0},{67,1},{68,2},{69,3},{70,4},{71,5},{64,6},{65,7},{74,8},{75... | collective-permute-start | bytes 417800 | tf_op jit(solution)/shard_map/ppermute | solution.py:47
  29.1 2.5 %own_pairs.1 = (bf16[768,768]{1,0:T(8,128)(2,1)S(1)}, f32[768,1]{1,0:T(8,128)S(1)}, bf16[1024,768]{1,0:T(8,128)(2,1)S(1)}, f32[8,1024]{1,0:T(8,128)S(1)}, bf16[1...) custom-call(f32[136,256]{1,0:T(8,128)S(1)} %copy-done, ...), custom_call_target="tpu_custom_call" | custom-call | tf_op jit(solution)/shard_map/own_pairs/pallas_call | solution.py:235
  31.6 2.4 %other_pairs.1 = (bf16[1024,768]{1,0:T(8,128)(2,1)S(1)}, f32[8,1024]{1,0:T(8,128)S(1)}, bf16[1024,128]{1,0:T(8,128)(2,1)S(1)}, bf16[1024,1024]{1,0:T(8,128)(2,1)...) custom-call(f32[8,136,256]{2,1,0:T(8,128)S(1)} %collective-permute-done.7.columns, ...), custom_call_target="tpu_custom_call" | custom-call | tf_op jit(solution)/shard_map/other_pairs/pallas_call | solution.py:235
  34.0 1.3 %collective-permute-done.5.refs_6_ = f32[136,256]{1,0:T(8,128)S(1)} collective-permute-done((f32[136,256]{1,0:T(8,128)S(1)}, f32[136,256]{1,0:T(8,128)S(1)}, u32[]{:S(2)}, u32[]{:S(2)}) %collective-permute-start.5) | collective-permute-done | bytes 139296 | tf_op jit(solution)/shard_map/ppermute | solution.py:47
  35.3 1.8 %late_pairs.1 = (bf16[1024,1024]{1,0:T(8,128)(2,1)S(1)}, bf16[1024,1024]{1,0:T(8,128)(2,1)S(1)}, bf16[1024,1024]{1,0:T(8,128)(2,1)S(1)}, bf16[1024,1024]{1,0:T(8,128)(2,1)S(1)}, f32[8,136,128]{2,1,0:T(8,128)S(1)}) custom-call(f32[136,256]{1,0:T(8,128)S(1)} %copy-done, ...), custom_call_target="tpu_custom_call", output_to_operand_aliasing={{0}: (15, {}), {1}: (16, {}), {2}: (17, {}), {3}: (18, {})} | custom-call | tf_op jit(solution)/shard_map/late_pairs/pallas_call | solution.py:235
  37.1 14.0 %all_to_all.25.blocks = f32[8,136,128]{2,1,0:T(8,128)S(1)} all-to-all(f32[8,136,128]{2,1,0:T(8,128)S(1)} %get-tuple-element.62), channel_id=1, replica_groups=mesh['y_lo'=2,'z'=4,'y_hi'=2,'x'=4,'core'=2] {'y_lo','x'}, dimensions={0} | all-to-all | bytes 1114112 | tf_op jit(solution)/shard_map/all_to_all | solution.py:36
  51.2 12.4 %all_to_all.26.own = f32[8,136,128]{2,1,0:T(8,128)S(1)} all-to-all(f32[8,136,128]{2,1,0:T(8,128)S(1)} %get-tuple-element.63), channel_id=1, replica_groups={{0,16,32,48,72,88,104,120},{1,17,33,49,73,89,105,121},{2,18,34,50,74,90..., dimensions={0} | all-to-all | bytes 1114112 | tf_op jit(solution)/shard_map/all_to_all | solution.py:40
  63.6 3.6 %collective-permute-start.8 = (f32[8,136,128]{2,1,0:T(8,128)S(1)}, f32[8,136,128]{2,1,0:T(8,128)S(1)}, u32[]{:S(2)}, u32[]{:S(2)}) collective-permute-start(f32[8,136,128]{2,1,0:T(8,128)S(1)} %all_to_all.26.own), channel_id=1, source_target_pairs={{0,1},{1,0},{2,3},{3,2},{4,5},{5,4},{6,7},{7,6},{8,9},{9,8},{10,11... | collective-permute-start | bytes 1671176 | tf_op jit(solution)/shard_map/ppermute | solution.py:252
  67.2 1.6 %collective-permute-done.8.other = f32[8,136,128]{2,1,0:T(8,128)S(1)} collective-permute-done((f32[8,136,128]{2,1,0:T(8,128)S(1)}, f32[8,136,128]{2,1,0:T(8,128)S(1)}, u32[]{:S(2)}, u32[]{:S(2)}) %collective-permute-start.8) | collective-permute-done | bytes 557088 | tf_op jit(solution)/shard_map/ppermute | solution.py:252
  68.7 2.7 %members.1 = (f32[8,136,128]{2,1,0:T(8,128)S(1)}, f32[128,128]{1,0:T(8,128)S(1)}) custom-call(f32[8,136,128]{2,1,0:T(8,128)S(1)} %all_to_all.26.own, f32[8,136,128]{2,1,0:T(8,128)S(1)} %collective-permute-done.8.other, bf16[1024,1024]{1,0:T(8,128)(2,1)S(1)} %get-tuple-element.64.own_high, bf16[1024,1024]{1,0:T(8,128)(2,1)S(1)} %get-tuple-element.65.own_low, ...), custom_call_target="tpu_custom_call" | custom-call | tf_op jit(solution)/shard_map/members/pallas_call | solution.py:235
  71.4 12.9 %all_to_all.27.blocks = f32[8,136,128]{2,1,0:T(8,128)S(1)} all-to-all(f32[8,136,128]{2,1,0:T(8,128)S(1)} %get-tuple-element.69), channel_id=1, replica_groups=mesh['y_lo'=2,'z'=4,'y_hi'=2,'x'=4,'core'=2] {'y_lo','x'}, dimensions={0} | all-to-all | bytes 1114112 | tf_op jit(solution)/shard_map/all_to_all | solution.py:36
  84.4 13.9 %all_to_all.28 = f32[128,1,128]{2,1,0:T(1,128)S(1)} all-to-all(f32[128,1,128]{2,1,0:T(1,128)S(1)} %broadcast_in_dim.3), channel_id=1, replica_groups=mesh['y_lo'=2,'z'=4,'y_hi'=2,'x'=4,'core'=2] {'y_lo','z','y_hi','x','core'}, dimensions={0} | all-to-all | bytes 131072 | tf_op jit(solution)/shard_map/all_to_all | solution.py:312
  98.4 0.8 final.1
  (12 shorter events, 0.3 us)
Async XLA Ops:
  2.1 8.5 %copy-start = (f32[136,256]{1,0:T(8,128)S(1)}, f32[136,256]{1,0:T(8,128)}, u32[]{:S(2)}) copy-start(f32[136,256]{1,0:T(8,128)} %get-tuple-element.41.refs_0_) | copy-start | bytes 417796
  2.1 23.1 %all-to-all-start = ((f32[8,136,256]{2,1,0:T(8,128)}), f32[8,136,256]{2,1,0:T(8,128)S(1)}, u32[]{:S(2)}, u32[]{:S(2)}) async-start(f32[8,136,256]{2,1,0:T(8,128)} %get-tuple-element.39), calls=%async_computation | async-start | bytes 2228224 | tf_op jit(solution)/shard_map/all_to_all | solution.py:40
  10.6 6.7 %collective-permute-start.4 = (f32[136,256]{1,0:T(8,128)S(1)}, f32[136,256]{1,0:T(8,128)S(1)}, u32[]{:S(2)}, u32[]{:S(2)}) collective-permute-start(f32[136,256]{1,0:T(8,128)S(1)} %copy-done), channel_id=1, source_target_pairs={{2,0},{3,1},{4,2},{5,3},{6,4},{7,5},{0,6},{1,7},{10,8},{11,9},{12,... | collective-permute-start | bytes 417800 | tf_op jit(solution)/shard_map/ppermute | solution.py:47
  13.1 5.7 %collective-permute-start.3 = (f32[136,256]{1,0:T(8,128)S(1)}, f32[136,256]{1,0:T(8,128)S(1)}, u32[]{:S(2)}, u32[]{:S(2)}) collective-permute-start(f32[136,256]{1,0:T(8,128)S(1)} %copy-done), channel_id=1, source_target_pairs={{4,0},{5,1},{6,2},{7,3},{0,4},{1,5},{2,6},{3,7},{12,8},{13,9},{14,... | collective-permute-start | bytes 417800 | tf_op jit(solution)/shard_map/ppermute | solution.py:47
  13.7 5.2 %collective-permute-start.2 = (f32[136,256]{1,0:T(8,128)S(1)}, f32[136,256]{1,0:T(8,128)S(1)}, u32[]{:S(2)}, u32[]{:S(2)}) collective-permute-start(f32[136,256]{1,0:T(8,128)S(1)} %copy-done), channel_id=1, source_target_pairs={{64,0},{65,1},{66,2},{67,3},{68,4},{69,5},{70,6},{71,7},{72,8},{73... | collective-permute-start | bytes 417800 | tf_op jit(solution)/shard_map/ppermute | solution.py:47
  13.7 7.3 %collective-permute-start.1 = (f32[136,256]{1,0:T(8,128)S(1)}, f32[136,256]{1,0:T(8,128)S(1)}, u32[]{:S(2)}, u32[]{:S(2)}) collective-permute-start(f32[136,256]{1,0:T(8,128)S(1)} %copy-done), channel_id=1, source_target_pairs={{70,0},{71,1},{64,2},{65,3},{66,4},{67,5},{68,6},{69,7},{78,8},{79... | collective-permute-start | bytes 417800 | tf_op jit(solution)/shard_map/ppermute | solution.py:47
  15.5 8.6 %collective-permute-start = (f32[136,256]{1,0:T(8,128)S(1)}, f32[136,256]{1,0:T(8,128)S(1)}, u32[]{:S(2)}, u32[]{:S(2)}) collective-permute-start(f32[136,256]{1,0:T(8,128)S(1)} %copy-done), channel_id=1, source_target_pairs={{68,0},{69,1},{70,2},{71,3},{64,4},{65,5},{66,6},{67,7},{76,8},{77... | collective-permute-start | bytes 417800 | tf_op jit(solution)/shard_map/ppermute | solution.py:47
  25.2 6.4 %collective-permute-start.7 = (f32[8,136,256]{2,1,0:T(8,128)S(1)}, f32[8,136,256]{2,1,0:T(8,128)S(1)}, u32[]{:S(2)}, u32[]{:S(2)}) collective-permute-start(f32[8,136,256]{2,1,0:T(8,128)S(1)} %all-to-all-done.refs_6_), channel_id=1, source_target_pairs={{0,1},{1,0},{2,3},{3,2},{4,5},{5,4},{6,7},{7,6},{8,9},{9,8},{10,11... | collective-permute-start | bytes 3342344 | tf_op jit(solution)/shard_map/ppermute | solution.py:252
  27.7 6.3 %collective-permute-start.6 = (f32[136,256]{1,0:T(8,128)S(1)}, f32[136,256]{1,0:T(8,128)S(1)}, u32[]{:S(2)}, u32[]{:S(2)}) collective-permute-start(f32[136,256]{1,0:T(8,128)S(1)} %copy-done), channel_id=1, source_target_pairs={{66,0},{67,1},{68,2},{69,3},{70,4},{71,5},{64,6},{65,7},{74,8},{75... | collective-permute-start | bytes 417800 | tf_op jit(solution)/shard_map/ppermute | solution.py:47
  29.1 6.2 %collective-permute-start.5 = (f32[136,256]{1,0:T(8,128)S(1)}, f32[136,256]{1,0:T(8,128)S(1)}, u32[]{:S(2)}, u32[]{:S(2)}) collective-permute-start(f32[136,256]{1,0:T(8,128)S(1)} %copy-done), channel_id=1, source_target_pairs={{6,0},{7,1},{0,2},{1,3},{2,4},{3,5},{4,6},{5,7},{14,8},{15,9},{8,1... | collective-permute-start | bytes 417800 | tf_op jit(solution)/shard_map/ppermute | solution.py:47
  63.6 5.2 %collective-permute-start.8 = (f32[8,136,128]{2,1,0:T(8,128)S(1)}, f32[8,136,128]{2,1,0:T(8,128)S(1)}, u32[]{:S(2)}, u32[]{:S(2)}) collective-permute-start(f32[8,136,128]{2,1,0:T(8,128)S(1)} %all_to_all.26.own), channel_id=1, source_target_pairs={{0,1},{1,0},{2,3},{3,2},{4,5},{5,4},{6,7},{7,6},{8,9},{9,8},{10,11... | collective-permute-start | bytes 1671176 | tf_op jit(solution)/shard_map/ppermute | solution.py:252

commit v24 on v20

--- a/solution.py
+++ b/solution.py
@@ -29,7 +29,7 @@
 
 
 COLUMN_GROUPS = column_groups()
-ROW_ORDER = ((0, 0), (1, 2), (1, 3), (1, 1), (0, 2), (0, 3), (0, 1), (1, 0))
+ROW_ORDER = ((0, 0), (1, 2), (1, 3), (1, 0), (0, 2), (0, 1), (0, 3), (1, 1))
 
 
 def exchange_rows(blocks):

time: 99.8 us -> 99.6 us (level)
  starting transfers between devices: 24.4 us -> 23 us
  waiting for transfers between devices: 8.85 us -> 10.1 us
    all_to_all x1, blocking collectives: 14.1 us -> 12.4 us  [exchange_columns(): lax.all_to_all(blocks, EVERY, 0, 0, axis_index_groups=COLUMN_GROUPS, tile...]
    all_to_all x2, blocking collectives: 25.4 us -> 26.9 us  [exchange_rows(): return lax.all_to_all(blocks, ('y_lo', 'x'), 0, 0, tiled=True)]
    all_to_all x1, waiting for transfers between devices: 0.01 us -> 1.18 us  [exchange_columns(): lax.all_to_all(blocks, EVERY, 0, 0, axis_index_groups=COLUMN_GROUPS, tile...]
    ppermute x7, starting transfers between devices: 9.29 us -> 8.13 us  [moved(): return lax.ppermute(x, EVERY, pairs)]
  transfers between devices with their start and end apart: 11 -> 11, of which waited for: 5 -> 7; matrix products, arithmetic and copies ran while one was open for 0% -> 0% of each run, Pallas kernels for 6% -> 6%
where the time goes in v24:
time: 99.6 us; the launch traced here: 99.3 us
  blocking collectives  53.2 us (53%)
  starting transfers between devices  23 us (23%)
  Pallas kernels  12.9 us (13%)
  waiting for transfers between devices  10.1 us (10%)
    all_to_all x2, blocking collectives, exchange_rows(): return lax.all_to_all(blocks, ('y_lo', 'x'), 0, 0, tiled=True)  26.9 us
    all_to_all x1, blocking collectives, shards(): parts = lax.all_to_all(copies(part, 128), EVERY, 0, 0, tiled=True)  13.9 us
    all_to_all x1, blocking collectives, exchange_columns(): lax.all_to_all(blocks, EVERY, 0, 0, axis_index_groups=COLUMN_GROUPS, tile...  12.4 us
    pallas_call x9, Pallas kernels, on_chip(): pl.pallas_call(kernel, out_shape=shapes, in_specs=specs, out_specs=[vmem]...  10.7 us
    all_to_all x1, starting transfers between devices, exchange_columns(): lax.all_to_all(blocks, EVERY, 0, 0, axis_index_groups=COLUMN_GROUPS, tile...  8.46 us
    ppermute x7, starting transfers between devices, moved(): return lax.ppermute(x, EVERY, pairs)  8.13 us
    ppermute x7, waiting for transfers between devices, moved(): return lax.ppermute(x, EVERY, pairs)  8.07 us
    ppermute x3, starting transfers between devices, other_core(): return lax.ppermute(x, 'core', [(0, 1), (1, 0)])  6.4 us
  transfers between devices with their start and end apart: 11, of which 7 were waited for; matrix products, arithmetic and copies ran while one was open for 0% of the time, Pallas kernels for 6%

profile of v24, /device:TPU:1, one launch (start us, length us, event | category | flops | bytes accessed | tf_op | source)
XLA Modules:
  0.0 99.3 jit_solution(6311324737472615863)
XLA Ops:
  0.0 2.1 %prepare.1 = (f32[136,256]{1,0:T(8,128)}, f32[8,136,256]{2,1,0:T(8,128)}) custom-call(f32[128,256]{1,0:T(8,128)} %embedding.1, s32[1,128]{1,0:T(1,128)} %bitcast.7), custom_call_target="tpu_custom_call" | custom-call | tf_op jit(solution)/shard_map/prepare/pallas_call | solution.py:278
  2.1 8.5 %all-to-all-start = ((f32[8,136,256]{2,1,0:T(8,128)}), f32[8,136,256]{2,1,0:T(8,128)S(1)}, u32[]{:S(2)}, u32[]{:S(2)}) async-start(f32[8,136,256]{2,1,0:T(8,128)} %get-tuple-element.42), calls=%async_computation | async-start | bytes 2228224 | tf_op jit(solution)/shard_map/all_to_all | solution.py:40
  10.6 2.5 %collective-permute-start.4 = (f32[136,256]{1,0:T(8,128)S(1)}, f32[136,256]{1,0:T(8,128)S(1)}, u32[]{:S(2)}, u32[]{:S(2)}) collective-permute-start(f32[136,256]{1,0:T(8,128)S(1)} %copy-done), channel_id=1, source_target_pairs={{2,0},{3,1},{4,2},{5,3},{6,4},{7,5},{0,6},{1,7},{10,8},{11,9},{12,... | collective-permute-start | bytes 417800 | tf_op jit(solution)/shard_map/ppermute | solution.py:47
  13.7 1.7 %collective-permute-start.1 = (f32[136,256]{1,0:T(8,128)S(1)}, f32[136,256]{1,0:T(8,128)S(1)}, u32[]{:S(2)}, u32[]{:S(2)}) collective-permute-start(f32[136,256]{1,0:T(8,128)S(1)} %copy-done), channel_id=1, source_target_pairs={{70,0},{71,1},{64,2},{65,3},{66,4},{67,5},{68,6},{69,7},{78,8},{79... | collective-permute-start | bytes 417800 | tf_op jit(solution)/shard_map/ppermute | solution.py:47
  15.5 1.8 %collective-permute-start = (f32[136,256]{1,0:T(8,128)S(1)}, f32[136,256]{1,0:T(8,128)S(1)}, u32[]{:S(2)}, u32[]{:S(2)}) collective-permute-start(f32[136,256]{1,0:T(8,128)S(1)} %copy-done), channel_id=1, source_target_pairs={{68,0},{69,1},{70,2},{71,3},{64,4},{65,5},{66,6},{67,7},{76,8},{77... | collective-permute-start | bytes 417800 | tf_op jit(solution)/shard_map/ppermute | solution.py:47
  17.3 1.5 %collective-permute-done.3.refs_4_ = f32[136,256]{1,0:T(8,128)S(1)} collective-permute-done((f32[136,256]{1,0:T(8,128)S(1)}, f32[136,256]{1,0:T(8,128)S(1)}, u32[]{:S(2)}, u32[]{:S(2)}) %collective-permute-start.3) | collective-permute-done | bytes 139296 | tf_op jit(solution)/shard_map/ppermute | solution.py:47
  18.9 2.2 %collective-permute-done.1.refs_2_ = f32[136,256]{1,0:T(8,128)S(1)} collective-permute-done((f32[136,256]{1,0:T(8,128)S(1)}, f32[136,256]{1,0:T(8,128)S(1)}, u32[]{:S(2)}, u32[]{:S(2)}) %collective-permute-start.1) | collective-permute-done | bytes 139296 | tf_op jit(solution)/shard_map/ppermute | solution.py:47
  21.1 3.0 %collective-permute-done.refs_1_ = f32[136,256]{1,0:T(8,128)S(1)} collective-permute-done((f32[136,256]{1,0:T(8,128)S(1)}, f32[136,256]{1,0:T(8,128)S(1)}, u32[]{:S(2)}, u32[]{:S(2)}) %collective-permute-start) | collective-permute-done | bytes 139296 | tf_op jit(solution)/shard_map/ppermute | solution.py:47
  24.0 1.2 %all-to-all-done.refs_6_ = f32[8,136,256]{2,1,0:T(8,128)S(1)} async-done(((f32[8,136,256]{2,1,0:T(8,128)}), f32[8,136,256]{2,1,0:T(8,128)S(1)}, u32[]{:S(2)}, u32[]{:S(2)}) %all-to-all-start) | async-done | bytes 1114144 | tf_op jit(solution)/shard_map/all_to_all | solution.py:40
  25.2 2.5 %collective-permute-start.7 = (f32[8,136,256]{2,1,0:T(8,128)S(1)}, f32[8,136,256]{2,1,0:T(8,128)S(1)}, u32[]{:S(2)}, u32[]{:S(2)}) collective-permute-start(f32[8,136,256]{2,1,0:T(8,128)S(1)} %all-to-all-done.refs_6_), channel_id=1, source_target_pairs={{0,1},{1,0},{2,3},{3,2},{4,5},{5,4},{6,7},{7,6},{8,9},{9,8},{10,11... | collective-permute-start | bytes 3342344 | tf_op jit(solution)/shard_map/ppermute | solution.py:264
  27.7 1.4 %collective-permute-start.6 = (f32[136,256]{1,0:T(8,128)S(1)}, f32[136,256]{1,0:T(8,128)S(1)}, u32[]{:S(2)}, u32[]{:S(2)}) collective-permute-start(f32[136,256]{1,0:T(8,128)S(1)} %copy-done), channel_id=1, source_target_pairs={{66,0},{67,1},{68,2},{69,3},{70,4},{71,5},{64,6},{65,7},{74,8},{75... | collective-permute-start | bytes 417800 | tf_op jit(solution)/shard_map/ppermute | solution.py:47
  29.1 2.5 %own_pairs.1 = (bf16[768,768]{1,0:T(8,128)(2,1)S(1)}, f32[768,1]{1,0:T(8,128)S(1)}, bf16[1024,768]{1,0:T(8,128)(2,1)S(1)}, f32[8,1024]{1,0:T(8,128)S(1)}, bf16[1...) custom-call(f32[136,256]{1,0:T(8,128)S(1)} %copy-done, ...), custom_call_target="tpu_custom_call" | custom-call | tf_op jit(solution)/shard_map/own_pairs/pallas_call | solution.py:247
  31.6 2.4 %other_pairs.1 = (bf16[1024,768]{1,0:T(8,128)(2,1)S(1)}, f32[8,1024]{1,0:T(8,128)S(1)}, bf16[1024,128]{1,0:T(8,128)(2,1)S(1)}, bf16[1024,1024]{1,0:T(8,128)(2,1)...) custom-call(f32[8,136,256]{2,1,0:T(8,128)S(1)} %collective-permute-done.7.columns, ...), custom_call_target="tpu_custom_call" | custom-call | tf_op jit(solution)/shard_map/other_pairs/pallas_call | solution.py:247
  34.0 1.3 %collective-permute-done.5.refs_6_ = f32[136,256]{1,0:T(8,128)S(1)} collective-permute-done((f32[136,256]{1,0:T(8,128)S(1)}, f32[136,256]{1,0:T(8,128)S(1)}, u32[]{:S(2)}, u32[]{:S(2)}) %collective-permute-start.5) | collective-permute-done | bytes 139296 | tf_op jit(solution)/shard_map/ppermute | solution.py:47
  35.3 1.8 %late_pairs.1 = (bf16[1024,1024]{1,0:T(8,128)(2,1)S(1)}, bf16[1024,1024]{1,0:T(8,128)(2,1)S(1)}, bf16[1024,1024]{1,0:T(8,128)(2,1)S(1)}, bf16[1024,1024]{1,0:T(8,128)(2,1)S(1)}, f32[8,136,128]{2,1,0:T(8,128)S(1)}) custom-call(f32[136,256]{1,0:T(8,128)S(1)} %copy-done, ...), custom_call_target="tpu_custom_call", output_to_operand_aliasing={{0}: (15, {}), {1}: (16, {}), {2}: (17, {}), {3}: (18, {})} | custom-call | tf_op jit(solution)/shard_map/late_pairs/pallas_call | solution.py:247
  37.1 14.0 %all_to_all.25.blocks = f32[8,136,128]{2,1,0:T(8,128)S(1)} all-to-all(f32[8,136,128]{2,1,0:T(8,128)S(1)} %get-tuple-element.65), channel_id=1, replica_groups=mesh['y_lo'=2,'z'=4,'y_hi'=2,'x'=4,'core'=2] {'y_lo','x'}, dimensions={0} | all-to-all | bytes 1114112 | tf_op jit(solution)/shard_map/all_to_all | solution.py:36
  51.2 12.4 %all_to_all.26.blocks = f32[8,136,128]{2,1,0:T(8,128)S(1)} all-to-all(f32[8,136,128]{2,1,0:T(8,128)S(1)} %get-tuple-element.66), channel_id=1, replica_groups={{0,16,32,48,72,88,104,120},{1,17,33,49,73,89,105,121},{2,18,34,50,74,90..., dimensions={0} | all-to-all | bytes 1114112 | tf_op jit(solution)/shard_map/all_to_all | solution.py:40
  63.6 3.6 %collective-permute-start.8 = (f32[8,128]{1,0:T(8,128)S(1)}, f32[8,128]{1,0:T(8,128)S(1)}, u32[]{:S(2)}, u32[]{:S(2)}) collective-permute-start(f32[8,128]{1,0:T(8,128)S(1)} %tails.1.tail), channel_id=1, source_target_pairs={{0,1},{1,0},{2,3},{3,2},{4,5},{5,4},{6,7},{7,6},{8,9},{9,8},{10,11... | collective-permute-start | bytes 12296 | tf_op jit(solution)/shard_map/ppermute | solution.py:264
  67.2 0.8 collective-permute-done.8.far_tail
  68.3 1.5 %own_members.1 = (f32[1024,128]{1,0:T(8,128)S(1)}, f32[8,128]{1,0:T(8,128)S(1)}, f32[128,128]{1,0:T(8,128)S(1)}) custom-call(f32[8,136,128]{2,1,0:T(8,128)S(1)} %all_to_all.26.blocks, f32[8,128]{1,0:T(8,128)S(1)} %tails.1.tail, f32[8,128]{1,0:T(8,128)S(1)} %collective-permute-done.8.far_tail, bf16[1024,1024]{1,0:T(8,128)(2,1)S(1)} %get-tuple-element.69.high, ...), custom_call_target="tpu_custom_call" | custom-call | tf_op jit(solution)/shard_map/own_members/pallas_call | solution.py:247
  70.0 1.6 %other_members.1 = f32[8,136,128]{2,1,0:T(8,128)S(1)} custom-call(f32[8,136,128]{2,1,0:T(8,128)S(1)} %collective-permute-done.9.blocks, f32[8,128]{1,0:T(8,128)S(1)} %get-tuple-element.72.sums, bf16[1024,1024]{1,0:T(8,128)(2,1)S(1)} %get-tuple-element.73.high, bf16[1024,1024]{1,0:T(8,128)(2,1)S(1)} %get-tuple-element.74.low, ...), custom_call_target="tpu_custom_call" | custom-call | tf_op jit(solution)/shard_map/other_members/pallas_call | solution.py:247
  71.5 12.9 %all_to_all.27.blocks = f32[8,136,128]{2,1,0:T(8,128)S(1)} all-to-all(f32[8,136,128]{2,1,0:T(8,128)S(1)} %other_members.1), channel_id=1, replica_groups=mesh['y_lo'=2,'z'=4,'y_hi'=2,'x'=4,'core'=2] {'y_lo','x'}, dimensions={0} | all-to-all | bytes 1114112 | tf_op jit(solution)/shard_map/all_to_all | solution.py:36
  84.5 13.9 %all_to_all.28 = f32[128,1,128]{2,1,0:T(1,128)S(1)} all-to-all(f32[128,1,128]{2,1,0:T(1,128)S(1)} %broadcast_in_dim.3), channel_id=1, replica_groups=mesh['y_lo'=2,'z'=4,'y_hi'=2,'x'=4,'core'=2] {'y_lo','z','y_hi','x','core'}, dimensions={0} | all-to-all | bytes 131072 | tf_op jit(solution)/shard_map/all_to_all | solution.py:336
  98.5 0.8 final.1
  (16 shorter events, 1.2 us)
Async XLA Ops:
  2.1 8.5 %copy-start = (f32[136,256]{1,0:T(8,128)S(1)}, f32[136,256]{1,0:T(8,128)}, u32[]{:S(2)}) copy-start(f32[136,256]{1,0:T(8,128)} %get-tuple-element.44.refs_0_) | copy-start | bytes 417796
  2.1 23.1 %all-to-all-start = ((f32[8,136,256]{2,1,0:T(8,128)}), f32[8,136,256]{2,1,0:T(8,128)S(1)}, u32[]{:S(2)}, u32[]{:S(2)}) async-start(f32[8,136,256]{2,1,0:T(8,128)} %get-tuple-element.42), calls=%async_computation | async-start | bytes 2228224 | tf_op jit(solution)/shard_map/all_to_all | solution.py:40
  10.6 6.7 %collective-permute-start.4 = (f32[136,256]{1,0:T(8,128)S(1)}, f32[136,256]{1,0:T(8,128)S(1)}, u32[]{:S(2)}, u32[]{:S(2)}) collective-permute-start(f32[136,256]{1,0:T(8,128)S(1)} %copy-done), channel_id=1, source_target_pairs={{2,0},{3,1},{4,2},{5,3},{6,4},{7,5},{0,6},{1,7},{10,8},{11,9},{12,... | collective-permute-start | bytes 417800 | tf_op jit(solution)/shard_map/ppermute | solution.py:47
  13.1 5.7 %collective-permute-start.3 = (f32[136,256]{1,0:T(8,128)S(1)}, f32[136,256]{1,0:T(8,128)S(1)}, u32[]{:S(2)}, u32[]{:S(2)}) collective-permute-start(f32[136,256]{1,0:T(8,128)S(1)} %copy-done), channel_id=1, source_target_pairs={{4,0},{5,1},{6,2},{7,3},{0,4},{1,5},{2,6},{3,7},{12,8},{13,9},{14,... | collective-permute-start | bytes 417800 | tf_op jit(solution)/shard_map/ppermute | solution.py:47
  13.7 5.2 %collective-permute-start.2 = (f32[136,256]{1,0:T(8,128)S(1)}, f32[136,256]{1,0:T(8,128)S(1)}, u32[]{:S(2)}, u32[]{:S(2)}) collective-permute-start(f32[136,256]{1,0:T(8,128)S(1)} %copy-done), channel_id=1, source_target_pairs={{64,0},{65,1},{66,2},{67,3},{68,4},{69,5},{70,6},{71,7},{72,8},{73... | collective-permute-start | bytes 417800 | tf_op jit(solution)/shard_map/ppermute | solution.py:47
  13.7 7.3 %collective-permute-start.1 = (f32[136,256]{1,0:T(8,128)S(1)}, f32[136,256]{1,0:T(8,128)S(1)}, u32[]{:S(2)}, u32[]{:S(2)}) collective-permute-start(f32[136,256]{1,0:T(8,128)S(1)} %copy-done), channel_id=1, source_target_pairs={{70,0},{71,1},{64,2},{65,3},{66,4},{67,5},{68,6},{69,7},{78,8},{79... | collective-permute-start | bytes 417800 | tf_op jit(solution)/shard_map/ppermute | solution.py:47
  15.5 8.6 %collective-permute-start = (f32[136,256]{1,0:T(8,128)S(1)}, f32[136,256]{1,0:T(8,128)S(1)}, u32[]{:S(2)}, u32[]{:S(2)}) collective-permute-start(f32[136,256]{1,0:T(8,128)S(1)} %copy-done), channel_id=1, source_target_pairs={{68,0},{69,1},{70,2},{71,3},{64,4},{65,5},{66,6},{67,7},{76,8},{77... | collective-permute-start | bytes 417800 | tf_op jit(solution)/shard_map/ppermute | solution.py:47
  25.2 6.4 %collective-permute-start.7 = (f32[8,136,256]{2,1,0:T(8,128)S(1)}, f32[8,136,256]{2,1,0:T(8,128)S(1)}, u32[]{:S(2)}, u32[]{:S(2)}) collective-permute-start(f32[8,136,256]{2,1,0:T(8,128)S(1)} %all-to-all-done.refs_6_), channel_id=1, source_target_pairs={{0,1},{1,0},{2,3},{3,2},{4,5},{5,4},{6,7},{7,6},{8,9},{9,8},{10,11... | collective-permute-start | bytes 3342344 | tf_op jit(solution)/shard_map/ppermute | solution.py:264
  27.7 6.3 %collective-permute-start.6 = (f32[136,256]{1,0:T(8,128)S(1)}, f32[136,256]{1,0:T(8,128)S(1)}, u32[]{:S(2)}, u32[]{:S(2)}) collective-permute-start(f32[136,256]{1,0:T(8,128)S(1)} %copy-done), channel_id=1, source_target_pairs={{66,0},{67,1},{68,2},{69,3},{70,4},{71,5},{64,6},{65,7},{74,8},{75... | collective-permute-start | bytes 417800 | tf_op jit(solution)/shard_map/ppermute | solution.py:47
  29.1 6.2 %collective-permute-start.5 = (f32[136,256]{1,0:T(8,128)S(1)}, f32[136,256]{1,0:T(8,128)S(1)}, u32[]{:S(2)}, u32[]{:S(2)}) collective-permute-start(f32[136,256]{1,0:T(8,128)S(1)} %copy-done), channel_id=1, source_target_pairs={{6,0},{7,1},{0,2},{1,3},{2,4},{3,5},{4,6},{5,7},{14,8},{15,9},{8,1... | collective-permute-start | bytes 417800 | tf_op jit(solution)/shard_map/ppermute | solution.py:47
  63.6 4.4 %collective-permute-start.8 = (f32[8,128]{1,0:T(8,128)S(1)}, f32[8,128]{1,0:T(8,128)S(1)}, u32[]{:S(2)}, u32[]{:S(2)}) collective-permute-start(f32[8,128]{1,0:T(8,128)S(1)} %tails.1.tail), channel_id=1, source_target_pairs={{0,1},{1,0},{2,3},{3,2},{4,5},{5,4},{6,7},{7,6},{8,9},{9,8},{10,11... | collective-permute-start | bytes 12296 | tf_op jit(solution)/shard_map/ppermute | solution.py:264
  68.0 2.0 %collective-permute-start.9 = (f32[8,136,128]{2,1,0:T(8,128)S(1)}, f32[8,136,128]{2,1,0:T(8,128)S(1)}, u32[]{:S(2)}, u32[]{:S(2)}) collective-permute-start(f32[8,136,128]{2,1,0:T(8,128)S(1)} %all_to_all.26.blocks), channel_id=1, source_target_pairs={{0,1},{1,0},{2,3},{3,2},{4,5},{5,4},{6,7},{7,6},{8,9},{9,8},{10,11... | collective-permute-start | bytes 1671176 | tf_op jit(solution)/shard_map/ppermute | solution.py:264

commit v25 on v23

--- a/solution.py
+++ b/solution.py
@@ -29,7 +29,7 @@
 
 
 COLUMN_GROUPS = column_groups()
-ROW_ORDER = ((0, 0), (1, 2), (1, 3), (1, 0), (0, 2), (0, 1), (0, 3), (1, 1))
+ROW_ORDER = ((0, 0), (1, 2), (1, 3), (1, 1), (0, 2), (0, 3), (1, 0), (0, 1))
 
 
 def exchange_rows(blocks):

time: 99.5 us -> 100 us (level)
  waiting for transfers between devices: 10.8 us -> 9.55 us
  starting transfers between devices: 22.6 us -> 23.7 us
    all_to_all x1, blocking collectives: 12.4 us -> 15 us  [exchange_columns(): lax.all_to_all(blocks, EVERY, 0, 0, axis_index_groups=COLUMN_GROUPS, tile...]
    all_to_all x2, blocking collectives: 26.9 us -> 25 us  [exchange_rows(): return lax.all_to_all(blocks, ('y_lo', 'x'), 0, 0, tiled=True)]
    all_to_all x1, waiting for transfers between devices: 1.18 us -> 0.01 us  [exchange_columns(): lax.all_to_all(blocks, EVERY, 0, 0, axis_index_groups=COLUMN_GROUPS, tile...]
    ppermute x7, starting transfers between devices: 8.13 us -> 9.29 us  [moved(): return lax.ppermute(x, EVERY, pairs)]
  transfers between devices with their start and end apart: 10 -> 10, of which waited for: 6 -> 4; matrix products, arithmetic and copies ran while one was open for 0% -> 0% of each run, Pallas kernels for 5% -> 5%
where the time goes in v25:
time: 100 us; the launch traced here: 99.8 us
  blocking collectives  54 us (54%)
  starting transfers between devices  23.7 us (24%)
  Pallas kernels  12.4 us (12%)
  waiting for transfers between devices  9.55 us (10%)
    all_to_all x2, blocking collectives, exchange_rows(): return lax.all_to_all(blocks, ('y_lo', 'x'), 0, 0, tiled=True)  25 us
    all_to_all x1, blocking collectives, exchange_columns(): lax.all_to_all(blocks, EVERY, 0, 0, axis_index_groups=COLUMN_GROUPS, tile...  15 us
    all_to_all x1, blocking collectives, shards(): parts = lax.all_to_all(copies(part, 128), EVERY, 0, 0, tiled=True)  14 us
    pallas_call x7, Pallas kernels, on_chip(): pl.pallas_call(kernel, out_shape=shapes, in_specs=specs, out_specs=[vmem]...  10.3 us
    ppermute x7, starting transfers between devices, moved(): return lax.ppermute(x, EVERY, pairs)  9.29 us
    all_to_all x1, starting transfers between devices, exchange_columns(): lax.all_to_all(blocks, EVERY, 0, 0, axis_index_groups=COLUMN_GROUPS, tile...  8.46 us
    ppermute x7, waiting for transfers between devices, moved(): return lax.ppermute(x, EVERY, pairs)  7.96 us
    ppermute x2, starting transfers between devices, other_core(): return lax.ppermute(x, 'core', [(0, 1), (1, 0)])  5.92 us
  transfers between devices with their start and end apart: 10, of which 4 were waited for; matrix products, arithmetic and copies ran while one was open for 0% of the time, Pallas kernels for 5%

profile of v25, /device:TPU:1, one launch (start us, length us, event | category | flops | bytes accessed | tf_op | source)
XLA Modules:
  0.0 99.8 jit_solution(12583472171025743739)
XLA Ops:
  0.0 2.1 %prepare.1 = (f32[136,256]{1,0:T(8,128)}, f32[8,136,256]{2,1,0:T(8,128)}) custom-call(f32[128,256]{1,0:T(8,128)} %embedding.1, s32[1,128]{1,0:T(1,128)} %bitcast.7), custom_call_target="tpu_custom_call" | custom-call | tf_op jit(solution)/shard_map/prepare/pallas_call | solution.py:266
  2.1 8.5 %all-to-all-start = ((f32[8,136,256]{2,1,0:T(8,128)}), f32[8,136,256]{2,1,0:T(8,128)S(1)}, u32[]{:S(2)}, u32[]{:S(2)}) async-start(f32[8,136,256]{2,1,0:T(8,128)} %get-tuple-element.39), calls=%async_computation | async-start | bytes 2228224 | tf_op jit(solution)/shard_map/all_to_all | solution.py:40
  10.6 1.3 %collective-permute-start.4 = (f32[136,256]{1,0:T(8,128)S(1)}, f32[136,256]{1,0:T(8,128)S(1)}, u32[]{:S(2)}, u32[]{:S(2)}) collective-permute-start(f32[136,256]{1,0:T(8,128)S(1)} %copy-done), channel_id=1, source_target_pairs={{6,0},{7,1},{0,2},{1,3},{2,4},{3,5},{4,6},{5,7},{14,8},{15,9},{8,1... | collective-permute-start | bytes 417800 | tf_op jit(solution)/shard_map/ppermute | solution.py:47
  11.9 2.5 %collective-permute-start.3 = (f32[136,256]{1,0:T(8,128)S(1)}, f32[136,256]{1,0:T(8,128)S(1)}, u32[]{:S(2)}, u32[]{:S(2)}) collective-permute-start(f32[136,256]{1,0:T(8,128)S(1)} %copy-done), channel_id=1, source_target_pairs={{4,0},{5,1},{6,2},{7,3},{0,4},{1,5},{2,6},{3,7},{12,8},{13,9},{14,... | collective-permute-start | bytes 417800 | tf_op jit(solution)/shard_map/ppermute | solution.py:47
  14.3 0.9 collective-permute-start.2
  15.3 1.4 %collective-permute-start.1 = (f32[136,256]{1,0:T(8,128)S(1)}, f32[136,256]{1,0:T(8,128)S(1)}, u32[]{:S(2)}, u32[]{:S(2)}) collective-permute-start(f32[136,256]{1,0:T(8,128)S(1)} %copy-done), channel_id=1, source_target_pairs={{70,0},{71,1},{64,2},{65,3},{66,4},{67,5},{68,6},{69,7},{78,8},{79... | collective-permute-start | bytes 417800 | tf_op jit(solution)/shard_map/ppermute | solution.py:47
  16.7 0.9 collective-permute-start
  17.6 2.5 %collective-permute-done.3.refs_4_ = f32[136,256]{1,0:T(8,128)S(1)} collective-permute-done((f32[136,256]{1,0:T(8,128)S(1)}, f32[136,256]{1,0:T(8,128)S(1)}, u32[]{:S(2)}, u32[]{:S(2)}) %collective-permute-start.3) | collective-permute-done | bytes 139296 | tf_op jit(solution)/shard_map/ppermute | solution.py:47
  20.1 3.9 %collective-permute-done.1.refs_2_ = f32[136,256]{1,0:T(8,128)S(1)} collective-permute-done((f32[136,256]{1,0:T(8,128)S(1)}, f32[136,256]{1,0:T(8,128)S(1)}, u32[]{:S(2)}, u32[]{:S(2)}) %collective-permute-start.1) | collective-permute-done | bytes 139296 | tf_op jit(solution)/shard_map/ppermute | solution.py:47
  24.0 1.6 %collective-permute-done.refs_1_ = f32[136,256]{1,0:T(8,128)S(1)} collective-permute-done((f32[136,256]{1,0:T(8,128)S(1)}, f32[136,256]{1,0:T(8,128)S(1)}, u32[]{:S(2)}, u32[]{:S(2)}) %collective-permute-start) | collective-permute-done | bytes 139296 | tf_op jit(solution)/shard_map/ppermute | solution.py:47
  25.5 2.4 %collective-permute-start.7 = (f32[8,136,256]{2,1,0:T(8,128)S(1)}, f32[8,136,256]{2,1,0:T(8,128)S(1)}, u32[]{:S(2)}, u32[]{:S(2)}) collective-permute-start(f32[8,136,256]{2,1,0:T(8,128)S(1)} %all-to-all-done.refs_6_), channel_id=1, source_target_pairs={{0,1},{1,0},{2,3},{3,2},{4,5},{5,4},{6,7},{7,6},{8,9},{9,8},{10,11... | collective-permute-start | bytes 3342344 | tf_op jit(solution)/shard_map/ppermute | solution.py:252
  28.0 2.2 %collective-permute-start.6 = (f32[136,256]{1,0:T(8,128)S(1)}, f32[136,256]{1,0:T(8,128)S(1)}, u32[]{:S(2)}, u32[]{:S(2)}) collective-permute-start(f32[136,256]{1,0:T(8,128)S(1)} %copy-done), channel_id=1, source_target_pairs={{2,0},{3,1},{4,2},{5,3},{6,4},{7,5},{0,6},{1,7},{10,8},{11,9},{12,... | collective-permute-start | bytes 417800 | tf_op jit(solution)/shard_map/ppermute | solution.py:47
  30.2 0.1 collective-permute-start.5
  30.3 2.5 %own_pairs.1 = (bf16[768,768]{1,0:T(8,128)(2,1)S(1)}, f32[768,1]{1,0:T(8,128)S(1)}, bf16[1024,768]{1,0:T(8,128)(2,1)S(1)}, f32[8,1024]{1,0:T(8,128)S(1)}, bf16[1...) custom-call(f32[136,256]{1,0:T(8,128)S(1)} %copy-done, ...), custom_call_target="tpu_custom_call" | custom-call | tf_op jit(solution)/shard_map/own_pairs/pallas_call | solution.py:235
  32.8 2.4 %other_pairs.1 = (bf16[1024,768]{1,0:T(8,128)(2,1)S(1)}, f32[8,1024]{1,0:T(8,128)S(1)}, bf16[1024,128]{1,0:T(8,128)(2,1)S(1)}, bf16[1024,1024]{1,0:T(8,128)(2,1)...) custom-call(f32[8,136,256]{2,1,0:T(8,128)S(1)} %collective-permute-done.7.columns, ...), custom_call_target="tpu_custom_call" | custom-call | tf_op jit(solution)/shard_map/other_pairs/pallas_call | solution.py:235
  35.2 1.9 %late_pairs.1 = (bf16[1024,1024]{1,0:T(8,128)(2,1)S(1)}, bf16[1024,1024]{1,0:T(8,128)(2,1)S(1)}, bf16[1024,1024]{1,0:T(8,128)(2,1)S(1)}, bf16[1024,1024]{1,0:T(8,128)(2,1)S(1)}, f32[8,136,128]{2,1,0:T(8,128)S(1)}) custom-call(f32[136,256]{1,0:T(8,128)S(1)} %copy-done, ...), custom_call_target="tpu_custom_call", output_to_operand_aliasing={{0}: (15, {}), {1}: (16, {}), {2}: (17, {}), {3}: (18, {})} | custom-call | tf_op jit(solution)/shard_map/late_pairs/pallas_call | solution.py:235
  37.0 12.1 %all_to_all.25.blocks = f32[8,136,128]{2,1,0:T(8,128)S(1)} all-to-all(f32[8,136,128]{2,1,0:T(8,128)S(1)} %get-tuple-element.62), channel_id=1, replica_groups=mesh['y_lo'=2,'z'=4,'y_hi'=2,'x'=4,'core'=2] {'y_lo','x'}, dimensions={0} | all-to-all | bytes 1114112 | tf_op jit(solution)/shard_map/all_to_all | solution.py:36
  49.2 15.0 %all_to_all.26.own = f32[8,136,128]{2,1,0:T(8,128)S(1)} all-to-all(f32[8,136,128]{2,1,0:T(8,128)S(1)} %get-tuple-element.63), channel_id=1, replica_groups={{0,16,32,48,72,88,104,120},{1,17,33,49,73,89,105,121},{2,18,34,50,74,90..., dimensions={0} | all-to-all | bytes 1114112 | tf_op jit(solution)/shard_map/all_to_all | solution.py:40
  64.2 3.5 %collective-permute-start.8 = (f32[8,136,128]{2,1,0:T(8,128)S(1)}, f32[8,136,128]{2,1,0:T(8,128)S(1)}, u32[]{:S(2)}, u32[]{:S(2)}) collective-permute-start(f32[8,136,128]{2,1,0:T(8,128)S(1)} %all_to_all.26.own), channel_id=1, source_target_pairs={{0,1},{1,0},{2,3},{3,2},{4,5},{5,4},{6,7},{7,6},{8,9},{9,8},{10,11... | collective-permute-start | bytes 1671176 | tf_op jit(solution)/shard_map/ppermute | solution.py:252
  67.7 1.6 %collective-permute-done.8.other = f32[8,136,128]{2,1,0:T(8,128)S(1)} collective-permute-done((f32[8,136,128]{2,1,0:T(8,128)S(1)}, f32[8,136,128]{2,1,0:T(8,128)S(1)}, u32[]{:S(2)}, u32[]{:S(2)}) %collective-permute-start.8) | collective-permute-done | bytes 557088 | tf_op jit(solution)/shard_map/ppermute | solution.py:252
  69.3 2.7 %members.1 = (f32[8,136,128]{2,1,0:T(8,128)S(1)}, f32[128,128]{1,0:T(8,128)S(1)}) custom-call(f32[8,136,128]{2,1,0:T(8,128)S(1)} %all_to_all.26.own, f32[8,136,128]{2,1,0:T(8,128)S(1)} %collective-permute-done.8.other, bf16[1024,1024]{1,0:T(8,128)(2,1)S(1)} %get-tuple-element.64.own_high, bf16[1024,1024]{1,0:T(8,128)(2,1)S(1)} %get-tuple-element.65.own_low, ...), custom_call_target="tpu_custom_call" | custom-call | tf_op jit(solution)/shard_map/members/pallas_call | solution.py:235
  72.0 12.9 %all_to_all.27.blocks = f32[8,136,128]{2,1,0:T(8,128)S(1)} all-to-all(f32[8,136,128]{2,1,0:T(8,128)S(1)} %get-tuple-element.69), channel_id=1, replica_groups=mesh['y_lo'=2,'z'=4,'y_hi'=2,'x'=4,'core'=2] {'y_lo','x'}, dimensions={0} | all-to-all | bytes 1114112 | tf_op jit(solution)/shard_map/all_to_all | solution.py:36
  85.0 14.0 %all_to_all.28 = f32[128,1,128]{2,1,0:T(1,128)S(1)} all-to-all(f32[128,1,128]{2,1,0:T(1,128)S(1)} %broadcast_in_dim.3), channel_id=1, replica_groups=mesh['y_lo'=2,'z'=4,'y_hi'=2,'x'=4,'core'=2] {'y_lo','z','y_hi','x','core'}, dimensions={0} | all-to-all | bytes 131072 | tf_op jit(solution)/shard_map/all_to_all | solution.py:312
  99.0 0.8 final.1
  (12 shorter events, 0.2 us)
Async XLA Ops:
  2.1 8.5 %copy-start = (f32[136,256]{1,0:T(8,128)S(1)}, f32[136,256]{1,0:T(8,128)}, u32[]{:S(2)}) copy-start(f32[136,256]{1,0:T(8,128)} %get-tuple-element.41.refs_0_) | copy-start | bytes 417796
  2.1 23.4 %all-to-all-start = ((f32[8,136,256]{2,1,0:T(8,128)}), f32[8,136,256]{2,1,0:T(8,128)S(1)}, u32[]{:S(2)}, u32[]{:S(2)}) async-start(f32[8,136,256]{2,1,0:T(8,128)} %get-tuple-element.39), calls=%async_computation | async-start | bytes 2228224 | tf_op jit(solution)/shard_map/all_to_all | solution.py:40
  10.6 7.0 %collective-permute-start.4 = (f32[136,256]{1,0:T(8,128)S(1)}, f32[136,256]{1,0:T(8,128)S(1)}, u32[]{:S(2)}, u32[]{:S(2)}) collective-permute-start(f32[136,256]{1,0:T(8,128)S(1)} %copy-done), channel_id=1, source_target_pairs={{6,0},{7,1},{0,2},{1,3},{2,4},{3,5},{4,6},{5,7},{14,8},{15,9},{8,1... | collective-permute-start | bytes 417800 | tf_op jit(solution)/shard_map/ppermute | solution.py:47
  11.9 8.2 %collective-permute-start.3 = (f32[136,256]{1,0:T(8,128)S(1)}, f32[136,256]{1,0:T(8,128)S(1)}, u32[]{:S(2)}, u32[]{:S(2)}) collective-permute-start(f32[136,256]{1,0:T(8,128)S(1)} %copy-done), channel_id=1, source_target_pairs={{4,0},{5,1},{6,2},{7,3},{0,4},{1,5},{2,6},{3,7},{12,8},{13,9},{14,... | collective-permute-start | bytes 417800 | tf_op jit(solution)/shard_map/ppermute | solution.py:47
  14.3 5.7 %collective-permute-start.2 = (f32[136,256]{1,0:T(8,128)S(1)}, f32[136,256]{1,0:T(8,128)S(1)}, u32[]{:S(2)}, u32[]{:S(2)}) collective-permute-start(f32[136,256]{1,0:T(8,128)S(1)} %copy-done), channel_id=1, source_target_pairs={{66,0},{67,1},{68,2},{69,3},{70,4},{71,5},{64,6},{65,7},{74,8},{75... | collective-permute-start | bytes 417800 | tf_op jit(solution)/shard_map/ppermute | solution.py:47
  15.3 8.7 %collective-permute-start.1 = (f32[136,256]{1,0:T(8,128)S(1)}, f32[136,256]{1,0:T(8,128)S(1)}, u32[]{:S(2)}, u32[]{:S(2)}) collective-permute-start(f32[136,256]{1,0:T(8,128)S(1)} %copy-done), channel_id=1, source_target_pairs={{70,0},{71,1},{64,2},{65,3},{66,4},{67,5},{68,6},{69,7},{78,8},{79... | collective-permute-start | bytes 417800 | tf_op jit(solution)/shard_map/ppermute | solution.py:47
  16.7 8.8 %collective-permute-start = (f32[136,256]{1,0:T(8,128)S(1)}, f32[136,256]{1,0:T(8,128)S(1)}, u32[]{:S(2)}, u32[]{:S(2)}) collective-permute-start(f32[136,256]{1,0:T(8,128)S(1)} %copy-done), channel_id=1, source_target_pairs={{68,0},{69,1},{70,2},{71,3},{64,4},{65,5},{66,6},{67,7},{76,8},{77... | collective-permute-start | bytes 417800 | tf_op jit(solution)/shard_map/ppermute | solution.py:47
  25.5 7.2 %collective-permute-start.7 = (f32[8,136,256]{2,1,0:T(8,128)S(1)}, f32[8,136,256]{2,1,0:T(8,128)S(1)}, u32[]{:S(2)}, u32[]{:S(2)}) collective-permute-start(f32[8,136,256]{2,1,0:T(8,128)S(1)} %all-to-all-done.refs_6_), channel_id=1, source_target_pairs={{0,1},{1,0},{2,3},{3,2},{4,5},{5,4},{6,7},{7,6},{8,9},{9,8},{10,11... | collective-permute-start | bytes 3342344 | tf_op jit(solution)/shard_map/ppermute | solution.py:252
  28.0 7.2 %collective-permute-start.6 = (f32[136,256]{1,0:T(8,128)S(1)}, f32[136,256]{1,0:T(8,128)S(1)}, u32[]{:S(2)}, u32[]{:S(2)}) collective-permute-start(f32[136,256]{1,0:T(8,128)S(1)} %copy-done), channel_id=1, source_target_pairs={{2,0},{3,1},{4,2},{5,3},{6,4},{7,5},{0,6},{1,7},{10,8},{11,9},{12,... | collective-permute-start | bytes 417800 | tf_op jit(solution)/shard_map/ppermute | solution.py:47
  30.2 5.0 %collective-permute-start.5 = (f32[136,256]{1,0:T(8,128)S(1)}, f32[136,256]{1,0:T(8,128)S(1)}, u32[]{:S(2)}, u32[]{:S(2)}) collective-permute-start(f32[136,256]{1,0:T(8,128)S(1)} %copy-done), channel_id=1, source_target_pairs={{64,0},{65,1},{66,2},{67,3},{68,4},{69,5},{70,6},{71,7},{72,8},{73... | collective-permute-start | bytes 417800 | tf_op jit(solution)/shard_map/ppermute | solution.py:47
  64.2 5.1 %collective-permute-start.8 = (f32[8,136,128]{2,1,0:T(8,128)S(1)}, f32[8,136,128]{2,1,0:T(8,128)S(1)}, u32[]{:S(2)}, u32[]{:S(2)}) collective-permute-start(f32[8,136,128]{2,1,0:T(8,128)S(1)} %all_to_all.26.own), channel_id=1, source_target_pairs={{0,1},{1,0},{2,3},{3,2},{4,5},{5,4},{6,7},{7,6},{8,9},{9,8},{10,11... | collective-permute-start | bytes 1671176 | tf_op jit(solution)/shard_map/ppermute | solution.py:252
